TPU v7x, 256 devices: a whole 4x4x8 slice. The times are simulated.
256 devices in a mesh: gx: 2 (over core), gy: 8 (over z), gz: 16 (over y, x).
Axes of the slice: x: 4, y: 4, z: 8, core: 2. Of those that a mesh axis runs over, the one named last changes fastest.
Arguments:
- residual: float32 [32, 128, 4096], P('gx', 'gy', 'gz'), may hold values from -6 to 6
- fdm_vectors: bfloat16 [2, 8, 16, 3, 10, 10, 128], P('gx', 'gy', 'gz'), may hold values from -2 to 2
- fdm_eigen: float32 [2, 8, 16, 3, 10, 128], P('gx', 'gy', 'gz'), may hold values from 0.1 to 4
- coarse_basis: float32 [8, 8, 8], replicated, may hold values from -0.75 to 0.75
- x_interior: float32 [2, 8, 16, 16, 16], P('gx', 'gy', 'gz'), may hold values from -1.5 to 1.5
- x_separator: float32 [2, 8, 16, 8, 16, 256], P('gx', 'gy', 'gz'), may hold values from -0.375 to 0.375
Outputs:
- preconditioned: float32 [32, 128, 4096], P('gx', 'gy', 'gz')
All inputs are finite; a program needn't handle non-finite values.
Results may differ from a plain program's by a relative error of at most 0.0003.
Values sent between devices are 32-bit elements; how exact they have to be, the bound alone decides.
No kernel may reach another device: no remote copies, remote signals or barrier semaphores. Data moves between devices by JAX's collectives and lax.ppermute only.
A program may use at most 128 MiB of HBM per device.

v0:
```python
import functools

import jax
import jax.numpy as jnp
from jax import lax
from jax.experimental import pallas as pl
from jax.experimental.pallas import tpu as pltpu
from jax.sharding import PartitionSpec as P

F32 = jnp.float32
VM = pl.BlockSpec(memory_space=pltpu.VMEM)


def iotas(rows=8):
    lane = lax.broadcasted_iota(jnp.int32, (rows, 128), 1)
    sub = lax.broadcasted_iota(jnp.int32, (rows, 128), 0)
    return lane, sub


def roll(value, shift):
    shift = shift % 128
    return value if shift == 0 else pltpu.roll(value, shift, value.ndim - 1)


def row(ref, index, rows=8):
    return jnp.broadcast_to(ref[pl.ds(index, 1), :], (rows, 128))


def total(terms):
    terms = list(terms)
    while len(terms) > 1:
        terms = [a + b for a, b in zip(terms[::2], terms[1::2])] + terms[len(terms) & ~1 :]
    return terms[0]


def chain(pairs):
    acc = None
    for a, b in pairs:
        acc = a * b if acc is None else acc + a * b
    return acc


def pre_kernel(x_ref, xface_ref, basis_ref, own_ref, sep_ref, e_ref, za_ref, zb_ref, part_ref, ownsol_ref, xt, ft):
    gx = lax.axis_index("gx")
    even = lax.rem(lax.axis_index("gz"), 2) == 0
    lane, _ = iotas()
    low_q = (lane & 32) == 0
    high_p = lane >= 64
    slot = lane & 31
    turned = x_ref[...].T
    xt[0] = turned[:, :128]
    xt[1] = turned[:, 128:]
    face = jnp.concatenate([xface_ref[...], jnp.zeros((112, 256), F32)], 0).T
    ft[...] = face
    for pair in range(4):
        k0, k1 = 2 * pair, 2 * pair + 1
        pieces = [xt[p, pl.ds(k, 32, stride=8), :] for p in range(2) for k in (k0, k1)]
        block = jnp.concatenate(pieces, 0).T
        for i in range(8):
            a = block[i * 16 : i * 16 + 8]
            b = block[i * 16 + 8 : i * 16 + 16]
            e_ref[i + 1, k0] = jnp.where(low_q, a, roll(b, 32))
            e_ref[i + 1, k1] = jnp.where(low_q, roll(a, 96), b)
    for half in range(2):
        pieces = [ft[pl.ds(half * 4 + k, 32, stride=8), :] for k in range(4)]
        block = jnp.concatenate(pieces, 0).T
        a, b = block[:8], block[8:16]
        for t in range(4):
            k = half * 4 + t
            got = jnp.where(low_q, roll(a, -32 * t), roll(b, 32 - 32 * t))
            below = jnp.where(gx == 1, got, 0.0)
            above = jnp.where(gx == 0, roll(got, 64), 0.0)
            e_ref[0, k] = jnp.where(high_p, roll(e_ref[8, k], 64), below)
            e_ref[9, k] = jnp.where(high_p, above, roll(e_ref[1, k], 64))
    upper = jnp.zeros((8, 128), F32)
    lower = jnp.zeros((8, 128), F32)
    for i in range(10):
        upper = jnp.where(slot == i, roll(e_ref[i, 7], i - 31), upper)
        lower = jnp.where(slot == i, roll(e_ref[i, 0], i), lower)
    za_ref[...] = jnp.where(even, upper, lower)
    zb_ref[...] = jnp.where(even, lower, upper)
    sums = []
    for i in range(8):
        weights = basis_ref[i]
        sums.append(chain((e_ref[i + 1, k], jnp.broadcast_to(weights[:, k : k + 1], (8, 128))) for k in range(8)))
    lanes = jnp.sum(total(sums), axis=0, keepdims=True)
    lane16, sub16 = iotas(16)
    spread = jnp.where(((lane16 & 31) >> 1) == sub16, jnp.broadcast_to(lanes, (16, 128)), 0.0)
    rhs = jnp.sum(spread, axis=1, keepdims=True)
    for level in range(sep_ref.shape[0]):
        part_ref[level : level + 1, :] = jnp.sum(sep_ref[level] * rhs, axis=0, keepdims=True)
    own = own_ref[...]
    coef = jnp.sum(own * rhs, axis=0, keepdims=True)
    ownsol_ref[...] = jnp.broadcast_to(jnp.sum(own * coef, axis=1, keepdims=True), (16, 128))


def z_halo(e_ref, za_ref, zb_ref, even, slot):
    from_above = jnp.where(even, za_ref[...], zb_ref[...])
    from_below = jnp.where(even, zb_ref[...], za_ref[...])
    first, last = [], []
    for i in range(10):
        first.append(jnp.where(slot == 0, roll(from_below, -i), roll(e_ref[i, 7], 1)))
        last.append(jnp.where(slot == 31, roll(from_above, 31 - i), roll(e_ref[i, 0], -1)))
    return first, last


def y_rows(first, last, e2_ref, scr):
    for i in range(10):
        scr[pl.ds(i * 8, 8), :] = first[i]
        scr[pl.ds(128 + i * 8, 8), :] = last[i]
    low = [e2_ref[pl.ds(i * 64, 8, stride=8), :] for i in range(10)]
    high = [e2_ref[pl.ds(i * 64 + 7, 8, stride=8), :] for i in range(10)]
    low_ends = [scr[pl.ds(b, 16, stride=8), :] for b in (0, 128)]
    high_ends = [scr[pl.ds(b + 7, 16, stride=8), :] for b in (0, 128)]
    return low, high, low_ends, high_ends


def yface_kernel(e_ref, e2_ref, za_ref, zb_ref, ya_ref, yb_ref, scr):
    even_z = lax.rem(lax.axis_index("gz"), 2) == 0
    even_y = lax.rem(lax.axis_index("gy"), 2) == 0
    lane, _ = iotas()
    low_q = (lane & 32) == 0
    first, last = z_halo(e_ref, za_ref, zb_ref, even_z, lane & 31)
    low, high, low_ends, high_ends = y_rows(first, last, e2_ref, scr)
    for i in range(5):
        down = jnp.where(low_q, low[i], roll(low[i + 5], 32))
        up = jnp.where(low_q, roll(high[i + 5], 96), high[i])
        ya_ref[i * 8 : i * 8 + 8] = jnp.where(even_y, up, down)
        yb_ref[i * 8 : i * 8 + 8] = jnp.where(even_y, down, up)
    low_q = (iotas(16)[0] & 32) == 0
    down = jnp.where(low_q, low_ends[0], roll(low_ends[1], 32))
    up = jnp.where(low_q, roll(high_ends[1], 96), high_ends[0])
    ya_ref[40:56] = jnp.where(even_y, up, down)
    yb_ref[40:56] = jnp.where(even_y, down, up)


def solve_kernel(
    e_ref, e2_ref, za_ref, zb_ref, ya_ref, yb_ref, vec_ref, eig_ref,
    l_ref, hl_ref, hh_ref, xs_ref, core, jl, jh, u, s, eg, scr,
):
    gx = lax.axis_index("gx")
    even_z = lax.rem(lax.axis_index("gz"), 2) == 0
    even_y = lax.rem(lax.axis_index("gy"), 2) == 0
    lane, sub = iotas()
    low_q = (lane & 32) == 0
    first, last = z_halo(e_ref, za_ref, zb_ref, even_z, lane & 31)
    low, high, low_ends, high_ends = y_rows(first, last, e2_ref, scr)
    for i in range(10):
        core[pl.ds(i * 80, 8), :] = first[i]
        core[pl.ds(i * 80 + 72, 8), :] = last[i]
        for k in range(8):
            core[pl.ds(i * 80 + 8 + k * 8, 8), :] = e_ref[i, k]
    for i in range(10):
        at = (i % 5) * 8
        a = ya_ref[at : at + 8]
        b = yb_ref[at : at + 8]
        above = jnp.where(even_y, a, b)
        below = jnp.where(even_y, b, a)
        if i < 5:
            above, below = roll(above, 32), roll(below, 96)
        jl[pl.ds(i * 8, 8), :] = jnp.where(low_q, below, roll(high[i], 32))
        jh[pl.ds(i * 8, 8), :] = jnp.where(low_q, roll(low[i], 96), above)
    low_q16 = (iotas(16)[0] & 32) == 0
    above = jnp.where(even_y, ya_ref[40:56], yb_ref[40:56])
    below = jnp.where(even_y, yb_ref[40:56], ya_ref[40:56])
    jl[80:96] = jnp.where(low_q16, roll(below, 96), roll(high_ends[0], 32))
    jl[96:112] = jnp.where(low_q16, below, roll(high_ends[1], 32))
    jh[80:96] = jnp.where(low_q16, roll(low_ends[0], 96), roll(above, 32))
    jh[96:112] = jnp.where(low_q16, roll(low_ends[1], 96), above)
    for d in range(3):
        eg[d * 16 : d * 16 + 16] = jnp.zeros((16, 128), F32)
        eg[d * 16 : d * 16 + 10] = eig_ref[d]
        for i in range(10):
            at = (d * 10 + i) * 16
            s[at : at + 16] = jnp.zeros((16, 128), F32)
            s[at : at + 10] = vec_ref[d, i].astype(F32)

    def factor(d, i, a):
        return row(s, (d * 10 + i) * 16 + a)

    def fwd_y(i, _):
        for k in range(10):
            edge = i * 8 + k - 1 if 1 <= k <= 8 else (80 + i if k == 0 else 96 + i)
            at = (i * 10 + k) * 8
            rows = [row(jl, edge)] + [row(core, at + j) for j in range(8)] + [row(jh, edge)]
            for h in range(2):
                out = chain((s[(10 + j) * 16 + 8 * h : (10 + j) * 16 + 8 * h + 8], rows[j]) for j in range(10))
                u[pl.ds((i * 10 + k) * 16 + 8 * h, 8), :] = out
        return 0

    lax.fori_loop(0, 10, fwd_y, 0)

    def along_x(transposed):
        def step(k, _):
            for h in range(2):
                at = k * 16 + 8 * h
                held = [u[pl.ds(i * 160 + at, 8), :] for i in range(10)]
                for a in range(10):
                    u[pl.ds(a * 160 + at, 8), :] = chain(
                        (factor(0, a, i) if transposed else factor(0, i, a), held[i]) for i in range(10)
                    )
            return 0

        lax.fori_loop(0, 10, step, 0)

    along_x(False)

    def along_z(a, _):
        for h in range(2):
            at = a * 160 + 8 * h
            held = [u[pl.ds(at + k * 16, 8), :] for k in range(10)]
            base = row(eg, a) + eg[16 + 8 * h : 24 + 8 * h]
            modes = []
            for c in range(10):
                modes.append(chain((factor(2, k, c), held[k]) for k in range(10)) / (base + row(eg, 32 + c)))
            for k in range(10):
                u[pl.ds(at + k * 16, 8), :] = chain((factor(2, k, c), modes[c]) for c in range(10))
        return 0

    lax.fori_loop(0, 10, along_z, 0)
    along_x(True)
    back = [s[pl.ds(11 * 16 + b, 8, stride=16), :] for b in range(10)]

    def back_y(i, _):
        for k in range(10):
            at = (i * 10 + k) * 16
            l_ref[i, k] = chain((back[b], row(u, at + b)) for b in range(10))
        for h in range(2):
            cut = [u[pl.ds(i * 160 + 128 * h + b, 8, stride=16), :] for b in range(10)]
            hl_ref[i, 8 * h : 8 * h + 8] = chain((factor(1, 0, b), cut[b]) for b in range(10))
            hh_ref[i, 8 * h : 8 * h + 8] = chain((factor(1, 9, b), cut[b]) for b in range(10))
        return 0

    lax.fori_loop(0, 10, back_y, 0)
    high_p = lane >= 64

    def outgoing(ref, k):
        return jnp.where(gx == 0, ref[9, k], roll(ref[0, k], 64))

    for k in range(5):
        xs_ref[k * 8 : k * 8 + 8] = jnp.where(high_p, outgoing(l_ref, k), roll(outgoing(l_ref, k + 5), 64))
    high_p = iotas(16)[0] >= 64
    edge_l = jnp.where(gx == 0, hl_ref[9], roll(hl_ref[0], 64))
    edge_h = jnp.where(gx == 0, hh_ref[9], roll(hh_ref[0], 64))
    xs_ref[40:56] = jnp.where(high_p, edge_l, roll(edge_h, 64))


def fold_x(value, i, opposite, received, gx, high_p):
    if i == 8:
        return value + jnp.where(high_p, jnp.where(gx == 0, received, 0.0), roll(opposite, 64))
    if i == 1:
        return value + jnp.where(high_p, roll(opposite, 64), jnp.where(gx == 1, roll(received, 64), 0.0))
    return value


def edge_rows(hl_ref, hh_ref, xr_ref, gx):
    high_p = iotas(16)[0] >= 64
    packed = xr_ref[40:56]
    low, high = [], []
    for i in range(1, 9):
        j = {1: 9, 8: 0}.get(i, i)
        low.append(fold_x(hl_ref[i], i, hl_ref[j], packed, gx, high_p))
        high.append(fold_x(hh_ref[i], i, hh_ref[j], roll(packed, 64), gx, high_p))
    return low, high


def yfold_send_kernel(hl_ref, hh_ref, xr_ref, ya_ref, yb_ref):
    gx = lax.axis_index("gx")
    even_y = lax.rem(lax.axis_index("gy"), 2) == 0
    low_q = (iotas(16)[0] & 32) == 0
    low, high = edge_rows(hl_ref, hh_ref, xr_ref, gx)
    for i in range(4):
        down = jnp.where(low_q, low[i], roll(low[i + 4], 32))
        up = jnp.where(low_q, roll(high[i + 4], 96), high[i])
        ya_ref[i * 16 : i * 16 + 16] = jnp.where(even_y, up, down)
        yb_ref[i * 16 : i * 16 + 16] = jnp.where(even_y, down, up)


def fold_rows(hl_ref, hh_ref, xr_ref, ya_ref, yb_ref, rows_first, rows_last, gx):
    even_y = lax.rem(lax.axis_index("gy"), 2) == 0
    low_q = (iotas(16)[0] & 32) == 0
    low, high = edge_rows(hl_ref, hh_ref, xr_ref, gx)
    for i in range(8):
        at = (i % 4) * 16
        a = ya_ref[at : at + 16]
        b = yb_ref[at : at + 16]
        above = jnp.where(even_y, a, b)
        below = jnp.where(even_y, b, a)
        if i < 4:
            above, below = roll(above, 32), roll(below, 96)
        rows_last[pl.ds(i * 16, 16), :] = jnp.where(low_q, roll(low[i], 96), above)
        rows_first[pl.ds(i * 16, 16), :] = jnp.where(low_q, below, roll(high[i], 32))


def folded_xy(l_ref, xr_ref, rows_first, rows_last, i, k, gx, lane, sub):
    high_p = lane >= 64
    value = l_ref[i, k]
    if i in (1, 8):
        packed = xr_ref[(k % 5) * 8 : (k % 5) * 8 + 8]
        received = packed if k < 5 else roll(packed, 64)
        value = fold_x(value, i, l_ref[9 if i == 1 else 0, k], received, gx, high_p)
    at = (i - 1) * 16 + k
    return value + jnp.where(sub == 0, row(rows_first, at), jnp.where(sub == 7, row(rows_last, at), 0.0))


def zfold_send_kernel(l_ref, hl_ref, hh_ref, xr_ref, ya_ref, yb_ref, za_ref, zb_ref, rows_first, rows_last):
    gx = lax.axis_index("gx")
    even_z = lax.rem(lax.axis_index("gz"), 2) == 0
    lane, sub = iotas()
    slot = lane & 31
    fold_rows(hl_ref, hh_ref, xr_ref, ya_ref, yb_ref, rows_first, rows_last, gx)
    down = jnp.zeros((8, 128), F32)
    up = jnp.zeros((8, 128), F32)
    for i in range(8):
        down = jnp.where(slot == i, roll(folded_xy(l_ref, xr_ref, rows_first, rows_last, i + 1, 0, gx, lane, sub), i), down)
        up = jnp.where(slot == i, roll(folded_xy(l_ref, xr_ref, rows_first, rows_last, i + 1, 9, gx, lane, sub), i - 31), up)
    za_ref[...] = jnp.where(even_z, up, down)
    zb_ref[...] = jnp.where(even_z, down, up)


def post_kernel(
    l_ref, hl_ref, hh_ref, xr_ref, ya_ref, yb_ref, za_ref, zb_ref, basis_ref, sep_ref, run_ref, ownsol_ref,
    out_ref, rows_first, rows_last, xt, grid,
):
    gx = lax.axis_index("gx")
    even_z = lax.rem(lax.axis_index("gz"), 2) == 0
    lane, sub = iotas()
    slot = lane & 31
    low_q = (lane & 32) == 0
    fold_rows(hl_ref, hh_ref, xr_ref, ya_ref, yb_ref, rows_first, rows_last, gx)
    weighted = total(sep_ref[level] * run_ref[level : level + 1, :] for level in range(sep_ref.shape[0]))
    solution_col = ownsol_ref[:, :1] + jnp.sum(weighted, axis=1, keepdims=True)
    lane16, sub16 = iotas(16)
    spread = jnp.where(((lane16 & 31) >> 1) == sub16, jnp.broadcast_to(solution_col, (16, 128)), 0.0)
    per_element = jnp.broadcast_to(jnp.sum(spread, axis=0, keepdims=True), (8, 128))
    from_above = jnp.where(even_z, za_ref[...], zb_ref[...])
    from_below = jnp.where(even_z, zb_ref[...], za_ref[...])
    for i in range(8):
        weights = basis_ref[i]
        get = functools.partial(folded_xy, l_ref, xr_ref, rows_first, rows_last, i + 1, gx=gx, lane=lane, sub=sub)
        before, after = get(0), get(9)
        for k in range(8):
            value = get(k + 1) + jnp.broadcast_to(weights[:, k : k + 1], (8, 128)) * per_element
            if k == 0:
                value = value + jnp.where(slot == 0, roll(from_below, -i), roll(after, 1))
            if k == 7:
                value = value + jnp.where(slot == 31, roll(from_above, 31 - i), roll(before, -1))
            grid[i, k] = value
    for pair in range(4):
        k0, k1 = 2 * pair, 2 * pair + 1
        pieces = []
        for i in range(8):
            c0, c1 = grid[i, k0], grid[i, k1]
            pieces.append(jnp.where(low_q, c0, roll(c1, 32)))
            pieces.append(jnp.where(low_q, roll(c0, 96), c1))
        block = jnp.concatenate(pieces, 0).T
        for p in range(2):
            for t, k in enumerate((k0, k1)):
                at = p * 64 + t * 32
                xt[p, pl.ds(k, 32, stride=8), :] = block[at : at + 32]
    out_ref[...] = jnp.concatenate([xt[0], xt[1]], 1).T


def call(kernel, outs, scratch, n_in, name):
    return pl.pallas_call(
        kernel,
        out_shape=[jax.ShapeDtypeStruct(shape, F32) for shape in outs],
        in_specs=[VM] * n_in,
        out_specs=[VM] * len(outs),
        scratch_shapes=[pltpu.VMEM(shape, F32) for shape in scratch],
        name=name,
    )


def swap(value, axis, distance):
    return lax.ppermute(value, axis, [(i, i ^ distance) for i in range(lax.axis_size(axis))])


def swap_odd(value, axis):
    pairs = []
    for i in range(1, lax.axis_size(axis) - 1, 2):
        pairs += [(i, i + 1), (i + 1, i)]
    return lax.ppermute(value, axis, pairs)


def on_device(residual, fdm_vectors, fdm_eigen, coarse_basis, x_interior, x_separator):
    levels, unknowns, width = x_separator.shape[3:]
    x = residual.reshape(256, 256)
    vectors = fdm_vectors.reshape(3, 10, 10, 128)
    eigen = fdm_eigen.reshape(3, 10, 128)
    own = x_interior.reshape(unknowns, unknowns)
    sep = x_separator.reshape(levels, unknowns, width)
    gx = lax.axis_index("gx")
    xface = swap(jnp.where(gx == 0, residual[15], residual[0]), "gx", 1)

    e, za, zb, running, ownsol = call(
        pre_kernel,
        [(10, 8, 8, 128), (8, 128), (8, 128), (levels, width), (16, 128)],
        [(2, 256, 128), (256, 128)],
        5,
        "pre",
    )(x, xface, coarse_basis, own, sep)

    row_of = lax.broadcasted_iota(jnp.int32, running.shape, 0)
    done = 0

    def climb(running, axis, distance):
        nonlocal done
        partner = swap(running, axis, distance)
        running = running + jnp.where(row_of >= done, partner, 0.0)
        done += 1
        return running

    za, zb = swap(za, "gz", 1), swap_odd(zb, "gz")
    for axis in ("gz", "gy", "gx"):
        distance = 1
        while distance < lax.axis_size(axis):
            running = climb(running, axis, distance)
            distance *= 2

    e2 = e.reshape(640, 128)
    ya, yb = call(yface_kernel, [(56, 128)] * 2, [(256, 128)], 4, "yface")(e, e2, za, zb)
    ya, yb = swap(ya, "gy", 1), swap_odd(yb, "gy")
    local, edge_l, edge_h, xs = call(
        solve_kernel,
        [(10, 10, 8, 128), (10, 16, 128), (10, 16, 128), (56, 128)],
        [(800, 128), (112, 128), (112, 128), (1696, 128), (480, 128), (48, 128), (256, 128)],
        8,
        "solve",
    )(e, e2, za, zb, ya, yb, vectors, eigen)
    xr = swap(xs, "gx", 1)
    ya, yb = call(yfold_send_kernel, [(64, 128)] * 2, [], 3, "yfold")(edge_l, edge_h, xr)
    ya, yb = swap(ya, "gy", 1), swap_odd(yb, "gy")
    za, zb = call(zfold_send_kernel, [(8, 128)] * 2, [(128, 128)] * 2, 6, "zfold")(local, edge_l, edge_h, xr, ya, yb)
    za, zb = swap(za, "gz", 1), swap_odd(zb, "gz")
    (out,) = call(
        post_kernel,
        [(256, 256)],
        [(128, 128), (128, 128), (2, 256, 128), (8, 8, 8, 128)],
        12,
        "post",
    )(local, edge_l, edge_h, xr, ya, yb, za, zb, coarse_basis, sep, running, ownsol)
    return out.reshape(residual.shape)


def solution(mesh):
    in_specs = (
        P("gx", "gy", "gz"),
        P("gx", "gy", "gz", None, None, None, None),
        P("gx", "gy", "gz", None, None, None),
        P(),
        P("gx", "gy", "gz", None, None),
        P("gx", "gy", "gz", None, None, None),
    )
    return jax.shard_map(
        on_device, mesh=mesh, in_specs=in_specs, out_specs=P("gx", "gy", "gz"), check_vma=False
    )
```

profile of v0, /device:TPU:112, one launch (start us, length us, event | category | flops | bytes accessed | tf_op | source)
XLA Modules:
  0.0 78.9 jit_solution(1239299201075299943)
XLA Ops:
  0.0 0.7 select_bitcast_fusion
  0.7 1.2 %collective-permute-done.xface_ref = f32[16,256]{1,0:T(8,128)S(1)} collective-permute-done((f32[16,256]{1,0:T(8,128)S(1)}, f32[16,256]{1,0:T(8,128)S(1)}, u32[]{:S(2)}, u32[]{:S(2)}) %collective-permute-start) | collective-permute-done | bytes 16416 | tf_op jit(solution)/shard_map/ppermute | solution.py:376
  1.9 0.6 copy-done.6
  2.5 2.7 %pre.1 = (f32[10,8,8,128]{3,2,1,0:T(8,128)}, f32[8,128]{1,0:T(8,128)}, f32[8,128]{1,0:T(8,128)}, f32[8,256]{1,0:T(8,128)}, f32[16,128]{1,0:T(8,128)}) custom-call(f32[256,256]{1,0:T(8,128)} %bitcast.18, f32[16,256]{1,0:T(8,128)} %copy-done.6, f32[8,8,8]{2,1,0:T(8,128)} %basis_ref.3, f32[16,16]{1,0:T(8,128)} %bitcast.20, f32[8,16,256]{2,1,0:T(8,128)} %bitcast.15), custom_call_target="tpu_custom_call" | custom-call | tf_op jit(solution)/shard_map/pre/pallas_call | solution.py:396
  5.2 1.5 %collective-permute-start.10 = (f32[8,256]{1,0:T(8,128)}, f32[8,256]{1,0:T(8,128)S(1)}, u32[]{:S(2)}, u32[]{:S(2)}) collective-permute-start(f32[8,256]{1,0:T(8,128)} %get-tuple-element.33), channel_id=1, source_target_pairs={{0,1},{1,0},{2,3},{3,2},{4,5},{5,4},{6,7},{7,6},{8,9},{9,8},{10,11... | collective-permute-start | bytes 24584 | tf_op jit(solution)/shard_map/ppermute | solution.py:376
  6.7 2.4 %collective-permute-done.10 = f32[8,256]{1,0:T(8,128)S(1)} collective-permute-done((f32[8,256]{1,0:T(8,128)}, f32[8,256]{1,0:T(8,128)S(1)}, u32[]{:S(2)}, u32[]{:S(2)}) %collective-permute-start.10) | collective-permute-done | bytes 8224 | tf_op jit(solution)/shard_map/ppermute | solution.py:376
  9.0 0.7 add.24
  9.7 3.0 %collective-permute-start.11 = (f32[8,256]{1,0:T(8,128)S(1)}, f32[8,256]{1,0:T(8,128)S(1)}, u32[]{:S(2)}, u32[]{:S(2)}) collective-permute-start(f32[8,256]{1,0:T(8,128)S(1)} %add.24), channel_id=1, source_target_pairs={{0,2},{1,3},{2,0},{3,1},{4,6},{5,7},{6,4},{7,5},{8,10},{9,11},{10,... | collective-permute-start | bytes 24584 | tf_op jit(solution)/shard_map/ppermute | solution.py:376
  12.8 2.1 %collective-permute-done.11 = f32[8,256]{1,0:T(8,128)S(1)} collective-permute-done((f32[8,256]{1,0:T(8,128)S(1)}, f32[8,256]{1,0:T(8,128)S(1)}, u32[]{:S(2)}, u32[]{:S(2)}) %collective-permute-start.11) | collective-permute-done | bytes 8224 | tf_op jit(solution)/shard_map/ppermute | solution.py:376
  15.0 1.3 %collective-permute-start.12 = (f32[8,256]{1,0:T(8,128)S(1)}, f32[8,256]{1,0:T(8,128)S(1)}, u32[]{:S(2)}, u32[]{:S(2)}) collective-permute-start(f32[8,256]{1,0:T(8,128)S(1)} %select_add_fusion.6), channel_id=1, source_target_pairs={{0,4},{1,5},{2,6},{3,7},{4,0},{5,1},{6,2},{7,3},{8,12},{9,13},{10,... | collective-permute-start | bytes 24584 | tf_op jit(solution)/shard_map/ppermute | solution.py:376
  16.3 2.4 %collective-permute-done.12 = f32[8,256]{1,0:T(8,128)S(1)} collective-permute-done((f32[8,256]{1,0:T(8,128)S(1)}, f32[8,256]{1,0:T(8,128)S(1)}, u32[]{:S(2)}, u32[]{:S(2)}) %collective-permute-start.12) | collective-permute-done | bytes 8224 | tf_op jit(solution)/shard_map/ppermute | solution.py:376
  19.0 4.9 %collective-permute-done.13 = f32[8,256]{1,0:T(8,128)S(1)} collective-permute-done((f32[8,256]{1,0:T(8,128)S(1)}, f32[8,256]{1,0:T(8,128)S(1)}, u32[]{:S(2)}, u32[]{:S(2)}) %collective-permute-start.13) | collective-permute-done | bytes 8224 | tf_op jit(solution)/shard_map/ppermute | solution.py:376
  24.1 1.5 %collective-permute-start.1 = (f32[8,128]{1,0:T(8,128)S(1)}, f32[8,128]{1,0:T(8,128)S(1)}, u32[]{:S(2)}, u32[]{:S(2)}) collective-permute-start(f32[8,128]{1,0:T(8,128)S(1)} %copy-done.13), channel_id=1, source_target_pairs={{0,1},{1,0},{2,3},{3,2},{4,5},{5,4},{6,7},{7,6},{8,9},{9,8},{10,11... | collective-permute-start | bytes 12296 | tf_op jit(solution)/shard_map/ppermute | solution.py:376
  25.7 3.8 %collective-permute-start.2 = (f32[8,128]{1,0:T(8,128)S(1)}, f32[8,128]{1,0:T(8,128)S(1)}, u32[]{:S(2)}, u32[]{:S(2)}) collective-permute-start(f32[8,128]{1,0:T(8,128)S(1)} %copy-done.12), channel_id=1, source_target_pairs={{1,2},{2,1},{3,4},{4,3},{5,6},{6,5},{7,8},{8,7},{9,10},{10,9},{11,... | collective-permute-start | bytes 12296 | tf_op jit(solution)/shard_map/ppermute | solution.py:383
  29.6 3.6 %collective-permute-done.2.zb_ref = f32[8,128]{1,0:T(8,128)S(1)} collective-permute-done((f32[8,128]{1,0:T(8,128)S(1)}, f32[8,128]{1,0:T(8,128)S(1)}, u32[]{:S(2)}, u32[]{:S(2)}) %collective-permute-start.2) | collective-permute-done | bytes 4128 | tf_op jit(solution)/shard_map/ppermute | solution.py:383
  33.8 1.9 %yface.1 = (f32[56,128]{1,0:T(8,128)}, f32[56,128]{1,0:T(8,128)}) custom-call(f32[10,8,8,128]{3,2,1,0:T(8,128)} %get-tuple-element.20.e_ref, f32[640,128]{1,0:T(8,128)} %bitcast.13, f32[8,128]{1,0:T(8,128)} %copy-done.7, f32[8,128]{1,0:T(8,128)} %copy-done.8), custom_call_target="tpu_custom_call" | custom-call | tf_op jit(solution)/shard_map/yface/pallas_call | solution.py:422
  35.7 1.9 %collective-permute-start.3 = (f32[56,128]{1,0:T(8,128)}, f32[56,128]{1,0:T(8,128)S(1)}, u32[]{:S(2)}, u32[]{:S(2)}) collective-permute-start(f32[56,128]{1,0:T(8,128)} %get-tuple-element.23), channel_id=1, source_target_pairs={{0,16},{16,0},{32,48},{48,32},{64,80},{80,64},{96,112},{112,96},{1... | collective-permute-start | bytes 86024 | tf_op jit(solution)/shard_map/ppermute | solution.py:376
  37.6 5.0 %collective-permute-start.4 = (f32[56,128]{1,0:T(8,128)}, f32[56,128]{1,0:T(8,128)S(1)}, u32[]{:S(2)}, u32[]{:S(2)}) collective-permute-start(f32[56,128]{1,0:T(8,128)} %get-tuple-element.24), channel_id=1, source_target_pairs={{16,32},{32,16},{48,64},{64,48},{80,96},{96,80},{17,33},{33,17},{4... | collective-permute-start | bytes 86024 | tf_op jit(solution)/shard_map/ppermute | solution.py:383
  43.5 0.7 copy.13
  44.2 0.6 collective-permute-done.4.yb_ref
  45.4 5.9 %solve.1 = (f32[10,10,8,128]{3,2,1,0:T(8,128)}, f32[10,16,128]{2,1,0:T(8,128)}, f32[10,16,128]{2,1,0:T(8,128)}, f32[56,128]{1,0:T(8,128)}) custom-call(f32[10,8,8,128]{3,2,1,0:T(8,128)} %get-tuple-element.20.e_ref, f32[640,128]{1,0:T(8,128)} %bitcast.14, f32[8,128]{1,0:T(8,128)} %copy-done.7, f32[8,128]{1,0:T(8,128)} %copy-done.8, f32[56,128]{1,0:T(8,128)} %copy-done.4, ...), custom_call_target="tpu_custom_call" | custom-call | tf_op jit(solution)/shard_map/solve/pallas_call | solution.py:424
  51.9 0.8 %collective-permute-done.5.xr_ref = f32[56,128]{1,0:T(8,128)S(1)} collective-permute-done((f32[56,128]{1,0:T(8,128)}, f32[56,128]{1,0:T(8,128)S(1)}, u32[]{:S(2)}, u32[]{:S(2)}) %collective-permute-start.5) | collective-permute-done | bytes 28704 | tf_op jit(solution)/shard_map/ppermute | solution.py:376
  52.7 0.6 copy-done
  53.3 1.7 %yfold.1 = (f32[64,128]{1,0:T(8,128)}, f32[64,128]{1,0:T(8,128)}) custom-call(f32[10,16,128]{2,1,0:T(8,128)} %get-tuple-element.26.hl_ref, f32[10,16,128]{2,1,0:T(8,128)} %get-tuple-element.27.hh_ref, f32[56,128]{1,0:T(8,128)} %copy-done), custom_call_target="tpu_custom_call" | custom-call | tf_op jit(solution)/shard_map/yfold/pallas_call | solution.py:432
  55.0 2.7 %collective-permute-start.6 = (f32[64,128]{1,0:T(8,128)}, f32[64,128]{1,0:T(8,128)S(1)}, u32[]{:S(2)}, u32[]{:S(2)}) collective-permute-start(f32[64,128]{1,0:T(8,128)} %get-tuple-element.29), channel_id=1, source_target_pairs={{0,16},{16,0},{32,48},{48,32},{64,80},{80,64},{96,112},{112,96},{1... | collective-permute-start | bytes 98312 | tf_op jit(solution)/shard_map/ppermute | solution.py:376
  57.7 2.4 %collective-permute-start.7 = (f32[64,128]{1,0:T(8,128)}, f32[64,128]{1,0:T(8,128)S(1)}, u32[]{:S(2)}, u32[]{:S(2)}) collective-permute-start(f32[64,128]{1,0:T(8,128)} %get-tuple-element.30), channel_id=1, source_target_pairs={{16,32},{32,16},{48,64},{64,48},{80,96},{96,80},{17,33},{33,17},{4... | collective-permute-start | bytes 98312 | tf_op jit(solution)/shard_map/ppermute | solution.py:383
  60.1 4.8 %collective-permute-done.7.yb_ref = f32[64,128]{1,0:T(8,128)S(1)} collective-permute-done((f32[64,128]{1,0:T(8,128)}, f32[64,128]{1,0:T(8,128)S(1)}, u32[]{:S(2)}, u32[]{:S(2)}) %collective-permute-start.7) | collective-permute-done | bytes 32800 | tf_op jit(solution)/shard_map/ppermute | solution.py:383
  65.5 2.0 %zfold.1 = (f32[8,128]{1,0:T(8,128)}, f32[8,128]{1,0:T(8,128)}) custom-call(f32[10,10,8,128]{3,2,1,0:T(8,128)} %get-tuple-element.25.l_ref, f32[10,16,128]{2,1,0:T(8,128)} %get-tuple-element.26.hl_ref, f32[10,16,128]{2,1,0:T(8,128)} %get-tuple-element.27.hh_ref, f32[56,128]{1,0:T(8,128)} %copy-done, f32[64,128]{1,0:T(8,128)} %copy-done.1, f32[64,128]{1,0:T(8,128)} %copy-done.2), custom_call_target="tpu_custom_call" | custom-call | tf_op jit(solution)/shard_map/zfold/pallas_call | solution.py:434
  67.5 3.8 %collective-permute-start.9 = (f32[8,128]{1,0:T(8,128)}, f32[8,128]{1,0:T(8,128)S(1)}, u32[]{:S(2)}, u32[]{:S(2)}) collective-permute-start(f32[8,128]{1,0:T(8,128)} %get-tuple-element.32), channel_id=1, source_target_pairs={{1,2},{2,1},{3,4},{4,3},{5,6},{6,5},{7,8},{8,7},{9,10},{10,9},{11,... | collective-permute-start | bytes 12296 | tf_op jit(solution)/shard_map/ppermute | solution.py:383
  71.3 0.7 select_add_fusion.run_ref
  72.0 3.3 %collective-permute-done.9.zb_ref = f32[8,128]{1,0:T(8,128)S(1)} collective-permute-done((f32[8,128]{1,0:T(8,128)}, f32[8,128]{1,0:T(8,128)S(1)}, u32[]{:S(2)}, u32[]{:S(2)}) %collective-permute-start.9) | collective-permute-done | bytes 4128 | tf_op jit(solution)/shard_map/ppermute | solution.py:383
  75.9 3.0 %post.1 = f32[256,256]{1,0:T(8,128)} custom-call(f32[10,10,8,128]{3,2,1,0:T(8,128)} %get-tuple-element.25.l_ref, f32[10,16,128]{2,1,0:T(8,128)} %get-tuple-element.26.hl_ref, f32[10,16,128]{2,1,0:T(8,128)} %get-tuple-element.27.hh_ref, f32[56,128]{1,0:T(8,128)} %copy-done, f32[64,128]{1,0:T(8,128)} %copy-done.1, f32[64,128]{1,0:T(8,128)} %copy-done.2, ...), custom_call_target="tpu_custom_call" | custom-call | tf_op jit(solution)/shard_map/post/pallas_call | solution.py:436
  (57 shorter events, 4.6 us)
Async XLA Ops:
  0.7 1.2 %collective-permute-start = (f32[16,256]{1,0:T(8,128)S(1)}, f32[16,256]{1,0:T(8,128)S(1)}, u32[]{:S(2)}, u32[]{:S(2)}) collective-permute-start(f32[16,256]{1,0:T(8,128)S(1)} %select_bitcast_fusion), channel_id=1, source_target_pairs={{0,128},{128,0},{1,129},{129,1},{2,130},{130,2},{3,131},{131,3},{4... | collective-permute-start | bytes 49160 | tf_op jit(solution)/shard_map/ppermute | solution.py:376
  1.9 0.6 copy-start.6
  5.2 3.9 %collective-permute-start.10 = (f32[8,256]{1,0:T(8,128)}, f32[8,256]{1,0:T(8,128)S(1)}, u32[]{:S(2)}, u32[]{:S(2)}) collective-permute-start(f32[8,256]{1,0:T(8,128)} %get-tuple-element.33), channel_id=1, source_target_pairs={{0,1},{1,0},{2,3},{3,2},{4,5},{5,4},{6,7},{7,6},{8,9},{9,8},{10,11... | collective-permute-start | bytes 24584 | tf_op jit(solution)/shard_map/ppermute | solution.py:376
  9.7 5.2 %collective-permute-start.11 = (f32[8,256]{1,0:T(8,128)S(1)}, f32[8,256]{1,0:T(8,128)S(1)}, u32[]{:S(2)}, u32[]{:S(2)}) collective-permute-start(f32[8,256]{1,0:T(8,128)S(1)} %add.24), channel_id=1, source_target_pairs={{0,2},{1,3},{2,0},{3,1},{4,6},{5,7},{6,4},{7,5},{8,10},{9,11},{10,... | collective-permute-start | bytes 24584 | tf_op jit(solution)/shard_map/ppermute | solution.py:376
  15.0 3.7 %collective-permute-start.12 = (f32[8,256]{1,0:T(8,128)S(1)}, f32[8,256]{1,0:T(8,128)S(1)}, u32[]{:S(2)}, u32[]{:S(2)}) collective-permute-start(f32[8,256]{1,0:T(8,128)S(1)} %select_add_fusion.6), channel_id=1, source_target_pairs={{0,4},{1,5},{2,6},{3,7},{4,0},{5,1},{6,2},{7,3},{8,12},{9,13},{10,... | collective-permute-start | bytes 24584 | tf_op jit(solution)/shard_map/ppermute | solution.py:376
  18.8 5.2 %collective-permute-start.13 = (f32[8,256]{1,0:T(8,128)S(1)}, f32[8,256]{1,0:T(8,128)S(1)}, u32[]{:S(2)}, u32[]{:S(2)}) collective-permute-start(f32[8,256]{1,0:T(8,128)S(1)} %select_add_fusion.5), channel_id=1, source_target_pairs={{0,8},{1,9},{2,10},{3,11},{4,12},{5,13},{6,14},{7,15},{8,0},{9,1},... | collective-permute-start | bytes 24584 | tf_op jit(solution)/shard_map/ppermute | solution.py:376
  19.0 5.1 %copy-start.13 = (f32[8,128]{1,0:T(8,128)S(1)}, f32[8,128]{1,0:T(8,128)}, u32[]{:S(2)}) copy-start(f32[8,128]{1,0:T(8,128)} %get-tuple-element.21) | copy-start | bytes 12292
  24.0 1.7 %copy-start.12 = (f32[8,128]{1,0:T(8,128)S(1)}, f32[8,128]{1,0:T(8,128)}, u32[]{:S(2)}) copy-start(f32[8,128]{1,0:T(8,128)} %get-tuple-element.22) | copy-start | bytes 12292
  24.0 5.5 %collective-permute-start.14 = (f32[8,256]{1,0:T(8,128)S(1)}, f32[8,256]{1,0:T(8,128)S(1)}, u32[]{:S(2)}, u32[]{:S(2)}) collective-permute-start(f32[8,256]{1,0:T(8,128)S(1)} %select_add_fusion.4), channel_id=1, source_target_pairs={{0,16},{16,0},{32,48},{48,32},{64,80},{80,64},{96,112},{112,96},{1... | collective-permute-start | bytes 24584 | tf_op jit(solution)/shard_map/ppermute | solution.py:376
  24.1 5.5 %collective-permute-start.1 = (f32[8,128]{1,0:T(8,128)S(1)}, f32[8,128]{1,0:T(8,128)S(1)}, u32[]{:S(2)}, u32[]{:S(2)}) collective-permute-start(f32[8,128]{1,0:T(8,128)S(1)} %copy-done.13), channel_id=1, source_target_pairs={{0,1},{1,0},{2,3},{3,2},{4,5},{5,4},{6,7},{7,6},{8,9},{9,8},{10,11... | collective-permute-start | bytes 12296 | tf_op jit(solution)/shard_map/ppermute | solution.py:376
  25.7 7.6 %collective-permute-start.2 = (f32[8,128]{1,0:T(8,128)S(1)}, f32[8,128]{1,0:T(8,128)S(1)}, u32[]{:S(2)}, u32[]{:S(2)}) collective-permute-start(f32[8,128]{1,0:T(8,128)S(1)} %copy-done.12), channel_id=1, source_target_pairs={{1,2},{2,1},{3,4},{4,3},{5,6},{6,5},{7,8},{8,7},{9,10},{10,9},{11,... | collective-permute-start | bytes 12296 | tf_op jit(solution)/shard_map/ppermute | solution.py:383
  29.6 13.1 %collective-permute-start.15 = (f32[8,256]{1,0:T(8,128)S(1)}, f32[8,256]{1,0:T(8,128)S(1)}, u32[]{:S(2)}, u32[]{:S(2)}) collective-permute-start(f32[8,256]{1,0:T(8,128)S(1)} %select_add_fusion.3), channel_id=1, source_target_pairs={{0,32},{16,48},{32,0},{48,16},{64,96},{80,112},{96,64},{112,80},{1... | collective-permute-start | bytes 24584 | tf_op jit(solution)/shard_map/ppermute | solution.py:376
  29.6 3.6 %copy-start.7 = (f32[8,128]{1,0:T(8,128)}, f32[8,128]{1,0:T(8,128)S(1)}, u32[]{:S(2)}) copy-start(f32[8,128]{1,0:T(8,128)S(1)} %collective-permute-done.1.za_ref) | copy-start | bytes 12292
  33.3 0.6 copy-start.8
  33.8 9.0 %copy-start.9 = (f32[1,1,1,3,10,128]{5,2,4,3,1,0:T(1,128)S(1)}, f32[1,1,1,3,10,128]{5,2,4,3,1,0:T(1,128)}, u32[]{:S(2)}) copy-start(f32[1,1,1,3,10,128]{5,2,4,3,1,0:T(1,128)} %param.8) | copy-start | bytes 46084
  35.7 7.8 %copy-start.3 = (bf16[1,1,1,3,10,10,128]{6,3,5,4,2,1,0:T(4,128)(2,1)S(1)}, bf16[1,1,1,3,10,10,128]{6,3,5,4,2,1,0:T(4,128)(2,1)}, u32[]{:S(2)}) copy-start(bf16[1,1,1,3,10,10,128]{6,3,5,4,2,1,0:T(4,128)(2,1)} %param.7) | copy-start | bytes 230404
  35.7 8.4 %collective-permute-start.3 = (f32[56,128]{1,0:T(8,128)}, f32[56,128]{1,0:T(8,128)S(1)}, u32[]{:S(2)}, u32[]{:S(2)}) collective-permute-start(f32[56,128]{1,0:T(8,128)} %get-tuple-element.23), channel_id=1, source_target_pairs={{0,16},{16,0},{32,48},{48,32},{64,80},{80,64},{96,112},{112,96},{1... | collective-permute-start | bytes 86024 | tf_op jit(solution)/shard_map/ppermute | solution.py:376
  37.6 7.2 %collective-permute-start.4 = (f32[56,128]{1,0:T(8,128)}, f32[56,128]{1,0:T(8,128)S(1)}, u32[]{:S(2)}, u32[]{:S(2)}) collective-permute-start(f32[56,128]{1,0:T(8,128)} %get-tuple-element.24), channel_id=1, source_target_pairs={{16,32},{32,16},{48,64},{64,48},{80,96},{96,80},{17,33},{33,17},{4... | collective-permute-start | bytes 86024 | tf_op jit(solution)/shard_map/ppermute | solution.py:383
  42.7 8.6 %collective-permute-start.16 = (f32[8,256]{1,0:T(8,128)S(1)}, f32[8,256]{1,0:T(8,128)S(1)}, u32[]{:S(2)}, u32[]{:S(2)}) collective-permute-start(f32[8,256]{1,0:T(8,128)S(1)} %select_add_fusion.2), channel_id=1, source_target_pairs={{0,64},{16,80},{32,96},{48,112},{64,0},{80,16},{96,32},{112,48},{1... | collective-permute-start | bytes 24584 | tf_op jit(solution)/shard_map/ppermute | solution.py:376
  44.2 0.6 copy-start.4
  44.8 0.6 copy-start.5
  51.3 1.4 %collective-permute-start.5 = (f32[56,128]{1,0:T(8,128)}, f32[56,128]{1,0:T(8,128)S(1)}, u32[]{:S(2)}, u32[]{:S(2)}) collective-permute-start(f32[56,128]{1,0:T(8,128)} %get-tuple-element.28), channel_id=1, source_target_pairs={{0,128},{128,0},{1,129},{129,1},{2,130},{130,2},{3,131},{131,3},{4... | collective-permute-start | bytes 86024 | tf_op jit(solution)/shard_map/ppermute | solution.py:376
  51.4 19.9 %collective-permute-start.17 = (f32[8,256]{1,0:T(8,128)S(1)}, f32[8,256]{1,0:T(8,128)S(1)}, u32[]{:S(2)}, u32[]{:S(2)}) collective-permute-start(f32[8,256]{1,0:T(8,128)S(1)} %select_add_fusion.1), channel_id=1, source_target_pairs={{0,128},{128,0},{1,129},{129,1},{2,130},{130,2},{3,131},{131,3},{4... | collective-permute-start | bytes 24584 | tf_op jit(solution)/shard_map/ppermute | solution.py:376
  52.7 0.6 copy-start
  55.0 5.1 %collective-permute-start.6 = (f32[64,128]{1,0:T(8,128)}, f32[64,128]{1,0:T(8,128)S(1)}, u32[]{:S(2)}, u32[]{:S(2)}) collective-permute-start(f32[64,128]{1,0:T(8,128)} %get-tuple-element.29), channel_id=1, source_target_pairs={{0,16},{16,0},{32,48},{48,32},{64,80},{80,64},{96,112},{112,96},{1... | collective-permute-start | bytes 98312 | tf_op jit(solution)/shard_map/ppermute | solution.py:376
  57.7 7.2 %collective-permute-start.7 = (f32[64,128]{1,0:T(8,128)}, f32[64,128]{1,0:T(8,128)S(1)}, u32[]{:S(2)}, u32[]{:S(2)}) collective-permute-start(f32[64,128]{1,0:T(8,128)} %get-tuple-element.30), channel_id=1, source_target_pairs={{16,32},{32,16},{48,64},{64,48},{80,96},{96,80},{17,33},{33,17},{4... | collective-permute-start | bytes 98312 | tf_op jit(solution)/shard_map/ppermute | solution.py:383
  60.1 4.8 %copy-start.1 = (f32[64,128]{1,0:T(8,128)}, f32[64,128]{1,0:T(8,128)S(1)}, u32[]{:S(2)}) copy-start(f32[64,128]{1,0:T(8,128)S(1)} %collective-permute-done.6.ya_ref) | copy-start | bytes 98308
  64.9 0.6 copy-start.2
  67.5 4.5 %collective-permute-start.8 = (f32[8,128]{1,0:T(8,128)}, f32[8,128]{1,0:T(8,128)S(1)}, u32[]{:S(2)}, u32[]{:S(2)}) collective-permute-start(f32[8,128]{1,0:T(8,128)} %get-tuple-element.31), channel_id=1, source_target_pairs={{0,1},{1,0},{2,3},{3,2},{4,5},{5,4},{6,7},{7,6},{8,9},{9,8},{10,11... | collective-permute-start | bytes 12296 | tf_op jit(solution)/shard_map/ppermute | solution.py:376
  67.5 7.8 %collective-permute-start.9 = (f32[8,128]{1,0:T(8,128)}, f32[8,128]{1,0:T(8,128)S(1)}, u32[]{:S(2)}, u32[]{:S(2)}) collective-permute-start(f32[8,128]{1,0:T(8,128)} %get-tuple-element.32), channel_id=1, source_target_pairs={{1,2},{2,1},{3,4},{4,3},{5,6},{6,5},{7,8},{8,7},{9,10},{10,9},{11,... | collective-permute-start | bytes 12296 | tf_op jit(solution)/shard_map/ppermute | solution.py:383
  72.0 3.3 %copy-start.10 = (f32[8,128]{1,0:T(8,128)}, f32[8,128]{1,0:T(8,128)S(1)}, u32[]{:S(2)}) copy-start(f32[8,128]{1,0:T(8,128)S(1)} %collective-permute-done.8.za_ref) | copy-start | bytes 12292
  75.3 0.6 copy-start.11
where the time goes:
time: 79.4 us; the launch traced here: 78.9 us
  starting transfers between devices  28 us (35%)
  waiting for transfers between devices  26.1 us (33%)
  Pallas kernels  17.2 us (22%)
  local copies, waits for them, and re-layouts  4.89 us (6%)
  other arithmetic  2.58 us (3%)
    ppermute x4, starting transfers between devices, swap_odd(): return lax.ppermute(value, axis, pairs)  15 us
    ppermute x14, waiting for transfers between devices, swap(): lax.ppermute(value, axis, [(i, i ^ distance) for i in range(lax.axis_size...  13.8 us
    ppermute x14, starting transfers between devices, swap(): lax.ppermute(value, axis, [(i, i ^ distance) for i in range(lax.axis_size...  13 us
    ppermute x4, waiting for transfers between devices, swap_odd(): return lax.ppermute(value, axis, pairs)  12.3 us
    pallas_call x1, Pallas kernels, on_device(): call(solve_kernel, [(10, 10, 8, 128), (10, 16, 128), (10, 16, 128), (56,...  5.94 us
    unnamed x30, local copies, waits for them, and re-layouts  4.29 us
    pallas_call x1, Pallas kernels, on_device(): call(post_kernel, [(256, 256)], [(128, 128), (128, 128), (2, 256, 128), (...  3.05 us
    pallas_call x1, Pallas kernels, on_device(): call(pre_kernel, [(10, 8, 8, 128), (8, 128), (8, 128), (levels, width), (...  2.65 us
  transfers between devices with their start and end apart: 18, of which 10 were waited for; matrix products, arithmetic and copies ran while one was open for 3% of the time, Pallas kernels for 15%

commit v1 on v0

--- a/solution.py
+++ b/solution.py
@@ -7,6 +7,7 @@
 from jax.experimental.pallas import tpu as pltpu
 from jax.sharding import PartitionSpec as P
 
+
 F32 = jnp.float32
 VM = pl.BlockSpec(memory_space=pltpu.VMEM)
 
@@ -40,7 +41,7 @@
     return acc
 
 
-def pre_kernel(x_ref, xface_ref, basis_ref, own_ref, sep_ref, e_ref, za_ref, zb_ref, part_ref, ownsol_ref, xt, ft):
+def pre_kernel(x_ref, xface_ref, basis_ref, own_ref, sep_ref, e_ref, za_ref, zb_ref, run_ref, ownsol_ref, xt, ft):
     gx = lax.axis_index("gx")
     even = lax.rem(lax.axis_index("gz"), 2) == 0
     lane, _ = iotas()
@@ -77,7 +78,7 @@
     for i in range(10):
         upper = jnp.where(slot == i, roll(e_ref[i, 7], i - 31), upper)
         lower = jnp.where(slot == i, roll(e_ref[i, 0], i), lower)
-    za_ref[...] = jnp.where(even, upper, lower)
+    za_ref[:8] = jnp.where(even, upper, lower)
     zb_ref[...] = jnp.where(even, lower, upper)
     sums = []
     for i in range(8):
@@ -88,15 +89,25 @@
     spread = jnp.where(((lane16 & 31) >> 1) == sub16, jnp.broadcast_to(lanes, (16, 128)), 0.0)
     rhs = jnp.sum(spread, axis=1, keepdims=True)
     for level in range(sep_ref.shape[0]):
-        part_ref[level : level + 1, :] = jnp.sum(sep_ref[level] * rhs, axis=0, keepdims=True)
+        part = jnp.sum(sep_ref[level] * rhs, axis=0, keepdims=True)
+        for h in range(2):
+            run_ref[8 * h + level : 8 * h + level + 1, :] = part[:, h * 128 : h * 128 + 128]
+    za_ref[8:24] = run_ref[...]
     own = own_ref[...]
     coef = jnp.sum(own * rhs, axis=0, keepdims=True)
     ownsol_ref[...] = jnp.broadcast_to(jnp.sum(own * coef, axis=1, keepdims=True), (16, 128))
 
 
-def z_halo(e_ref, za_ref, zb_ref, even, slot):
-    from_above = jnp.where(even, za_ref[...], zb_ref[...])
-    from_below = jnp.where(even, zb_ref[...], za_ref[...])
+def sides(a, b, axis):
+    index = lax.axis_index(axis)
+    even = lax.rem(index, 2) == 0
+    above = jnp.where(index == lax.axis_size(axis) - 1, 0.0, jnp.where(even, a, b))
+    below = jnp.where(index == 0, 0.0, jnp.where(even, b, a))
+    return above, below
+
+
+def z_halo(e_ref, za_ref, zb_ref, slot):
+    from_above, from_below = sides(za_ref[:8], zb_ref[...], "gz")
     first, last = [], []
     for i in range(10):
         first.append(jnp.where(slot == 0, roll(from_below, -i), roll(e_ref[i, 7], 1)))
@@ -115,12 +126,13 @@
     return low, high, low_ends, high_ends
 
 
-def yface_kernel(e_ref, e2_ref, za_ref, zb_ref, ya_ref, yb_ref, scr):
-    even_z = lax.rem(lax.axis_index("gz"), 2) == 0
+def yface_kernel(e_ref, e2_ref, za_ref, zb_ref, part_ref, ya_ref, yb_ref, run_ref, scr):
+    run_ref[...] = part_ref[...] + za_ref[8:24]
+    ya_ref[56:72] = run_ref[...]
     even_y = lax.rem(lax.axis_index("gy"), 2) == 0
     lane, _ = iotas()
     low_q = (lane & 32) == 0
-    first, last = z_halo(e_ref, za_ref, zb_ref, even_z, lane & 31)
+    first, last = z_halo(e_ref, za_ref, zb_ref, lane & 31)
     low, high, low_ends, high_ends = y_rows(first, last, e2_ref, scr)
     for i in range(5):
         down = jnp.where(low_q, low[i], roll(low[i + 5], 32))
@@ -139,11 +151,9 @@
     l_ref, hl_ref, hh_ref, xs_ref, core, jl, jh, u, s, eg, scr,
 ):
     gx = lax.axis_index("gx")
-    even_z = lax.rem(lax.axis_index("gz"), 2) == 0
-    even_y = lax.rem(lax.axis_index("gy"), 2) == 0
-    lane, sub = iotas()
+    lane, _ = iotas()
     low_q = (lane & 32) == 0
-    first, last = z_halo(e_ref, za_ref, zb_ref, even_z, lane & 31)
+    first, last = z_halo(e_ref, za_ref, zb_ref, lane & 31)
     low, high, low_ends, high_ends = y_rows(first, last, e2_ref, scr)
     for i in range(10):
         core[pl.ds(i * 80, 8), :] = first[i]
@@ -152,31 +162,30 @@
             core[pl.ds(i * 80 + 8 + k * 8, 8), :] = e_ref[i, k]
     for i in range(10):
         at = (i % 5) * 8
-        a = ya_ref[at : at + 8]
-        b = yb_ref[at : at + 8]
-        above = jnp.where(even_y, a, b)
-        below = jnp.where(even_y, b, a)
+        above, below = sides(ya_ref[at : at + 8], yb_ref[at : at + 8], "gy")
         if i < 5:
             above, below = roll(above, 32), roll(below, 96)
         jl[pl.ds(i * 8, 8), :] = jnp.where(low_q, below, roll(high[i], 32))
         jh[pl.ds(i * 8, 8), :] = jnp.where(low_q, roll(low[i], 96), above)
     low_q16 = (iotas(16)[0] & 32) == 0
-    above = jnp.where(even_y, ya_ref[40:56], yb_ref[40:56])
-    below = jnp.where(even_y, yb_ref[40:56], ya_ref[40:56])
+    above, below = sides(ya_ref[40:56], yb_ref[40:56], "gy")
     jl[80:96] = jnp.where(low_q16, roll(below, 96), roll(high_ends[0], 32))
     jl[96:112] = jnp.where(low_q16, below, roll(high_ends[1], 32))
     jh[80:96] = jnp.where(low_q16, roll(low_ends[0], 96), roll(above, 32))
     jh[96:112] = jnp.where(low_q16, roll(low_ends[1], 96), above)
-    for d in range(3):
-        eg[d * 16 : d * 16 + 16] = jnp.zeros((16, 128), F32)
-        eg[d * 16 : d * 16 + 10] = eig_ref[d]
+    eg[...] = jnp.ones((16, 128), F32)
+    for a in range(10):
+        eg[a : a + 1] = eig_ref[1, a]
         for i in range(10):
-            at = (d * 10 + i) * 16
-            s[at : at + 16] = jnp.zeros((16, 128), F32)
-            s[at : at + 10] = vec_ref[d, i].astype(F32)
+            s[(i * 10 + a) * 8 : (i * 10 + a) * 8 + 3] = vec_ref[i, a].astype(F32)
 
     def factor(d, i, a):
-        return row(s, (d * 10 + i) * 16 + a)
+        return row(s, (i * 10 + a) * 8 + d)
+
+    def wide(value):
+        return jnp.broadcast_to(value, (8, 128))
+
+    front = [[s[pl.ds((j * 10 + 8 * h) * 8 + 1, 8, stride=8), :] for j in range(10)] for h in range(2)]
 
     def fwd_y(i, _):
         for k in range(10):
@@ -184,7 +193,7 @@
             at = (i * 10 + k) * 8
             rows = [row(jl, edge)] + [row(core, at + j) for j in range(8)] + [row(jh, edge)]
             for h in range(2):
-                out = chain((s[(10 + j) * 16 + 8 * h : (10 + j) * 16 + 8 * h + 8], rows[j]) for j in range(10))
+                out = chain((front[h][j], rows[j]) for j in range(10))
                 u[pl.ds((i * 10 + k) * 16 + 8 * h, 8), :] = out
         return 0
 
@@ -209,17 +218,17 @@
         for h in range(2):
             at = a * 160 + 8 * h
             held = [u[pl.ds(at + k * 16, 8), :] for k in range(10)]
-            base = row(eg, a) + eg[16 + 8 * h : 24 + 8 * h]
+            base = wide(eig_ref[0, a]) + eg[8 * h : 8 * h + 8]
             modes = []
             for c in range(10):
-                modes.append(chain((factor(2, k, c), held[k]) for k in range(10)) / (base + row(eg, 32 + c)))
+                modes.append(chain((factor(2, k, c), held[k]) for k in range(10)) / (base + wide(eig_ref[2, c])))
             for k in range(10):
                 u[pl.ds(at + k * 16, 8), :] = chain((factor(2, k, c), modes[c]) for c in range(10))
         return 0
 
     lax.fori_loop(0, 10, along_z, 0)
     along_x(True)
-    back = [s[pl.ds(11 * 16 + b, 8, stride=16), :] for b in range(10)]
+    back = [s[pl.ds((10 + b) * 8 + 1, 8, stride=80), :] for b in range(10)]
 
     def back_y(i, _):
         for k in range(10):
@@ -277,15 +286,11 @@
 
 
 def fold_rows(hl_ref, hh_ref, xr_ref, ya_ref, yb_ref, rows_first, rows_last, gx):
-    even_y = lax.rem(lax.axis_index("gy"), 2) == 0
     low_q = (iotas(16)[0] & 32) == 0
     low, high = edge_rows(hl_ref, hh_ref, xr_ref, gx)
     for i in range(8):
         at = (i % 4) * 16
-        a = ya_ref[at : at + 16]
-        b = yb_ref[at : at + 16]
-        above = jnp.where(even_y, a, b)
-        below = jnp.where(even_y, b, a)
+        above, below = sides(ya_ref[at : at + 16], yb_ref[at : at + 16], "gy")
         if i < 4:
             above, below = roll(above, 32), roll(below, 96)
         rows_last[pl.ds(i * 16, 16), :] = jnp.where(low_q, roll(low[i], 96), above)
@@ -323,18 +328,20 @@
     out_ref, rows_first, rows_last, xt, grid,
 ):
     gx = lax.axis_index("gx")
-    even_z = lax.rem(lax.axis_index("gz"), 2) == 0
     lane, sub = iotas()
     slot = lane & 31
     low_q = (lane & 32) == 0
     fold_rows(hl_ref, hh_ref, xr_ref, ya_ref, yb_ref, rows_first, rows_last, gx)
-    weighted = total(sep_ref[level] * run_ref[level : level + 1, :] for level in range(sep_ref.shape[0]))
+    weighted = total(
+        sep_ref[level][:, h * 128 : h * 128 + 128] * run_ref[8 * h + level : 8 * h + level + 1, :]
+        for h in range(2)
+        for level in range(sep_ref.shape[0])
+    )
     solution_col = ownsol_ref[:, :1] + jnp.sum(weighted, axis=1, keepdims=True)
     lane16, sub16 = iotas(16)
     spread = jnp.where(((lane16 & 31) >> 1) == sub16, jnp.broadcast_to(solution_col, (16, 128)), 0.0)
     per_element = jnp.broadcast_to(jnp.sum(spread, axis=0, keepdims=True), (8, 128))
-    from_above = jnp.where(even_z, za_ref[...], zb_ref[...])
-    from_below = jnp.where(even_z, zb_ref[...], za_ref[...])
+    from_above, from_below = sides(za_ref[...], zb_ref[...], "gz")
     for i in range(8):
         weights = basis_ref[i]
         get = functools.partial(folded_xy, l_ref, xr_ref, rows_first, rows_last, i + 1, gx=gx, lane=lane, sub=sub)
@@ -361,14 +368,14 @@
     out_ref[...] = jnp.concatenate([xt[0], xt[1]], 1).T
 
 
-def call(kernel, outs, scratch, n_in, name):
+def call(kernel, outs, scratch, n_in, limit=4 << 20):
     return pl.pallas_call(
         kernel,
         out_shape=[jax.ShapeDtypeStruct(shape, F32) for shape in outs],
         in_specs=[VM] * n_in,
         out_specs=[VM] * len(outs),
         scratch_shapes=[pltpu.VMEM(shape, F32) for shape in scratch],
-        name=name,
+        compiler_params=pltpu.CompilerParams(vmem_limit_bytes=limit),
     )
 
 
@@ -377,68 +384,53 @@
 
 
 def swap_odd(value, axis):
-    pairs = []
-    for i in range(1, lax.axis_size(axis) - 1, 2):
-        pairs += [(i, i + 1), (i + 1, i)]
-    return lax.ppermute(value, axis, pairs)
-
-
-def on_device(residual, fdm_vectors, fdm_eigen, coarse_basis, x_interior, x_separator):
+    count = lax.axis_size(axis)
+    return lax.ppermute(value, axis, [(i, (i + 1 if i % 2 else i - 1) % count) for i in range(count)])
+
+
+def work(residual, fdm_vectors, fdm_eigen, coarse_basis, x_interior, x_separator):
     levels, unknowns, width = x_separator.shape[3:]
     x = residual.reshape(256, 256)
-    vectors = fdm_vectors.reshape(3, 10, 10, 128)
-    eigen = fdm_eigen.reshape(3, 10, 128)
+    vectors = fdm_vectors.reshape(3, 10, 10, 128).transpose(1, 2, 0, 3)
+    eigen = fdm_eigen.reshape(3, 10, 1, 128)
     own = x_interior.reshape(unknowns, unknowns)
     sep = x_separator.reshape(levels, unknowns, width)
     gx = lax.axis_index("gx")
+    level_of = lax.broadcasted_iota(jnp.int32, (16, 128), 0) & 7
+
+    def climb(running, axis, bit, first):
+        return running + jnp.where(level_of >= first, swap(running, axis, 1 << bit), 0.0)
+
+    def climb_two(running, axis, bit, first):
+        one, two, three = (swap(running, axis, d << bit) for d in (1, 2, 3))
+        return running + jnp.where(level_of > first, one + (two + three), jnp.where(level_of == first, one, 0.0))
+
     xface = swap(jnp.where(gx == 0, residual[15], residual[0]), "gx", 1)
-
-    e, za, zb, running, ownsol = call(
-        pre_kernel,
-        [(10, 8, 8, 128), (8, 128), (8, 128), (levels, width), (16, 128)],
-        [(2, 256, 128), (256, 128)],
-        5,
-        "pre",
+    e, za, zb, partial, ownsol = call(
+        pre_kernel, [(10, 8, 8, 128), (24, 128), (8, 128), (16, 128), (16, 128)], [(2, 256, 128), (256, 128)], 5
     )(x, xface, coarse_basis, own, sep)
-
-    row_of = lax.broadcasted_iota(jnp.int32, running.shape, 0)
-    done = 0
-
-    def climb(running, axis, distance):
-        nonlocal done
-        partner = swap(running, axis, distance)
-        running = running + jnp.where(row_of >= done, partner, 0.0)
-        done += 1
-        return running
-
     za, zb = swap(za, "gz", 1), swap_odd(zb, "gz")
-    for axis in ("gz", "gy", "gx"):
-        distance = 1
-        while distance < lax.axis_size(axis):
-            running = climb(running, axis, distance)
-            distance *= 2
-
     e2 = e.reshape(640, 128)
-    ya, yb = call(yface_kernel, [(56, 128)] * 2, [(256, 128)], 4, "yface")(e, e2, za, zb)
+    ya, yb, running = call(yface_kernel, [(72, 128), (56, 128), (16, 128)], [(256, 128)], 5)(e, e2, za, zb, partial)
     ya, yb = swap(ya, "gy", 1), swap_odd(yb, "gy")
+    running = running + jnp.where(level_of >= 4, ya[56:72], 0.0)
+    running = climb_two(running, "gy", 1, 5)
     local, edge_l, edge_h, xs = call(
         solve_kernel,
         [(10, 10, 8, 128), (10, 16, 128), (10, 16, 128), (56, 128)],
-        [(800, 128), (112, 128), (112, 128), (1696, 128), (480, 128), (48, 128), (256, 128)],
+        [(800, 128), (112, 128), (112, 128), (1696, 128), (848, 128), (16, 128), (256, 128)],
         8,
-        "solve",
     )(e, e2, za, zb, ya, yb, vectors, eigen)
     xr = swap(xs, "gx", 1)
-    ya, yb = call(yfold_send_kernel, [(64, 128)] * 2, [], 3, "yfold")(edge_l, edge_h, xr)
+    running = climb(running, "gx", 0, 7)
+    ya, yb = call(yfold_send_kernel, [(64, 128)] * 2, [], 3)(edge_l, edge_h, xr)
     ya, yb = swap(ya, "gy", 1), swap_odd(yb, "gy")
-    za, zb = call(zfold_send_kernel, [(8, 128)] * 2, [(128, 128)] * 2, 6, "zfold")(local, edge_l, edge_h, xr, ya, yb)
+    running = climb_two(running, "gz", 1, 1)
+    za, zb = call(zfold_send_kernel, [(8, 128)] * 2, [(128, 128)] * 2, 6)(local, edge_l, edge_h, xr, ya, yb)
     za, zb = swap(za, "gz", 1), swap_odd(zb, "gz")
+    running = climb(running, "gz", 3, 3)
     (out,) = call(
-        post_kernel,
-        [(256, 256)],
-        [(128, 128), (128, 128), (2, 256, 128), (8, 8, 8, 128)],
-        12,
-        "post",
+        post_kernel, [(256, 256)], [(128, 128), (128, 128), (2, 256, 128), (8, 8, 8, 128)], 12
     )(local, edge_l, edge_h, xr, ya, yb, za, zb, coarse_basis, sep, running, ownsol)
     return out.reshape(residual.shape)
 
@@ -452,6 +444,4 @@
         P("gx", "gy", "gz", None, None),
         P("gx", "gy", "gz", None, None, None),
     )
-    return jax.shard_map(
-        on_device, mesh=mesh, in_specs=in_specs, out_specs=P("gx", "gy", "gz"), check_vma=False
-    )
+    return jax.shard_map(work, mesh=mesh, in_specs=in_specs, out_specs=P("gx", "gy", "gz"), check_vma=False)

time: 79.4 us -> 59.4 us (0.75)
  the two profiles are of different devices: /device:TPU:112 before, /device:TPU:8 now
where the time goes in v1:
time: 59.4 us; the launch traced here: 59.2 us
  starting transfers between devices  29.1 us (49%)
  waiting for transfers between devices  19.4 us (33%)
  Pallas kernels  7.57 us (13%)
  local copies, waits for them, and re-layouts  1.87 us (3%)
  other arithmetic  1.15 us (2%)
    ppermute x14, starting transfers between devices, swap(): lax.ppermute(value, axis, [(i, i ^ distance) for i in range(lax.axis_size...  22 us
    ppermute x14, waiting for transfers between devices, swap(): lax.ppermute(value, axis, [(i, i ^ distance) for i in range(lax.axis_size...  10.2 us
    ppermute x4, waiting for transfers between devices, swap_odd(): lax.ppermute(value, axis, [(i, (i + 1 if i % 2 else i - 1) % count) for i...  9.24 us
    ppermute x4, starting transfers between devices, swap_odd(): lax.ppermute(value, axis, [(i, (i + 1 if i % 2 else i - 1) % count) for i...  7.06 us
    pallas_call x1, Pallas kernels, work(): call(solve_kernel, [(10, 10, 8, 128), (10, 16, 128), (10, 16, 128), (56,...  4.03 us
    pallas_call x1, Pallas kernels, work(): call(post_kernel, [(256, 256)], [(128, 128), (128, 128), (2, 256, 128), (...  1.89 us
    unnamed x14, local copies, waits for them, and re-layouts  1.87 us
  transfers between devices with their start and end apart: 18, of which 8 were waited for; matrix products, arithmetic and copies ran while one was open for 0% of the time, Pallas kernels for 8%

profile of v1, /device:TPU:8, one launch (start us, length us, event | category | flops | bytes accessed | tf_op | source)
XLA Modules:
  0.0 59.2 jit_solution(14709575945353089551)
XLA Ops:
  0.0 0.7 %select_bitcast_fusion = f32[16,256]{1,0:T(8,128)S(1)} fusion(f32[16,16,256]{2,1,0:T(8,128)} %param.6, pred[]{:T(512)S(6)} %eq.11), kind=kLoop, calls=%fused_computation | loop fusion | flops 4096 | bytes 49153 | tf_op jit(solution)/shard_map/jit(_where)/select_n | solution.py:408
  0.8 1.2 %collective-permute-done.xface_ref = f32[16,256]{1,0:T(8,128)S(1)} collective-permute-done((f32[16,256]{1,0:T(8,128)S(1)}, f32[16,256]{1,0:T(8,128)S(1)}, u32[]{:S(2)}, u32[]{:S(2)}) %collective-permute-start) | collective-permute-done | bytes 16416 | tf_op jit(solution)/shard_map/ppermute | solution.py:383
  1.9 0.9 %copy-done = f32[1,1,1,8,16,256]{5,4,3,2,1,0:T(8,128)S(1)} copy-done((f32[1,1,1,8,16,256]{5,4,3,2,1,0:T(8,128)S(1)}, f32[1,1,1,8,16,256]{5,4,3,2,1,0:T(8,128)}, u32[]{:S(2)}) %copy-start) | copy-done | bytes 131096
  2.9 0.9 %copy-done.2 = f32[16,16,256]{2,1,0:T(8,128)S(1)} copy-done((f32[16,16,256]{2,1,0:T(8,128)S(1)}, f32[16,16,256]{2,1,0:T(8,128)}, u32[]{:S(2)}) %copy-start.2) | copy-done | bytes 262168
  3.8 1.0 %shard_map.64 = (f32[10,8,8,128]{3,2,1,0:T(8,128)S(1)}, f32[24,128]{1,0:T(8,128)S(1)}, f32[8,128]{1,0:T(8,128)S(1)}, f32[16,128]{1,0:T(8,128)S(1)}, f32[16,128]{1,0:T(8,128)S(1)}) custom-call(f32[256,256]{1,0:T(8,128)S(1)} %bitcast.15, f32[16,256]{1,0:T(8,128)S(1)} %collective-permute-done.xface_ref, f32[8,8,8]{2,1,0:T(8,128)S(1)} %copy-done.3, ...), custom_call_target="tpu_custom_call" | custom-call | tf_op jit(solution)/shard_map/pallas_call | solution.py:409
  4.8 1.5 %collective-permute-start.1 = (f32[24,128]{1,0:T(8,128)S(1)}, f32[24,128]{1,0:T(8,128)S(1)}, u32[]{:S(2)}, u32[]{:S(2)}) collective-permute-start(f32[24,128]{1,0:T(8,128)S(1)} %get-tuple-element.22), channel_id=1, source_target_pairs={{0,1},{1,0},{2,3},{3,2},{4,5},{5,4},{6,7},{7,6},{8,9},{9,8},{10,11... | collective-permute-start | bytes 36872 | tf_op jit(solution)/shard_map/ppermute | solution.py:383
  6.4 2.0 %collective-permute-start.2 = (f32[8,128]{1,0:T(8,128)S(1)}, f32[8,128]{1,0:T(8,128)S(1)}, u32[]{:S(2)}, u32[]{:S(2)}) collective-permute-start(f32[8,128]{1,0:T(8,128)S(1)} %get-tuple-element.23), channel_id=1, source_target_pairs={{0,15},{1,2},{2,1},{3,4},{4,3},{5,6},{6,5},{7,8},{8,7},{9,10},{10,... | collective-permute-start | bytes 12296 | tf_op jit(solution)/shard_map/ppermute | solution.py:388
  8.3 3.7 %collective-permute-done.2.zb_ref = f32[8,128]{1,0:T(8,128)S(1)} collective-permute-done((f32[8,128]{1,0:T(8,128)S(1)}, f32[8,128]{1,0:T(8,128)S(1)}, u32[]{:S(2)}, u32[]{:S(2)}) %collective-permute-start.2) | collective-permute-done | bytes 4128 | tf_op jit(solution)/shard_map/ppermute | solution.py:388
  12.1 0.2 shard_map.65
  12.3 2.0 %collective-permute-start.3 = (f32[72,128]{1,0:T(8,128)S(1)}, f32[72,128]{1,0:T(8,128)S(1)}, u32[]{:S(2)}, u32[]{:S(2)}) collective-permute-start(f32[72,128]{1,0:T(8,128)S(1)} %get-tuple-element.25), channel_id=1, source_target_pairs={{0,16},{16,0},{32,48},{48,32},{64,80},{80,64},{96,112},{112,96},{1... | collective-permute-start | bytes 110600 | tf_op jit(solution)/shard_map/ppermute | solution.py:383
  14.3 2.0 %collective-permute-done.3.ya_ref = f32[72,128]{1,0:T(8,128)S(1)} collective-permute-done((f32[72,128]{1,0:T(8,128)S(1)}, f32[72,128]{1,0:T(8,128)S(1)}, u32[]{:S(2)}, u32[]{:S(2)}) %collective-permute-start.3) | collective-permute-done | bytes 36896 | tf_op jit(solution)/shard_map/ppermute | solution.py:383
  16.4 6.3 %collective-permute-start.12 = (f32[16,128]{1,0:T(8,128)S(1)}, f32[16,128]{1,0:T(8,128)S(1)}, u32[]{:S(2)}, u32[]{:S(2)}) collective-permute-start(f32[16,128]{1,0:T(8,128)S(1)} %fusion), channel_id=1, source_target_pairs={{0,96},{16,112},{32,64},{48,80},{64,32},{80,48},{96,0},{112,16},{1... | collective-permute-start | bytes 24584 | tf_op jit(solution)/shard_map/ppermute | solution.py:383
  22.7 1.1 %collective-permute-start.11 = (f32[16,128]{1,0:T(8,128)S(1)}, f32[16,128]{1,0:T(8,128)S(1)}, u32[]{:S(2)}, u32[]{:S(2)}) collective-permute-start(f32[16,128]{1,0:T(8,128)S(1)} %fusion), channel_id=1, source_target_pairs={{0,64},{16,80},{32,96},{48,112},{64,0},{80,16},{96,32},{112,48},{1... | collective-permute-start | bytes 24584 | tf_op jit(solution)/shard_map/ppermute | solution.py:383
  23.8 1.4 %collective-permute-start.10 = (f32[16,128]{1,0:T(8,128)S(1)}, f32[16,128]{1,0:T(8,128)S(1)}, u32[]{:S(2)}, u32[]{:S(2)}) collective-permute-start(f32[16,128]{1,0:T(8,128)S(1)} %fusion), channel_id=1, source_target_pairs={{0,32},{16,48},{32,0},{48,16},{64,96},{80,112},{96,64},{112,80},{1... | collective-permute-start | bytes 24584 | tf_op jit(solution)/shard_map/ppermute | solution.py:383
  25.2 5.1 %collective-permute-done.11 = f32[16,128]{1,0:T(8,128)S(1)} collective-permute-done((f32[16,128]{1,0:T(8,128)S(1)}, f32[16,128]{1,0:T(8,128)S(1)}, u32[]{:S(2)}, u32[]{:S(2)}) %collective-permute-start.11) | collective-permute-done | bytes 8224 | tf_op jit(solution)/shard_map/ppermute | solution.py:383
  30.4 1.7 %collective-permute-start.4 = (f32[56,128]{1,0:T(8,128)S(1)}, f32[56,128]{1,0:T(8,128)S(1)}, u32[]{:S(2)}, u32[]{:S(2)}) collective-permute-start(f32[56,128]{1,0:T(8,128)S(1)} %get-tuple-element.26), channel_id=1, source_target_pairs={{0,112},{16,32},{32,16},{48,64},{64,48},{80,96},{96,80},{112,0},{1... | collective-permute-start | bytes 86024 | tf_op jit(solution)/shard_map/ppermute | solution.py:388
  32.1 0.5 collective-permute-start.16
  32.6 1.6 %collective-permute-start.15 = (f32[16,128]{1,0:T(8,128)S(1)}, f32[16,128]{1,0:T(8,128)S(1)}, u32[]{:S(2)}, u32[]{:S(2)}) collective-permute-start(f32[16,128]{1,0:T(8,128)S(1)} %select_add_fusion.2), channel_id=1, source_target_pairs={{0,4},{1,5},{2,6},{3,7},{4,0},{5,1},{6,2},{7,3},{8,12},{9,13},{10,... | collective-permute-start | bytes 24584 | tf_op jit(solution)/shard_map/ppermute | solution.py:383
  34.2 2.9 %collective-permute-start.14 = (f32[16,128]{1,0:T(8,128)S(1)}, f32[16,128]{1,0:T(8,128)S(1)}, u32[]{:S(2)}, u32[]{:S(2)}) collective-permute-start(f32[16,128]{1,0:T(8,128)S(1)} %select_add_fusion.2), channel_id=1, source_target_pairs={{0,2},{1,3},{2,0},{3,1},{4,6},{5,7},{6,4},{7,5},{8,10},{9,11},{10,... | collective-permute-start | bytes 24584 | tf_op jit(solution)/shard_map/ppermute | solution.py:383
  37.2 4.0 %shard_map.66 = (f32[10,10,8,128]{3,2,1,0:T(8,128)S(1)}, f32[10,16,128]{2,1,0:T(8,128)S(1)}, f32[10,16,128]{2,1,0:T(8,128)S(1)}, f32[56,128]{1,0:T(8,128)S(1)}) custom-call(f32[10,8,8,128]{3,2,1,0:T(8,128)S(1)} %get-tuple-element.21.e_ref, f32[640,128]{1,0:T(8,128)S(1)} %bitcast.12, f32[24,128]{1,0:T(8,128)S(1)} %collective-permute-done.1.za_ref, ...), custom_call_target="tpu_custom_call" | custom-call | tf_op jit(solution)/shard_map/pallas_call | solution.py:418
  41.3 2.3 %collective-permute-start.17 = (f32[16,128]{1,0:T(8,128)S(1)}, f32[16,128]{1,0:T(8,128)S(1)}, u32[]{:S(2)}, u32[]{:S(2)}) collective-permute-start(f32[16,128]{1,0:T(8,128)S(1)} %select_add_fusion.1), channel_id=1, source_target_pairs={{0,8},{1,9},{2,10},{3,11},{4,12},{5,13},{6,14},{7,15},{8,0},{9,1},... | collective-permute-start | bytes 24584 | tf_op jit(solution)/shard_map/ppermute | solution.py:383
  43.7 0.1 shard_map.67
  43.8 0.6 %collective-permute-start.6 = (f32[64,128]{1,0:T(8,128)S(1)}, f32[64,128]{1,0:T(8,128)S(1)}, u32[]{:S(2)}, u32[]{:S(2)}) collective-permute-start(f32[64,128]{1,0:T(8,128)S(1)} %get-tuple-element.31), channel_id=1, source_target_pairs={{0,16},{16,0},{32,48},{48,32},{64,80},{80,64},{96,112},{112,96},{1... | collective-permute-start | bytes 98312 | tf_op jit(solution)/shard_map/ppermute | solution.py:383
  44.4 1.6 %collective-permute-start.7 = (f32[64,128]{1,0:T(8,128)S(1)}, f32[64,128]{1,0:T(8,128)S(1)}, u32[]{:S(2)}, u32[]{:S(2)}) collective-permute-start(f32[64,128]{1,0:T(8,128)S(1)} %get-tuple-element.32), channel_id=1, source_target_pairs={{0,112},{16,32},{32,16},{48,64},{64,48},{80,96},{96,80},{112,0},{1... | collective-permute-start | bytes 98312 | tf_op jit(solution)/shard_map/ppermute | solution.py:388
  46.0 1.8 %collective-permute-done.6.ya_ref = f32[64,128]{1,0:T(8,128)S(1)} collective-permute-done((f32[64,128]{1,0:T(8,128)S(1)}, f32[64,128]{1,0:T(8,128)S(1)}, u32[]{:S(2)}, u32[]{:S(2)}) %collective-permute-start.6) | collective-permute-done | bytes 32800 | tf_op jit(solution)/shard_map/ppermute | solution.py:383
  47.8 1.7 %collective-permute-done.7.yb_ref = f32[64,128]{1,0:T(8,128)S(1)} collective-permute-done((f32[64,128]{1,0:T(8,128)S(1)}, f32[64,128]{1,0:T(8,128)S(1)}, u32[]{:S(2)}, u32[]{:S(2)}) %collective-permute-start.7) | collective-permute-done | bytes 32800 | tf_op jit(solution)/shard_map/ppermute | solution.py:388
  49.6 0.3 shard_map.68
  49.8 1.7 %collective-permute-start.8 = (f32[8,128]{1,0:T(8,128)S(1)}, f32[8,128]{1,0:T(8,128)S(1)}, u32[]{:S(2)}, u32[]{:S(2)}) collective-permute-start(f32[8,128]{1,0:T(8,128)S(1)} %get-tuple-element.33), channel_id=1, source_target_pairs={{0,1},{1,0},{2,3},{3,2},{4,5},{5,4},{6,7},{7,6},{8,9},{9,8},{10,11... | collective-permute-start | bytes 12296 | tf_op jit(solution)/shard_map/ppermute | solution.py:383
  51.6 1.8 %collective-permute-start.9 = (f32[8,128]{1,0:T(8,128)S(1)}, f32[8,128]{1,0:T(8,128)S(1)}, u32[]{:S(2)}, u32[]{:S(2)}) collective-permute-start(f32[8,128]{1,0:T(8,128)S(1)} %get-tuple-element.34), channel_id=1, source_target_pairs={{0,15},{1,2},{2,1},{3,4},{4,3},{5,6},{6,5},{7,8},{8,7},{9,10},{10,... | collective-permute-start | bytes 12296 | tf_op jit(solution)/shard_map/ppermute | solution.py:388
  53.4 0.1 collective-permute-done.8.za_ref
  53.5 3.8 %collective-permute-done.9.zb_ref = f32[8,128]{1,0:T(8,128)S(1)} collective-permute-done((f32[8,128]{1,0:T(8,128)S(1)}, f32[8,128]{1,0:T(8,128)S(1)}, u32[]{:S(2)}, u32[]{:S(2)}) %collective-permute-start.9) | collective-permute-done | bytes 4128 | tf_op jit(solution)/shard_map/ppermute | solution.py:388
  57.3 1.9 %shard_map.69 = f32[256,256]{1,0:T(8,128)} custom-call(f32[10,10,8,128]{3,2,1,0:T(8,128)S(1)} %get-tuple-element.27.l_ref, f32[10,16,128]{2,1,0:T(8,128)S(1)} %get-tuple-element.28.hl_ref, f32[10,16,128]{2,1,0:T(8,128)S(1)} %get-tuple-element.29.hh_ref, f32[56,128]{1,0:T(8,128)S(1)} %collective-permute-done.5.xr_ref, ...), custom_call_target="tpu_custom_call" | custom-call | tf_op jit(solution)/shard_map/pallas_call | solution.py:432
  (35 shorter events, 0.5 us)
Async XLA Ops:
  0.0 1.9 %copy-start.3 = (f32[8,8,8]{2,1,0:T(8,128)S(1)}, f32[8,8,8]{2,1,0:T(8,128)}, u32[]{:S(2)}) copy-start(f32[8,8,8]{2,1,0:T(8,128)} %basis_ref.3) | copy-start | bytes 6148
  0.0 1.9 %copy-start.6 = (f32[1,1,1,16,16]{4,3,2,1,0:T(8,128)S(1)}, f32[1,1,1,16,16]{4,3,2,1,0:T(8,128)}, u32[]{:S(2)}) copy-start(f32[1,1,1,16,16]{4,3,2,1,0:T(8,128)} %param.10) | copy-start | bytes 3076
  0.8 1.2 %collective-permute-start = (f32[16,256]{1,0:T(8,128)S(1)}, f32[16,256]{1,0:T(8,128)S(1)}, u32[]{:S(2)}, u32[]{:S(2)}) collective-permute-start(f32[16,256]{1,0:T(8,128)S(1)} %select_bitcast_fusion), channel_id=1, source_target_pairs={{0,128},{128,0},{1,129},{129,1},{2,130},{130,2},{3,131},{131,3},{4... | collective-permute-start | bytes 49160 | tf_op jit(solution)/shard_map/ppermute | solution.py:383
  1.9 0.9 %copy-start = (f32[1,1,1,8,16,256]{5,4,3,2,1,0:T(8,128)S(1)}, f32[1,1,1,8,16,256]{5,4,3,2,1,0:T(8,128)}, u32[]{:S(2)}) copy-start(f32[1,1,1,8,16,256]{5,4,3,2,1,0:T(8,128)} %param.11) | copy-start | bytes 393220
  2.8 0.9 %copy-start.2 = (f32[16,16,256]{2,1,0:T(8,128)S(1)}, f32[16,16,256]{2,1,0:T(8,128)}, u32[]{:S(2)}) copy-start(f32[16,16,256]{2,1,0:T(8,128)} %param.6) | copy-start | bytes 786436
  4.8 7.2 %collective-permute-start.1 = (f32[24,128]{1,0:T(8,128)S(1)}, f32[24,128]{1,0:T(8,128)S(1)}, u32[]{:S(2)}, u32[]{:S(2)}) collective-permute-start(f32[24,128]{1,0:T(8,128)S(1)} %get-tuple-element.22), channel_id=1, source_target_pairs={{0,1},{1,0},{2,3},{3,2},{4,5},{5,4},{6,7},{7,6},{8,9},{9,8},{10,11... | collective-permute-start | bytes 36872 | tf_op jit(solution)/shard_map/ppermute | solution.py:383
  6.4 5.7 %collective-permute-start.2 = (f32[8,128]{1,0:T(8,128)S(1)}, f32[8,128]{1,0:T(8,128)S(1)}, u32[]{:S(2)}, u32[]{:S(2)}) collective-permute-start(f32[8,128]{1,0:T(8,128)S(1)} %get-tuple-element.23), channel_id=1, source_target_pairs={{0,15},{1,2},{2,1},{3,4},{4,3},{5,6},{6,5},{7,8},{8,7},{9,10},{10,... | collective-permute-start | bytes 12296 | tf_op jit(solution)/shard_map/ppermute | solution.py:388
  12.1 25.1 %copy-start.5 = (f32[1,1,1,3,10,128]{5,2,4,3,1,0:T(1,128)S(1)}, f32[1,1,1,3,10,128]{5,2,4,3,1,0:T(1,128)}, u32[]{:S(2)}) copy-start(f32[1,1,1,3,10,128]{5,2,4,3,1,0:T(1,128)} %param.8) | copy-start | bytes 46084
  12.3 24.9 %copy-start.4 = (bf16[1,1,1,3,10,10,128]{6,3,5,4,2,1,0:T(4,128)(2,1)S(1)}, bf16[1,1,1,3,10,10,128]{6,3,5,4,2,1,0:T(4,128)(2,1)}, u32[]{:S(2)}) copy-start(bf16[1,1,1,3,10,10,128]{6,3,5,4,2,1,0:T(4,128)(2,1)} %param.7) | copy-start | bytes 230404
  12.3 4.0 %collective-permute-start.3 = (f32[72,128]{1,0:T(8,128)S(1)}, f32[72,128]{1,0:T(8,128)S(1)}, u32[]{:S(2)}, u32[]{:S(2)}) collective-permute-start(f32[72,128]{1,0:T(8,128)S(1)} %get-tuple-element.25), channel_id=1, source_target_pairs={{0,16},{16,0},{32,48},{48,32},{64,80},{80,64},{96,112},{112,96},{1... | collective-permute-start | bytes 110600 | tf_op jit(solution)/shard_map/ppermute | solution.py:383
  16.4 8.8 %collective-permute-start.12 = (f32[16,128]{1,0:T(8,128)S(1)}, f32[16,128]{1,0:T(8,128)S(1)}, u32[]{:S(2)}, u32[]{:S(2)}) collective-permute-start(f32[16,128]{1,0:T(8,128)S(1)} %fusion), channel_id=1, source_target_pairs={{0,96},{16,112},{32,64},{48,80},{64,32},{80,48},{96,0},{112,16},{1... | collective-permute-start | bytes 24584 | tf_op jit(solution)/shard_map/ppermute | solution.py:383
  22.7 7.6 %collective-permute-start.11 = (f32[16,128]{1,0:T(8,128)S(1)}, f32[16,128]{1,0:T(8,128)S(1)}, u32[]{:S(2)}, u32[]{:S(2)}) collective-permute-start(f32[16,128]{1,0:T(8,128)S(1)} %fusion), channel_id=1, source_target_pairs={{0,64},{16,80},{32,96},{48,112},{64,0},{80,16},{96,32},{112,48},{1... | collective-permute-start | bytes 24584 | tf_op jit(solution)/shard_map/ppermute | solution.py:383
  23.8 6.5 %collective-permute-start.10 = (f32[16,128]{1,0:T(8,128)S(1)}, f32[16,128]{1,0:T(8,128)S(1)}, u32[]{:S(2)}, u32[]{:S(2)}) collective-permute-start(f32[16,128]{1,0:T(8,128)S(1)} %fusion), channel_id=1, source_target_pairs={{0,32},{16,48},{32,0},{48,16},{64,96},{80,112},{96,64},{112,80},{1... | collective-permute-start | bytes 24584 | tf_op jit(solution)/shard_map/ppermute | solution.py:383
  30.3 1.7 %collective-permute-start.13 = (f32[16,128]{1,0:T(8,128)S(1)}, f32[16,128]{1,0:T(8,128)S(1)}, u32[]{:S(2)}, u32[]{:S(2)}) collective-permute-start(f32[16,128]{1,0:T(8,128)S(1)} %select_add_fusion.3), channel_id=1, source_target_pairs={{0,128},{128,0},{1,129},{129,1},{2,130},{130,2},{3,131},{131,3},{4... | collective-permute-start | bytes 24584 | tf_op jit(solution)/shard_map/ppermute | solution.py:383
  30.4 6.8 %collective-permute-start.4 = (f32[56,128]{1,0:T(8,128)S(1)}, f32[56,128]{1,0:T(8,128)S(1)}, u32[]{:S(2)}, u32[]{:S(2)}) collective-permute-start(f32[56,128]{1,0:T(8,128)S(1)} %get-tuple-element.26), channel_id=1, source_target_pairs={{0,112},{16,32},{32,16},{48,64},{64,48},{80,96},{96,80},{112,0},{1... | collective-permute-start | bytes 86024 | tf_op jit(solution)/shard_map/ppermute | solution.py:388
  32.1 9.1 %collective-permute-start.16 = (f32[16,128]{1,0:T(8,128)S(1)}, f32[16,128]{1,0:T(8,128)S(1)}, u32[]{:S(2)}, u32[]{:S(2)}) collective-permute-start(f32[16,128]{1,0:T(8,128)S(1)} %select_add_fusion.2), channel_id=1, source_target_pairs={{0,6},{1,7},{2,4},{3,5},{4,2},{5,3},{6,0},{7,1},{8,14},{9,15},{10,... | collective-permute-start | bytes 24584 | tf_op jit(solution)/shard_map/ppermute | solution.py:383
  32.6 8.6 %collective-permute-start.15 = (f32[16,128]{1,0:T(8,128)S(1)}, f32[16,128]{1,0:T(8,128)S(1)}, u32[]{:S(2)}, u32[]{:S(2)}) collective-permute-start(f32[16,128]{1,0:T(8,128)S(1)} %select_add_fusion.2), channel_id=1, source_target_pairs={{0,4},{1,5},{2,6},{3,7},{4,0},{5,1},{6,2},{7,3},{8,12},{9,13},{10,... | collective-permute-start | bytes 24584 | tf_op jit(solution)/shard_map/ppermute | solution.py:383
  34.2 7.0 %collective-permute-start.14 = (f32[16,128]{1,0:T(8,128)S(1)}, f32[16,128]{1,0:T(8,128)S(1)}, u32[]{:S(2)}, u32[]{:S(2)}) collective-permute-start(f32[16,128]{1,0:T(8,128)S(1)} %select_add_fusion.2), channel_id=1, source_target_pairs={{0,2},{1,3},{2,0},{3,1},{4,6},{5,7},{6,4},{7,5},{8,10},{9,11},{10,... | collective-permute-start | bytes 24584 | tf_op jit(solution)/shard_map/ppermute | solution.py:383
  41.2 2.5 %collective-permute-start.5 = (f32[56,128]{1,0:T(8,128)S(1)}, f32[56,128]{1,0:T(8,128)S(1)}, u32[]{:S(2)}, u32[]{:S(2)}) collective-permute-start(f32[56,128]{1,0:T(8,128)S(1)} %get-tuple-element.30), channel_id=1, source_target_pairs={{0,128},{128,0},{1,129},{129,1},{2,130},{130,2},{3,131},{131,3},{4... | collective-permute-start | bytes 86024 | tf_op jit(solution)/shard_map/ppermute | solution.py:383
  41.3 12.0 %collective-permute-start.17 = (f32[16,128]{1,0:T(8,128)S(1)}, f32[16,128]{1,0:T(8,128)S(1)}, u32[]{:S(2)}, u32[]{:S(2)}) collective-permute-start(f32[16,128]{1,0:T(8,128)S(1)} %select_add_fusion.1), channel_id=1, source_target_pairs={{0,8},{1,9},{2,10},{3,11},{4,12},{5,13},{6,14},{7,15},{8,0},{9,1},... | collective-permute-start | bytes 24584 | tf_op jit(solution)/shard_map/ppermute | solution.py:383
  43.8 4.0 %collective-permute-start.6 = (f32[64,128]{1,0:T(8,128)S(1)}, f32[64,128]{1,0:T(8,128)S(1)}, u32[]{:S(2)}, u32[]{:S(2)}) collective-permute-start(f32[64,128]{1,0:T(8,128)S(1)} %get-tuple-element.31), channel_id=1, source_target_pairs={{0,16},{16,0},{32,48},{48,32},{64,80},{80,64},{96,112},{112,96},{1... | collective-permute-start | bytes 98312 | tf_op jit(solution)/shard_map/ppermute | solution.py:383
  44.4 5.1 %collective-permute-start.7 = (f32[64,128]{1,0:T(8,128)S(1)}, f32[64,128]{1,0:T(8,128)S(1)}, u32[]{:S(2)}, u32[]{:S(2)}) collective-permute-start(f32[64,128]{1,0:T(8,128)S(1)} %get-tuple-element.32), channel_id=1, source_target_pairs={{0,112},{16,32},{32,16},{48,64},{64,48},{80,96},{96,80},{112,0},{1... | collective-permute-start | bytes 98312 | tf_op jit(solution)/shard_map/ppermute | solution.py:388
  49.5 7.7 %copy-start.1 = (f32[1,1,1,8,16,256]{5,4,3,2,1,0:T(8,128)S(1)}, f32[1,1,1,8,16,256]{5,4,3,2,1,0:T(8,128)}, u32[]{:S(2)}) copy-start(f32[1,1,1,8,16,256]{5,4,3,2,1,0:T(8,128)} %param.11) | copy-start | bytes 393220
  49.8 3.7 %collective-permute-start.8 = (f32[8,128]{1,0:T(8,128)S(1)}, f32[8,128]{1,0:T(8,128)S(1)}, u32[]{:S(2)}, u32[]{:S(2)}) collective-permute-start(f32[8,128]{1,0:T(8,128)S(1)} %get-tuple-element.33), channel_id=1, source_target_pairs={{0,1},{1,0},{2,3},{3,2},{4,5},{5,4},{6,7},{7,6},{8,9},{9,8},{10,11... | collective-permute-start | bytes 12296 | tf_op jit(solution)/shard_map/ppermute | solution.py:383
  51.6 5.7 %collective-permute-start.9 = (f32[8,128]{1,0:T(8,128)S(1)}, f32[8,128]{1,0:T(8,128)S(1)}, u32[]{:S(2)}, u32[]{:S(2)}) collective-permute-start(f32[8,128]{1,0:T(8,128)S(1)} %get-tuple-element.34), channel_id=1, source_target_pairs={{0,15},{1,2},{2,1},{3,4},{4,3},{5,6},{6,5},{7,8},{8,7},{9,10},{10,... | collective-permute-start | bytes 12296 | tf_op jit(solution)/shard_map/ppermute | solution.py:388

commit v2 on v1

--- a/solution.py
+++ b/solution.py
@@ -41,18 +41,23 @@
     return acc
 
 
-def pre_kernel(x_ref, xface_ref, basis_ref, own_ref, sep_ref, e_ref, za_ref, zb_ref, run_ref, ownsol_ref, xt, ft):
-    gx = lax.axis_index("gx")
-    even = lax.rem(lax.axis_index("gz"), 2) == 0
+def pre_kernel(
+    x_ref, sep_ref, basis_ref, own_ref, core_ref, xs_ref, run_ref, ownsol_ref, xv, xt, sepv, basisv, ownv, xsem, sems
+):
+    copies = [pltpu.make_async_copy(x_ref.at[pl.ds(p * 128, 128), :], xv.at[p], xsem.at[p]) for p in range(2)]
+    small = [
+        pltpu.make_async_copy(a, b, sems.at[n])
+        for n, (a, b) in enumerate(((basis_ref, basisv), (own_ref, ownv), (sep_ref, sepv)))
+    ]
+    for copy in copies + small:
+        copy.start()
+    gx = lax.axis_index("gx")
     lane, _ = iotas()
     low_q = (lane & 32) == 0
     high_p = lane >= 64
-    slot = lane & 31
-    turned = x_ref[...].T
-    xt[0] = turned[:, :128]
-    xt[1] = turned[:, 128:]
-    face = jnp.concatenate([xface_ref[...], jnp.zeros((112, 256), F32)], 0).T
-    ft[...] = face
+    for p in range(2):
+        copies[p].wait()
+        xt[p] = xv[p].T
     for pair in range(4):
         k0, k1 = 2 * pair, 2 * pair + 1
         pieces = [xt[p, pl.ds(k, 32, stride=8), :] for p in range(2) for k in (k0, k1)]
@@ -60,42 +65,58 @@
         for i in range(8):
             a = block[i * 16 : i * 16 + 8]
             b = block[i * 16 + 8 : i * 16 + 16]
-            e_ref[i + 1, k0] = jnp.where(low_q, a, roll(b, 32))
-            e_ref[i + 1, k1] = jnp.where(low_q, roll(a, 96), b)
-    for half in range(2):
-        pieces = [ft[pl.ds(half * 4 + k, 32, stride=8), :] for k in range(4)]
-        block = jnp.concatenate(pieces, 0).T
-        a, b = block[:8], block[8:16]
-        for t in range(4):
-            k = half * 4 + t
-            got = jnp.where(low_q, roll(a, -32 * t), roll(b, 32 - 32 * t))
-            below = jnp.where(gx == 1, got, 0.0)
-            above = jnp.where(gx == 0, roll(got, 64), 0.0)
-            e_ref[0, k] = jnp.where(high_p, roll(e_ref[8, k], 64), below)
-            e_ref[9, k] = jnp.where(high_p, above, roll(e_ref[1, k], 64))
-    upper = jnp.zeros((8, 128), F32)
-    lower = jnp.zeros((8, 128), F32)
-    for i in range(10):
-        upper = jnp.where(slot == i, roll(e_ref[i, 7], i - 31), upper)
-        lower = jnp.where(slot == i, roll(e_ref[i, 0], i), lower)
-    za_ref[:8] = jnp.where(even, upper, lower)
-    zb_ref[...] = jnp.where(even, lower, upper)
+            core_ref[i, k0] = jnp.where(low_q, a, roll(b, 32))
+            core_ref[i, k1] = jnp.where(low_q, roll(a, 96), b)
+
+    def outgoing(k):
+        return jnp.where(gx == 0, core_ref[7, k], roll(core_ref[0, k], 64))
+
+    for k in range(4):
+        xs_ref[k * 8 : k * 8 + 8] = jnp.where(high_p, outgoing(k), roll(outgoing(k + 4), 64))
+    small[0].wait()
     sums = []
     for i in range(8):
-        weights = basis_ref[i]
-        sums.append(chain((e_ref[i + 1, k], jnp.broadcast_to(weights[:, k : k + 1], (8, 128))) for k in range(8)))
+        weights = basisv[i]
+        sums.append(chain((core_ref[i, k], jnp.broadcast_to(weights[:, k : k + 1], (8, 128))) for k in range(8)))
     lanes = jnp.sum(total(sums), axis=0, keepdims=True)
     lane16, sub16 = iotas(16)
     spread = jnp.where(((lane16 & 31) >> 1) == sub16, jnp.broadcast_to(lanes, (16, 128)), 0.0)
     rhs = jnp.sum(spread, axis=1, keepdims=True)
+    small[1].wait()
+    own = ownv[...]
+    coef = jnp.sum(own * rhs, axis=0, keepdims=True)
+    ownsol_ref[...] = jnp.broadcast_to(jnp.sum(own * coef, axis=1, keepdims=True), (16, 128))
+    small[2].wait()
     for level in range(sep_ref.shape[0]):
-        part = jnp.sum(sep_ref[level] * rhs, axis=0, keepdims=True)
+        part = jnp.sum(sepv[level] * rhs, axis=0, keepdims=True)
         for h in range(2):
             run_ref[8 * h + level : 8 * h + level + 1, :] = part[:, h * 128 : h * 128 + 128]
-    za_ref[8:24] = run_ref[...]
-    own = own_ref[...]
-    coef = jnp.sum(own * rhs, axis=0, keepdims=True)
-    ownsol_ref[...] = jnp.broadcast_to(jnp.sum(own * coef, axis=1, keepdims=True), (16, 128))
+
+
+def zface_kernel(core_ref, xr_ref, ends_ref, za_ref, zb_ref):
+    gx = lax.axis_index("gx")
+    even = lax.rem(lax.axis_index("gz"), 2) == 0
+    lane, _ = iotas()
+    high_p = lane >= 64
+    slot = lane & 31
+    for k in range(8):
+        at = (k % 4) * 8
+        got = xr_ref[at : at + 8]
+        if k >= 4:
+            got = roll(got, 64)
+        ends_ref[0, k] = jnp.where(high_p, roll(core_ref[7, k], 64), jnp.where(gx == 1, roll(got, 64), 0.0))
+        ends_ref[1, k] = jnp.where(high_p, jnp.where(gx == 0, got, 0.0), roll(core_ref[0, k], 64))
+    upper = jnp.zeros((8, 128), F32)
+    lower = jnp.zeros((8, 128), F32)
+    for i in range(10):
+        upper = jnp.where(slot == i, roll(plane(core_ref, ends_ref, i, 7), i - 31), upper)
+        lower = jnp.where(slot == i, roll(plane(core_ref, ends_ref, i, 0), i), lower)
+    za_ref[...] = jnp.where(even, upper, lower)
+    zb_ref[...] = jnp.where(even, lower, upper)
+
+
+def plane(core_ref, ends_ref, i, k):
+    return core_ref[i - 1, k] if 1 <= i <= 8 else ends_ref[i // 9, k]
 
 
 def sides(a, b, axis):
@@ -106,34 +127,36 @@
     return above, below
 
 
-def z_halo(e_ref, za_ref, zb_ref, slot):
-    from_above, from_below = sides(za_ref[:8], zb_ref[...], "gz")
+def z_halo(core_ref, ends_ref, za_ref, zb_ref, slot):
+    from_above, from_below = sides(za_ref[...], zb_ref[...], "gz")
     first, last = [], []
     for i in range(10):
-        first.append(jnp.where(slot == 0, roll(from_below, -i), roll(e_ref[i, 7], 1)))
-        last.append(jnp.where(slot == 31, roll(from_above, 31 - i), roll(e_ref[i, 0], -1)))
+        first.append(jnp.where(slot == 0, roll(from_below, -i), roll(plane(core_ref, ends_ref, i, 7), 1)))
+        last.append(jnp.where(slot == 31, roll(from_above, 31 - i), roll(plane(core_ref, ends_ref, i, 0), -1)))
     return first, last
 
 
-def y_rows(first, last, e2_ref, scr):
+def y_rows(first, last, core2_ref, ends2_ref, scr):
     for i in range(10):
         scr[pl.ds(i * 8, 8), :] = first[i]
         scr[pl.ds(128 + i * 8, 8), :] = last[i]
-    low = [e2_ref[pl.ds(i * 64, 8, stride=8), :] for i in range(10)]
-    high = [e2_ref[pl.ds(i * 64 + 7, 8, stride=8), :] for i in range(10)]
+    low, high = [], []
+    for i in range(10):
+        ref, at = (core2_ref, (i - 1) * 64) if 1 <= i <= 8 else (ends2_ref, (i // 9) * 64)
+        low.append(ref[pl.ds(at, 8, stride=8), :])
+        high.append(ref[pl.ds(at + 7, 8, stride=8), :])
     low_ends = [scr[pl.ds(b, 16, stride=8), :] for b in (0, 128)]
     high_ends = [scr[pl.ds(b + 7, 16, stride=8), :] for b in (0, 128)]
     return low, high, low_ends, high_ends
 
 
-def yface_kernel(e_ref, e2_ref, za_ref, zb_ref, part_ref, ya_ref, yb_ref, run_ref, scr):
-    run_ref[...] = part_ref[...] + za_ref[8:24]
+def yface_kernel(core_ref, core2_ref, ends_ref, ends2_ref, za_ref, zb_ref, run_ref, ya_ref, yb_ref, scr):
     ya_ref[56:72] = run_ref[...]
     even_y = lax.rem(lax.axis_index("gy"), 2) == 0
     lane, _ = iotas()
     low_q = (lane & 32) == 0
-    first, last = z_halo(e_ref, za_ref, zb_ref, lane & 31)
-    low, high, low_ends, high_ends = y_rows(first, last, e2_ref, scr)
+    first, last = z_halo(core_ref, ends_ref, za_ref, zb_ref, lane & 31)
+    low, high, low_ends, high_ends = y_rows(first, last, core2_ref, ends2_ref, scr)
     for i in range(5):
         down = jnp.where(low_q, low[i], roll(low[i + 5], 32))
         up = jnp.where(low_q, roll(high[i + 5], 96), high[i])
@@ -146,20 +169,44 @@
     yb_ref[40:56] = jnp.where(even_y, down, up)
 
 
-def solve_kernel(
-    e_ref, e2_ref, za_ref, zb_ref, ya_ref, yb_ref, vec_ref, eig_ref,
-    l_ref, hl_ref, hh_ref, xs_ref, core, jl, jh, u, s, eg, scr,
+def load_factors(vec_ref, s):
+    for a in range(10):
+        for i in range(10):
+            s[(i * 10 + a) * 8 : (i * 10 + a) * 8 + 3] = vec_ref[i, a].astype(F32)
+
+    def factor(d, i, a):
+        return row(s, (i * 10 + a) * 8 + d)
+
+    return factor
+
+
+def along_x(source, target, factor, transposed):
+    def step(k, _):
+        for h in range(2):
+            at = k * 16 + 8 * h
+            held = [source[pl.ds(i * 160 + at, 8), :] for i in range(10)]
+            for a in range(10):
+                target[pl.ds(a * 160 + at, 8), :] = chain(
+                    (factor(0, a, i) if transposed else factor(0, i, a), held[i]) for i in range(10)
+                )
+        return 0
+
+    lax.fori_loop(0, 10, step, 0)
+
+
+def modes_kernel(
+    core_ref, core2_ref, ends_ref, ends2_ref, za_ref, zb_ref, ya_ref, yb_ref, vec_ref, eig_ref,
+    u, block, jl, jh, s, eg, scr,
 ):
-    gx = lax.axis_index("gx")
     lane, _ = iotas()
     low_q = (lane & 32) == 0
-    first, last = z_halo(e_ref, za_ref, zb_ref, lane & 31)
-    low, high, low_ends, high_ends = y_rows(first, last, e2_ref, scr)
-    for i in range(10):
-        core[pl.ds(i * 80, 8), :] = first[i]
-        core[pl.ds(i * 80 + 72, 8), :] = last[i]
+    first, last = z_halo(core_ref, ends_ref, za_ref, zb_ref, lane & 31)
+    low, high, low_ends, high_ends = y_rows(first, last, core2_ref, ends2_ref, scr)
+    for i in range(10):
+        block[pl.ds(i * 80, 8), :] = first[i]
+        block[pl.ds(i * 80 + 72, 8), :] = last[i]
         for k in range(8):
-            core[pl.ds(i * 80 + 8 + k * 8, 8), :] = e_ref[i, k]
+            block[pl.ds(i * 80 + 8 + k * 8, 8), :] = plane(core_ref, ends_ref, i, k)
     for i in range(10):
         at = (i % 5) * 8
         above, below = sides(ya_ref[at : at + 8], yb_ref[at : at + 8], "gy")
@@ -176,11 +223,7 @@
     eg[...] = jnp.ones((16, 128), F32)
     for a in range(10):
         eg[a : a + 1] = eig_ref[1, a]
-        for i in range(10):
-            s[(i * 10 + a) * 8 : (i * 10 + a) * 8 + 3] = vec_ref[i, a].astype(F32)
-
-    def factor(d, i, a):
-        return row(s, (i * 10 + a) * 8 + d)
+    factor = load_factors(vec_ref, s)
 
     def wide(value):
         return jnp.broadcast_to(value, (8, 128))
@@ -191,7 +234,7 @@
         for k in range(10):
             edge = i * 8 + k - 1 if 1 <= k <= 8 else (80 + i if k == 0 else 96 + i)
             at = (i * 10 + k) * 8
-            rows = [row(jl, edge)] + [row(core, at + j) for j in range(8)] + [row(jh, edge)]
+            rows = [row(jl, edge)] + [row(block, at + j) for j in range(8)] + [row(jh, edge)]
             for h in range(2):
                 out = chain((front[h][j], rows[j]) for j in range(10))
                 u[pl.ds((i * 10 + k) * 16 + 8 * h, 8), :] = out
@@ -199,20 +242,7 @@
 
     lax.fori_loop(0, 10, fwd_y, 0)
 
-    def along_x(transposed):
-        def step(k, _):
-            for h in range(2):
-                at = k * 16 + 8 * h
-                held = [u[pl.ds(i * 160 + at, 8), :] for i in range(10)]
-                for a in range(10):
-                    u[pl.ds(a * 160 + at, 8), :] = chain(
-                        (factor(0, a, i) if transposed else factor(0, i, a), held[i]) for i in range(10)
-                    )
-            return 0
-
-        lax.fori_loop(0, 10, step, 0)
-
-    along_x(False)
+    along_x(u, u, factor, False)
 
     def along_z(a, _):
         for h in range(2):
@@ -227,7 +257,13 @@
         return 0
 
     lax.fori_loop(0, 10, along_z, 0)
-    along_x(True)
+
+
+def points_kernel(u_ref, vec_ref, l_ref, hl_ref, hh_ref, xs_ref, u, s):
+    gx = lax.axis_index("gx")
+    lane, _ = iotas()
+    factor = load_factors(vec_ref, s)
+    along_x(u_ref, u, factor, True)
     back = [s[pl.ds((10 + b) * 8 + 1, 8, stride=80), :] for b in range(10)]
 
     def back_y(i, _):
@@ -308,7 +344,8 @@
     return value + jnp.where(sub == 0, row(rows_first, at), jnp.where(sub == 7, row(rows_last, at), 0.0))
 
 
-def zfold_send_kernel(l_ref, hl_ref, hh_ref, xr_ref, ya_ref, yb_ref, za_ref, zb_ref, rows_first, rows_last):
+def zfold_send_kernel(l_ref, hl_ref, hh_ref, xr_ref, ya_ref, yb_ref, run_ref, za_ref, zb_ref, rows_first, rows_last):
+    za_ref[8:24] = run_ref[...]
     gx = lax.axis_index("gx")
     even_z = lax.rem(lax.axis_index("gz"), 2) == 0
     lane, sub = iotas()
@@ -319,7 +356,7 @@
     for i in range(8):
         down = jnp.where(slot == i, roll(folded_xy(l_ref, xr_ref, rows_first, rows_last, i + 1, 0, gx, lane, sub), i), down)
         up = jnp.where(slot == i, roll(folded_xy(l_ref, xr_ref, rows_first, rows_last, i + 1, 9, gx, lane, sub), i - 31), up)
-    za_ref[...] = jnp.where(even_z, up, down)
+    za_ref[:8] = jnp.where(even_z, up, down)
     zb_ref[...] = jnp.where(even_z, down, up)
 
 
@@ -332,8 +369,9 @@
     slot = lane & 31
     low_q = (lane & 32) == 0
     fold_rows(hl_ref, hh_ref, xr_ref, ya_ref, yb_ref, rows_first, rows_last, gx)
+    running = run_ref[...] + za_ref[8:24]
     weighted = total(
-        sep_ref[level][:, h * 128 : h * 128 + 128] * run_ref[8 * h + level : 8 * h + level + 1, :]
+        sep_ref[level][:, h * 128 : h * 128 + 128] * running[8 * h + level : 8 * h + level + 1, :]
         for h in range(2)
         for level in range(sep_ref.shape[0])
     )
@@ -341,7 +379,7 @@
     lane16, sub16 = iotas(16)
     spread = jnp.where(((lane16 & 31) >> 1) == sub16, jnp.broadcast_to(solution_col, (16, 128)), 0.0)
     per_element = jnp.broadcast_to(jnp.sum(spread, axis=0, keepdims=True), (8, 128))
-    from_above, from_below = sides(za_ref[...], zb_ref[...], "gz")
+    from_above, from_below = sides(za_ref[:8], zb_ref[...], "gz")
     for i in range(8):
         weights = basis_ref[i]
         get = functools.partial(folded_xy, l_ref, xr_ref, rows_first, rows_last, i + 1, gx=gx, lane=lane, sub=sub)
@@ -368,15 +406,19 @@
     out_ref[...] = jnp.concatenate([xt[0], xt[1]], 1).T
 
 
-def call(kernel, outs, scratch, n_in, limit=4 << 20):
+def call(kernel, outs, scratch, n_in, limit=4 << 20, far=0, semaphores=()):
     return pl.pallas_call(
         kernel,
         out_shape=[jax.ShapeDtypeStruct(shape, F32) for shape in outs],
-        in_specs=[VM] * n_in,
+        in_specs=[pl.BlockSpec(memory_space=pltpu.HBM)] * far + [VM] * (n_in - far),
         out_specs=[VM] * len(outs),
-        scratch_shapes=[pltpu.VMEM(shape, F32) for shape in scratch],
+        scratch_shapes=[pltpu.VMEM(shape, F32) for shape in scratch] + list(semaphores),
         compiler_params=pltpu.CompilerParams(vmem_limit_bytes=limit),
     )
+
+
+def far(value):
+    return pltpu.with_memory_space_constraint(value, pltpu.HBM)
 
 
 def swap(value, axis, distance):
@@ -395,43 +437,47 @@
     eigen = fdm_eigen.reshape(3, 10, 1, 128)
     own = x_interior.reshape(unknowns, unknowns)
     sep = x_separator.reshape(levels, unknowns, width)
-    gx = lax.axis_index("gx")
     level_of = lax.broadcasted_iota(jnp.int32, (16, 128), 0) & 7
 
-    def climb(running, axis, bit, first):
-        return running + jnp.where(level_of >= first, swap(running, axis, 1 << bit), 0.0)
-
-    def climb_two(running, axis, bit, first):
-        one, two, three = (swap(running, axis, d << bit) for d in (1, 2, 3))
-        return running + jnp.where(level_of > first, one + (two + three), jnp.where(level_of == first, one, 0.0))
-
-    xface = swap(jnp.where(gx == 0, residual[15], residual[0]), "gx", 1)
-    e, za, zb, partial, ownsol = call(
-        pre_kernel, [(10, 8, 8, 128), (24, 128), (8, 128), (16, 128), (16, 128)], [(2, 256, 128), (256, 128)], 5
-    )(x, xface, coarse_basis, own, sep)
+    def climb(running, axis, distance, first):
+        return running + jnp.where(level_of >= first, swap(running, axis, distance), 0.0)
+
+    core, xs, running, ownsol = call(
+        pre_kernel,
+        [(8, 8, 8, 128), (32, 128), (16, 128), (16, 128)],
+        [(2, 128, 256), (2, 256, 128), (levels, unknowns, width), (8, 8, 8), (unknowns, unknowns)],
+        4,
+        far=4,
+        semaphores=(pltpu.SemaphoreType.DMA((2,)), pltpu.SemaphoreType.DMA((3,))),
+    )(far(x), far(sep), far(coarse_basis), far(own))
+    xr = swap(xs, "gx", 1)
+    running = climb(running, "gz", 2, 1)
+    ends, za, zb = call(zface_kernel, [(2, 8, 8, 128), (8, 128), (8, 128)], [], 2)(core, xr)
     za, zb = swap(za, "gz", 1), swap_odd(zb, "gz")
-    e2 = e.reshape(640, 128)
-    ya, yb, running = call(yface_kernel, [(72, 128), (56, 128), (16, 128)], [(256, 128)], 5)(e, e2, za, zb, partial)
+    running = climb(running, "gy", 2, 5)
+    block = (core, core.reshape(512, 128), ends, ends.reshape(128, 128), za, zb)
+    ya, yb = call(yface_kernel, [(72, 128), (56, 128)], [(256, 128)], 7)(*block, running)
     ya, yb = swap(ya, "gy", 1), swap_odd(yb, "gy")
     running = running + jnp.where(level_of >= 4, ya[56:72], 0.0)
-    running = climb_two(running, "gy", 1, 5)
+    running = climb(running, "gy", 6, 6)
+    (modes,) = call(
+        modes_kernel, [(1696, 128)], [(800, 128), (112, 128), (112, 128), (848, 128), (16, 128), (256, 128)], 10
+    )(*block, ya, yb, vectors, eigen)
+    running = climb(running, "gz", 4, 2)
     local, edge_l, edge_h, xs = call(
-        solve_kernel,
-        [(10, 10, 8, 128), (10, 16, 128), (10, 16, 128), (56, 128)],
-        [(800, 128), (112, 128), (112, 128), (1696, 128), (848, 128), (16, 128), (256, 128)],
-        8,
-    )(e, e2, za, zb, ya, yb, vectors, eigen)
+        points_kernel, [(10, 10, 8, 128), (10, 16, 128), (10, 16, 128), (56, 128)], [(1696, 128), (848, 128)], 2
+    )(modes, vectors)
     xr = swap(xs, "gx", 1)
-    running = climb(running, "gx", 0, 7)
+    running = climb(running, "gx", 1, 7)
     ya, yb = call(yfold_send_kernel, [(64, 128)] * 2, [], 3)(edge_l, edge_h, xr)
     ya, yb = swap(ya, "gy", 1), swap_odd(yb, "gy")
-    running = climb_two(running, "gz", 1, 1)
-    za, zb = call(zfold_send_kernel, [(8, 128)] * 2, [(128, 128)] * 2, 6)(local, edge_l, edge_h, xr, ya, yb)
+    running = climb(running, "gz", 8, 3)
+    parts = (local, edge_l, edge_h, xr, ya, yb)
+    za, zb = call(zfold_send_kernel, [(24, 128), (8, 128)], [(128, 128)] * 2, 7)(*parts, running)
     za, zb = swap(za, "gz", 1), swap_odd(zb, "gz")
-    running = climb(running, "gz", 3, 3)
     (out,) = call(
         post_kernel, [(256, 256)], [(128, 128), (128, 128), (2, 256, 128), (8, 8, 8, 128)], 12
-    )(local, edge_l, edge_h, xr, ya, yb, za, zb, coarse_basis, sep, running, ownsol)
+    )(*parts, za, zb, coarse_basis, sep, running, ownsol)
     return out.reshape(residual.shape)
 
 

time: 59.4 us -> 56.9 us (0.958)
  the two profiles are of different devices: /device:TPU:8 before, /device:TPU:6 now
where the time goes in v2:
time: 56.9 us; the launch traced here: 56.8 us
  starting transfers between devices  27.4 us (48%)
  waiting for transfers between devices  20.1 us (35%)
  Pallas kernels  8.59 us (15%)
    ppermute x12, starting transfers between devices, swap(): lax.ppermute(value, axis, [(i, i ^ distance) for i in range(lax.axis_size...  18.2 us
    ppermute x4, waiting for transfers between devices, swap_odd(): lax.ppermute(value, axis, [(i, (i + 1 if i % 2 else i - 1) % count) for i...  11.7 us
    ppermute x4, starting transfers between devices, swap_odd(): lax.ppermute(value, axis, [(i, (i + 1 if i % 2 else i - 1) % count) for i...  9.25 us
    ppermute x12, waiting for transfers between devices, swap(): lax.ppermute(value, axis, [(i, i ^ distance) for i in range(lax.axis_size...  8.47 us
    pallas_call x1, Pallas kernels, work(): call(modes_kernel, [(1696, 128)], [(800, 128), (112, 128), (112, 128), (8...  2.66 us
    pallas_call x1, Pallas kernels, work(): call(post_kernel, [(256, 256)], [(128, 128), (128, 128), (2, 256, 128), (...  1.89 us
    pallas_call x1, Pallas kernels, work(): call(pre_kernel, [(8, 8, 8, 128), (32, 128), (16, 128), (16, 128)], [(2,...  1.84 us
    pallas_call x1, Pallas kernels, work(): call(points_kernel, [(10, 10, 8, 128), (10, 16, 128), (10, 16, 128), (56,...  1.39 us
  transfers between devices with their start and end apart: 16, of which 9 were waited for; matrix products, arithmetic and copies ran while one was open for 1% of the time, Pallas kernels for 8%

profile of v2, /device:TPU:6, one launch (start us, length us, event | category | flops | bytes accessed | tf_op | source)
XLA Modules:
  0.0 56.8 jit_solution(17226742114341374930)
XLA Ops:
  0.0 1.8 %shard_map.64 = (f32[8,8,8,128]{3,2,1,0:T(8,128)S(1)}, f32[32,128]{1,0:T(8,128)S(1)}, f32[16,128]{1,0:T(8,128)S(1)}, f32[16,128]{1,0:T(8,128)S(1)}) custom-call(f32[256,256]{1,0:T(8,128)} %bitcast.19, f32[8,16,256]{2,1,0:T(8,128)} %bitcast.14, f32[8,8,8]{2,1,0:T(8,128)} %basis_ref.3, f32[16,16]{1,0:T(8,128)} %bitcast.20), custom_call_target="tpu_custom_call" | custom-call | tf_op jit(solution)/shard_map/pallas_call | solution.py:445
  1.8 1.5 %collective-permute-start.3 = (f32[16,128]{1,0:T(8,128)S(1)}, f32[16,128]{1,0:T(8,128)S(1)}, u32[]{:S(2)}, u32[]{:S(2)}) collective-permute-start(f32[16,128]{1,0:T(8,128)S(1)} %get-tuple-element.27), channel_id=1, source_target_pairs={{0,2},{1,3},{2,0},{3,1},{4,6},{5,7},{6,4},{7,5},{8,10},{9,11},{10,... | collective-permute-start | bytes 24584 | tf_op jit(solution)/shard_map/ppermute | solution.py:425
  3.4 3.7 %collective-permute-done.3 = f32[16,128]{1,0:T(8,128)S(1)} collective-permute-done((f32[16,128]{1,0:T(8,128)S(1)}, f32[16,128]{1,0:T(8,128)S(1)}, u32[]{:S(2)}, u32[]{:S(2)}) %collective-permute-start.3) | collective-permute-done | bytes 8224 | tf_op jit(solution)/shard_map/ppermute | solution.py:425
  7.2 3.3 %collective-permute-start.4 = (f32[16,128]{1,0:T(8,128)S(1)}, f32[16,128]{1,0:T(8,128)S(1)}, u32[]{:S(2)}, u32[]{:S(2)}) collective-permute-start(f32[16,128]{1,0:T(8,128)S(1)} %select_add_fusion.5), channel_id=1, source_target_pairs={{0,32},{16,48},{32,0},{48,16},{64,96},{80,112},{96,64},{112,80},{1... | collective-permute-start | bytes 24584 | tf_op jit(solution)/shard_map/ppermute | solution.py:425
  10.5 0.2 shard_map.65
  10.7 0.9 %collective-permute-start.1 = (f32[8,128]{1,0:T(8,128)S(1)}, f32[8,128]{1,0:T(8,128)S(1)}, u32[]{:S(2)}, u32[]{:S(2)}) collective-permute-start(f32[8,128]{1,0:T(8,128)S(1)} %get-tuple-element.25), channel_id=1, source_target_pairs={{0,1},{1,0},{2,3},{3,2},{4,5},{5,4},{6,7},{7,6},{8,9},{9,8},{10,11... | collective-permute-start | bytes 12296 | tf_op jit(solution)/shard_map/ppermute | solution.py:425
  11.6 2.2 %collective-permute-start.2 = (f32[8,128]{1,0:T(8,128)S(1)}, f32[8,128]{1,0:T(8,128)S(1)}, u32[]{:S(2)}, u32[]{:S(2)}) collective-permute-start(f32[8,128]{1,0:T(8,128)S(1)} %get-tuple-element.26), channel_id=1, source_target_pairs={{0,15},{1,2},{2,1},{3,4},{4,3},{5,6},{6,5},{7,8},{8,7},{9,10},{10,... | collective-permute-start | bytes 12296 | tf_op jit(solution)/shard_map/ppermute | solution.py:430
  13.8 0.5 collective-permute-done.1.za_ref
  14.4 2.9 %collective-permute-done.2.zb_ref = f32[8,128]{1,0:T(8,128)S(1)} collective-permute-done((f32[8,128]{1,0:T(8,128)S(1)}, f32[8,128]{1,0:T(8,128)S(1)}, u32[]{:S(2)}, u32[]{:S(2)}) %collective-permute-start.2) | collective-permute-done | bytes 4128 | tf_op jit(solution)/shard_map/ppermute | solution.py:430
  17.3 0.2 shard_map.66
  17.5 2.0 %collective-permute-start.5 = (f32[72,128]{1,0:T(8,128)S(1)}, f32[72,128]{1,0:T(8,128)S(1)}, u32[]{:S(2)}, u32[]{:S(2)}) collective-permute-start(f32[72,128]{1,0:T(8,128)S(1)} %get-tuple-element.28), channel_id=1, source_target_pairs={{0,16},{16,0},{32,48},{48,32},{64,80},{80,64},{96,112},{112,96},{1... | collective-permute-start | bytes 110600 | tf_op jit(solution)/shard_map/ppermute | solution.py:425
  19.5 2.0 %collective-permute-done.5.ya_ref = f32[72,128]{1,0:T(8,128)S(1)} collective-permute-done((f32[72,128]{1,0:T(8,128)S(1)}, f32[72,128]{1,0:T(8,128)S(1)}, u32[]{:S(2)}, u32[]{:S(2)}) %collective-permute-start.5) | collective-permute-done | bytes 36896 | tf_op jit(solution)/shard_map/ppermute | solution.py:425
  21.5 0.1 fusion
  21.6 4.5 %collective-permute-start.10 = (f32[16,128]{1,0:T(8,128)S(1)}, f32[16,128]{1,0:T(8,128)S(1)}, u32[]{:S(2)}, u32[]{:S(2)}) collective-permute-start(f32[16,128]{1,0:T(8,128)S(1)} %fusion), channel_id=1, source_target_pairs={{0,96},{16,112},{32,64},{48,80},{64,32},{80,48},{96,0},{112,16},{1... | collective-permute-start | bytes 24584 | tf_op jit(solution)/shard_map/ppermute | solution.py:425
  26.1 1.6 %collective-permute-done.10 = f32[16,128]{1,0:T(8,128)S(1)} collective-permute-done((f32[16,128]{1,0:T(8,128)S(1)}, f32[16,128]{1,0:T(8,128)S(1)}, u32[]{:S(2)}, u32[]{:S(2)}) %collective-permute-start.10) | collective-permute-done | bytes 8224 | tf_op jit(solution)/shard_map/ppermute | solution.py:425
  27.8 1.6 %collective-permute-start.11 = (f32[16,128]{1,0:T(8,128)S(1)}, f32[16,128]{1,0:T(8,128)S(1)}, u32[]{:S(2)}, u32[]{:S(2)}) collective-permute-start(f32[16,128]{1,0:T(8,128)S(1)} %select_add_fusion.3), channel_id=1, source_target_pairs={{0,4},{1,5},{2,6},{3,7},{4,0},{5,1},{6,2},{7,3},{8,12},{9,13},{10,... | collective-permute-start | bytes 24584 | tf_op jit(solution)/shard_map/ppermute | solution.py:425
  29.4 3.7 %collective-permute-start.6 = (f32[56,128]{1,0:T(8,128)S(1)}, f32[56,128]{1,0:T(8,128)S(1)}, u32[]{:S(2)}, u32[]{:S(2)}) collective-permute-start(f32[56,128]{1,0:T(8,128)S(1)} %get-tuple-element.29), channel_id=1, source_target_pairs={{0,112},{16,32},{32,16},{48,64},{64,48},{80,96},{96,80},{112,0},{1... | collective-permute-start | bytes 86024 | tf_op jit(solution)/shard_map/ppermute | solution.py:430
  33.2 1.7 %collective-permute-done.6.yb_ref = f32[56,128]{1,0:T(8,128)S(1)} collective-permute-done((f32[56,128]{1,0:T(8,128)S(1)}, f32[56,128]{1,0:T(8,128)S(1)}, u32[]{:S(2)}, u32[]{:S(2)}) %collective-permute-start.6) | collective-permute-done | bytes 28704 | tf_op jit(solution)/shard_map/ppermute | solution.py:430
  35.0 2.7 %shard_map.67.u_ref = f32[1696,128]{1,0:T(8,128)S(1)} custom-call(f32[8,8,8,128]{3,2,1,0:T(8,128)S(1)} %get-tuple-element.22.core_ref, f32[512,128]{1,0:T(8,128)S(1)} %bitcast.11, f32[2,8,8,128]{3,2,1,0:T(8,128)S(1)} %get-tuple-element.24.ends_ref, f32[128,128]{1,0:T(8,128)S(1)} %bitcast.13, f32[8,128]{1,0:T(8,128)S(1)} %collective-permute-done.1.za_ref, ...), custom_call_target="tpu_custom_call" | custom-call | tf_op jit(solution)/shard_map/pallas_call | solution.py:463
  37.6 1.4 %shard_map.68 = (f32[10,10,8,128]{3,2,1,0:T(8,128)S(1)}, f32[10,16,128]{2,1,0:T(8,128)S(1)}, f32[10,16,128]{2,1,0:T(8,128)S(1)}, f32[56,128]{1,0:T(8,128)S(1)}) custom-call(f32[1696,128]{1,0:T(8,128)S(1)} %shard_map.67.u_ref, bf16[10,10,3,128]{3,2,1,0:T(4,128)(2,1)S(1)} %bitcast.17), custom_call_target="tpu_custom_call" | custom-call | tf_op jit(solution)/shard_map/pallas_call | solution.py:467
  39.1 0.1 select_add_fusion.1
  39.1 4.1 %collective-permute-start.13 = (f32[16,128]{1,0:T(8,128)S(1)}, f32[16,128]{1,0:T(8,128)S(1)}, u32[]{:S(2)}, u32[]{:S(2)}) collective-permute-start(f32[16,128]{1,0:T(8,128)S(1)} %select_add_fusion.1), channel_id=1, source_target_pairs={{0,8},{1,9},{2,10},{3,11},{4,12},{5,13},{6,14},{7,15},{8,0},{9,1},... | collective-permute-start | bytes 24584 | tf_op jit(solution)/shard_map/ppermute | solution.py:425
  43.3 0.1 shard_map.69
  43.4 0.1 collective-permute-start.8
  43.5 3.3 %collective-permute-start.9 = (f32[64,128]{1,0:T(8,128)S(1)}, f32[64,128]{1,0:T(8,128)S(1)}, u32[]{:S(2)}, u32[]{:S(2)}) collective-permute-start(f32[64,128]{1,0:T(8,128)S(1)} %get-tuple-element.35), channel_id=1, source_target_pairs={{0,112},{16,32},{32,16},{48,64},{64,48},{80,96},{96,80},{112,0},{1... | collective-permute-start | bytes 98312 | tf_op jit(solution)/shard_map/ppermute | solution.py:430
  46.9 0.5 collective-permute-done.8.ya_ref
  47.4 1.3 %collective-permute-done.9.yb_ref = f32[64,128]{1,0:T(8,128)S(1)} collective-permute-done((f32[64,128]{1,0:T(8,128)S(1)}, f32[64,128]{1,0:T(8,128)S(1)}, u32[]{:S(2)}, u32[]{:S(2)}) %collective-permute-start.9) | collective-permute-done | bytes 32800 | tf_op jit(solution)/shard_map/ppermute | solution.py:430
  48.7 0.3 shard_map.70
  49.0 0.1 collective-permute-start.14
  49.1 0.1 collective-permute-start.15
  49.2 5.7 %collective-permute-done.15.zb_ref = f32[8,128]{1,0:T(8,128)S(1)} collective-permute-done((f32[8,128]{1,0:T(8,128)S(1)}, f32[8,128]{1,0:T(8,128)S(1)}, u32[]{:S(2)}, u32[]{:S(2)}) %collective-permute-start.15) | collective-permute-done | bytes 4128 | tf_op jit(solution)/shard_map/ppermute | solution.py:430
  54.9 1.9 %shard_map.71 = f32[256,256]{1,0:T(8,128)} custom-call(f32[10,10,8,128]{3,2,1,0:T(8,128)S(1)} %get-tuple-element.30.l_ref, f32[10,16,128]{2,1,0:T(8,128)S(1)} %get-tuple-element.31.hl_ref, f32[10,16,128]{2,1,0:T(8,128)S(1)} %get-tuple-element.32.hh_ref, f32[56,128]{1,0:T(8,128)S(1)} %collective-permute-done.7.xr_ref, ...), custom_call_target="tpu_custom_call" | custom-call | tf_op jit(solution)/shard_map/pallas_call | solution.py:478
  (30 shorter events, 0.5 us)
Async XLA Ops:
  1.8 5.2 %collective-permute-start.3 = (f32[16,128]{1,0:T(8,128)S(1)}, f32[16,128]{1,0:T(8,128)S(1)}, u32[]{:S(2)}, u32[]{:S(2)}) collective-permute-start(f32[16,128]{1,0:T(8,128)S(1)} %get-tuple-element.27), channel_id=1, source_target_pairs={{0,2},{1,3},{2,0},{3,1},{4,6},{5,7},{6,4},{7,5},{8,10},{9,11},{10,... | collective-permute-start | bytes 24584 | tf_op jit(solution)/shard_map/ppermute | solution.py:425
  3.3 7.1 %collective-permute-start = (f32[32,128]{1,0:T(8,128)S(1)}, f32[32,128]{1,0:T(8,128)S(1)}, u32[]{:S(2)}, u32[]{:S(2)}) collective-permute-start(f32[32,128]{1,0:T(8,128)S(1)} %get-tuple-element.23), channel_id=1, source_target_pairs={{0,128},{128,0},{1,129},{129,1},{2,130},{130,2},{3,131},{131,3},{4... | collective-permute-start | bytes 49160 | tf_op jit(solution)/shard_map/ppermute | solution.py:425
  7.2 6.6 %collective-permute-start.4 = (f32[16,128]{1,0:T(8,128)S(1)}, f32[16,128]{1,0:T(8,128)S(1)}, u32[]{:S(2)}, u32[]{:S(2)}) collective-permute-start(f32[16,128]{1,0:T(8,128)S(1)} %select_add_fusion.5), channel_id=1, source_target_pairs={{0,32},{16,48},{32,0},{48,16},{64,96},{80,112},{96,64},{112,80},{1... | collective-permute-start | bytes 24584 | tf_op jit(solution)/shard_map/ppermute | solution.py:425
  10.7 3.7 %collective-permute-start.1 = (f32[8,128]{1,0:T(8,128)S(1)}, f32[8,128]{1,0:T(8,128)S(1)}, u32[]{:S(2)}, u32[]{:S(2)}) collective-permute-start(f32[8,128]{1,0:T(8,128)S(1)} %get-tuple-element.25), channel_id=1, source_target_pairs={{0,1},{1,0},{2,3},{3,2},{4,5},{5,4},{6,7},{7,6},{8,9},{9,8},{10,11... | collective-permute-start | bytes 12296 | tf_op jit(solution)/shard_map/ppermute | solution.py:425
  11.6 5.7 %collective-permute-start.2 = (f32[8,128]{1,0:T(8,128)S(1)}, f32[8,128]{1,0:T(8,128)S(1)}, u32[]{:S(2)}, u32[]{:S(2)}) collective-permute-start(f32[8,128]{1,0:T(8,128)S(1)} %get-tuple-element.26), channel_id=1, source_target_pairs={{0,15},{1,2},{2,1},{3,4},{4,3},{5,6},{6,5},{7,8},{8,7},{9,10},{10,... | collective-permute-start | bytes 12296 | tf_op jit(solution)/shard_map/ppermute | solution.py:430
  17.3 17.6 %copy-start.1 = (bf16[1,1,1,3,10,10,128]{6,3,5,4,2,1,0:T(4,128)(2,1)S(1)}, bf16[1,1,1,3,10,10,128]{6,3,5,4,2,1,0:T(4,128)(2,1)}, u32[]{:S(2)}) copy-start(bf16[1,1,1,3,10,10,128]{6,3,5,4,2,1,0:T(4,128)(2,1)} %param.7) | copy-start | bytes 230404
  17.5 4.0 %collective-permute-start.5 = (f32[72,128]{1,0:T(8,128)S(1)}, f32[72,128]{1,0:T(8,128)S(1)}, u32[]{:S(2)}, u32[]{:S(2)}) collective-permute-start(f32[72,128]{1,0:T(8,128)S(1)} %get-tuple-element.28), channel_id=1, source_target_pairs={{0,16},{16,0},{32,48},{48,32},{64,80},{80,64},{96,112},{112,96},{1... | collective-permute-start | bytes 110600 | tf_op jit(solution)/shard_map/ppermute | solution.py:425
  21.6 6.1 %collective-permute-start.10 = (f32[16,128]{1,0:T(8,128)S(1)}, f32[16,128]{1,0:T(8,128)S(1)}, u32[]{:S(2)}, u32[]{:S(2)}) collective-permute-start(f32[16,128]{1,0:T(8,128)S(1)} %fusion), channel_id=1, source_target_pairs={{0,96},{16,112},{32,64},{48,80},{64,32},{80,48},{96,0},{112,16},{1... | collective-permute-start | bytes 24584 | tf_op jit(solution)/shard_map/ppermute | solution.py:425
  27.8 5.3 %collective-permute-start.11 = (f32[16,128]{1,0:T(8,128)S(1)}, f32[16,128]{1,0:T(8,128)S(1)}, u32[]{:S(2)}, u32[]{:S(2)}) collective-permute-start(f32[16,128]{1,0:T(8,128)S(1)} %select_add_fusion.3), channel_id=1, source_target_pairs={{0,4},{1,5},{2,6},{3,7},{4,0},{5,1},{6,2},{7,3},{8,12},{9,13},{10,... | collective-permute-start | bytes 24584 | tf_op jit(solution)/shard_map/ppermute | solution.py:425
  29.4 5.5 %copy-start.3 = (f32[1,1,1,3,10,128]{5,2,4,3,1,0:T(1,128)S(1)}, f32[1,1,1,3,10,128]{5,2,4,3,1,0:T(1,128)}, u32[]{:S(2)}) copy-start(f32[1,1,1,3,10,128]{5,2,4,3,1,0:T(1,128)} %param.8) | copy-start | bytes 46084
  29.4 5.5 %collective-permute-start.6 = (f32[56,128]{1,0:T(8,128)S(1)}, f32[56,128]{1,0:T(8,128)S(1)}, u32[]{:S(2)}, u32[]{:S(2)}) collective-permute-start(f32[56,128]{1,0:T(8,128)S(1)} %get-tuple-element.29), channel_id=1, source_target_pairs={{0,112},{16,32},{32,16},{48,64},{64,48},{80,96},{96,80},{112,0},{1... | collective-permute-start | bytes 86024 | tf_op jit(solution)/shard_map/ppermute | solution.py:430
  33.2 5.9 %collective-permute-start.12 = (f32[16,128]{1,0:T(8,128)S(1)}, f32[16,128]{1,0:T(8,128)S(1)}, u32[]{:S(2)}, u32[]{:S(2)}) collective-permute-start(f32[16,128]{1,0:T(8,128)S(1)} %select_add_fusion.2), channel_id=1, source_target_pairs={{0,128},{128,0},{1,129},{129,1},{2,130},{130,2},{3,131},{131,3},{4... | collective-permute-start | bytes 24584 | tf_op jit(solution)/shard_map/ppermute | solution.py:425
  39.0 4.3 %collective-permute-start.7 = (f32[56,128]{1,0:T(8,128)S(1)}, f32[56,128]{1,0:T(8,128)S(1)}, u32[]{:S(2)}, u32[]{:S(2)}) collective-permute-start(f32[56,128]{1,0:T(8,128)S(1)} %get-tuple-element.33), channel_id=1, source_target_pairs={{0,128},{128,0},{1,129},{129,1},{2,130},{130,2},{3,131},{131,3},{4... | collective-permute-start | bytes 86024 | tf_op jit(solution)/shard_map/ppermute | solution.py:425
  39.1 7.7 %collective-permute-start.13 = (f32[16,128]{1,0:T(8,128)S(1)}, f32[16,128]{1,0:T(8,128)S(1)}, u32[]{:S(2)}, u32[]{:S(2)}) collective-permute-start(f32[16,128]{1,0:T(8,128)S(1)} %select_add_fusion.1), channel_id=1, source_target_pairs={{0,8},{1,9},{2,10},{3,11},{4,12},{5,13},{6,14},{7,15},{8,0},{9,1},... | collective-permute-start | bytes 24584 | tf_op jit(solution)/shard_map/ppermute | solution.py:425
  43.4 4.0 %collective-permute-start.8 = (f32[64,128]{1,0:T(8,128)S(1)}, f32[64,128]{1,0:T(8,128)S(1)}, u32[]{:S(2)}, u32[]{:S(2)}) collective-permute-start(f32[64,128]{1,0:T(8,128)S(1)} %get-tuple-element.34), channel_id=1, source_target_pairs={{0,16},{16,0},{32,48},{48,32},{64,80},{80,64},{96,112},{112,96},{1... | collective-permute-start | bytes 98312 | tf_op jit(solution)/shard_map/ppermute | solution.py:425
  43.5 5.2 %collective-permute-start.9 = (f32[64,128]{1,0:T(8,128)S(1)}, f32[64,128]{1,0:T(8,128)S(1)}, u32[]{:S(2)}, u32[]{:S(2)}) collective-permute-start(f32[64,128]{1,0:T(8,128)S(1)} %get-tuple-element.35), channel_id=1, source_target_pairs={{0,112},{16,32},{32,16},{48,64},{64,48},{80,96},{96,80},{112,0},{1... | collective-permute-start | bytes 98312 | tf_op jit(solution)/shard_map/ppermute | solution.py:430
  48.7 6.2 %copy-start = (f32[1,1,1,8,16,256]{5,4,3,2,1,0:T(8,128)S(1)}, f32[1,1,1,8,16,256]{5,4,3,2,1,0:T(8,128)}, u32[]{:S(2)}) copy-start(f32[1,1,1,8,16,256]{5,4,3,2,1,0:T(8,128)} %param.11) | copy-start | bytes 393220
  48.7 6.2 %copy-start.2 = (f32[8,8,8]{2,1,0:T(8,128)S(1)}, f32[8,8,8]{2,1,0:T(8,128)}, u32[]{:S(2)}) copy-start(f32[8,8,8]{2,1,0:T(8,128)} %basis_ref.3) | copy-start | bytes 6148
  49.0 5.9 %collective-permute-start.14 = (f32[24,128]{1,0:T(8,128)S(1)}, f32[24,128]{1,0:T(8,128)S(1)}, u32[]{:S(2)}, u32[]{:S(2)}) collective-permute-start(f32[24,128]{1,0:T(8,128)S(1)} %get-tuple-element.36), channel_id=1, source_target_pairs={{0,1},{1,0},{2,3},{3,2},{4,5},{5,4},{6,7},{7,6},{8,9},{9,8},{10,11... | collective-permute-start | bytes 36872 | tf_op jit(solution)/shard_map/ppermute | solution.py:425
  49.1 5.8 %collective-permute-start.15 = (f32[8,128]{1,0:T(8,128)S(1)}, f32[8,128]{1,0:T(8,128)S(1)}, u32[]{:S(2)}, u32[]{:S(2)}) collective-permute-start(f32[8,128]{1,0:T(8,128)S(1)} %get-tuple-element.37), channel_id=1, source_target_pairs={{0,15},{1,2},{2,1},{3,4},{4,3},{5,6},{6,5},{7,8},{8,7},{9,10},{10,... | collective-permute-start | bytes 12296 | tf_op jit(solution)/shard_map/ppermute | solution.py:430

commit v3 on v2

--- a/solution.py
+++ b/solution.py
@@ -150,8 +150,7 @@
     return low, high, low_ends, high_ends
 
 
-def yface_kernel(core_ref, core2_ref, ends_ref, ends2_ref, za_ref, zb_ref, run_ref, ya_ref, yb_ref, scr):
-    ya_ref[56:72] = run_ref[...]
+def yface_kernel(core_ref, core2_ref, ends_ref, ends2_ref, za_ref, zb_ref, ya_ref, yb_ref, scr):
     even_y = lax.rem(lax.axis_index("gy"), 2) == 0
     lane, _ = iotas()
     low_q = (lane & 32) == 0
@@ -195,8 +194,7 @@
 
 
 def modes_kernel(
-    core_ref, core2_ref, ends_ref, ends2_ref, za_ref, zb_ref, ya_ref, yb_ref, vec_ref, eig_ref,
-    u, block, jl, jh, s, eg, scr,
+    core_ref, core2_ref, ends_ref, ends2_ref, za_ref, zb_ref, ya_ref, yb_ref, vec_ref, u, block, jl, jh, s, scr
 ):
     lane, _ = iotas()
     low_q = (lane & 32) == 0
@@ -220,14 +218,7 @@
     jl[96:112] = jnp.where(low_q16, below, roll(high_ends[1], 32))
     jh[80:96] = jnp.where(low_q16, roll(low_ends[0], 96), roll(above, 32))
     jh[96:112] = jnp.where(low_q16, roll(low_ends[1], 96), above)
-    eg[...] = jnp.ones((16, 128), F32)
-    for a in range(10):
-        eg[a : a + 1] = eig_ref[1, a]
     factor = load_factors(vec_ref, s)
-
-    def wide(value):
-        return jnp.broadcast_to(value, (8, 128))
-
     front = [[s[pl.ds((j * 10 + 8 * h) * 8 + 1, 8, stride=8), :] for j in range(10)] for h in range(2)]
 
     def fwd_y(i, _):
@@ -244,10 +235,20 @@
 
     along_x(u, u, factor, False)
 
+
+def middle_kernel(u_ref, vec_ref, eig_ref, u, s, eg):
+    eg[...] = jnp.ones((16, 128), F32)
+    for a in range(10):
+        eg[a : a + 1] = eig_ref[1, a]
+    factor = load_factors(vec_ref, s)
+
+    def wide(value):
+        return jnp.broadcast_to(value, (8, 128))
+
     def along_z(a, _):
         for h in range(2):
             at = a * 160 + 8 * h
-            held = [u[pl.ds(at + k * 16, 8), :] for k in range(10)]
+            held = [u_ref[pl.ds(at + k * 16, 8), :] for k in range(10)]
             base = wide(eig_ref[0, a]) + eg[8 * h : 8 * h + 8]
             modes = []
             for c in range(10):
@@ -309,7 +310,8 @@
     return low, high
 
 
-def yfold_send_kernel(hl_ref, hh_ref, xr_ref, ya_ref, yb_ref):
+def yfold_send_kernel(hl_ref, hh_ref, xr_ref, run_ref, ya_ref, yb_ref):
+    ya_ref[64:80] = run_ref[...]
     gx = lax.axis_index("gx")
     even_y = lax.rem(lax.axis_index("gy"), 2) == 0
     low_q = (iotas(16)[0] & 32) == 0
@@ -344,8 +346,10 @@
     return value + jnp.where(sub == 0, row(rows_first, at), jnp.where(sub == 7, row(rows_last, at), 0.0))
 
 
-def zfold_send_kernel(l_ref, hl_ref, hh_ref, xr_ref, ya_ref, yb_ref, run_ref, za_ref, zb_ref, rows_first, rows_last):
-    za_ref[8:24] = run_ref[...]
+def zfold_send_kernel(l_ref, hl_ref, hh_ref, xr_ref, ya_ref, yb_ref, run_ref, za_ref, zb_ref, sum_ref, rows_first, rows_last):
+    level = iotas(16)[1] & 7
+    sum_ref[...] = run_ref[...] + jnp.where(level >= 4, ya_ref[64:80], 0.0)
+    za_ref[8:24] = sum_ref[...]
     gx = lax.axis_index("gx")
     even_z = lax.rem(lax.axis_index("gz"), 2) == 0
     lane, sub = iotas()
@@ -451,29 +455,29 @@
         semaphores=(pltpu.SemaphoreType.DMA((2,)), pltpu.SemaphoreType.DMA((3,))),
     )(far(x), far(sep), far(coarse_basis), far(own))
     xr = swap(xs, "gx", 1)
-    running = climb(running, "gz", 2, 1)
+    running = climb(running, "gx", 1, 7)
     ends, za, zb = call(zface_kernel, [(2, 8, 8, 128), (8, 128), (8, 128)], [], 2)(core, xr)
+    running = climb(running, "gy", 2, 5)
     za, zb = swap(za, "gz", 1), swap_odd(zb, "gz")
-    running = climb(running, "gy", 2, 5)
+    running = climb(running, "gy", 6, 6)
     block = (core, core.reshape(512, 128), ends, ends.reshape(128, 128), za, zb)
-    ya, yb = call(yface_kernel, [(72, 128), (56, 128)], [(256, 128)], 7)(*block, running)
+    ya, yb = call(yface_kernel, [(56, 128), (56, 128)], [(256, 128)], 6)(*block)
     ya, yb = swap(ya, "gy", 1), swap_odd(yb, "gy")
-    running = running + jnp.where(level_of >= 4, ya[56:72], 0.0)
-    running = climb(running, "gy", 6, 6)
+    running = climb(running, "gz", 4, 2)
     (modes,) = call(
-        modes_kernel, [(1696, 128)], [(800, 128), (112, 128), (112, 128), (848, 128), (16, 128), (256, 128)], 10
-    )(*block, ya, yb, vectors, eigen)
-    running = climb(running, "gz", 4, 2)
+        modes_kernel, [(1696, 128)], [(800, 128), (112, 128), (112, 128), (848, 128), (256, 128)], 9
+    )(*block, ya, yb, vectors)
+    running = climb(running, "gz", 12, 3)
+    (modes,) = call(middle_kernel, [(1696, 128)], [(848, 128), (16, 128)], 3)(modes, vectors, eigen)
+    running = climb(running, "gz", 3, 1)
     local, edge_l, edge_h, xs = call(
         points_kernel, [(10, 10, 8, 128), (10, 16, 128), (10, 16, 128), (56, 128)], [(1696, 128), (848, 128)], 2
     )(modes, vectors)
     xr = swap(xs, "gx", 1)
-    running = climb(running, "gx", 1, 7)
-    ya, yb = call(yfold_send_kernel, [(64, 128)] * 2, [], 3)(edge_l, edge_h, xr)
+    ya, yb = call(yfold_send_kernel, [(80, 128), (64, 128)], [], 4)(edge_l, edge_h, xr, running)
     ya, yb = swap(ya, "gy", 1), swap_odd(yb, "gy")
-    running = climb(running, "gz", 8, 3)
     parts = (local, edge_l, edge_h, xr, ya, yb)
-    za, zb = call(zfold_send_kernel, [(24, 128), (8, 128)], [(128, 128)] * 2, 7)(*parts, running)
+    za, zb, running = call(zfold_send_kernel, [(24, 128), (8, 128), (16, 128)], [(128, 128)] * 2, 7)(*parts, running)
     za, zb = swap(za, "gz", 1), swap_odd(zb, "gz")
     (out,) = call(
         post_kernel, [(256, 256)], [(128, 128), (128, 128), (2, 256, 128), (8, 8, 8, 128)], 12

time: 56.9 us -> 52.3 us (0.919)
  the two profiles are of different devices: /device:TPU:6 before, /device:TPU:1 now
where the time goes in v3:
time: 52.3 us; the launch traced here: 52.2 us
  starting transfers between devices  32.8 us (63%)
  waiting for transfers between devices  10.2 us (20%)
  Pallas kernels  8.63 us (17%)
    ppermute x12, starting transfers between devices, swap(): lax.ppermute(value, axis, [(i, i ^ distance) for i in range(lax.axis_size...  19.7 us
    ppermute x4, starting transfers between devices, swap_odd(): lax.ppermute(value, axis, [(i, (i + 1 if i % 2 else i - 1) % count) for i...  13.1 us
    ppermute x4, waiting for transfers between devices, swap_odd(): lax.ppermute(value, axis, [(i, (i + 1 if i % 2 else i - 1) % count) for i...  5.5 us
    ppermute x12, waiting for transfers between devices, swap(): lax.ppermute(value, axis, [(i, i ^ distance) for i in range(lax.axis_size...  4.67 us
    pallas_call x1, Pallas kernels, work(): call(post_kernel, [(256, 256)], [(128, 128), (128, 128), (2, 256, 128), (...  1.89 us
    pallas_call x1, Pallas kernels, work(): call(pre_kernel, [(8, 8, 8, 128), (32, 128), (16, 128), (16, 128)], [(2,...  1.84 us
    pallas_call x1, Pallas kernels, work(): call(modes_kernel, [(1696, 128)], [(800, 128), (112, 128), (112, 128), (8...  1.46 us
    pallas_call x1, Pallas kernels, work(): call(points_kernel, [(10, 10, 8, 128), (10, 16, 128), (10, 16, 128), (56,...  1.41 us
  transfers between devices with their start and end apart: 16, of which 8 were waited for; matrix products, arithmetic and copies ran while one was open for 1% of the time, Pallas kernels for 9%

profile of v3, /device:TPU:1, one launch (start us, length us, event | category | flops | bytes accessed | tf_op | source)
XLA Modules:
  0.0 52.2 jit_solution(10957618862842788537)
XLA Ops:
  0.0 1.8 %shard_map.64 = (f32[8,8,8,128]{3,2,1,0:T(8,128)S(1)}, f32[32,128]{1,0:T(8,128)S(1)}, f32[16,128]{1,0:T(8,128)S(1)}, f32[16,128]{1,0:T(8,128)S(1)}) custom-call(f32[256,256]{1,0:T(8,128)} %bitcast.20, f32[8,16,256]{2,1,0:T(8,128)} %bitcast.17, f32[8,8,8]{2,1,0:T(8,128)} %basis_ref.3, f32[16,16]{1,0:T(8,128)} %bitcast.21), custom_call_target="tpu_custom_call" | custom-call | tf_op jit(solution)/shard_map/pallas_call | solution.py:449
  1.8 3.3 %collective-permute-start.6 = (f32[16,128]{1,0:T(8,128)S(1)}, f32[16,128]{1,0:T(8,128)S(1)}, u32[]{:S(2)}, u32[]{:S(2)}) collective-permute-start(f32[16,128]{1,0:T(8,128)S(1)} %get-tuple-element.34), channel_id=1, source_target_pairs={{0,128},{128,0},{1,129},{129,1},{2,130},{130,2},{3,131},{131,3},{4... | collective-permute-start | bytes 24584 | tf_op jit(solution)/shard_map/ppermute | solution.py:429
  5.1 0.1 collective-permute-start
  5.2 0.7 %collective-permute-done.6 = f32[16,128]{1,0:T(8,128)S(1)} collective-permute-done((f32[16,128]{1,0:T(8,128)S(1)}, f32[16,128]{1,0:T(8,128)S(1)}, u32[]{:S(2)}, u32[]{:S(2)}) %collective-permute-start.6) | collective-permute-done | bytes 8224 | tf_op jit(solution)/shard_map/ppermute | solution.py:429
  6.0 1.3 %collective-permute-start.7 = (f32[16,128]{1,0:T(8,128)S(1)}, f32[16,128]{1,0:T(8,128)S(1)}, u32[]{:S(2)}, u32[]{:S(2)}) collective-permute-start(f32[16,128]{1,0:T(8,128)S(1)} %select_add_fusion.5), channel_id=1, source_target_pairs={{0,32},{16,48},{32,0},{48,16},{64,96},{80,112},{96,64},{112,80},{1... | collective-permute-start | bytes 24584 | tf_op jit(solution)/shard_map/ppermute | solution.py:429
  7.3 2.1 %collective-permute-done.7 = f32[16,128]{1,0:T(8,128)S(1)} collective-permute-done((f32[16,128]{1,0:T(8,128)S(1)}, f32[16,128]{1,0:T(8,128)S(1)}, u32[]{:S(2)}, u32[]{:S(2)}) %collective-permute-start.7) | collective-permute-done | bytes 8224 | tf_op jit(solution)/shard_map/ppermute | solution.py:429
  9.5 4.3 %collective-permute-start.8 = (f32[16,128]{1,0:T(8,128)S(1)}, f32[16,128]{1,0:T(8,128)S(1)}, u32[]{:S(2)}, u32[]{:S(2)}) collective-permute-start(f32[16,128]{1,0:T(8,128)S(1)} %select_add_fusion.4), channel_id=1, source_target_pairs={{0,96},{16,112},{32,64},{48,80},{64,32},{80,48},{96,0},{112,16},{1... | collective-permute-start | bytes 24584 | tf_op jit(solution)/shard_map/ppermute | solution.py:429
  13.9 1.0 %collective-permute-done.8 = f32[16,128]{1,0:T(8,128)S(1)} collective-permute-done((f32[16,128]{1,0:T(8,128)S(1)}, f32[16,128]{1,0:T(8,128)S(1)}, u32[]{:S(2)}, u32[]{:S(2)}) %collective-permute-start.8) | collective-permute-done | bytes 8224 | tf_op jit(solution)/shard_map/ppermute | solution.py:429
  15.0 1.3 %collective-permute-start.9 = (f32[16,128]{1,0:T(8,128)S(1)}, f32[16,128]{1,0:T(8,128)S(1)}, u32[]{:S(2)}, u32[]{:S(2)}) collective-permute-start(f32[16,128]{1,0:T(8,128)S(1)} %select_add_fusion.3), channel_id=1, source_target_pairs={{0,4},{1,5},{2,6},{3,7},{4,0},{5,1},{6,2},{7,3},{8,12},{9,13},{10,... | collective-permute-start | bytes 24584 | tf_op jit(solution)/shard_map/ppermute | solution.py:429
  16.3 0.2 shard_map.65
  16.5 1.3 %collective-permute-start.1 = (f32[8,128]{1,0:T(8,128)S(1)}, f32[8,128]{1,0:T(8,128)S(1)}, u32[]{:S(2)}, u32[]{:S(2)}) collective-permute-start(f32[8,128]{1,0:T(8,128)S(1)} %get-tuple-element.26), channel_id=1, source_target_pairs={{0,1},{1,0},{2,3},{3,2},{4,5},{5,4},{6,7},{7,6},{8,9},{9,8},{10,11... | collective-permute-start | bytes 12296 | tf_op jit(solution)/shard_map/ppermute | solution.py:429
  17.8 3.4 %collective-permute-start.2 = (f32[8,128]{1,0:T(8,128)S(1)}, f32[8,128]{1,0:T(8,128)S(1)}, u32[]{:S(2)}, u32[]{:S(2)}) collective-permute-start(f32[8,128]{1,0:T(8,128)S(1)} %get-tuple-element.27), channel_id=1, source_target_pairs={{0,15},{1,2},{2,1},{3,4},{4,3},{5,6},{6,5},{7,8},{8,7},{9,10},{10,... | collective-permute-start | bytes 12296 | tf_op jit(solution)/shard_map/ppermute | solution.py:434
  21.3 1.0 %collective-permute-start.10 = (f32[16,128]{1,0:T(8,128)S(1)}, f32[16,128]{1,0:T(8,128)S(1)}, u32[]{:S(2)}, u32[]{:S(2)}) collective-permute-start(f32[16,128]{1,0:T(8,128)S(1)} %select_add_fusion.2), channel_id=1, source_target_pairs={{0,12},{1,13},{2,14},{3,15},{4,8},{5,9},{6,10},{7,11},{8,4},{9,5},... | collective-permute-start | bytes 24584 | tf_op jit(solution)/shard_map/ppermute | solution.py:429
  22.4 1.2 %collective-permute-done.2.zb_ref = f32[8,128]{1,0:T(8,128)S(1)} collective-permute-done((f32[8,128]{1,0:T(8,128)S(1)}, f32[8,128]{1,0:T(8,128)S(1)}, u32[]{:S(2)}, u32[]{:S(2)}) %collective-permute-start.2) | collective-permute-done | bytes 4128 | tf_op jit(solution)/shard_map/ppermute | solution.py:434
  23.6 0.2 shard_map.66
  23.8 0.8 %collective-permute-start.3 = (f32[56,128]{1,0:T(8,128)S(1)}, f32[56,128]{1,0:T(8,128)S(1)}, u32[]{:S(2)}, u32[]{:S(2)}) collective-permute-start(f32[56,128]{1,0:T(8,128)S(1)} %get-tuple-element.28), channel_id=1, source_target_pairs={{0,16},{16,0},{32,48},{48,32},{64,80},{80,64},{96,112},{112,96},{1... | collective-permute-start | bytes 86024 | tf_op jit(solution)/shard_map/ppermute | solution.py:429
  24.6 3.1 %collective-permute-start.4 = (f32[56,128]{1,0:T(8,128)S(1)}, f32[56,128]{1,0:T(8,128)S(1)}, u32[]{:S(2)}, u32[]{:S(2)}) collective-permute-start(f32[56,128]{1,0:T(8,128)S(1)} %get-tuple-element.29), channel_id=1, source_target_pairs={{0,112},{16,32},{32,16},{48,64},{64,48},{80,96},{96,80},{112,0},{1... | collective-permute-start | bytes 86024 | tf_op jit(solution)/shard_map/ppermute | solution.py:434
  27.8 0.6 %collective-permute-start.11 = (f32[16,128]{1,0:T(8,128)S(1)}, f32[16,128]{1,0:T(8,128)S(1)}, u32[]{:S(2)}, u32[]{:S(2)}) collective-permute-start(f32[16,128]{1,0:T(8,128)S(1)} %select_add_fusion.1), channel_id=1, source_target_pairs={{0,3},{1,2},{2,1},{3,0},{4,7},{5,6},{6,5},{7,4},{8,11},{9,10},{10,... | collective-permute-start | bytes 24584 | tf_op jit(solution)/shard_map/ppermute | solution.py:429
  28.4 0.6 %collective-permute-done.4.yb_ref = f32[56,128]{1,0:T(8,128)S(1)} collective-permute-done((f32[56,128]{1,0:T(8,128)S(1)}, f32[56,128]{1,0:T(8,128)S(1)}, u32[]{:S(2)}, u32[]{:S(2)}) %collective-permute-start.4) | collective-permute-done | bytes 28704 | tf_op jit(solution)/shard_map/ppermute | solution.py:434
  29.0 1.5 %shard_map.67.u_ref = f32[1696,128]{1,0:T(8,128)S(1)} custom-call(f32[8,8,8,128]{3,2,1,0:T(8,128)S(1)} %get-tuple-element.23.core_ref, f32[512,128]{1,0:T(8,128)S(1)} %bitcast.11, f32[2,8,8,128]{3,2,1,0:T(8,128)S(1)} %get-tuple-element.25.ends_ref, f32[128,128]{1,0:T(8,128)S(1)} %bitcast.13, f32[8,128]{1,0:T(8,128)S(1)} %collective-permute-done.1.za_ref, ...), custom_call_target="tpu_custom_call" | custom-call | tf_op jit(solution)/shard_map/pallas_call | solution.py:467
  30.5 1.2 %shard_map.68.u_ref = f32[1696,128]{1,0:T(8,128)S(1)} custom-call(f32[1696,128]{1,0:T(8,128)S(1)} %shard_map.67.u_ref, bf16[10,10,3,128]{3,2,1,0:T(4,128)(2,1)S(1)} %bitcast.15, f32[3,10,1,128]{3,2,1,0:T(1,128)S(1)} %bitcast.19), custom_call_target="tpu_custom_call" | custom-call | tf_op jit(solution)/shard_map/pallas_call | solution.py:471
  31.8 1.4 %shard_map.69 = (f32[10,10,8,128]{3,2,1,0:T(8,128)S(1)}, f32[10,16,128]{2,1,0:T(8,128)S(1)}, f32[10,16,128]{2,1,0:T(8,128)S(1)}, f32[56,128]{1,0:T(8,128)S(1)}) custom-call(f32[1696,128]{1,0:T(8,128)S(1)} %shard_map.68.u_ref, bf16[10,10,3,128]{3,2,1,0:T(4,128)(2,1)S(1)} %bitcast.16), custom_call_target="tpu_custom_call" | custom-call | tf_op jit(solution)/shard_map/pallas_call | solution.py:473
  33.2 5.5 %collective-permute-start.5 = (f32[56,128]{1,0:T(8,128)S(1)}, f32[56,128]{1,0:T(8,128)S(1)}, u32[]{:S(2)}, u32[]{:S(2)}) collective-permute-start(f32[56,128]{1,0:T(8,128)S(1)} %get-tuple-element.33), channel_id=1, source_target_pairs={{0,128},{128,0},{1,129},{129,1},{2,130},{130,2},{3,131},{131,3},{4... | collective-permute-start | bytes 86024 | tf_op jit(solution)/shard_map/ppermute | solution.py:429
  38.7 0.8 %collective-permute-done.5.xr_ref = f32[56,128]{1,0:T(8,128)S(1)} collective-permute-done((f32[56,128]{1,0:T(8,128)S(1)}, f32[56,128]{1,0:T(8,128)S(1)}, u32[]{:S(2)}, u32[]{:S(2)}) %collective-permute-start.5) | collective-permute-done | bytes 28704 | tf_op jit(solution)/shard_map/ppermute | solution.py:429
  39.5 0.1 shard_map.70
  39.7 3.0 %collective-permute-start.13 = (f32[64,128]{1,0:T(8,128)S(1)}, f32[64,128]{1,0:T(8,128)S(1)}, u32[]{:S(2)}, u32[]{:S(2)}) collective-permute-start(f32[64,128]{1,0:T(8,128)S(1)} %get-tuple-element.36), channel_id=1, source_target_pairs={{0,112},{16,32},{32,16},{48,64},{64,48},{80,96},{96,80},{112,0},{1... | collective-permute-start | bytes 98312 | tf_op jit(solution)/shard_map/ppermute | solution.py:434
  42.7 1.3 %collective-permute-done.13.yb_ref = f32[64,128]{1,0:T(8,128)S(1)} collective-permute-done((f32[64,128]{1,0:T(8,128)S(1)}, f32[64,128]{1,0:T(8,128)S(1)}, u32[]{:S(2)}, u32[]{:S(2)}) %collective-permute-start.13) | collective-permute-done | bytes 32800 | tf_op jit(solution)/shard_map/ppermute | solution.py:434
  44.1 0.3 shard_map.71
  44.3 0.1 collective-permute-start.14
  44.4 3.5 %collective-permute-start.15 = (f32[8,128]{1,0:T(8,128)S(1)}, f32[8,128]{1,0:T(8,128)S(1)}, u32[]{:S(2)}, u32[]{:S(2)}) collective-permute-start(f32[8,128]{1,0:T(8,128)S(1)} %get-tuple-element.38), channel_id=1, source_target_pairs={{0,15},{1,2},{2,1},{3,4},{4,3},{5,6},{6,5},{7,8},{8,7},{9,10},{10,... | collective-permute-start | bytes 12296 | tf_op jit(solution)/shard_map/ppermute | solution.py:434
  48.0 2.3 %collective-permute-done.15.zb_ref = f32[8,128]{1,0:T(8,128)S(1)} collective-permute-done((f32[8,128]{1,0:T(8,128)S(1)}, f32[8,128]{1,0:T(8,128)S(1)}, u32[]{:S(2)}, u32[]{:S(2)}) %collective-permute-start.15) | collective-permute-done | bytes 4128 | tf_op jit(solution)/shard_map/ppermute | solution.py:434
  50.3 1.9 %shard_map.72 = f32[256,256]{1,0:T(8,128)} custom-call(f32[10,10,8,128]{3,2,1,0:T(8,128)S(1)} %get-tuple-element.30.l_ref, f32[10,16,128]{2,1,0:T(8,128)S(1)} %get-tuple-element.31.hl_ref, f32[10,16,128]{2,1,0:T(8,128)S(1)} %get-tuple-element.32.hh_ref, f32[56,128]{1,0:T(8,128)S(1)} %collective-permute-done.5.xr_ref, ...), custom_call_target="tpu_custom_call" | custom-call | tf_op jit(solution)/shard_map/pallas_call | solution.py:482
  (29 shorter events, 0.6 us)
Async XLA Ops:
  1.8 4.1 %collective-permute-start.6 = (f32[16,128]{1,0:T(8,128)S(1)}, f32[16,128]{1,0:T(8,128)S(1)}, u32[]{:S(2)}, u32[]{:S(2)}) collective-permute-start(f32[16,128]{1,0:T(8,128)S(1)} %get-tuple-element.34), channel_id=1, source_target_pairs={{0,128},{128,0},{1,129},{129,1},{2,130},{130,2},{3,131},{131,3},{4... | collective-permute-start | bytes 24584 | tf_op jit(solution)/shard_map/ppermute | solution.py:429
  5.1 11.2 %collective-permute-start = (f32[32,128]{1,0:T(8,128)S(1)}, f32[32,128]{1,0:T(8,128)S(1)}, u32[]{:S(2)}, u32[]{:S(2)}) collective-permute-start(f32[32,128]{1,0:T(8,128)S(1)} %get-tuple-element.24), channel_id=1, source_target_pairs={{0,128},{128,0},{1,129},{129,1},{2,130},{130,2},{3,131},{131,3},{4... | collective-permute-start | bytes 49160 | tf_op jit(solution)/shard_map/ppermute | solution.py:429
  6.0 3.4 %collective-permute-start.7 = (f32[16,128]{1,0:T(8,128)S(1)}, f32[16,128]{1,0:T(8,128)S(1)}, u32[]{:S(2)}, u32[]{:S(2)}) collective-permute-start(f32[16,128]{1,0:T(8,128)S(1)} %select_add_fusion.5), channel_id=1, source_target_pairs={{0,32},{16,48},{32,0},{48,16},{64,96},{80,112},{96,64},{112,80},{1... | collective-permute-start | bytes 24584 | tf_op jit(solution)/shard_map/ppermute | solution.py:429
  9.5 5.4 %collective-permute-start.8 = (f32[16,128]{1,0:T(8,128)S(1)}, f32[16,128]{1,0:T(8,128)S(1)}, u32[]{:S(2)}, u32[]{:S(2)}) collective-permute-start(f32[16,128]{1,0:T(8,128)S(1)} %select_add_fusion.4), channel_id=1, source_target_pairs={{0,96},{16,112},{32,64},{48,80},{64,32},{80,48},{96,0},{112,16},{1... | collective-permute-start | bytes 24584 | tf_op jit(solution)/shard_map/ppermute | solution.py:429
  15.0 6.3 %collective-permute-start.9 = (f32[16,128]{1,0:T(8,128)S(1)}, f32[16,128]{1,0:T(8,128)S(1)}, u32[]{:S(2)}, u32[]{:S(2)}) collective-permute-start(f32[16,128]{1,0:T(8,128)S(1)} %select_add_fusion.3), channel_id=1, source_target_pairs={{0,4},{1,5},{2,6},{3,7},{4,0},{5,1},{6,2},{7,3},{8,12},{9,13},{10,... | collective-permute-start | bytes 24584 | tf_op jit(solution)/shard_map/ppermute | solution.py:429
  16.5 5.8 %collective-permute-start.1 = (f32[8,128]{1,0:T(8,128)S(1)}, f32[8,128]{1,0:T(8,128)S(1)}, u32[]{:S(2)}, u32[]{:S(2)}) collective-permute-start(f32[8,128]{1,0:T(8,128)S(1)} %get-tuple-element.26), channel_id=1, source_target_pairs={{0,1},{1,0},{2,3},{3,2},{4,5},{5,4},{6,7},{7,6},{8,9},{9,8},{10,11... | collective-permute-start | bytes 12296 | tf_op jit(solution)/shard_map/ppermute | solution.py:429
  17.8 5.8 %collective-permute-start.2 = (f32[8,128]{1,0:T(8,128)S(1)}, f32[8,128]{1,0:T(8,128)S(1)}, u32[]{:S(2)}, u32[]{:S(2)}) collective-permute-start(f32[8,128]{1,0:T(8,128)S(1)} %get-tuple-element.27), channel_id=1, source_target_pairs={{0,15},{1,2},{2,1},{3,4},{4,3},{5,6},{6,5},{7,8},{8,7},{9,10},{10,... | collective-permute-start | bytes 12296 | tf_op jit(solution)/shard_map/ppermute | solution.py:434
  21.3 6.4 %collective-permute-start.10 = (f32[16,128]{1,0:T(8,128)S(1)}, f32[16,128]{1,0:T(8,128)S(1)}, u32[]{:S(2)}, u32[]{:S(2)}) collective-permute-start(f32[16,128]{1,0:T(8,128)S(1)} %select_add_fusion.2), channel_id=1, source_target_pairs={{0,12},{1,13},{2,14},{3,15},{4,8},{5,9},{6,10},{7,11},{8,4},{9,5},... | collective-permute-start | bytes 24584 | tf_op jit(solution)/shard_map/ppermute | solution.py:429
  23.6 5.4 %copy-start = (bf16[1,1,1,3,10,10,128]{6,3,5,4,2,1,0:T(4,128)(2,1)S(1)}, bf16[1,1,1,3,10,10,128]{6,3,5,4,2,1,0:T(4,128)(2,1)}, u32[]{:S(2)}) copy-start(bf16[1,1,1,3,10,10,128]{6,3,5,4,2,1,0:T(4,128)(2,1)} %param.7) | copy-start | bytes 230404
  23.8 4.6 %collective-permute-start.3 = (f32[56,128]{1,0:T(8,128)S(1)}, f32[56,128]{1,0:T(8,128)S(1)}, u32[]{:S(2)}, u32[]{:S(2)}) collective-permute-start(f32[56,128]{1,0:T(8,128)S(1)} %get-tuple-element.28), channel_id=1, source_target_pairs={{0,16},{16,0},{32,48},{48,32},{64,80},{80,64},{96,112},{112,96},{1... | collective-permute-start | bytes 86024 | tf_op jit(solution)/shard_map/ppermute | solution.py:429
  24.6 4.5 %collective-permute-start.4 = (f32[56,128]{1,0:T(8,128)S(1)}, f32[56,128]{1,0:T(8,128)S(1)}, u32[]{:S(2)}, u32[]{:S(2)}) collective-permute-start(f32[56,128]{1,0:T(8,128)S(1)} %get-tuple-element.29), channel_id=1, source_target_pairs={{0,112},{16,32},{32,16},{48,64},{64,48},{80,96},{96,80},{112,0},{1... | collective-permute-start | bytes 86024 | tf_op jit(solution)/shard_map/ppermute | solution.py:434
  27.8 10.9 %collective-permute-start.11 = (f32[16,128]{1,0:T(8,128)S(1)}, f32[16,128]{1,0:T(8,128)S(1)}, u32[]{:S(2)}, u32[]{:S(2)}) collective-permute-start(f32[16,128]{1,0:T(8,128)S(1)} %select_add_fusion.1), channel_id=1, source_target_pairs={{0,3},{1,2},{2,1},{3,0},{4,7},{5,6},{6,5},{7,4},{8,11},{9,10},{10,... | collective-permute-start | bytes 24584 | tf_op jit(solution)/shard_map/ppermute | solution.py:429
  29.0 1.5 %copy-start.3 = (f32[1,1,1,3,10,128]{5,2,4,3,1,0:T(1,128)S(1)}, f32[1,1,1,3,10,128]{5,2,4,3,1,0:T(1,128)}, u32[]{:S(2)}) copy-start(f32[1,1,1,3,10,128]{5,2,4,3,1,0:T(1,128)} %param.8) | copy-start | bytes 46084
  33.2 6.3 %collective-permute-start.5 = (f32[56,128]{1,0:T(8,128)S(1)}, f32[56,128]{1,0:T(8,128)S(1)}, u32[]{:S(2)}, u32[]{:S(2)}) collective-permute-start(f32[56,128]{1,0:T(8,128)S(1)} %get-tuple-element.33), channel_id=1, source_target_pairs={{0,128},{128,0},{1,129},{129,1},{2,130},{130,2},{3,131},{131,3},{4... | collective-permute-start | bytes 86024 | tf_op jit(solution)/shard_map/ppermute | solution.py:429
  39.6 4.4 %collective-permute-start.12 = (f32[80,128]{1,0:T(8,128)S(1)}, f32[80,128]{1,0:T(8,128)S(1)}, u32[]{:S(2)}, u32[]{:S(2)}) collective-permute-start(f32[80,128]{1,0:T(8,128)S(1)} %get-tuple-element.35), channel_id=1, source_target_pairs={{0,16},{16,0},{32,48},{48,32},{64,80},{80,64},{96,112},{112,96},{1... | collective-permute-start | bytes 122888 | tf_op jit(solution)/shard_map/ppermute | solution.py:429
  39.7 4.3 %collective-permute-start.13 = (f32[64,128]{1,0:T(8,128)S(1)}, f32[64,128]{1,0:T(8,128)S(1)}, u32[]{:S(2)}, u32[]{:S(2)}) collective-permute-start(f32[64,128]{1,0:T(8,128)S(1)} %get-tuple-element.36), channel_id=1, source_target_pairs={{0,112},{16,32},{32,16},{48,64},{64,48},{80,96},{96,80},{112,0},{1... | collective-permute-start | bytes 98312 | tf_op jit(solution)/shard_map/ppermute | solution.py:434
  44.1 6.3 %copy-start.1 = (f32[1,1,1,8,16,256]{5,4,3,2,1,0:T(8,128)S(1)}, f32[1,1,1,8,16,256]{5,4,3,2,1,0:T(8,128)}, u32[]{:S(2)}) copy-start(f32[1,1,1,8,16,256]{5,4,3,2,1,0:T(8,128)} %param.11) | copy-start | bytes 393220
  44.1 6.3 %copy-start.2 = (f32[8,8,8]{2,1,0:T(8,128)S(1)}, f32[8,8,8]{2,1,0:T(8,128)}, u32[]{:S(2)}) copy-start(f32[8,8,8]{2,1,0:T(8,128)} %basis_ref.3) | copy-start | bytes 6148
  44.3 6.0 %collective-permute-start.14 = (f32[24,128]{1,0:T(8,128)S(1)}, f32[24,128]{1,0:T(8,128)S(1)}, u32[]{:S(2)}, u32[]{:S(2)}) collective-permute-start(f32[24,128]{1,0:T(8,128)S(1)} %get-tuple-element.37), channel_id=1, source_target_pairs={{0,1},{1,0},{2,3},{3,2},{4,5},{5,4},{6,7},{7,6},{8,9},{9,8},{10,11... | collective-permute-start | bytes 36872 | tf_op jit(solution)/shard_map/ppermute | solution.py:429
  44.4 5.9 %collective-permute-start.15 = (f32[8,128]{1,0:T(8,128)S(1)}, f32[8,128]{1,0:T(8,128)S(1)}, u32[]{:S(2)}, u32[]{:S(2)}) collective-permute-start(f32[8,128]{1,0:T(8,128)S(1)} %get-tuple-element.38), channel_id=1, source_target_pairs={{0,15},{1,2},{2,1},{3,4},{4,3},{5,6},{6,5},{7,8},{8,7},{9,10},{10,... | collective-permute-start | bytes 12296 | tf_op jit(solution)/shard_map/ppermute | solution.py:434

commit v4 on v3

--- a/solution.py
+++ b/solution.py
@@ -150,7 +150,8 @@
     return low, high, low_ends, high_ends
 
 
-def yface_kernel(core_ref, core2_ref, ends_ref, ends2_ref, za_ref, zb_ref, ya_ref, yb_ref, scr):
+def yface_kernel(core_ref, core2_ref, ends_ref, ends2_ref, za_ref, zb_ref, run_ref, ya_ref, yb_ref, scr):
+    ya_ref[56:72] = run_ref[...]
     even_y = lax.rem(lax.axis_index("gy"), 2) == 0
     lane, _ = iotas()
     low_q = (lane & 32) == 0
@@ -310,8 +311,7 @@
     return low, high
 
 
-def yfold_send_kernel(hl_ref, hh_ref, xr_ref, run_ref, ya_ref, yb_ref):
-    ya_ref[64:80] = run_ref[...]
+def yfold_send_kernel(hl_ref, hh_ref, xr_ref, ya_ref, yb_ref):
     gx = lax.axis_index("gx")
     even_y = lax.rem(lax.axis_index("gy"), 2) == 0
     low_q = (iotas(16)[0] & 32) == 0
@@ -346,10 +346,8 @@
     return value + jnp.where(sub == 0, row(rows_first, at), jnp.where(sub == 7, row(rows_last, at), 0.0))
 
 
-def zfold_send_kernel(l_ref, hl_ref, hh_ref, xr_ref, ya_ref, yb_ref, run_ref, za_ref, zb_ref, sum_ref, rows_first, rows_last):
-    level = iotas(16)[1] & 7
-    sum_ref[...] = run_ref[...] + jnp.where(level >= 4, ya_ref[64:80], 0.0)
-    za_ref[8:24] = sum_ref[...]
+def zfold_send_kernel(l_ref, hl_ref, hh_ref, xr_ref, ya_ref, yb_ref, run_ref, za_ref, zb_ref, rows_first, rows_last):
+    za_ref[8:24] = run_ref[...]
     gx = lax.axis_index("gx")
     even_z = lax.rem(lax.axis_index("gz"), 2) == 0
     lane, sub = iotas()
@@ -459,25 +457,26 @@
     ends, za, zb = call(zface_kernel, [(2, 8, 8, 128), (8, 128), (8, 128)], [], 2)(core, xr)
     running = climb(running, "gy", 2, 5)
     za, zb = swap(za, "gz", 1), swap_odd(zb, "gz")
-    running = climb(running, "gy", 6, 6)
+    running = climb(running, "gz", 4, 2)
     block = (core, core.reshape(512, 128), ends, ends.reshape(128, 128), za, zb)
-    ya, yb = call(yface_kernel, [(56, 128), (56, 128)], [(256, 128)], 6)(*block)
+    ya, yb = call(yface_kernel, [(72, 128), (56, 128)], [(256, 128)], 7)(*block, running)
     ya, yb = swap(ya, "gy", 1), swap_odd(yb, "gy")
-    running = climb(running, "gz", 4, 2)
+    running = running + jnp.where(level_of >= 4, ya[56:72], 0.0)
+    running = climb(running, "gz", 3, 1)
     (modes,) = call(
         modes_kernel, [(1696, 128)], [(800, 128), (112, 128), (112, 128), (848, 128), (256, 128)], 9
     )(*block, ya, yb, vectors)
-    running = climb(running, "gz", 12, 3)
+    running = climb(running, "gy", 6, 6)
     (modes,) = call(middle_kernel, [(1696, 128)], [(848, 128), (16, 128)], 3)(modes, vectors, eigen)
-    running = climb(running, "gz", 3, 1)
     local, edge_l, edge_h, xs = call(
         points_kernel, [(10, 10, 8, 128), (10, 16, 128), (10, 16, 128), (56, 128)], [(1696, 128), (848, 128)], 2
     )(modes, vectors)
     xr = swap(xs, "gx", 1)
-    ya, yb = call(yfold_send_kernel, [(80, 128), (64, 128)], [], 4)(edge_l, edge_h, xr, running)
+    ya, yb = call(yfold_send_kernel, [(64, 128), (64, 128)], [], 3)(edge_l, edge_h, xr)
     ya, yb = swap(ya, "gy", 1), swap_odd(yb, "gy")
+    running = climb(running, "gz", 12, 3)
     parts = (local, edge_l, edge_h, xr, ya, yb)
-    za, zb, running = call(zfold_send_kernel, [(24, 128), (8, 128), (16, 128)], [(128, 128)] * 2, 7)(*parts, running)
+    za, zb = call(zfold_send_kernel, [(24, 128), (8, 128)], [(128, 128)] * 2, 7)(*parts, running)
     za, zb = swap(za, "gz", 1), swap_odd(zb, "gz")
     (out,) = call(
         post_kernel, [(256, 256)], [(128, 128), (128, 128), (2, 256, 128), (8, 8, 8, 128)], 12

time: 52.3 us -> 54.1 us (1.034)
  the two profiles are of different devices: /device:TPU:1 before, /device:TPU:6 now
where the time goes in v4:
time: 54.1 us; the launch traced here: 54 us
  starting transfers between devices  26.2 us (48%)
  waiting for transfers between devices  18.5 us (34%)
  Pallas kernels  8.64 us (16%)
  other arithmetic  0.56 us (1%)
    ppermute x12, starting transfers between devices, swap(): lax.ppermute(value, axis, [(i, i ^ distance) for i in range(lax.axis_size...  18.4 us
    ppermute x4, waiting for transfers between devices, swap_odd(): lax.ppermute(value, axis, [(i, (i + 1 if i % 2 else i - 1) % count) for i...  10.8 us
    ppermute x4, starting transfers between devices, swap_odd(): lax.ppermute(value, axis, [(i, (i + 1 if i % 2 else i - 1) % count) for i...  7.8 us
    ppermute x12, waiting for transfers between devices, swap(): lax.ppermute(value, axis, [(i, i ^ distance) for i in range(lax.axis_size...  7.68 us
    pallas_call x1, Pallas kernels, work(): call(post_kernel, [(256, 256)], [(128, 128), (128, 128), (2, 256, 128), (...  1.89 us
    pallas_call x1, Pallas kernels, work(): call(pre_kernel, [(8, 8, 8, 128), (32, 128), (16, 128), (16, 128)], [(2,...  1.84 us
    pallas_call x1, Pallas kernels, work(): call(modes_kernel, [(1696, 128)], [(800, 128), (112, 128), (112, 128), (8...  1.46 us
    pallas_call x1, Pallas kernels, work(): call(points_kernel, [(10, 10, 8, 128), (10, 16, 128), (10, 16, 128), (56,...  1.41 us
  transfers between devices with their start and end apart: 16, of which 8 were waited for; matrix products, arithmetic and copies ran while one was open for 1% of the time, Pallas kernels for 8%

profile of v4, /device:TPU:6, one launch (start us, length us, event | category | flops | bytes accessed | tf_op | source)
XLA Modules:
  0.0 54.0 jit_solution(6855729339784652023)
XLA Ops:
  0.0 1.8 %shard_map.64 = (f32[8,8,8,128]{3,2,1,0:T(8,128)S(1)}, f32[32,128]{1,0:T(8,128)S(1)}, f32[16,128]{1,0:T(8,128)S(1)}, f32[16,128]{1,0:T(8,128)S(1)}) custom-call(f32[256,256]{1,0:T(8,128)} %bitcast.20, f32[8,16,256]{2,1,0:T(8,128)} %bitcast.17, f32[8,8,8]{2,1,0:T(8,128)} %basis_ref.3, f32[16,16]{1,0:T(8,128)} %bitcast.21), custom_call_target="tpu_custom_call" | custom-call | tf_op jit(solution)/shard_map/pallas_call | solution.py:447
  1.8 0.1 collective-permute-start.3
  1.9 0.5 collective-permute-start
  2.5 0.7 %collective-permute-done.3 = f32[16,128]{1,0:T(8,128)S(1)} collective-permute-done((f32[16,128]{1,0:T(8,128)S(1)}, f32[16,128]{1,0:T(8,128)S(1)}, u32[]{:S(2)}, u32[]{:S(2)}) %collective-permute-start.3) | collective-permute-done | bytes 8224 | tf_op jit(solution)/shard_map/ppermute | solution.py:427
  3.2 3.3 %collective-permute-start.4 = (f32[16,128]{1,0:T(8,128)S(1)}, f32[16,128]{1,0:T(8,128)S(1)}, u32[]{:S(2)}, u32[]{:S(2)}) collective-permute-start(f32[16,128]{1,0:T(8,128)S(1)} %select_add_fusion.5), channel_id=1, source_target_pairs={{0,32},{16,48},{32,0},{48,16},{64,96},{80,112},{96,64},{112,80},{1... | collective-permute-start | bytes 24584 | tf_op jit(solution)/shard_map/ppermute | solution.py:427
  6.5 1.6 %collective-permute-done.4 = f32[16,128]{1,0:T(8,128)S(1)} collective-permute-done((f32[16,128]{1,0:T(8,128)S(1)}, f32[16,128]{1,0:T(8,128)S(1)}, u32[]{:S(2)}, u32[]{:S(2)}) %collective-permute-start.4) | collective-permute-done | bytes 8224 | tf_op jit(solution)/shard_map/ppermute | solution.py:427
  8.2 1.6 %collective-permute-start.5 = (f32[16,128]{1,0:T(8,128)S(1)}, f32[16,128]{1,0:T(8,128)S(1)}, u32[]{:S(2)}, u32[]{:S(2)}) collective-permute-start(f32[16,128]{1,0:T(8,128)S(1)} %select_add_fusion.4), channel_id=1, source_target_pairs={{0,4},{1,5},{2,6},{3,7},{4,0},{5,1},{6,2},{7,3},{8,12},{9,13},{10,... | collective-permute-start | bytes 24584 | tf_op jit(solution)/shard_map/ppermute | solution.py:427
  9.8 0.2 shard_map.65
  10.0 0.9 %collective-permute-start.1 = (f32[8,128]{1,0:T(8,128)S(1)}, f32[8,128]{1,0:T(8,128)S(1)}, u32[]{:S(2)}, u32[]{:S(2)}) collective-permute-start(f32[8,128]{1,0:T(8,128)S(1)} %get-tuple-element.25), channel_id=1, source_target_pairs={{0,1},{1,0},{2,3},{3,2},{4,5},{5,4},{6,7},{7,6},{8,9},{9,8},{10,11... | collective-permute-start | bytes 12296 | tf_op jit(solution)/shard_map/ppermute | solution.py:427
  10.9 1.1 %collective-permute-start.2 = (f32[8,128]{1,0:T(8,128)S(1)}, f32[8,128]{1,0:T(8,128)S(1)}, u32[]{:S(2)}, u32[]{:S(2)}) collective-permute-start(f32[8,128]{1,0:T(8,128)S(1)} %get-tuple-element.26), channel_id=1, source_target_pairs={{0,15},{1,2},{2,1},{3,4},{4,3},{5,6},{6,5},{7,8},{8,7},{9,10},{10,... | collective-permute-start | bytes 12296 | tf_op jit(solution)/shard_map/ppermute | solution.py:432
  12.1 1.6 %collective-permute-done.1.za_ref = f32[8,128]{1,0:T(8,128)S(1)} collective-permute-done((f32[8,128]{1,0:T(8,128)S(1)}, f32[8,128]{1,0:T(8,128)S(1)}, u32[]{:S(2)}, u32[]{:S(2)}) %collective-permute-start.1) | collective-permute-done | bytes 4128 | tf_op jit(solution)/shard_map/ppermute | solution.py:427
  13.7 2.9 %collective-permute-done.2.zb_ref = f32[8,128]{1,0:T(8,128)S(1)} collective-permute-done((f32[8,128]{1,0:T(8,128)S(1)}, f32[8,128]{1,0:T(8,128)S(1)}, u32[]{:S(2)}, u32[]{:S(2)}) %collective-permute-start.2) | collective-permute-done | bytes 4128 | tf_op jit(solution)/shard_map/ppermute | solution.py:432
  16.6 0.2 shard_map.66
  16.8 2.0 %collective-permute-start.6 = (f32[72,128]{1,0:T(8,128)S(1)}, f32[72,128]{1,0:T(8,128)S(1)}, u32[]{:S(2)}, u32[]{:S(2)}) collective-permute-start(f32[72,128]{1,0:T(8,128)S(1)} %get-tuple-element.28), channel_id=1, source_target_pairs={{0,16},{16,0},{32,48},{48,32},{64,80},{80,64},{96,112},{112,96},{1... | collective-permute-start | bytes 110600 | tf_op jit(solution)/shard_map/ppermute | solution.py:427
  18.8 2.0 %collective-permute-done.6.ya_ref = f32[72,128]{1,0:T(8,128)S(1)} collective-permute-done((f32[72,128]{1,0:T(8,128)S(1)}, f32[72,128]{1,0:T(8,128)S(1)}, u32[]{:S(2)}, u32[]{:S(2)}) %collective-permute-start.6) | collective-permute-done | bytes 36896 | tf_op jit(solution)/shard_map/ppermute | solution.py:427
  20.9 2.4 %collective-permute-start.11 = (f32[16,128]{1,0:T(8,128)S(1)}, f32[16,128]{1,0:T(8,128)S(1)}, u32[]{:S(2)}, u32[]{:S(2)}) collective-permute-start(f32[16,128]{1,0:T(8,128)S(1)} %fusion), channel_id=1, source_target_pairs={{0,3},{1,2},{2,1},{3,0},{4,7},{5,6},{6,5},{7,4},{8,11},{9,10},{10,... | collective-permute-start | bytes 24584 | tf_op jit(solution)/shard_map/ppermute | solution.py:427
  23.3 5.5 %collective-permute-start.7 = (f32[56,128]{1,0:T(8,128)S(1)}, f32[56,128]{1,0:T(8,128)S(1)}, u32[]{:S(2)}, u32[]{:S(2)}) collective-permute-start(f32[56,128]{1,0:T(8,128)S(1)} %get-tuple-element.29), channel_id=1, source_target_pairs={{0,112},{16,32},{32,16},{48,64},{64,48},{80,96},{96,80},{112,0},{1... | collective-permute-start | bytes 86024 | tf_op jit(solution)/shard_map/ppermute | solution.py:432
  28.9 3.0 %collective-permute-start.12 = (f32[16,128]{1,0:T(8,128)S(1)}, f32[16,128]{1,0:T(8,128)S(1)}, u32[]{:S(2)}, u32[]{:S(2)}) collective-permute-start(f32[16,128]{1,0:T(8,128)S(1)} %select_add_fusion.2), channel_id=1, source_target_pairs={{0,96},{16,112},{32,64},{48,80},{64,32},{80,48},{96,0},{112,16},{1... | collective-permute-start | bytes 24584 | tf_op jit(solution)/shard_map/ppermute | solution.py:427
  31.9 1.5 %shard_map.67.u_ref = f32[1696,128]{1,0:T(8,128)S(1)} custom-call(f32[8,8,8,128]{3,2,1,0:T(8,128)S(1)} %get-tuple-element.22.core_ref, f32[512,128]{1,0:T(8,128)S(1)} %bitcast.11, f32[2,8,8,128]{3,2,1,0:T(8,128)S(1)} %get-tuple-element.24.ends_ref, f32[128,128]{1,0:T(8,128)S(1)} %bitcast.13, f32[8,128]{1,0:T(8,128)S(1)} %collective-permute-done.1.za_ref, ...), custom_call_target="tpu_custom_call" | custom-call | tf_op jit(solution)/shard_map/pallas_call | solution.py:466
  33.4 1.2 %shard_map.68.u_ref = f32[1696,128]{1,0:T(8,128)S(1)} custom-call(f32[1696,128]{1,0:T(8,128)S(1)} %shard_map.67.u_ref, bf16[10,10,3,128]{3,2,1,0:T(4,128)(2,1)S(1)} %bitcast.15, f32[3,10,1,128]{3,2,1,0:T(1,128)S(1)} %bitcast.19), custom_call_target="tpu_custom_call" | custom-call | tf_op jit(solution)/shard_map/pallas_call | solution.py:470
  34.6 1.4 %shard_map.69 = (f32[10,10,8,128]{3,2,1,0:T(8,128)S(1)}, f32[10,16,128]{2,1,0:T(8,128)S(1)}, f32[10,16,128]{2,1,0:T(8,128)S(1)}, f32[56,128]{1,0:T(8,128)S(1)}) custom-call(f32[1696,128]{1,0:T(8,128)S(1)} %shard_map.68.u_ref, bf16[10,10,3,128]{3,2,1,0:T(4,128)(2,1)S(1)} %bitcast.16), custom_call_target="tpu_custom_call" | custom-call | tf_op jit(solution)/shard_map/pallas_call | solution.py:471
  36.1 3.4 %collective-permute-start.13 = (f32[16,128]{1,0:T(8,128)S(1)}, f32[16,128]{1,0:T(8,128)S(1)}, u32[]{:S(2)}, u32[]{:S(2)}) collective-permute-start(f32[16,128]{1,0:T(8,128)S(1)} %select_add_fusion.1), channel_id=1, source_target_pairs={{0,12},{1,13},{2,14},{3,15},{4,8},{5,9},{6,10},{7,11},{8,4},{9,5},... | collective-permute-start | bytes 24584 | tf_op jit(solution)/shard_map/ppermute | solution.py:427
  39.6 0.1 shard_map.70
  39.7 1.1 %collective-permute-start.9 = (f32[64,128]{1,0:T(8,128)S(1)}, f32[64,128]{1,0:T(8,128)S(1)}, u32[]{:S(2)}, u32[]{:S(2)}) collective-permute-start(f32[64,128]{1,0:T(8,128)S(1)} %get-tuple-element.34), channel_id=1, source_target_pairs={{0,16},{16,0},{32,48},{48,32},{64,80},{80,64},{96,112},{112,96},{1... | collective-permute-start | bytes 98312 | tf_op jit(solution)/shard_map/ppermute | solution.py:427
  40.8 1.1 %collective-permute-start.10 = (f32[64,128]{1,0:T(8,128)S(1)}, f32[64,128]{1,0:T(8,128)S(1)}, u32[]{:S(2)}, u32[]{:S(2)}) collective-permute-start(f32[64,128]{1,0:T(8,128)S(1)} %get-tuple-element.35), channel_id=1, source_target_pairs={{0,112},{16,32},{32,16},{48,64},{64,48},{80,96},{96,80},{112,0},{1... | collective-permute-start | bytes 98312 | tf_op jit(solution)/shard_map/ppermute | solution.py:432
  42.0 1.7 %collective-permute-done.9.ya_ref = f32[64,128]{1,0:T(8,128)S(1)} collective-permute-done((f32[64,128]{1,0:T(8,128)S(1)}, f32[64,128]{1,0:T(8,128)S(1)}, u32[]{:S(2)}, u32[]{:S(2)}) %collective-permute-start.9) | collective-permute-done | bytes 32800 | tf_op jit(solution)/shard_map/ppermute | solution.py:427
  43.7 2.2 %collective-permute-done.10.yb_ref = f32[64,128]{1,0:T(8,128)S(1)} collective-permute-done((f32[64,128]{1,0:T(8,128)S(1)}, f32[64,128]{1,0:T(8,128)S(1)}, u32[]{:S(2)}, u32[]{:S(2)}) %collective-permute-start.10) | collective-permute-done | bytes 32800 | tf_op jit(solution)/shard_map/ppermute | solution.py:432
  45.9 0.3 shard_map.71
  46.2 0.1 collective-permute-start.14
  46.3 0.1 collective-permute-start.15
  46.4 5.7 %collective-permute-done.15.zb_ref = f32[8,128]{1,0:T(8,128)S(1)} collective-permute-done((f32[8,128]{1,0:T(8,128)S(1)}, f32[8,128]{1,0:T(8,128)S(1)}, u32[]{:S(2)}, u32[]{:S(2)}) %collective-permute-start.15) | collective-permute-done | bytes 4128 | tf_op jit(solution)/shard_map/ppermute | solution.py:432
  52.1 1.9 %shard_map.72 = f32[256,256]{1,0:T(8,128)} custom-call(f32[10,10,8,128]{3,2,1,0:T(8,128)S(1)} %get-tuple-element.30.l_ref, f32[10,16,128]{2,1,0:T(8,128)S(1)} %get-tuple-element.31.hl_ref, f32[10,16,128]{2,1,0:T(8,128)S(1)} %get-tuple-element.32.hh_ref, f32[56,128]{1,0:T(8,128)S(1)} %collective-permute-done.8.xr_ref, ...), custom_call_target="tpu_custom_call" | custom-call | tf_op jit(solution)/shard_map/pallas_call | solution.py:481
  (31 shorter events, 0.6 us)
Async XLA Ops:
  1.8 1.3 %collective-permute-start.3 = (f32[16,128]{1,0:T(8,128)S(1)}, f32[16,128]{1,0:T(8,128)S(1)}, u32[]{:S(2)}, u32[]{:S(2)}) collective-permute-start(f32[16,128]{1,0:T(8,128)S(1)} %get-tuple-element.27), channel_id=1, source_target_pairs={{0,128},{128,0},{1,129},{129,1},{2,130},{130,2},{3,131},{131,3},{4... | collective-permute-start | bytes 24584 | tf_op jit(solution)/shard_map/ppermute | solution.py:427
  1.9 7.8 %collective-permute-start = (f32[32,128]{1,0:T(8,128)S(1)}, f32[32,128]{1,0:T(8,128)S(1)}, u32[]{:S(2)}, u32[]{:S(2)}) collective-permute-start(f32[32,128]{1,0:T(8,128)S(1)} %get-tuple-element.23), channel_id=1, source_target_pairs={{0,128},{128,0},{1,129},{129,1},{2,130},{130,2},{3,131},{131,3},{4... | collective-permute-start | bytes 49160 | tf_op jit(solution)/shard_map/ppermute | solution.py:427
  3.2 4.9 %collective-permute-start.4 = (f32[16,128]{1,0:T(8,128)S(1)}, f32[16,128]{1,0:T(8,128)S(1)}, u32[]{:S(2)}, u32[]{:S(2)}) collective-permute-start(f32[16,128]{1,0:T(8,128)S(1)} %select_add_fusion.5), channel_id=1, source_target_pairs={{0,32},{16,48},{32,0},{48,16},{64,96},{80,112},{96,64},{112,80},{1... | collective-permute-start | bytes 24584 | tf_op jit(solution)/shard_map/ppermute | solution.py:427
  8.2 3.8 %collective-permute-start.5 = (f32[16,128]{1,0:T(8,128)S(1)}, f32[16,128]{1,0:T(8,128)S(1)}, u32[]{:S(2)}, u32[]{:S(2)}) collective-permute-start(f32[16,128]{1,0:T(8,128)S(1)} %select_add_fusion.4), channel_id=1, source_target_pairs={{0,4},{1,5},{2,6},{3,7},{4,0},{5,1},{6,2},{7,3},{8,12},{9,13},{10,... | collective-permute-start | bytes 24584 | tf_op jit(solution)/shard_map/ppermute | solution.py:427
  10.0 3.7 %collective-permute-start.1 = (f32[8,128]{1,0:T(8,128)S(1)}, f32[8,128]{1,0:T(8,128)S(1)}, u32[]{:S(2)}, u32[]{:S(2)}) collective-permute-start(f32[8,128]{1,0:T(8,128)S(1)} %get-tuple-element.25), channel_id=1, source_target_pairs={{0,1},{1,0},{2,3},{3,2},{4,5},{5,4},{6,7},{7,6},{8,9},{9,8},{10,11... | collective-permute-start | bytes 12296 | tf_op jit(solution)/shard_map/ppermute | solution.py:427
  10.9 5.7 %collective-permute-start.2 = (f32[8,128]{1,0:T(8,128)S(1)}, f32[8,128]{1,0:T(8,128)S(1)}, u32[]{:S(2)}, u32[]{:S(2)}) collective-permute-start(f32[8,128]{1,0:T(8,128)S(1)} %get-tuple-element.26), channel_id=1, source_target_pairs={{0,15},{1,2},{2,1},{3,4},{4,3},{5,6},{6,5},{7,8},{8,7},{9,10},{10,... | collective-permute-start | bytes 12296 | tf_op jit(solution)/shard_map/ppermute | solution.py:432
  16.6 15.2 %copy-start = (bf16[1,1,1,3,10,10,128]{6,3,5,4,2,1,0:T(4,128)(2,1)S(1)}, bf16[1,1,1,3,10,10,128]{6,3,5,4,2,1,0:T(4,128)(2,1)}, u32[]{:S(2)}) copy-start(bf16[1,1,1,3,10,10,128]{6,3,5,4,2,1,0:T(4,128)(2,1)} %param.7) | copy-start | bytes 230404
  16.8 4.0 %collective-permute-start.6 = (f32[72,128]{1,0:T(8,128)S(1)}, f32[72,128]{1,0:T(8,128)S(1)}, u32[]{:S(2)}, u32[]{:S(2)}) collective-permute-start(f32[72,128]{1,0:T(8,128)S(1)} %get-tuple-element.28), channel_id=1, source_target_pairs={{0,16},{16,0},{32,48},{48,32},{64,80},{80,64},{96,112},{112,96},{1... | collective-permute-start | bytes 110600 | tf_op jit(solution)/shard_map/ppermute | solution.py:427
  20.9 7.9 %collective-permute-start.11 = (f32[16,128]{1,0:T(8,128)S(1)}, f32[16,128]{1,0:T(8,128)S(1)}, u32[]{:S(2)}, u32[]{:S(2)}) collective-permute-start(f32[16,128]{1,0:T(8,128)S(1)} %fusion), channel_id=1, source_target_pairs={{0,3},{1,2},{2,1},{3,0},{4,7},{5,6},{6,5},{7,4},{8,11},{9,10},{10,... | collective-permute-start | bytes 24584 | tf_op jit(solution)/shard_map/ppermute | solution.py:427
  23.3 8.6 %collective-permute-start.7 = (f32[56,128]{1,0:T(8,128)S(1)}, f32[56,128]{1,0:T(8,128)S(1)}, u32[]{:S(2)}, u32[]{:S(2)}) collective-permute-start(f32[56,128]{1,0:T(8,128)S(1)} %get-tuple-element.29), channel_id=1, source_target_pairs={{0,112},{16,32},{32,16},{48,64},{64,48},{80,96},{96,80},{112,0},{1... | collective-permute-start | bytes 86024 | tf_op jit(solution)/shard_map/ppermute | solution.py:432
  28.9 7.2 %collective-permute-start.12 = (f32[16,128]{1,0:T(8,128)S(1)}, f32[16,128]{1,0:T(8,128)S(1)}, u32[]{:S(2)}, u32[]{:S(2)}) collective-permute-start(f32[16,128]{1,0:T(8,128)S(1)} %select_add_fusion.2), channel_id=1, source_target_pairs={{0,96},{16,112},{32,64},{48,80},{64,32},{80,48},{96,0},{112,16},{1... | collective-permute-start | bytes 24584 | tf_op jit(solution)/shard_map/ppermute | solution.py:427
  31.9 1.5 %copy-start.3 = (f32[1,1,1,3,10,128]{5,2,4,3,1,0:T(1,128)S(1)}, f32[1,1,1,3,10,128]{5,2,4,3,1,0:T(1,128)}, u32[]{:S(2)}) copy-start(f32[1,1,1,3,10,128]{5,2,4,3,1,0:T(1,128)} %param.8) | copy-start | bytes 46084
  36.0 3.6 %collective-permute-start.8 = (f32[56,128]{1,0:T(8,128)S(1)}, f32[56,128]{1,0:T(8,128)S(1)}, u32[]{:S(2)}, u32[]{:S(2)}) collective-permute-start(f32[56,128]{1,0:T(8,128)S(1)} %get-tuple-element.33), channel_id=1, source_target_pairs={{0,128},{128,0},{1,129},{129,1},{2,130},{130,2},{3,131},{131,3},{4... | collective-permute-start | bytes 86024 | tf_op jit(solution)/shard_map/ppermute | solution.py:427
  36.1 5.8 %collective-permute-start.13 = (f32[16,128]{1,0:T(8,128)S(1)}, f32[16,128]{1,0:T(8,128)S(1)}, u32[]{:S(2)}, u32[]{:S(2)}) collective-permute-start(f32[16,128]{1,0:T(8,128)S(1)} %select_add_fusion.1), channel_id=1, source_target_pairs={{0,12},{1,13},{2,14},{3,15},{4,8},{5,9},{6,10},{7,11},{8,4},{9,5},... | collective-permute-start | bytes 24584 | tf_op jit(solution)/shard_map/ppermute | solution.py:427
  39.7 4.0 %collective-permute-start.9 = (f32[64,128]{1,0:T(8,128)S(1)}, f32[64,128]{1,0:T(8,128)S(1)}, u32[]{:S(2)}, u32[]{:S(2)}) collective-permute-start(f32[64,128]{1,0:T(8,128)S(1)} %get-tuple-element.34), channel_id=1, source_target_pairs={{0,16},{16,0},{32,48},{48,32},{64,80},{80,64},{96,112},{112,96},{1... | collective-permute-start | bytes 98312 | tf_op jit(solution)/shard_map/ppermute | solution.py:427
  40.8 5.1 %collective-permute-start.10 = (f32[64,128]{1,0:T(8,128)S(1)}, f32[64,128]{1,0:T(8,128)S(1)}, u32[]{:S(2)}, u32[]{:S(2)}) collective-permute-start(f32[64,128]{1,0:T(8,128)S(1)} %get-tuple-element.35), channel_id=1, source_target_pairs={{0,112},{16,32},{32,16},{48,64},{64,48},{80,96},{96,80},{112,0},{1... | collective-permute-start | bytes 98312 | tf_op jit(solution)/shard_map/ppermute | solution.py:432
  45.9 6.2 %copy-start.1 = (f32[1,1,1,8,16,256]{5,4,3,2,1,0:T(8,128)S(1)}, f32[1,1,1,8,16,256]{5,4,3,2,1,0:T(8,128)}, u32[]{:S(2)}) copy-start(f32[1,1,1,8,16,256]{5,4,3,2,1,0:T(8,128)} %param.11) | copy-start | bytes 393220
  45.9 6.2 %copy-start.2 = (f32[8,8,8]{2,1,0:T(8,128)S(1)}, f32[8,8,8]{2,1,0:T(8,128)}, u32[]{:S(2)}) copy-start(f32[8,8,8]{2,1,0:T(8,128)} %basis_ref.3) | copy-start | bytes 6148
  46.2 5.9 %collective-permute-start.14 = (f32[24,128]{1,0:T(8,128)S(1)}, f32[24,128]{1,0:T(8,128)S(1)}, u32[]{:S(2)}, u32[]{:S(2)}) collective-permute-start(f32[24,128]{1,0:T(8,128)S(1)} %get-tuple-element.36), channel_id=1, source_target_pairs={{0,1},{1,0},{2,3},{3,2},{4,5},{5,4},{6,7},{7,6},{8,9},{9,8},{10,11... | collective-permute-start | bytes 36872 | tf_op jit(solution)/shard_map/ppermute | solution.py:427
  46.3 5.8 %collective-permute-start.15 = (f32[8,128]{1,0:T(8,128)S(1)}, f32[8,128]{1,0:T(8,128)S(1)}, u32[]{:S(2)}, u32[]{:S(2)}) collective-permute-start(f32[8,128]{1,0:T(8,128)S(1)} %get-tuple-element.37), channel_id=1, source_target_pairs={{0,15},{1,2},{2,1},{3,4},{4,3},{5,6},{6,5},{7,8},{8,7},{9,10},{10,... | collective-permute-start | bytes 12296 | tf_op jit(solution)/shard_map/ppermute | solution.py:432

commit v5 on v3

--- a/solution.py
+++ b/solution.py
@@ -168,15 +168,14 @@
     yb_ref[40:56] = jnp.where(even_y, down, up)
 
 
-def load_factors(vec_ref, s):
+def factors_kernel(vec_ref, s_ref):
     for a in range(10):
         for i in range(10):
-            s[(i * 10 + a) * 8 : (i * 10 + a) * 8 + 3] = vec_ref[i, a].astype(F32)
-
-    def factor(d, i, a):
-        return row(s, (i * 10 + a) * 8 + d)
-
-    return factor
+            s_ref[(i * 10 + a) * 8 : (i * 10 + a) * 8 + 3] = vec_ref[i, a].astype(F32)
+
+
+def factor_of(s):
+    return lambda d, i, a: row(s, (i * 10 + a) * 8 + d)
 
 
 def along_x(source, target, factor, transposed):
@@ -194,7 +193,7 @@
 
 
 def modes_kernel(
-    core_ref, core2_ref, ends_ref, ends2_ref, za_ref, zb_ref, ya_ref, yb_ref, vec_ref, u, block, jl, jh, s, scr
+    core_ref, core2_ref, ends_ref, ends2_ref, za_ref, zb_ref, ya_ref, yb_ref, s, u, block, jl, jh, scr
 ):
     lane, _ = iotas()
     low_q = (lane & 32) == 0
@@ -218,7 +217,7 @@
     jl[96:112] = jnp.where(low_q16, below, roll(high_ends[1], 32))
     jh[80:96] = jnp.where(low_q16, roll(low_ends[0], 96), roll(above, 32))
     jh[96:112] = jnp.where(low_q16, roll(low_ends[1], 96), above)
-    factor = load_factors(vec_ref, s)
+    factor = factor_of(s)
     front = [[s[pl.ds((j * 10 + 8 * h) * 8 + 1, 8, stride=8), :] for j in range(10)] for h in range(2)]
 
     def fwd_y(i, _):
@@ -236,11 +235,11 @@
     along_x(u, u, factor, False)
 
 
-def middle_kernel(u_ref, vec_ref, eig_ref, u, s, eg):
+def middle_kernel(u_ref, s, eig_ref, u, eg):
     eg[...] = jnp.ones((16, 128), F32)
     for a in range(10):
         eg[a : a + 1] = eig_ref[1, a]
-    factor = load_factors(vec_ref, s)
+    factor = factor_of(s)
 
     def wide(value):
         return jnp.broadcast_to(value, (8, 128))
@@ -260,10 +259,10 @@
     lax.fori_loop(0, 10, along_z, 0)
 
 
-def points_kernel(u_ref, vec_ref, l_ref, hl_ref, hh_ref, xs_ref, u, s):
+def points_kernel(u_ref, s, l_ref, hl_ref, hh_ref, xs_ref, u):
     gx = lax.axis_index("gx")
     lane, _ = iotas()
-    factor = load_factors(vec_ref, s)
+    factor = factor_of(s)
     along_x(u_ref, u, factor, True)
     back = [s[pl.ds((10 + b) * 8 + 1, 8, stride=80), :] for b in range(10)]
 
@@ -346,10 +345,8 @@
     return value + jnp.where(sub == 0, row(rows_first, at), jnp.where(sub == 7, row(rows_last, at), 0.0))
 
 
-def zfold_send_kernel(l_ref, hl_ref, hh_ref, xr_ref, ya_ref, yb_ref, run_ref, za_ref, zb_ref, sum_ref, rows_first, rows_last):
-    level = iotas(16)[1] & 7
-    sum_ref[...] = run_ref[...] + jnp.where(level >= 4, ya_ref[64:80], 0.0)
-    za_ref[8:24] = sum_ref[...]
+def zfold_send_kernel(l_ref, hl_ref, hh_ref, xr_ref, ya_ref, yb_ref, run_ref, za_ref, zb_ref, rows_first, rows_last):
+    za_ref[8:24] = run_ref[...]
     gx = lax.axis_index("gx")
     even_z = lax.rem(lax.axis_index("gz"), 2) == 0
     lane, sub = iotas()
@@ -364,37 +361,26 @@
     zb_ref[...] = jnp.where(even_z, down, up)
 
 
-def post_kernel(
-    l_ref, hl_ref, hh_ref, xr_ref, ya_ref, yb_ref, za_ref, zb_ref, basis_ref, sep_ref, run_ref, ownsol_ref,
-    out_ref, rows_first, rows_last, xt, grid,
+def gather_kernel(
+    l_ref, hl_ref, hh_ref, xr_ref, ya_ref, yb_ref, basis_ref, sum_ref, tile_ref, rows_first, rows_last, xt, grid
 ):
     gx = lax.axis_index("gx")
     lane, sub = iotas()
     slot = lane & 31
     low_q = (lane & 32) == 0
     fold_rows(hl_ref, hh_ref, xr_ref, ya_ref, yb_ref, rows_first, rows_last, gx)
-    running = run_ref[...] + za_ref[8:24]
-    weighted = total(
-        sep_ref[level][:, h * 128 : h * 128 + 128] * running[8 * h + level : 8 * h + level + 1, :]
-        for h in range(2)
-        for level in range(sep_ref.shape[0])
-    )
-    solution_col = ownsol_ref[:, :1] + jnp.sum(weighted, axis=1, keepdims=True)
-    lane16, sub16 = iotas(16)
-    spread = jnp.where(((lane16 & 31) >> 1) == sub16, jnp.broadcast_to(solution_col, (16, 128)), 0.0)
-    per_element = jnp.broadcast_to(jnp.sum(spread, axis=0, keepdims=True), (8, 128))
-    from_above, from_below = sides(za_ref[:8], zb_ref[...], "gz")
     for i in range(8):
-        weights = basis_ref[i]
         get = functools.partial(folded_xy, l_ref, xr_ref, rows_first, rows_last, i + 1, gx=gx, lane=lane, sub=sub)
         before, after = get(0), get(9)
         for k in range(8):
-            value = get(k + 1) + jnp.broadcast_to(weights[:, k : k + 1], (8, 128)) * per_element
+            value = get(k + 1)
             if k == 0:
-                value = value + jnp.where(slot == 0, roll(from_below, -i), roll(after, 1))
+                value = value + jnp.where(slot == 0, 0.0, roll(after, 1))
             if k == 7:
-                value = value + jnp.where(slot == 31, roll(from_above, 31 - i), roll(before, -1))
+                value = value + jnp.where(slot == 31, 0.0, roll(before, -1))
             grid[i, k] = value
+        weights = jnp.concatenate([basis_ref[i]] * 16, 1)
+        tile_ref[i * 8 : i * 8 + 8] = weights
     for pair in range(4):
         k0, k1 = 2 * pair, 2 * pair + 1
         pieces = []
@@ -407,15 +393,49 @@
             for t, k in enumerate((k0, k1)):
                 at = p * 64 + t * 32
                 xt[p, pl.ds(k, 32, stride=8), :] = block[at : at + 32]
-    out_ref[...] = jnp.concatenate([xt[0], xt[1]], 1).T
-
-
-def call(kernel, outs, scratch, n_in, limit=4 << 20, far=0, semaphores=()):
+    sum_ref[...] = jnp.concatenate([xt[0], xt[1]], 1).T
+
+
+def post_kernel(sum_ref, tile_ref, za_ref, zb_ref, sep_ref, run_ref, ownsol_ref, out_ref, total_ref, sems):
+    lane, _ = iotas()
+    running = run_ref[...] + za_ref[8:24]
+    weighted = total(
+        sep_ref[level][:, h * 128 : h * 128 + 128] * running[8 * h + level : 8 * h + level + 1, :]
+        for h in range(2)
+        for level in range(sep_ref.shape[0])
+    )
+    solution_col = ownsol_ref[:, :1] + jnp.sum(weighted, axis=1, keepdims=True)
+    lane16, sub16 = iotas(16)
+    along_z = []
+    for t in range(2):
+        spread = jnp.where((lane16 >> 4) + 8 * t == sub16, jnp.broadcast_to(solution_col, (16, 128)), 0.0)
+        along_z.append(jnp.broadcast_to(jnp.sum(spread, axis=0, keepdims=True), (8, 128)))
+    from_above, from_below = sides(za_ref[:8], zb_ref[...], "gz")
+    copies = []
+    for p in range(2):
+        for i in range(8):
+            weights = tile_ref[i * 8 : i * 8 + 8]
+            low, high = weights * along_z[0], weights * along_z[1]
+            for q in range(2):
+                at = ((p * 8 + i) * 2 + q) * 8
+                source = p * 64 + q * 32 + i
+                first = sum_ref[at : at + 8, :128] + low
+                last = sum_ref[at : at + 8, 128:] + high
+                total_ref[at : at + 8, :128] = first + jnp.where(lane == 0, roll(from_below, -source), 0.0)
+                total_ref[at : at + 8, 128:] = last + jnp.where(lane == 127, roll(from_above, 127 - source), 0.0)
+        rows = pl.ds(p * 128, 128)
+        copies.append(pltpu.make_async_copy(total_ref.at[rows, :], out_ref.at[rows, :], sems.at[p]))
+        copies[p].start()
+    for copy in copies:
+        copy.wait()
+
+
+def call(kernel, outs, scratch, n_in, limit=4 << 20, far=0, semaphores=(), out_space=pltpu.VMEM):
     return pl.pallas_call(
         kernel,
         out_shape=[jax.ShapeDtypeStruct(shape, F32) for shape in outs],
         in_specs=[pl.BlockSpec(memory_space=pltpu.HBM)] * far + [VM] * (n_in - far),
-        out_specs=[VM] * len(outs),
+        out_specs=[pl.BlockSpec(memory_space=out_space)] * len(outs),
         scratch_shapes=[pltpu.VMEM(shape, F32) for shape in scratch] + list(semaphores),
         compiler_params=pltpu.CompilerParams(vmem_limit_bytes=limit),
     )
@@ -455,33 +475,38 @@
         semaphores=(pltpu.SemaphoreType.DMA((2,)), pltpu.SemaphoreType.DMA((3,))),
     )(far(x), far(sep), far(coarse_basis), far(own))
     xr = swap(xs, "gx", 1)
-    running = climb(running, "gx", 1, 7)
     ends, za, zb = call(zface_kernel, [(2, 8, 8, 128), (8, 128), (8, 128)], [], 2)(core, xr)
     running = climb(running, "gy", 2, 5)
     za, zb = swap(za, "gz", 1), swap_odd(zb, "gz")
     running = climb(running, "gy", 6, 6)
+    (factors,) = call(factors_kernel, [(848, 128)], [], 1)(vectors)
     block = (core, core.reshape(512, 128), ends, ends.reshape(128, 128), za, zb)
     ya, yb = call(yface_kernel, [(56, 128), (56, 128)], [(256, 128)], 6)(*block)
     ya, yb = swap(ya, "gy", 1), swap_odd(yb, "gy")
     running = climb(running, "gz", 4, 2)
     (modes,) = call(
-        modes_kernel, [(1696, 128)], [(800, 128), (112, 128), (112, 128), (848, 128), (256, 128)], 9
-    )(*block, ya, yb, vectors)
+        modes_kernel, [(1696, 128)], [(800, 128), (112, 128), (112, 128), (256, 128)], 9
+    )(*block, ya, yb, factors)
     running = climb(running, "gz", 12, 3)
-    (modes,) = call(middle_kernel, [(1696, 128)], [(848, 128), (16, 128)], 3)(modes, vectors, eigen)
+    (modes,) = call(middle_kernel, [(1696, 128)], [(16, 128)], 3)(modes, factors, eigen)
     running = climb(running, "gz", 3, 1)
     local, edge_l, edge_h, xs = call(
-        points_kernel, [(10, 10, 8, 128), (10, 16, 128), (10, 16, 128), (56, 128)], [(1696, 128), (848, 128)], 2
-    )(modes, vectors)
+        points_kernel, [(10, 10, 8, 128), (10, 16, 128), (10, 16, 128), (56, 128)], [(1696, 128)], 2
+    )(modes, factors)
     xr = swap(xs, "gx", 1)
     ya, yb = call(yfold_send_kernel, [(80, 128), (64, 128)], [], 4)(edge_l, edge_h, xr, running)
     ya, yb = swap(ya, "gy", 1), swap_odd(yb, "gy")
+    running = running + jnp.where(level_of >= 4, ya[64:80], 0.0)
+    running = climb(running, "gx", 1, 7)
     parts = (local, edge_l, edge_h, xr, ya, yb)
-    za, zb, running = call(zfold_send_kernel, [(24, 128), (8, 128), (16, 128)], [(128, 128)] * 2, 7)(*parts, running)
+    za, zb = call(zfold_send_kernel, [(24, 128), (8, 128)], [(128, 128)] * 2, 7)(*parts, running)
     za, zb = swap(za, "gz", 1), swap_odd(zb, "gz")
+    smooth, tile = call(
+        gather_kernel, [(256, 256), (64, 128)], [(128, 128), (128, 128), (2, 256, 128), (8, 8, 8, 128)], 7
+    )(*parts, coarse_basis)
     (out,) = call(
-        post_kernel, [(256, 256)], [(128, 128), (128, 128), (2, 256, 128), (8, 8, 8, 128)], 12
-    )(*parts, za, zb, coarse_basis, sep, running, ownsol)
+        post_kernel, [(256, 256)], [(256, 256)], 7, semaphores=(pltpu.SemaphoreType.DMA((2,)),), out_space=pltpu.HBM
+    )(smooth, tile, za, zb, sep, running, ownsol)
     return out.reshape(residual.shape)
 
 

time: 52.3 us -> 54.8 us (1.048)
  starting transfers between devices: 32.8 us -> 35.9 us
  waiting for transfers between devices: 10.2 us -> 9.45 us
    ppermute x12, starting transfers between devices: 19.7 us -> 22.9 us  [swap(): lax.ppermute(value, axis, [(i, i ^ distance) for i in range(lax.axis_size...]
    ppermute x4, waiting for transfers between devices: 5.5 us -> 4.71 us  [swap_odd(): lax.ppermute(value, axis, [(i, (i + 1 if i % 2 else i - 1) % count) for i...]
    pallas_call x4 -> x6, Pallas kernels: 4.87 us -> 4.91 us  [the longest x1 1.46 us: work(): call(modes_kernel, [(1696, 128)], [(800, 128), (112, 128), (112, 128), (2...]
  transfers between devices with their start and end apart: 16 -> 16, of which waited for: 8 -> 8; matrix products, arithmetic and copies ran while one was open for 1% -> 1% of each run, Pallas kernels for 9% -> 10%
where the time goes in v5:
time: 54.8 us; the launch traced here: 54.7 us
  starting transfers between devices  35.9 us (66%)
  waiting for transfers between devices  9.45 us (17%)
  Pallas kernels  8.66 us (16%)
  other arithmetic  0.55 us (1%)
    ppermute x12, starting transfers between devices, swap(): lax.ppermute(value, axis, [(i, i ^ distance) for i in range(lax.axis_size...  22.9 us
    ppermute x4, starting transfers between devices, swap_odd(): lax.ppermute(value, axis, [(i, (i + 1 if i % 2 else i - 1) % count) for i...  13 us
    ppermute x12, waiting for transfers between devices, swap(): lax.ppermute(value, axis, [(i, i ^ distance) for i in range(lax.axis_size...  4.74 us
    ppermute x4, waiting for transfers between devices, swap_odd(): lax.ppermute(value, axis, [(i, (i + 1 if i % 2 else i - 1) % count) for i...  4.71 us
    pallas_call x1, Pallas kernels, work(): call(pre_kernel, [(8, 8, 8, 128), (32, 128), (16, 128), (16, 128)], [(2,...  1.84 us
    pallas_call x1, Pallas kernels, work(): call(modes_kernel, [(1696, 128)], [(800, 128), (112, 128), (112, 128), (2...  1.46 us
    pallas_call x1, Pallas kernels, work(): call(points_kernel, [(10, 10, 8, 128), (10, 16, 128), (10, 16, 128), (56,...  1.38 us
    pallas_call x1, Pallas kernels, work(): call(middle_kernel, [(1696, 128)], [(16, 128)], 3)(modes, factors, eigen)  1.29 us
  transfers between devices with their start and end apart: 16, of which 8 were waited for; matrix products, arithmetic and copies ran while one was open for 1% of the time, Pallas kernels for 10%

profile of v5, /device:TPU:1, one launch (start us, length us, event | category | flops | bytes accessed | tf_op | source)
XLA Modules:
  0.0 54.7 jit_solution(15456770149464223453)
XLA Ops:
  0.0 1.8 %shard_map.64 = (f32[8,8,8,128]{3,2,1,0:T(8,128)S(1)}, f32[32,128]{1,0:T(8,128)S(1)}, f32[16,128]{1,0:T(8,128)S(1)}, f32[16,128]{1,0:T(8,128)S(1)}) custom-call(f32[256,256]{1,0:T(8,128)} %bitcast.18, f32[8,16,256]{2,1,0:T(8,128)} %bitcast.14, f32[8,8,8]{2,1,0:T(8,128)} %basis_ref.3, f32[16,16]{1,0:T(8,128)} %bitcast.19), custom_call_target="tpu_custom_call" | custom-call | tf_op jit(solution)/shard_map/pallas_call | solution.py:469
  1.8 3.9 %collective-permute-start.6 = (f32[16,128]{1,0:T(8,128)S(1)}, f32[16,128]{1,0:T(8,128)S(1)}, u32[]{:S(2)}, u32[]{:S(2)}) collective-permute-start(f32[16,128]{1,0:T(8,128)S(1)} %get-tuple-element.35), channel_id=1, source_target_pairs={{0,32},{16,48},{32,0},{48,16},{64,96},{80,112},{96,64},{112,80},{1... | collective-permute-start | bytes 24584 | tf_op jit(solution)/shard_map/ppermute | solution.py:449
  5.7 1.0 %collective-permute-start = (f32[32,128]{1,0:T(8,128)S(1)}, f32[32,128]{1,0:T(8,128)S(1)}, u32[]{:S(2)}, u32[]{:S(2)}) collective-permute-start(f32[32,128]{1,0:T(8,128)S(1)} %get-tuple-element.25), channel_id=1, source_target_pairs={{0,128},{128,0},{1,129},{129,1},{2,130},{130,2},{3,131},{131,3},{4... | collective-permute-start | bytes 49160 | tf_op jit(solution)/shard_map/ppermute | solution.py:449
  6.9 5.4 %collective-permute-start.7 = (f32[16,128]{1,0:T(8,128)S(1)}, f32[16,128]{1,0:T(8,128)S(1)}, u32[]{:S(2)}, u32[]{:S(2)}) collective-permute-start(f32[16,128]{1,0:T(8,128)S(1)} %select_add_fusion.5), channel_id=1, source_target_pairs={{0,96},{16,112},{32,64},{48,80},{64,32},{80,48},{96,0},{112,16},{1... | collective-permute-start | bytes 24584 | tf_op jit(solution)/shard_map/ppermute | solution.py:449
  12.3 1.0 %collective-permute-done.7 = f32[16,128]{1,0:T(8,128)S(1)} collective-permute-done((f32[16,128]{1,0:T(8,128)S(1)}, f32[16,128]{1,0:T(8,128)S(1)}, u32[]{:S(2)}, u32[]{:S(2)}) %collective-permute-start.7) | collective-permute-done | bytes 8224 | tf_op jit(solution)/shard_map/ppermute | solution.py:449
  13.4 1.3 %collective-permute-start.8 = (f32[16,128]{1,0:T(8,128)S(1)}, f32[16,128]{1,0:T(8,128)S(1)}, u32[]{:S(2)}, u32[]{:S(2)}) collective-permute-start(f32[16,128]{1,0:T(8,128)S(1)} %select_add_fusion.4), channel_id=1, source_target_pairs={{0,4},{1,5},{2,6},{3,7},{4,0},{5,1},{6,2},{7,3},{8,12},{9,13},{10,... | collective-permute-start | bytes 24584 | tf_op jit(solution)/shard_map/ppermute | solution.py:449
  14.7 0.2 shard_map.65
  14.9 1.3 %collective-permute-start.1 = (f32[8,128]{1,0:T(8,128)S(1)}, f32[8,128]{1,0:T(8,128)S(1)}, u32[]{:S(2)}, u32[]{:S(2)}) collective-permute-start(f32[8,128]{1,0:T(8,128)S(1)} %get-tuple-element.27), channel_id=1, source_target_pairs={{0,1},{1,0},{2,3},{3,2},{4,5},{5,4},{6,7},{7,6},{8,9},{9,8},{10,11... | collective-permute-start | bytes 12296 | tf_op jit(solution)/shard_map/ppermute | solution.py:449
  16.2 3.4 %collective-permute-start.2 = (f32[8,128]{1,0:T(8,128)S(1)}, f32[8,128]{1,0:T(8,128)S(1)}, u32[]{:S(2)}, u32[]{:S(2)}) collective-permute-start(f32[8,128]{1,0:T(8,128)S(1)} %get-tuple-element.28), channel_id=1, source_target_pairs={{0,15},{1,2},{2,1},{3,4},{4,3},{5,6},{6,5},{7,8},{8,7},{9,10},{10,... | collective-permute-start | bytes 12296 | tf_op jit(solution)/shard_map/ppermute | solution.py:454
  19.7 1.0 %collective-permute-start.9 = (f32[16,128]{1,0:T(8,128)S(1)}, f32[16,128]{1,0:T(8,128)S(1)}, u32[]{:S(2)}, u32[]{:S(2)}) collective-permute-start(f32[16,128]{1,0:T(8,128)S(1)} %select_add_fusion.3), channel_id=1, source_target_pairs={{0,12},{1,13},{2,14},{3,15},{4,8},{5,9},{6,10},{7,11},{8,4},{9,5},... | collective-permute-start | bytes 24584 | tf_op jit(solution)/shard_map/ppermute | solution.py:449
  20.8 1.2 %collective-permute-done.2.zb_ref = f32[8,128]{1,0:T(8,128)S(1)} collective-permute-done((f32[8,128]{1,0:T(8,128)S(1)}, f32[8,128]{1,0:T(8,128)S(1)}, u32[]{:S(2)}, u32[]{:S(2)}) %collective-permute-start.2) | collective-permute-done | bytes 4128 | tf_op jit(solution)/shard_map/ppermute | solution.py:454
  22.0 0.2 shard_map.66
  22.2 0.8 %collective-permute-start.3 = (f32[56,128]{1,0:T(8,128)S(1)}, f32[56,128]{1,0:T(8,128)S(1)}, u32[]{:S(2)}, u32[]{:S(2)}) collective-permute-start(f32[56,128]{1,0:T(8,128)S(1)} %get-tuple-element.29), channel_id=1, source_target_pairs={{0,16},{16,0},{32,48},{48,32},{64,80},{80,64},{96,112},{112,96},{1... | collective-permute-start | bytes 86024 | tf_op jit(solution)/shard_map/ppermute | solution.py:449
  23.0 3.1 %collective-permute-start.4 = (f32[56,128]{1,0:T(8,128)S(1)}, f32[56,128]{1,0:T(8,128)S(1)}, u32[]{:S(2)}, u32[]{:S(2)}) collective-permute-start(f32[56,128]{1,0:T(8,128)S(1)} %get-tuple-element.30), channel_id=1, source_target_pairs={{0,112},{16,32},{32,16},{48,64},{64,48},{80,96},{96,80},{112,0},{1... | collective-permute-start | bytes 86024 | tf_op jit(solution)/shard_map/ppermute | solution.py:454
  26.2 0.6 %collective-permute-start.10 = (f32[16,128]{1,0:T(8,128)S(1)}, f32[16,128]{1,0:T(8,128)S(1)}, u32[]{:S(2)}, u32[]{:S(2)}) collective-permute-start(f32[16,128]{1,0:T(8,128)S(1)} %select_add_fusion.2), channel_id=1, source_target_pairs={{0,3},{1,2},{2,1},{3,0},{4,7},{5,6},{6,5},{7,4},{8,11},{9,10},{10,... | collective-permute-start | bytes 24584 | tf_op jit(solution)/shard_map/ppermute | solution.py:449
  26.9 0.5 collective-permute-done.4.yb_ref
  27.4 1.5 %shard_map.68.u_ref = f32[1696,128]{1,0:T(8,128)S(1)} custom-call(f32[8,8,8,128]{3,2,1,0:T(8,128)S(1)} %get-tuple-element.24.core_ref, f32[512,128]{1,0:T(8,128)S(1)} %bitcast.11, f32[2,8,8,128]{3,2,1,0:T(8,128)S(1)} %get-tuple-element.26.ends_ref, f32[128,128]{1,0:T(8,128)S(1)} %bitcast.13, f32[8,128]{1,0:T(8,128)S(1)} %collective-permute-done.1.za_ref, ...), custom_call_target="tpu_custom_call" | custom-call | tf_op jit(solution)/shard_map/pallas_call | solution.py:487
  28.8 1.3 %shard_map.69.u_ref = f32[1696,128]{1,0:T(8,128)S(1)} custom-call(f32[1696,128]{1,0:T(8,128)S(1)} %shard_map.68.u_ref, f32[848,128]{1,0:T(8,128)S(1)} %shard_map.67.s, f32[3,10,1,128]{3,2,1,0:T(1,128)S(1)} %bitcast.17), custom_call_target="tpu_custom_call" | custom-call | tf_op jit(solution)/shard_map/pallas_call | solution.py:491
  30.1 1.4 %shard_map.70 = (f32[10,10,8,128]{3,2,1,0:T(8,128)S(1)}, f32[10,16,128]{2,1,0:T(8,128)S(1)}, f32[10,16,128]{2,1,0:T(8,128)S(1)}, f32[56,128]{1,0:T(8,128)S(1)}) custom-call(f32[1696,128]{1,0:T(8,128)S(1)} %shard_map.69.u_ref, f32[848,128]{1,0:T(8,128)S(1)} %shard_map.67.s), custom_call_target="tpu_custom_call" | custom-call | tf_op jit(solution)/shard_map/pallas_call | solution.py:493
  31.5 5.9 %collective-permute-start.5 = (f32[56,128]{1,0:T(8,128)S(1)}, f32[56,128]{1,0:T(8,128)S(1)}, u32[]{:S(2)}, u32[]{:S(2)}) collective-permute-start(f32[56,128]{1,0:T(8,128)S(1)} %get-tuple-element.34), channel_id=1, source_target_pairs={{0,128},{128,0},{1,129},{129,1},{2,130},{130,2},{3,131},{131,3},{4... | collective-permute-start | bytes 86024 | tf_op jit(solution)/shard_map/ppermute | solution.py:449
  37.5 0.8 %collective-permute-done.5.xr_ref = f32[56,128]{1,0:T(8,128)S(1)} collective-permute-done((f32[56,128]{1,0:T(8,128)S(1)}, f32[56,128]{1,0:T(8,128)S(1)}, u32[]{:S(2)}, u32[]{:S(2)}) %collective-permute-start.5) | collective-permute-done | bytes 28704 | tf_op jit(solution)/shard_map/ppermute | solution.py:449
  38.2 0.1 shard_map.71
  38.5 2.8 %collective-permute-done.11.ya_ref = f32[80,128]{1,0:T(8,128)S(1)} collective-permute-done((f32[80,128]{1,0:T(8,128)S(1)}, f32[80,128]{1,0:T(8,128)S(1)}, u32[]{:S(2)}, u32[]{:S(2)}) %collective-permute-start.11) | collective-permute-done | bytes 40992 | tf_op jit(solution)/shard_map/ppermute | solution.py:449
  41.4 1.5 %collective-permute-start.13 = (f32[16,128]{1,0:T(8,128)S(1)}, f32[16,128]{1,0:T(8,128)S(1)}, u32[]{:S(2)}, u32[]{:S(2)}) collective-permute-start(f32[16,128]{1,0:T(8,128)S(1)} %fusion), channel_id=1, source_target_pairs={{0,128},{128,0},{1,129},{129,1},{2,130},{130,2},{3,131},{131,3},{4... | collective-permute-start | bytes 24584 | tf_op jit(solution)/shard_map/ppermute | solution.py:449
  42.9 3.0 %collective-permute-start.12 = (f32[64,128]{1,0:T(8,128)S(1)}, f32[64,128]{1,0:T(8,128)S(1)}, u32[]{:S(2)}, u32[]{:S(2)}) collective-permute-start(f32[64,128]{1,0:T(8,128)S(1)} %get-tuple-element.37), channel_id=1, source_target_pairs={{0,112},{16,32},{32,16},{48,64},{64,48},{80,96},{96,80},{112,0},{1... | collective-permute-start | bytes 98312 | tf_op jit(solution)/shard_map/ppermute | solution.py:454
  45.9 1.6 %collective-permute-done.12.yb_ref = f32[64,128]{1,0:T(8,128)S(1)} collective-permute-done((f32[64,128]{1,0:T(8,128)S(1)}, f32[64,128]{1,0:T(8,128)S(1)}, u32[]{:S(2)}, u32[]{:S(2)}) %collective-permute-start.12) | collective-permute-done | bytes 32800 | tf_op jit(solution)/shard_map/ppermute | solution.py:454
  47.5 0.3 shard_map.73
  47.8 0.1 collective-permute-start.14
  47.9 3.5 %collective-permute-start.15 = (f32[8,128]{1,0:T(8,128)S(1)}, f32[8,128]{1,0:T(8,128)S(1)}, u32[]{:S(2)}, u32[]{:S(2)}) collective-permute-start(f32[8,128]{1,0:T(8,128)S(1)} %get-tuple-element.41), channel_id=1, source_target_pairs={{0,15},{1,2},{2,1},{3,4},{4,3},{5,6},{6,5},{7,8},{8,7},{9,10},{10,... | collective-permute-start | bytes 12296 | tf_op jit(solution)/shard_map/ppermute | solution.py:454
  51.4 0.9 %shard_map.72 = (f32[256,256]{1,0:T(8,128)S(1)}, f32[64,128]{1,0:T(8,128)S(1)}) custom-call(f32[10,10,8,128]{3,2,1,0:T(8,128)S(1)} %get-tuple-element.31.l_ref, f32[10,16,128]{2,1,0:T(8,128)S(1)} %get-tuple-element.32.hl_ref, f32[10,16,128]{2,1,0:T(8,128)S(1)} %get-tuple-element.33.hh_ref, f32[56,128]{1,0:T(8,128)S(1)} %collective-permute-done.5.xr_ref, ...), custom_call_target="tpu_custom_call" | custom-call | tf_op jit(solution)/shard_map/pallas_call | solution.py:504
  52.4 1.4 %collective-permute-done.15.zb_ref = f32[8,128]{1,0:T(8,128)S(1)} collective-permute-done((f32[8,128]{1,0:T(8,128)S(1)}, f32[8,128]{1,0:T(8,128)S(1)}, u32[]{:S(2)}, u32[]{:S(2)}) %collective-permute-start.15) | collective-permute-done | bytes 4128 | tf_op jit(solution)/shard_map/ppermute | solution.py:454
  53.8 0.9 %shard_map.74 = f32[256,256]{1,0:T(8,128)} custom-call(f32[256,256]{1,0:T(8,128)S(1)} %get-tuple-element.38.sum_ref, f32[64,128]{1,0:T(8,128)S(1)} %get-tuple-element.39.tile_ref, f32[24,128]{1,0:T(8,128)S(1)} %collective-permute-done.14.za_ref, f32[8,128]{1,0:T(8,128)S(1)} %collective-permute-done.15.zb_ref, f32[8,16,256]{2,1,0:T(8,128)S(1)} %bitcast.15, ...), custom_call_target="tpu_custom_call" | custom-call | tf_op jit(solution)/shard_map/pallas_call | solution.py:507
  (33 shorter events, 0.8 us)
Async XLA Ops:
  1.8 4.9 %collective-permute-start.6 = (f32[16,128]{1,0:T(8,128)S(1)}, f32[16,128]{1,0:T(8,128)S(1)}, u32[]{:S(2)}, u32[]{:S(2)}) collective-permute-start(f32[16,128]{1,0:T(8,128)S(1)} %get-tuple-element.35), channel_id=1, source_target_pairs={{0,32},{16,48},{32,0},{48,16},{64,96},{80,112},{96,64},{112,80},{1... | collective-permute-start | bytes 24584 | tf_op jit(solution)/shard_map/ppermute | solution.py:449
  5.7 9.0 %collective-permute-start = (f32[32,128]{1,0:T(8,128)S(1)}, f32[32,128]{1,0:T(8,128)S(1)}, u32[]{:S(2)}, u32[]{:S(2)}) collective-permute-start(f32[32,128]{1,0:T(8,128)S(1)} %get-tuple-element.25), channel_id=1, source_target_pairs={{0,128},{128,0},{1,129},{129,1},{2,130},{130,2},{3,131},{131,3},{4... | collective-permute-start | bytes 49160 | tf_op jit(solution)/shard_map/ppermute | solution.py:449
  6.9 6.5 %collective-permute-start.7 = (f32[16,128]{1,0:T(8,128)S(1)}, f32[16,128]{1,0:T(8,128)S(1)}, u32[]{:S(2)}, u32[]{:S(2)}) collective-permute-start(f32[16,128]{1,0:T(8,128)S(1)} %select_add_fusion.5), channel_id=1, source_target_pairs={{0,96},{16,112},{32,64},{48,80},{64,32},{80,48},{96,0},{112,16},{1... | collective-permute-start | bytes 24584 | tf_op jit(solution)/shard_map/ppermute | solution.py:449
  13.4 6.3 %collective-permute-start.8 = (f32[16,128]{1,0:T(8,128)S(1)}, f32[16,128]{1,0:T(8,128)S(1)}, u32[]{:S(2)}, u32[]{:S(2)}) collective-permute-start(f32[16,128]{1,0:T(8,128)S(1)} %select_add_fusion.4), channel_id=1, source_target_pairs={{0,4},{1,5},{2,6},{3,7},{4,0},{5,1},{6,2},{7,3},{8,12},{9,13},{10,... | collective-permute-start | bytes 24584 | tf_op jit(solution)/shard_map/ppermute | solution.py:449
  14.9 5.8 %collective-permute-start.1 = (f32[8,128]{1,0:T(8,128)S(1)}, f32[8,128]{1,0:T(8,128)S(1)}, u32[]{:S(2)}, u32[]{:S(2)}) collective-permute-start(f32[8,128]{1,0:T(8,128)S(1)} %get-tuple-element.27), channel_id=1, source_target_pairs={{0,1},{1,0},{2,3},{3,2},{4,5},{5,4},{6,7},{7,6},{8,9},{9,8},{10,11... | collective-permute-start | bytes 12296 | tf_op jit(solution)/shard_map/ppermute | solution.py:449
  16.2 5.8 %collective-permute-start.2 = (f32[8,128]{1,0:T(8,128)S(1)}, f32[8,128]{1,0:T(8,128)S(1)}, u32[]{:S(2)}, u32[]{:S(2)}) collective-permute-start(f32[8,128]{1,0:T(8,128)S(1)} %get-tuple-element.28), channel_id=1, source_target_pairs={{0,15},{1,2},{2,1},{3,4},{4,3},{5,6},{6,5},{7,8},{8,7},{9,10},{10,... | collective-permute-start | bytes 12296 | tf_op jit(solution)/shard_map/ppermute | solution.py:454
  19.7 6.4 %collective-permute-start.9 = (f32[16,128]{1,0:T(8,128)S(1)}, f32[16,128]{1,0:T(8,128)S(1)}, u32[]{:S(2)}, u32[]{:S(2)}) collective-permute-start(f32[16,128]{1,0:T(8,128)S(1)} %select_add_fusion.3), channel_id=1, source_target_pairs={{0,12},{1,13},{2,14},{3,15},{4,8},{5,9},{6,10},{7,11},{8,4},{9,5},... | collective-permute-start | bytes 24584 | tf_op jit(solution)/shard_map/ppermute | solution.py:449
  22.0 4.8 %copy-start.2 = (bf16[1,1,1,3,10,10,128]{6,3,5,4,2,1,0:T(4,128)(2,1)S(1)}, bf16[1,1,1,3,10,10,128]{6,3,5,4,2,1,0:T(4,128)(2,1)}, u32[]{:S(2)}) copy-start(bf16[1,1,1,3,10,10,128]{6,3,5,4,2,1,0:T(4,128)(2,1)} %param.7) | copy-start | bytes 230404
  22.2 4.7 %collective-permute-start.3 = (f32[56,128]{1,0:T(8,128)S(1)}, f32[56,128]{1,0:T(8,128)S(1)}, u32[]{:S(2)}, u32[]{:S(2)}) collective-permute-start(f32[56,128]{1,0:T(8,128)S(1)} %get-tuple-element.29), channel_id=1, source_target_pairs={{0,16},{16,0},{32,48},{48,32},{64,80},{80,64},{96,112},{112,96},{1... | collective-permute-start | bytes 86024 | tf_op jit(solution)/shard_map/ppermute | solution.py:449
  23.0 4.4 %collective-permute-start.4 = (f32[56,128]{1,0:T(8,128)S(1)}, f32[56,128]{1,0:T(8,128)S(1)}, u32[]{:S(2)}, u32[]{:S(2)}) collective-permute-start(f32[56,128]{1,0:T(8,128)S(1)} %get-tuple-element.30), channel_id=1, source_target_pairs={{0,112},{16,32},{32,16},{48,64},{64,48},{80,96},{96,80},{112,0},{1... | collective-permute-start | bytes 86024 | tf_op jit(solution)/shard_map/ppermute | solution.py:454
  26.2 11.2 %collective-permute-start.10 = (f32[16,128]{1,0:T(8,128)S(1)}, f32[16,128]{1,0:T(8,128)S(1)}, u32[]{:S(2)}, u32[]{:S(2)}) collective-permute-start(f32[16,128]{1,0:T(8,128)S(1)} %select_add_fusion.2), channel_id=1, source_target_pairs={{0,3},{1,2},{2,1},{3,0},{4,7},{5,6},{6,5},{7,4},{8,11},{9,10},{10,... | collective-permute-start | bytes 24584 | tf_op jit(solution)/shard_map/ppermute | solution.py:449
  26.8 2.0 %copy-start.3 = (f32[1,1,1,3,10,128]{5,2,4,3,1,0:T(1,128)S(1)}, f32[1,1,1,3,10,128]{5,2,4,3,1,0:T(1,128)}, u32[]{:S(2)}) copy-start(f32[1,1,1,3,10,128]{5,2,4,3,1,0:T(1,128)} %param.8) | copy-start | bytes 46084
  31.5 6.7 %collective-permute-start.5 = (f32[56,128]{1,0:T(8,128)S(1)}, f32[56,128]{1,0:T(8,128)S(1)}, u32[]{:S(2)}, u32[]{:S(2)}) collective-permute-start(f32[56,128]{1,0:T(8,128)S(1)} %get-tuple-element.34), channel_id=1, source_target_pairs={{0,128},{128,0},{1,129},{129,1},{2,130},{130,2},{3,131},{131,3},{4... | collective-permute-start | bytes 86024 | tf_op jit(solution)/shard_map/ppermute | solution.py:449
  38.4 2.9 %collective-permute-start.11 = (f32[80,128]{1,0:T(8,128)S(1)}, f32[80,128]{1,0:T(8,128)S(1)}, u32[]{:S(2)}, u32[]{:S(2)}) collective-permute-start(f32[80,128]{1,0:T(8,128)S(1)} %get-tuple-element.36), channel_id=1, source_target_pairs={{0,16},{16,0},{32,48},{48,32},{64,80},{80,64},{96,112},{112,96},{1... | collective-permute-start | bytes 122888 | tf_op jit(solution)/shard_map/ppermute | solution.py:449
  41.4 4.5 %collective-permute-start.13 = (f32[16,128]{1,0:T(8,128)S(1)}, f32[16,128]{1,0:T(8,128)S(1)}, u32[]{:S(2)}, u32[]{:S(2)}) collective-permute-start(f32[16,128]{1,0:T(8,128)S(1)} %fusion), channel_id=1, source_target_pairs={{0,128},{128,0},{1,129},{129,1},{2,130},{130,2},{3,131},{131,3},{4... | collective-permute-start | bytes 24584 | tf_op jit(solution)/shard_map/ppermute | solution.py:449
  42.9 4.6 %collective-permute-start.12 = (f32[64,128]{1,0:T(8,128)S(1)}, f32[64,128]{1,0:T(8,128)S(1)}, u32[]{:S(2)}, u32[]{:S(2)}) collective-permute-start(f32[64,128]{1,0:T(8,128)S(1)} %get-tuple-element.37), channel_id=1, source_target_pairs={{0,112},{16,32},{32,16},{48,64},{64,48},{80,96},{96,80},{112,0},{1... | collective-permute-start | bytes 98312 | tf_op jit(solution)/shard_map/ppermute | solution.py:454
  47.5 3.9 %copy-start.1 = (f32[8,8,8]{2,1,0:T(8,128)S(1)}, f32[8,8,8]{2,1,0:T(8,128)}, u32[]{:S(2)}) copy-start(f32[8,8,8]{2,1,0:T(8,128)} %basis_ref.3) | copy-start | bytes 6148
  47.8 6.0 %collective-permute-start.14 = (f32[24,128]{1,0:T(8,128)S(1)}, f32[24,128]{1,0:T(8,128)S(1)}, u32[]{:S(2)}, u32[]{:S(2)}) collective-permute-start(f32[24,128]{1,0:T(8,128)S(1)} %get-tuple-element.40), channel_id=1, source_target_pairs={{0,1},{1,0},{2,3},{3,2},{4,5},{5,4},{6,7},{7,6},{8,9},{9,8},{10,11... | collective-permute-start | bytes 36872 | tf_op jit(solution)/shard_map/ppermute | solution.py:449
  47.9 5.9 %copy-start = (f32[1,1,1,8,16,256]{5,4,3,2,1,0:T(8,128)S(1)}, f32[1,1,1,8,16,256]{5,4,3,2,1,0:T(8,128)}, u32[]{:S(2)}) copy-start(f32[1,1,1,8,16,256]{5,4,3,2,1,0:T(8,128)} %param.11) | copy-start | bytes 393220
  47.9 5.9 %collective-permute-start.15 = (f32[8,128]{1,0:T(8,128)S(1)}, f32[8,128]{1,0:T(8,128)S(1)}, u32[]{:S(2)}, u32[]{:S(2)}) collective-permute-start(f32[8,128]{1,0:T(8,128)S(1)} %get-tuple-element.41), channel_id=1, source_target_pairs={{0,15},{1,2},{2,1},{3,4},{4,3},{5,6},{6,5},{7,8},{8,7},{9,10},{10,... | collective-permute-start | bytes 12296 | tf_op jit(solution)/shard_map/ppermute | solution.py:454

commit v6 on v5

--- a/solution.py
+++ b/solution.py
@@ -487,9 +487,10 @@
     (modes,) = call(
         modes_kernel, [(1696, 128)], [(800, 128), (112, 128), (112, 128), (256, 128)], 9
     )(*block, ya, yb, factors)
-    running = climb(running, "gz", 12, 3)
+    three, twelve, fifteen = (swap(running, "gz", d) for d in (3, 12, 15))
     (modes,) = call(middle_kernel, [(1696, 128)], [(16, 128)], 3)(modes, factors, eigen)
-    running = climb(running, "gz", 3, 1)
+    both = jnp.where(level_of >= 3, three + (twelve + fifteen), three)
+    running = running + jnp.where(level_of >= 1, both, 0.0)
     local, edge_l, edge_h, xs = call(
         points_kernel, [(10, 10, 8, 128), (10, 16, 128), (10, 16, 128), (56, 128)], [(1696, 128)], 2
     )(modes, factors)

time: 54.8 us -> 58.4 us (1.066)
  waiting for transfers between devices: 9.45 us -> 12.4 us
  starting transfers between devices: 35.9 us -> 36.7 us
    ppermute x12 -> x13, starting transfers between devices: 22.9 us -> 26.6 us  [swap(): lax.ppermute(value, axis, [(i, i ^ distance) for i in range(lax.axis_size...]
    ppermute x4, starting transfers between devices: 13 us -> 10.1 us  [swap_odd(): lax.ppermute(value, axis, [(i, (i + 1 if i % 2 else i - 1) % count) for i...]
    ppermute x4, waiting for transfers between devices: 4.71 us -> 6.82 us  [swap_odd(): lax.ppermute(value, axis, [(i, (i + 1 if i % 2 else i - 1) % count) for i...]
    ppermute x12 -> x13, waiting for transfers between devices: 4.74 us -> 5.54 us  [swap(): lax.ppermute(value, axis, [(i, i ^ distance) for i in range(lax.axis_size...]
  transfers between devices with their start and end apart: 16 -> 17, of which waited for: 8 -> 8; matrix products, arithmetic and copies ran while one was open for 1% -> 1% of each run, Pallas kernels for 10% -> 9%
where the time goes in v6:
time: 58.4 us; the launch traced here: 58.3 us
  starting transfers between devices  36.7 us (63%)
  waiting for transfers between devices  12.4 us (21%)
  Pallas kernels  8.66 us (15%)
    ppermute x13, starting transfers between devices, swap(): lax.ppermute(value, axis, [(i, i ^ distance) for i in range(lax.axis_size...  26.6 us
    ppermute x4, starting transfers between devices, swap_odd(): lax.ppermute(value, axis, [(i, (i + 1 if i % 2 else i - 1) % count) for i...  10.1 us
    ppermute x4, waiting for transfers between devices, swap_odd(): lax.ppermute(value, axis, [(i, (i + 1 if i % 2 else i - 1) % count) for i...  6.82 us
    ppermute x13, waiting for transfers between devices, swap(): lax.ppermute(value, axis, [(i, i ^ distance) for i in range(lax.axis_size...  5.54 us
    pallas_call x1, Pallas kernels, work(): call(pre_kernel, [(8, 8, 8, 128), (32, 128), (16, 128), (16, 128)], [(2,...  1.84 us
    pallas_call x1, Pallas kernels, work(): call(modes_kernel, [(1696, 128)], [(800, 128), (112, 128), (112, 128), (2...  1.46 us
    pallas_call x1, Pallas kernels, work(): call(points_kernel, [(10, 10, 8, 128), (10, 16, 128), (10, 16, 128), (56,...  1.38 us
    pallas_call x1, Pallas kernels, work(): call(middle_kernel, [(1696, 128)], [(16, 128)], 3)(modes, factors, eigen)  1.29 us
  transfers between devices with their start and end apart: 17, of which 8 were waited for; matrix products, arithmetic and copies ran while one was open for 1% of the time, Pallas kernels for 9%

profile of v6, /device:TPU:1, one launch (start us, length us, event | category | flops | bytes accessed | tf_op | source)
XLA Modules:
  0.0 58.3 jit_solution(17770188541021417419)
XLA Ops:
  0.0 1.8 %shard_map.64 = (f32[8,8,8,128]{3,2,1,0:T(8,128)S(1)}, f32[32,128]{1,0:T(8,128)S(1)}, f32[16,128]{1,0:T(8,128)S(1)}, f32[16,128]{1,0:T(8,128)S(1)}) custom-call(f32[256,256]{1,0:T(8,128)} %bitcast.18, f32[8,16,256]{2,1,0:T(8,128)} %bitcast.14, f32[8,8,8]{2,1,0:T(8,128)} %basis_ref.3, f32[16,16]{1,0:T(8,128)} %bitcast.19), custom_call_target="tpu_custom_call" | custom-call | tf_op jit(solution)/shard_map/pallas_call | solution.py:469
  1.8 3.9 %collective-permute-start.6 = (f32[16,128]{1,0:T(8,128)S(1)}, f32[16,128]{1,0:T(8,128)S(1)}, u32[]{:S(2)}, u32[]{:S(2)}) collective-permute-start(f32[16,128]{1,0:T(8,128)S(1)} %get-tuple-element.35), channel_id=1, source_target_pairs={{0,32},{16,48},{32,0},{48,16},{64,96},{80,112},{96,64},{112,80},{1... | collective-permute-start | bytes 24584 | tf_op jit(solution)/shard_map/ppermute | solution.py:449
  5.7 1.0 %collective-permute-start = (f32[32,128]{1,0:T(8,128)S(1)}, f32[32,128]{1,0:T(8,128)S(1)}, u32[]{:S(2)}, u32[]{:S(2)}) collective-permute-start(f32[32,128]{1,0:T(8,128)S(1)} %get-tuple-element.25), channel_id=1, source_target_pairs={{0,128},{128,0},{1,129},{129,1},{2,130},{130,2},{3,131},{131,3},{4... | collective-permute-start | bytes 49160 | tf_op jit(solution)/shard_map/ppermute | solution.py:449
  6.9 5.4 %collective-permute-start.7 = (f32[16,128]{1,0:T(8,128)S(1)}, f32[16,128]{1,0:T(8,128)S(1)}, u32[]{:S(2)}, u32[]{:S(2)}) collective-permute-start(f32[16,128]{1,0:T(8,128)S(1)} %select_add_fusion.3), channel_id=1, source_target_pairs={{0,96},{16,112},{32,64},{48,80},{64,32},{80,48},{96,0},{112,16},{1... | collective-permute-start | bytes 24584 | tf_op jit(solution)/shard_map/ppermute | solution.py:449
  12.3 1.0 %collective-permute-done.7 = f32[16,128]{1,0:T(8,128)S(1)} collective-permute-done((f32[16,128]{1,0:T(8,128)S(1)}, f32[16,128]{1,0:T(8,128)S(1)}, u32[]{:S(2)}, u32[]{:S(2)}) %collective-permute-start.7) | collective-permute-done | bytes 8224 | tf_op jit(solution)/shard_map/ppermute | solution.py:449
  13.4 1.3 %collective-permute-start.8 = (f32[16,128]{1,0:T(8,128)S(1)}, f32[16,128]{1,0:T(8,128)S(1)}, u32[]{:S(2)}, u32[]{:S(2)}) collective-permute-start(f32[16,128]{1,0:T(8,128)S(1)} %select_add_fusion.2), channel_id=1, source_target_pairs={{0,4},{1,5},{2,6},{3,7},{4,0},{5,1},{6,2},{7,3},{8,12},{9,13},{10,... | collective-permute-start | bytes 24584 | tf_op jit(solution)/shard_map/ppermute | solution.py:449
  14.7 0.2 shard_map.65
  14.9 1.3 %collective-permute-start.1 = (f32[8,128]{1,0:T(8,128)S(1)}, f32[8,128]{1,0:T(8,128)S(1)}, u32[]{:S(2)}, u32[]{:S(2)}) collective-permute-start(f32[8,128]{1,0:T(8,128)S(1)} %get-tuple-element.27), channel_id=1, source_target_pairs={{0,1},{1,0},{2,3},{3,2},{4,5},{5,4},{6,7},{7,6},{8,9},{9,8},{10,11... | collective-permute-start | bytes 12296 | tf_op jit(solution)/shard_map/ppermute | solution.py:449
  16.2 3.4 %collective-permute-start.2 = (f32[8,128]{1,0:T(8,128)S(1)}, f32[8,128]{1,0:T(8,128)S(1)}, u32[]{:S(2)}, u32[]{:S(2)}) collective-permute-start(f32[8,128]{1,0:T(8,128)S(1)} %get-tuple-element.28), channel_id=1, source_target_pairs={{0,15},{1,2},{2,1},{3,4},{4,3},{5,6},{6,5},{7,8},{8,7},{9,10},{10,... | collective-permute-start | bytes 12296 | tf_op jit(solution)/shard_map/ppermute | solution.py:454
  19.7 2.3 %collective-permute-done.2.zb_ref = f32[8,128]{1,0:T(8,128)S(1)} collective-permute-done((f32[8,128]{1,0:T(8,128)S(1)}, f32[8,128]{1,0:T(8,128)S(1)}, u32[]{:S(2)}, u32[]{:S(2)}) %collective-permute-start.2) | collective-permute-done | bytes 4128 | tf_op jit(solution)/shard_map/ppermute | solution.py:454
  22.0 0.2 shard_map.66
  22.2 0.8 %collective-permute-start.3 = (f32[56,128]{1,0:T(8,128)S(1)}, f32[56,128]{1,0:T(8,128)S(1)}, u32[]{:S(2)}, u32[]{:S(2)}) collective-permute-start(f32[56,128]{1,0:T(8,128)S(1)} %get-tuple-element.29), channel_id=1, source_target_pairs={{0,16},{16,0},{32,48},{48,32},{64,80},{80,64},{96,112},{112,96},{1... | collective-permute-start | bytes 86024 | tf_op jit(solution)/shard_map/ppermute | solution.py:449
  23.0 3.1 %collective-permute-start.4 = (f32[56,128]{1,0:T(8,128)S(1)}, f32[56,128]{1,0:T(8,128)S(1)}, u32[]{:S(2)}, u32[]{:S(2)}) collective-permute-start(f32[56,128]{1,0:T(8,128)S(1)} %get-tuple-element.30), channel_id=1, source_target_pairs={{0,112},{16,32},{32,16},{48,64},{64,48},{80,96},{96,80},{112,0},{1... | collective-permute-start | bytes 86024 | tf_op jit(solution)/shard_map/ppermute | solution.py:454
  26.2 0.7 %collective-permute-start.10 = (f32[16,128]{1,0:T(8,128)S(1)}, f32[16,128]{1,0:T(8,128)S(1)}, u32[]{:S(2)}, u32[]{:S(2)}) collective-permute-start(f32[16,128]{1,0:T(8,128)S(1)} %select_add_fusion.1), channel_id=1, source_target_pairs={{0,12},{1,13},{2,14},{3,15},{4,8},{5,9},{6,10},{7,11},{8,4},{9,5},... | collective-permute-start | bytes 24584 | tf_op jit(solution)/shard_map/ppermute | solution.py:449
  26.9 2.8 %collective-permute-start.11 = (f32[16,128]{1,0:T(8,128)S(1)}, f32[16,128]{1,0:T(8,128)S(1)}, u32[]{:S(2)}, u32[]{:S(2)}) collective-permute-start(f32[16,128]{1,0:T(8,128)S(1)} %select_add_fusion.1), channel_id=1, source_target_pairs={{0,15},{1,14},{2,13},{3,12},{4,11},{5,10},{6,9},{7,8},{8,7},{9,6},... | collective-permute-start | bytes 24584 | tf_op jit(solution)/shard_map/ppermute | solution.py:449
  29.7 1.5 %collective-permute-start.9 = (f32[16,128]{1,0:T(8,128)S(1)}, f32[16,128]{1,0:T(8,128)S(1)}, u32[]{:S(2)}, u32[]{:S(2)}) collective-permute-start(f32[16,128]{1,0:T(8,128)S(1)} %select_add_fusion.1), channel_id=1, source_target_pairs={{0,3},{1,2},{2,1},{3,0},{4,7},{5,6},{6,5},{7,4},{8,11},{9,10},{10,... | collective-permute-start | bytes 24584 | tf_op jit(solution)/shard_map/ppermute | solution.py:449
  31.3 1.5 %shard_map.68.u_ref = f32[1696,128]{1,0:T(8,128)S(1)} custom-call(f32[8,8,8,128]{3,2,1,0:T(8,128)S(1)} %get-tuple-element.24.core_ref, f32[512,128]{1,0:T(8,128)S(1)} %bitcast.11, f32[2,8,8,128]{3,2,1,0:T(8,128)S(1)} %get-tuple-element.26.ends_ref, f32[128,128]{1,0:T(8,128)S(1)} %bitcast.13, f32[8,128]{1,0:T(8,128)S(1)} %collective-permute-done.1.za_ref, ...), custom_call_target="tpu_custom_call" | custom-call | tf_op jit(solution)/shard_map/pallas_call | solution.py:487
  32.8 1.3 %shard_map.69.u_ref = f32[1696,128]{1,0:T(8,128)S(1)} custom-call(f32[1696,128]{1,0:T(8,128)S(1)} %shard_map.68.u_ref, f32[848,128]{1,0:T(8,128)S(1)} %shard_map.67.s, f32[3,10,1,128]{3,2,1,0:T(1,128)S(1)} %bitcast.17), custom_call_target="tpu_custom_call" | custom-call | tf_op jit(solution)/shard_map/pallas_call | solution.py:491
  34.1 1.4 %shard_map.70 = (f32[10,10,8,128]{3,2,1,0:T(8,128)S(1)}, f32[10,16,128]{2,1,0:T(8,128)S(1)}, f32[10,16,128]{2,1,0:T(8,128)S(1)}, f32[56,128]{1,0:T(8,128)S(1)}) custom-call(f32[1696,128]{1,0:T(8,128)S(1)} %shard_map.69.u_ref, f32[848,128]{1,0:T(8,128)S(1)} %shard_map.67.s), custom_call_target="tpu_custom_call" | custom-call | tf_op jit(solution)/shard_map/pallas_call | solution.py:494
  35.5 6.1 %collective-permute-start.5 = (f32[56,128]{1,0:T(8,128)S(1)}, f32[56,128]{1,0:T(8,128)S(1)}, u32[]{:S(2)}, u32[]{:S(2)}) collective-permute-start(f32[56,128]{1,0:T(8,128)S(1)} %get-tuple-element.34), channel_id=1, source_target_pairs={{0,128},{128,0},{1,129},{129,1},{2,130},{130,2},{3,131},{131,3},{4... | collective-permute-start | bytes 86024 | tf_op jit(solution)/shard_map/ppermute | solution.py:449
  41.7 0.8 %collective-permute-done.5.xr_ref = f32[56,128]{1,0:T(8,128)S(1)} collective-permute-done((f32[56,128]{1,0:T(8,128)S(1)}, f32[56,128]{1,0:T(8,128)S(1)}, u32[]{:S(2)}, u32[]{:S(2)}) %collective-permute-start.5) | collective-permute-done | bytes 28704 | tf_op jit(solution)/shard_map/ppermute | solution.py:449
  42.5 0.1 shard_map.71
  42.7 2.8 %collective-permute-done.12.ya_ref = f32[80,128]{1,0:T(8,128)S(1)} collective-permute-done((f32[80,128]{1,0:T(8,128)S(1)}, f32[80,128]{1,0:T(8,128)S(1)}, u32[]{:S(2)}, u32[]{:S(2)}) %collective-permute-start.12) | collective-permute-done | bytes 40992 | tf_op jit(solution)/shard_map/ppermute | solution.py:449
  45.6 1.5 %collective-permute-start.14 = (f32[16,128]{1,0:T(8,128)S(1)}, f32[16,128]{1,0:T(8,128)S(1)}, u32[]{:S(2)}, u32[]{:S(2)}) collective-permute-start(f32[16,128]{1,0:T(8,128)S(1)} %fusion.2), channel_id=1, source_target_pairs={{0,128},{128,0},{1,129},{129,1},{2,130},{130,2},{3,131},{131,3},{4... | collective-permute-start | bytes 24584 | tf_op jit(solution)/shard_map/ppermute | solution.py:449
  47.1 0.8 %collective-permute-done.14 = f32[16,128]{1,0:T(8,128)S(1)} collective-permute-done((f32[16,128]{1,0:T(8,128)S(1)}, f32[16,128]{1,0:T(8,128)S(1)}, u32[]{:S(2)}, u32[]{:S(2)}) %collective-permute-start.14) | collective-permute-done | bytes 8224 | tf_op jit(solution)/shard_map/ppermute | solution.py:449
  48.0 3.1 %collective-permute-done.13.yb_ref = f32[64,128]{1,0:T(8,128)S(1)} collective-permute-done((f32[64,128]{1,0:T(8,128)S(1)}, f32[64,128]{1,0:T(8,128)S(1)}, u32[]{:S(2)}, u32[]{:S(2)}) %collective-permute-start.13) | collective-permute-done | bytes 32800 | tf_op jit(solution)/shard_map/ppermute | solution.py:454
  51.1 0.3 shard_map.73
  51.4 0.1 collective-permute-start.15
  51.5 3.5 %collective-permute-start.16 = (f32[8,128]{1,0:T(8,128)S(1)}, f32[8,128]{1,0:T(8,128)S(1)}, u32[]{:S(2)}, u32[]{:S(2)}) collective-permute-start(f32[8,128]{1,0:T(8,128)S(1)} %get-tuple-element.41), channel_id=1, source_target_pairs={{0,15},{1,2},{2,1},{3,4},{4,3},{5,6},{6,5},{7,8},{8,7},{9,10},{10,... | collective-permute-start | bytes 12296 | tf_op jit(solution)/shard_map/ppermute | solution.py:454
  55.0 0.9 %shard_map.72 = (f32[256,256]{1,0:T(8,128)S(1)}, f32[64,128]{1,0:T(8,128)S(1)}) custom-call(f32[10,10,8,128]{3,2,1,0:T(8,128)S(1)} %get-tuple-element.31.l_ref, f32[10,16,128]{2,1,0:T(8,128)S(1)} %get-tuple-element.32.hl_ref, f32[10,16,128]{2,1,0:T(8,128)S(1)} %get-tuple-element.33.hh_ref, f32[56,128]{1,0:T(8,128)S(1)} %collective-permute-done.5.xr_ref, ...), custom_call_target="tpu_custom_call" | custom-call | tf_op jit(solution)/shard_map/pallas_call | solution.py:505
  56.0 1.4 %collective-permute-done.16.zb_ref = f32[8,128]{1,0:T(8,128)S(1)} collective-permute-done((f32[8,128]{1,0:T(8,128)S(1)}, f32[8,128]{1,0:T(8,128)S(1)}, u32[]{:S(2)}, u32[]{:S(2)}) %collective-permute-start.16) | collective-permute-done | bytes 4128 | tf_op jit(solution)/shard_map/ppermute | solution.py:454
  57.4 0.9 %shard_map.74 = f32[256,256]{1,0:T(8,128)} custom-call(f32[256,256]{1,0:T(8,128)S(1)} %get-tuple-element.38.sum_ref, f32[64,128]{1,0:T(8,128)S(1)} %get-tuple-element.39.tile_ref, f32[24,128]{1,0:T(8,128)S(1)} %collective-permute-done.15.za_ref, f32[8,128]{1,0:T(8,128)S(1)} %collective-permute-done.16.zb_ref, f32[8,16,256]{2,1,0:T(8,128)S(1)} %bitcast.15, ...), custom_call_target="tpu_custom_call" | custom-call | tf_op jit(solution)/shard_map/pallas_call | solution.py:508
  (33 shorter events, 0.7 us)
Async XLA Ops:
  1.8 4.9 %collective-permute-start.6 = (f32[16,128]{1,0:T(8,128)S(1)}, f32[16,128]{1,0:T(8,128)S(1)}, u32[]{:S(2)}, u32[]{:S(2)}) collective-permute-start(f32[16,128]{1,0:T(8,128)S(1)} %get-tuple-element.35), channel_id=1, source_target_pairs={{0,32},{16,48},{32,0},{48,16},{64,96},{80,112},{96,64},{112,80},{1... | collective-permute-start | bytes 24584 | tf_op jit(solution)/shard_map/ppermute | solution.py:449
  5.7 9.0 %collective-permute-start = (f32[32,128]{1,0:T(8,128)S(1)}, f32[32,128]{1,0:T(8,128)S(1)}, u32[]{:S(2)}, u32[]{:S(2)}) collective-permute-start(f32[32,128]{1,0:T(8,128)S(1)} %get-tuple-element.25), channel_id=1, source_target_pairs={{0,128},{128,0},{1,129},{129,1},{2,130},{130,2},{3,131},{131,3},{4... | collective-permute-start | bytes 49160 | tf_op jit(solution)/shard_map/ppermute | solution.py:449
  6.9 6.5 %collective-permute-start.7 = (f32[16,128]{1,0:T(8,128)S(1)}, f32[16,128]{1,0:T(8,128)S(1)}, u32[]{:S(2)}, u32[]{:S(2)}) collective-permute-start(f32[16,128]{1,0:T(8,128)S(1)} %select_add_fusion.3), channel_id=1, source_target_pairs={{0,96},{16,112},{32,64},{48,80},{64,32},{80,48},{96,0},{112,16},{1... | collective-permute-start | bytes 24584 | tf_op jit(solution)/shard_map/ppermute | solution.py:449
  13.4 12.7 %collective-permute-start.8 = (f32[16,128]{1,0:T(8,128)S(1)}, f32[16,128]{1,0:T(8,128)S(1)}, u32[]{:S(2)}, u32[]{:S(2)}) collective-permute-start(f32[16,128]{1,0:T(8,128)S(1)} %select_add_fusion.2), channel_id=1, source_target_pairs={{0,4},{1,5},{2,6},{3,7},{4,0},{5,1},{6,2},{7,3},{8,12},{9,13},{10,... | collective-permute-start | bytes 24584 | tf_op jit(solution)/shard_map/ppermute | solution.py:449
  14.9 4.7 %collective-permute-start.1 = (f32[8,128]{1,0:T(8,128)S(1)}, f32[8,128]{1,0:T(8,128)S(1)}, u32[]{:S(2)}, u32[]{:S(2)}) collective-permute-start(f32[8,128]{1,0:T(8,128)S(1)} %get-tuple-element.27), channel_id=1, source_target_pairs={{0,1},{1,0},{2,3},{3,2},{4,5},{5,4},{6,7},{7,6},{8,9},{9,8},{10,11... | collective-permute-start | bytes 12296 | tf_op jit(solution)/shard_map/ppermute | solution.py:449
  16.2 5.8 %collective-permute-start.2 = (f32[8,128]{1,0:T(8,128)S(1)}, f32[8,128]{1,0:T(8,128)S(1)}, u32[]{:S(2)}, u32[]{:S(2)}) collective-permute-start(f32[8,128]{1,0:T(8,128)S(1)} %get-tuple-element.28), channel_id=1, source_target_pairs={{0,15},{1,2},{2,1},{3,4},{4,3},{5,6},{6,5},{7,8},{8,7},{9,10},{10,... | collective-permute-start | bytes 12296 | tf_op jit(solution)/shard_map/ppermute | solution.py:454
  22.0 9.3 %copy-start.2 = (bf16[1,1,1,3,10,10,128]{6,3,5,4,2,1,0:T(4,128)(2,1)S(1)}, bf16[1,1,1,3,10,10,128]{6,3,5,4,2,1,0:T(4,128)(2,1)}, u32[]{:S(2)}) copy-start(bf16[1,1,1,3,10,10,128]{6,3,5,4,2,1,0:T(4,128)(2,1)} %param.7) | copy-start | bytes 230404
  22.2 9.1 %collective-permute-start.3 = (f32[56,128]{1,0:T(8,128)S(1)}, f32[56,128]{1,0:T(8,128)S(1)}, u32[]{:S(2)}, u32[]{:S(2)}) collective-permute-start(f32[56,128]{1,0:T(8,128)S(1)} %get-tuple-element.29), channel_id=1, source_target_pairs={{0,16},{16,0},{32,48},{48,32},{64,80},{80,64},{96,112},{112,96},{1... | collective-permute-start | bytes 86024 | tf_op jit(solution)/shard_map/ppermute | solution.py:449
  23.0 8.3 %collective-permute-start.4 = (f32[56,128]{1,0:T(8,128)S(1)}, f32[56,128]{1,0:T(8,128)S(1)}, u32[]{:S(2)}, u32[]{:S(2)}) collective-permute-start(f32[56,128]{1,0:T(8,128)S(1)} %get-tuple-element.30), channel_id=1, source_target_pairs={{0,112},{16,32},{32,16},{48,64},{64,48},{80,96},{96,80},{112,0},{1... | collective-permute-start | bytes 86024 | tf_op jit(solution)/shard_map/ppermute | solution.py:454
  26.2 15.4 %collective-permute-start.10 = (f32[16,128]{1,0:T(8,128)S(1)}, f32[16,128]{1,0:T(8,128)S(1)}, u32[]{:S(2)}, u32[]{:S(2)}) collective-permute-start(f32[16,128]{1,0:T(8,128)S(1)} %select_add_fusion.1), channel_id=1, source_target_pairs={{0,12},{1,13},{2,14},{3,15},{4,8},{5,9},{6,10},{7,11},{8,4},{9,5},... | collective-permute-start | bytes 24584 | tf_op jit(solution)/shard_map/ppermute | solution.py:449
  26.9 14.7 %collective-permute-start.11 = (f32[16,128]{1,0:T(8,128)S(1)}, f32[16,128]{1,0:T(8,128)S(1)}, u32[]{:S(2)}, u32[]{:S(2)}) collective-permute-start(f32[16,128]{1,0:T(8,128)S(1)} %select_add_fusion.1), channel_id=1, source_target_pairs={{0,15},{1,14},{2,13},{3,12},{4,11},{5,10},{6,9},{7,8},{8,7},{9,6},... | collective-permute-start | bytes 24584 | tf_op jit(solution)/shard_map/ppermute | solution.py:449
  29.7 11.9 %collective-permute-start.9 = (f32[16,128]{1,0:T(8,128)S(1)}, f32[16,128]{1,0:T(8,128)S(1)}, u32[]{:S(2)}, u32[]{:S(2)}) collective-permute-start(f32[16,128]{1,0:T(8,128)S(1)} %select_add_fusion.1), channel_id=1, source_target_pairs={{0,3},{1,2},{2,1},{3,0},{4,7},{5,6},{6,5},{7,4},{8,11},{9,10},{10,... | collective-permute-start | bytes 24584 | tf_op jit(solution)/shard_map/ppermute | solution.py:449
  31.3 1.5 %copy-start.3 = (f32[1,1,1,3,10,128]{5,2,4,3,1,0:T(1,128)S(1)}, f32[1,1,1,3,10,128]{5,2,4,3,1,0:T(1,128)}, u32[]{:S(2)}) copy-start(f32[1,1,1,3,10,128]{5,2,4,3,1,0:T(1,128)} %param.8) | copy-start | bytes 46084
  35.5 7.0 %collective-permute-start.5 = (f32[56,128]{1,0:T(8,128)S(1)}, f32[56,128]{1,0:T(8,128)S(1)}, u32[]{:S(2)}, u32[]{:S(2)}) collective-permute-start(f32[56,128]{1,0:T(8,128)S(1)} %get-tuple-element.34), channel_id=1, source_target_pairs={{0,128},{128,0},{1,129},{129,1},{2,130},{130,2},{3,131},{131,3},{4... | collective-permute-start | bytes 86024 | tf_op jit(solution)/shard_map/ppermute | solution.py:449
  42.6 2.9 %collective-permute-start.12 = (f32[80,128]{1,0:T(8,128)S(1)}, f32[80,128]{1,0:T(8,128)S(1)}, u32[]{:S(2)}, u32[]{:S(2)}) collective-permute-start(f32[80,128]{1,0:T(8,128)S(1)} %get-tuple-element.36), channel_id=1, source_target_pairs={{0,16},{16,0},{32,48},{48,32},{64,80},{80,64},{96,112},{112,96},{1... | collective-permute-start | bytes 122888 | tf_op jit(solution)/shard_map/ppermute | solution.py:449
  45.6 2.4 %collective-permute-start.14 = (f32[16,128]{1,0:T(8,128)S(1)}, f32[16,128]{1,0:T(8,128)S(1)}, u32[]{:S(2)}, u32[]{:S(2)}) collective-permute-start(f32[16,128]{1,0:T(8,128)S(1)} %fusion.2), channel_id=1, source_target_pairs={{0,128},{128,0},{1,129},{129,1},{2,130},{130,2},{3,131},{131,3},{4... | collective-permute-start | bytes 24584 | tf_op jit(solution)/shard_map/ppermute | solution.py:449
  47.1 4.0 %collective-permute-start.13 = (f32[64,128]{1,0:T(8,128)S(1)}, f32[64,128]{1,0:T(8,128)S(1)}, u32[]{:S(2)}, u32[]{:S(2)}) collective-permute-start(f32[64,128]{1,0:T(8,128)S(1)} %get-tuple-element.37), channel_id=1, source_target_pairs={{0,112},{16,32},{32,16},{48,64},{64,48},{80,96},{96,80},{112,0},{1... | collective-permute-start | bytes 98312 | tf_op jit(solution)/shard_map/ppermute | solution.py:454
  51.1 3.9 %copy-start.1 = (f32[8,8,8]{2,1,0:T(8,128)S(1)}, f32[8,8,8]{2,1,0:T(8,128)}, u32[]{:S(2)}) copy-start(f32[8,8,8]{2,1,0:T(8,128)} %basis_ref.3) | copy-start | bytes 6148
  51.4 6.0 %collective-permute-start.15 = (f32[24,128]{1,0:T(8,128)S(1)}, f32[24,128]{1,0:T(8,128)S(1)}, u32[]{:S(2)}, u32[]{:S(2)}) collective-permute-start(f32[24,128]{1,0:T(8,128)S(1)} %get-tuple-element.40), channel_id=1, source_target_pairs={{0,1},{1,0},{2,3},{3,2},{4,5},{5,4},{6,7},{7,6},{8,9},{9,8},{10,11... | collective-permute-start | bytes 36872 | tf_op jit(solution)/shard_map/ppermute | solution.py:449
  51.5 5.9 %copy-start = (f32[1,1,1,8,16,256]{5,4,3,2,1,0:T(8,128)S(1)}, f32[1,1,1,8,16,256]{5,4,3,2,1,0:T(8,128)}, u32[]{:S(2)}) copy-start(f32[1,1,1,8,16,256]{5,4,3,2,1,0:T(8,128)} %param.11) | copy-start | bytes 393220
  51.5 5.9 %collective-permute-start.16 = (f32[8,128]{1,0:T(8,128)S(1)}, f32[8,128]{1,0:T(8,128)S(1)}, u32[]{:S(2)}, u32[]{:S(2)}) collective-permute-start(f32[8,128]{1,0:T(8,128)S(1)} %get-tuple-element.41), channel_id=1, source_target_pairs={{0,15},{1,2},{2,1},{3,4},{4,3},{5,6},{6,5},{7,8},{8,7},{9,10},{10,... | collective-permute-start | bytes 12296 | tf_op jit(solution)/shard_map/ppermute | solution.py:454

commit v7 on v5

--- a/solution.py
+++ b/solution.py
@@ -192,47 +192,77 @@
     lax.fori_loop(0, 10, step, 0)
 
 
-def modes_kernel(
-    core_ref, core2_ref, ends_ref, ends2_ref, za_ref, zb_ref, ya_ref, yb_ref, s, u, block, jl, jh, scr
-):
+def y_factors(s):
+    return [[s[pl.ds((j * 10 + 8 * h) * 8 + 1, 8, stride=8), :] for j in range(10)] for h in range(2)]
+
+
+def front_kernel(core_ref, ends_ref, za_ref, zb_ref, s, u, edge_ref, block):
     lane, _ = iotas()
-    low_q = (lane & 32) == 0
     first, last = z_halo(core_ref, ends_ref, za_ref, zb_ref, lane & 31)
-    low, high, low_ends, high_ends = y_rows(first, last, core2_ref, ends2_ref, scr)
     for i in range(10):
         block[pl.ds(i * 80, 8), :] = first[i]
         block[pl.ds(i * 80 + 72, 8), :] = last[i]
         for k in range(8):
             block[pl.ds(i * 80 + 8 + k * 8, 8), :] = plane(core_ref, ends_ref, i, k)
     for i in range(10):
+        edge_ref[i * 16 : i * 16 + 16] = roll(block[pl.ds(i * 80 + 7, 16, stride=8), :], 32)
+        edge_ref[160 + i * 16 : 176 + i * 16] = roll(block[pl.ds(i * 80, 16, stride=8), :], 96)
+    factor = factor_of(s)
+    front = y_factors(s)
+
+    def along(k, _):
+        held = [block[pl.ds(i * 80 + k * 8, 8), :] for i in range(10)]
+        for a in range(10):
+            block[pl.ds(a * 80 + k * 8, 8), :] = chain((factor(0, i, a), held[i]) for i in range(10))
+        return 0
+
+    lax.fori_loop(0, 10, along, 0)
+
+    def own_rows(a, _):
+        for k in range(10):
+            at = (a * 10 + k) * 8
+            rows = [row(block, at + j) for j in range(8)]
+            for h in range(2):
+                u[pl.ds(at * 2 + 8 * h, 8), :] = chain((front[h][j + 1], rows[j]) for j in range(8))
+        return 0
+
+    lax.fori_loop(0, 10, own_rows, 0)
+
+
+def modes_kernel(u_ref, edge_ref, ya_ref, yb_ref, s, u, rows):
+    low_q = (iotas(16)[0] & 32) == 0
+    ends_above, ends_below = sides(ya_ref[40:56], yb_ref[40:56], "gy")
+    for i in range(10):
         at = (i % 5) * 8
         above, below = sides(ya_ref[at : at + 8], yb_ref[at : at + 8], "gy")
         if i < 5:
             above, below = roll(above, 32), roll(below, 96)
-        jl[pl.ds(i * 8, 8), :] = jnp.where(low_q, below, roll(high[i], 32))
-        jh[pl.ds(i * 8, 8), :] = jnp.where(low_q, roll(low[i], 96), above)
-    low_q16 = (iotas(16)[0] & 32) == 0
-    above, below = sides(ya_ref[40:56], yb_ref[40:56], "gy")
-    jl[80:96] = jnp.where(low_q16, roll(below, 96), roll(high_ends[0], 32))
-    jl[96:112] = jnp.where(low_q16, below, roll(high_ends[1], 32))
-    jh[80:96] = jnp.where(low_q16, roll(low_ends[0], 96), roll(above, 32))
-    jh[96:112] = jnp.where(low_q16, roll(low_ends[1], 96), above)
-    factor = factor_of(s)
-    front = [[s[pl.ds((j * 10 + 8 * h) * 8 + 1, 8, stride=8), :] for j in range(10)] for h in range(2)]
-
-    def fwd_y(i, _):
+        for base, middle, zero, nine in (
+            (0, below, roll(ends_below, 96), ends_below),
+            (160, above, roll(ends_above, 32), ends_above),
+        ):
+            rows[base + i * 16 + 1 : base + i * 16 + 9] = middle
+            rows[base + i * 16 : base + i * 16 + 1] = zero[i : i + 1]
+            rows[base + i * 16 + 9 : base + i * 16 + 10] = nine[i : i + 1]
+    low = [jnp.where(low_q, rows[i * 16 : i * 16 + 16], edge_ref[i * 16 : i * 16 + 16]) for i in range(10)]
+    high = [
+        jnp.where(low_q, edge_ref[160 + i * 16 : 176 + i * 16], rows[160 + i * 16 : 176 + i * 16]) for i in range(10)
+    ]
+    front = y_factors(s)
+    for a in range(10):
+        weights = [row(s, (i * 10 + a) * 8, 16) for i in range(10)]
+        rows[320 + a * 16 : 336 + a * 16] = chain((weights[i], low[i]) for i in range(10))
+        rows[480 + a * 16 : 496 + a * 16] = chain((weights[i], high[i]) for i in range(10))
+
+    def add_edges(a, _):
         for k in range(10):
-            edge = i * 8 + k - 1 if 1 <= k <= 8 else (80 + i if k == 0 else 96 + i)
-            at = (i * 10 + k) * 8
-            rows = [row(jl, edge)] + [row(block, at + j) for j in range(8)] + [row(jh, edge)]
+            before, after = row(rows, 320 + a * 16 + k), row(rows, 480 + a * 16 + k)
             for h in range(2):
-                out = chain((front[h][j], rows[j]) for j in range(10))
-                u[pl.ds((i * 10 + k) * 16 + 8 * h, 8), :] = out
+                at = (a * 10 + k) * 16 + 8 * h
+                u[pl.ds(at, 8), :] = u_ref[pl.ds(at, 8), :] + (front[h][0] * before + front[h][9] * after)
         return 0
 
-    lax.fori_loop(0, 10, fwd_y, 0)
-
-    along_x(u, u, factor, False)
+    lax.fori_loop(0, 10, add_edges, 0)
 
 
 def middle_kernel(u_ref, s, eig_ref, u, eg):
@@ -484,9 +514,8 @@
     ya, yb = call(yface_kernel, [(56, 128), (56, 128)], [(256, 128)], 6)(*block)
     ya, yb = swap(ya, "gy", 1), swap_odd(yb, "gy")
     running = climb(running, "gz", 4, 2)
-    (modes,) = call(
-        modes_kernel, [(1696, 128)], [(800, 128), (112, 128), (112, 128), (256, 128)], 9
-    )(*block, ya, yb, factors)
+    modes, edges = call(front_kernel, [(1696, 128), (320, 128)], [(848, 128)], 5)(core, ends, *block[4:], factors)
+    (modes,) = call(modes_kernel, [(1696, 128)], [(640, 128)], 5)(modes, edges, ya, yb, factors)
     running = climb(running, "gz", 12, 3)
     (modes,) = call(middle_kernel, [(1696, 128)], [(16, 128)], 3)(modes, factors, eigen)
     running = climb(running, "gz", 3, 1)

time: 54.8 us -> 53.7 us (0.980)
  the two profiles are of different devices: /device:TPU:1 before, /device:TPU:24 now
where the time goes in v7:
time: 53.7 us; the launch traced here: 53.6 us
  starting transfers between devices  26.2 us (49%)
  waiting for transfers between devices  17.8 us (33%)
  Pallas kernels  8.52 us (16%)
  other arithmetic  0.56 us (1%)
    ppermute x12, starting transfers between devices, swap(): lax.ppermute(value, axis, [(i, i ^ distance) for i in range(lax.axis_size...  18.3 us
    ppermute x4, waiting for transfers between devices, swap_odd(): lax.ppermute(value, axis, [(i, (i + 1 if i % 2 else i - 1) % count) for i...  8.96 us
    ppermute x12, waiting for transfers between devices, swap(): lax.ppermute(value, axis, [(i, i ^ distance) for i in range(lax.axis_size...  8.84 us
    ppermute x4, starting transfers between devices, swap_odd(): lax.ppermute(value, axis, [(i, (i + 1 if i % 2 else i - 1) % count) for i...  7.87 us
    pallas_call x1, Pallas kernels, work(): call(pre_kernel, [(8, 8, 8, 128), (32, 128), (16, 128), (16, 128)], [(2,...  1.84 us
    pallas_call x1, Pallas kernels, work(): call(points_kernel, [(10, 10, 8, 128), (10, 16, 128), (10, 16, 128), (56,...  1.38 us
    pallas_call x1, Pallas kernels, work(): call(middle_kernel, [(1696, 128)], [(16, 128)], 3)(modes, factors, eigen)  1.19 us
  transfers between devices with their start and end apart: 16, of which 8 were waited for; matrix products, arithmetic and copies ran while one was open for 1% of the time, Pallas kernels for 10%

profile of v7, /device:TPU:24, one launch (start us, length us, event | category | flops | bytes accessed | tf_op | source)
XLA Modules:
  0.0 53.6 jit_solution(12355568776904622491)
XLA Ops:
  0.0 1.8 %shard_map.64 = (f32[8,8,8,128]{3,2,1,0:T(8,128)S(1)}, f32[32,128]{1,0:T(8,128)S(1)}, f32[16,128]{1,0:T(8,128)S(1)}, f32[16,128]{1,0:T(8,128)S(1)}) custom-call(f32[256,256]{1,0:T(8,128)} %bitcast.16, f32[8,16,256]{2,1,0:T(8,128)} %bitcast.12, f32[8,8,8]{2,1,0:T(8,128)} %basis_ref.3, f32[16,16]{1,0:T(8,128)} %bitcast.17), custom_call_target="tpu_custom_call" | custom-call | tf_op jit(solution)/shard_map/pallas_call | solution.py:499
  1.8 3.4 %collective-permute-start.6 = (f32[16,128]{1,0:T(8,128)S(1)}, f32[16,128]{1,0:T(8,128)S(1)}, u32[]{:S(2)}, u32[]{:S(2)}) collective-permute-start(f32[16,128]{1,0:T(8,128)S(1)} %get-tuple-element.39), channel_id=1, source_target_pairs={{0,32},{16,48},{32,0},{48,16},{64,96},{80,112},{96,64},{112,80},{1... | collective-permute-start | bytes 24584 | tf_op jit(solution)/shard_map/ppermute | solution.py:479
  5.2 1.6 %collective-permute-done.6 = f32[16,128]{1,0:T(8,128)S(1)} collective-permute-done((f32[16,128]{1,0:T(8,128)S(1)}, f32[16,128]{1,0:T(8,128)S(1)}, u32[]{:S(2)}, u32[]{:S(2)}) %collective-permute-start.6) | collective-permute-done | bytes 8224 | tf_op jit(solution)/shard_map/ppermute | solution.py:479
  6.9 6.0 %collective-permute-start.7 = (f32[16,128]{1,0:T(8,128)S(1)}, f32[16,128]{1,0:T(8,128)S(1)}, u32[]{:S(2)}, u32[]{:S(2)}) collective-permute-start(f32[16,128]{1,0:T(8,128)S(1)} %select_add_fusion.5), channel_id=1, source_target_pairs={{0,96},{16,112},{32,64},{48,80},{64,32},{80,48},{96,0},{112,16},{1... | collective-permute-start | bytes 24584 | tf_op jit(solution)/shard_map/ppermute | solution.py:479
  12.9 1.6 %collective-permute-done.7 = f32[16,128]{1,0:T(8,128)S(1)} collective-permute-done((f32[16,128]{1,0:T(8,128)S(1)}, f32[16,128]{1,0:T(8,128)S(1)}, u32[]{:S(2)}, u32[]{:S(2)}) %collective-permute-start.7) | collective-permute-done | bytes 8224 | tf_op jit(solution)/shard_map/ppermute | solution.py:479
  14.6 0.8 %collective-permute-start.8 = (f32[16,128]{1,0:T(8,128)S(1)}, f32[16,128]{1,0:T(8,128)S(1)}, u32[]{:S(2)}, u32[]{:S(2)}) collective-permute-start(f32[16,128]{1,0:T(8,128)S(1)} %select_add_fusion.4), channel_id=1, source_target_pairs={{0,4},{1,5},{2,6},{3,7},{4,0},{5,1},{6,2},{7,3},{8,12},{9,13},{10,... | collective-permute-start | bytes 24584 | tf_op jit(solution)/shard_map/ppermute | solution.py:479
  15.4 0.2 shard_map.65
  15.6 1.6 %collective-permute-start.1 = (f32[8,128]{1,0:T(8,128)S(1)}, f32[8,128]{1,0:T(8,128)S(1)}, u32[]{:S(2)}, u32[]{:S(2)}) collective-permute-start(f32[8,128]{1,0:T(8,128)S(1)} %get-tuple-element.29), channel_id=1, source_target_pairs={{0,1},{1,0},{2,3},{3,2},{4,5},{5,4},{6,7},{7,6},{8,9},{9,8},{10,11... | collective-permute-start | bytes 12296 | tf_op jit(solution)/shard_map/ppermute | solution.py:479
  17.2 2.8 %collective-permute-start.2 = (f32[8,128]{1,0:T(8,128)S(1)}, f32[8,128]{1,0:T(8,128)S(1)}, u32[]{:S(2)}, u32[]{:S(2)}) collective-permute-start(f32[8,128]{1,0:T(8,128)S(1)} %get-tuple-element.30), channel_id=1, source_target_pairs={{0,15},{1,2},{2,1},{3,4},{4,3},{5,6},{6,5},{7,8},{8,7},{9,10},{10,... | collective-permute-start | bytes 12296 | tf_op jit(solution)/shard_map/ppermute | solution.py:484
  20.1 2.0 %collective-permute-start.9 = (f32[16,128]{1,0:T(8,128)S(1)}, f32[16,128]{1,0:T(8,128)S(1)}, u32[]{:S(2)}, u32[]{:S(2)}) collective-permute-start(f32[16,128]{1,0:T(8,128)S(1)} %select_add_fusion.3), channel_id=1, source_target_pairs={{0,12},{1,13},{2,14},{3,15},{4,8},{5,9},{6,10},{7,11},{8,4},{9,5},... | collective-permute-start | bytes 24584 | tf_op jit(solution)/shard_map/ppermute | solution.py:479
  22.0 0.8 %collective-permute-done.2.zb_ref = f32[8,128]{1,0:T(8,128)S(1)} collective-permute-done((f32[8,128]{1,0:T(8,128)S(1)}, f32[8,128]{1,0:T(8,128)S(1)}, u32[]{:S(2)}, u32[]{:S(2)}) %collective-permute-start.2) | collective-permute-done | bytes 4128 | tf_op jit(solution)/shard_map/ppermute | solution.py:484
  22.9 0.2 shard_map.68
  23.1 1.1 %collective-permute-start.3 = (f32[56,128]{1,0:T(8,128)S(1)}, f32[56,128]{1,0:T(8,128)S(1)}, u32[]{:S(2)}, u32[]{:S(2)}) collective-permute-start(f32[56,128]{1,0:T(8,128)S(1)} %get-tuple-element.33), channel_id=1, source_target_pairs={{0,16},{16,0},{32,48},{48,32},{64,80},{80,64},{96,112},{112,96},{1... | collective-permute-start | bytes 86024 | tf_op jit(solution)/shard_map/ppermute | solution.py:479
  24.1 3.7 %collective-permute-start.4 = (f32[56,128]{1,0:T(8,128)S(1)}, f32[56,128]{1,0:T(8,128)S(1)}, u32[]{:S(2)}, u32[]{:S(2)}) collective-permute-start(f32[56,128]{1,0:T(8,128)S(1)} %get-tuple-element.34), channel_id=1, source_target_pairs={{0,112},{16,32},{32,16},{48,64},{64,48},{80,96},{96,80},{112,0},{1... | collective-permute-start | bytes 86024 | tf_op jit(solution)/shard_map/ppermute | solution.py:484
  27.9 3.3 %collective-permute-start.10 = (f32[16,128]{1,0:T(8,128)S(1)}, f32[16,128]{1,0:T(8,128)S(1)}, u32[]{:S(2)}, u32[]{:S(2)}) collective-permute-start(f32[16,128]{1,0:T(8,128)S(1)} %select_add_fusion.2), channel_id=1, source_target_pairs={{0,3},{1,2},{2,1},{3,0},{4,7},{5,6},{6,5},{7,4},{8,11},{9,10},{10,... | collective-permute-start | bytes 24584 | tf_op jit(solution)/shard_map/ppermute | solution.py:479
  31.3 1.1 %shard_map.67 = (f32[1696,128]{1,0:T(8,128)S(1)}, f32[320,128]{1,0:T(8,128)S(1)}) custom-call(f32[8,8,8,128]{3,2,1,0:T(8,128)S(1)} %get-tuple-element.26.core_ref, f32[2,8,8,128]{3,2,1,0:T(8,128)S(1)} %get-tuple-element.28.ends_ref, f32[8,128]{1,0:T(8,128)S(1)} %collective-permute-done.1.za_ref, f32[8,128]{1,0:T(8,128)S(1)} %collective-permute-done.2.zb_ref, ...), custom_call_target="tpu_custom_call" | custom-call | tf_op jit(solution)/shard_map/pallas_call | solution.py:517
  32.3 0.4 shard_map.69.u_ref
  32.7 0.3 copy-done.3
  33.1 1.2 %shard_map.70.u_ref = f32[1696,128]{1,0:T(8,128)S(1)} custom-call(f32[1696,128]{1,0:T(8,128)S(1)} %shard_map.69.u_ref, f32[848,128]{1,0:T(8,128)S(1)} %shard_map.66.s, f32[3,10,1,128]{3,2,1,0:T(1,128)S(1)} %bitcast.15), custom_call_target="tpu_custom_call" | custom-call | tf_op jit(solution)/shard_map/pallas_call | solution.py:520
  34.2 1.4 %shard_map.71 = (f32[10,10,8,128]{3,2,1,0:T(8,128)S(1)}, f32[10,16,128]{2,1,0:T(8,128)S(1)}, f32[10,16,128]{2,1,0:T(8,128)S(1)}, f32[56,128]{1,0:T(8,128)S(1)}) custom-call(f32[1696,128]{1,0:T(8,128)S(1)} %shard_map.70.u_ref, f32[848,128]{1,0:T(8,128)S(1)} %shard_map.66.s), custom_call_target="tpu_custom_call" | custom-call | tf_op jit(solution)/shard_map/pallas_call | solution.py:522
  35.8 1.1 %collective-permute-done.5.xr_ref = f32[56,128]{1,0:T(8,128)S(1)} collective-permute-done((f32[56,128]{1,0:T(8,128)S(1)}, f32[56,128]{1,0:T(8,128)S(1)}, u32[]{:S(2)}, u32[]{:S(2)}) %collective-permute-start.5) | collective-permute-done | bytes 28704 | tf_op jit(solution)/shard_map/ppermute | solution.py:479
  36.9 0.1 shard_map.72
  37.1 4.0 %collective-permute-done.11.ya_ref = f32[80,128]{1,0:T(8,128)S(1)} collective-permute-done((f32[80,128]{1,0:T(8,128)S(1)}, f32[80,128]{1,0:T(8,128)S(1)}, u32[]{:S(2)}, u32[]{:S(2)}) %collective-permute-start.11) | collective-permute-done | bytes 40992 | tf_op jit(solution)/shard_map/ppermute | solution.py:479
  41.2 0.6 %collective-permute-start.12 = (f32[64,128]{1,0:T(8,128)S(1)}, f32[64,128]{1,0:T(8,128)S(1)}, u32[]{:S(2)}, u32[]{:S(2)}) collective-permute-start(f32[64,128]{1,0:T(8,128)S(1)} %get-tuple-element.41), channel_id=1, source_target_pairs={{0,112},{16,32},{32,16},{48,64},{64,48},{80,96},{96,80},{112,0},{1... | collective-permute-start | bytes 98312 | tf_op jit(solution)/shard_map/ppermute | solution.py:484
  41.9 0.5 collective-permute-done.13
  42.4 4.0 %collective-permute-done.12.yb_ref = f32[64,128]{1,0:T(8,128)S(1)} collective-permute-done((f32[64,128]{1,0:T(8,128)S(1)}, f32[64,128]{1,0:T(8,128)S(1)}, u32[]{:S(2)}, u32[]{:S(2)}) %collective-permute-start.12) | collective-permute-done | bytes 32800 | tf_op jit(solution)/shard_map/ppermute | solution.py:484
  46.4 0.3 shard_map.74
  46.7 0.1 collective-permute-start.14
  46.8 0.7 %collective-permute-start.15 = (f32[8,128]{1,0:T(8,128)S(1)}, f32[8,128]{1,0:T(8,128)S(1)}, u32[]{:S(2)}, u32[]{:S(2)}) collective-permute-start(f32[8,128]{1,0:T(8,128)S(1)} %get-tuple-element.45), channel_id=1, source_target_pairs={{0,15},{1,2},{2,1},{3,4},{4,3},{5,6},{6,5},{7,8},{8,7},{9,10},{10,... | collective-permute-start | bytes 12296 | tf_op jit(solution)/shard_map/ppermute | solution.py:484
  47.6 0.9 %shard_map.73 = (f32[256,256]{1,0:T(8,128)S(1)}, f32[64,128]{1,0:T(8,128)S(1)}) custom-call(f32[10,10,8,128]{3,2,1,0:T(8,128)S(1)} %get-tuple-element.35.l_ref, f32[10,16,128]{2,1,0:T(8,128)S(1)} %get-tuple-element.36.hl_ref, f32[10,16,128]{2,1,0:T(8,128)S(1)} %get-tuple-element.37.hh_ref, f32[56,128]{1,0:T(8,128)S(1)} %collective-permute-done.5.xr_ref, ...), custom_call_target="tpu_custom_call" | custom-call | tf_op jit(solution)/shard_map/pallas_call | solution.py:533
  48.5 4.1 %collective-permute-done.15.zb_ref = f32[8,128]{1,0:T(8,128)S(1)} collective-permute-done((f32[8,128]{1,0:T(8,128)S(1)}, f32[8,128]{1,0:T(8,128)S(1)}, u32[]{:S(2)}, u32[]{:S(2)}) %collective-permute-start.15) | collective-permute-done | bytes 4128 | tf_op jit(solution)/shard_map/ppermute | solution.py:484
  52.6 0.9 %shard_map.75 = f32[256,256]{1,0:T(8,128)} custom-call(f32[256,256]{1,0:T(8,128)S(1)} %get-tuple-element.42.sum_ref, f32[64,128]{1,0:T(8,128)S(1)} %get-tuple-element.43.tile_ref, f32[24,128]{1,0:T(8,128)S(1)} %collective-permute-done.14.za_ref, f32[8,128]{1,0:T(8,128)S(1)} %collective-permute-done.15.zb_ref, f32[8,16,256]{2,1,0:T(8,128)S(1)} %bitcast.13, ...), custom_call_target="tpu_custom_call" | custom-call | tf_op jit(solution)/shard_map/pallas_call | solution.py:536
  (34 shorter events, 0.8 us)
Async XLA Ops:
  1.8 5.0 %collective-permute-start.6 = (f32[16,128]{1,0:T(8,128)S(1)}, f32[16,128]{1,0:T(8,128)S(1)}, u32[]{:S(2)}, u32[]{:S(2)}) collective-permute-start(f32[16,128]{1,0:T(8,128)S(1)} %get-tuple-element.39), channel_id=1, source_target_pairs={{0,32},{16,48},{32,0},{48,16},{64,96},{80,112},{96,64},{112,80},{1... | collective-permute-start | bytes 24584 | tf_op jit(solution)/shard_map/ppermute | solution.py:479
  5.2 10.2 %collective-permute-start = (f32[32,128]{1,0:T(8,128)S(1)}, f32[32,128]{1,0:T(8,128)S(1)}, u32[]{:S(2)}, u32[]{:S(2)}) collective-permute-start(f32[32,128]{1,0:T(8,128)S(1)} %get-tuple-element.27), channel_id=1, source_target_pairs={{0,128},{128,0},{1,129},{129,1},{2,130},{130,2},{3,131},{131,3},{4... | collective-permute-start | bytes 49160 | tf_op jit(solution)/shard_map/ppermute | solution.py:479
  6.9 7.6 %collective-permute-start.7 = (f32[16,128]{1,0:T(8,128)S(1)}, f32[16,128]{1,0:T(8,128)S(1)}, u32[]{:S(2)}, u32[]{:S(2)}) collective-permute-start(f32[16,128]{1,0:T(8,128)S(1)} %select_add_fusion.5), channel_id=1, source_target_pairs={{0,96},{16,112},{32,64},{48,80},{64,32},{80,48},{96,0},{112,16},{1... | collective-permute-start | bytes 24584 | tf_op jit(solution)/shard_map/ppermute | solution.py:479
  14.6 5.4 %collective-permute-start.8 = (f32[16,128]{1,0:T(8,128)S(1)}, f32[16,128]{1,0:T(8,128)S(1)}, u32[]{:S(2)}, u32[]{:S(2)}) collective-permute-start(f32[16,128]{1,0:T(8,128)S(1)} %select_add_fusion.4), channel_id=1, source_target_pairs={{0,4},{1,5},{2,6},{3,7},{4,0},{5,1},{6,2},{7,3},{8,12},{9,13},{10,... | collective-permute-start | bytes 24584 | tf_op jit(solution)/shard_map/ppermute | solution.py:479
  15.6 6.5 %collective-permute-start.1 = (f32[8,128]{1,0:T(8,128)S(1)}, f32[8,128]{1,0:T(8,128)S(1)}, u32[]{:S(2)}, u32[]{:S(2)}) collective-permute-start(f32[8,128]{1,0:T(8,128)S(1)} %get-tuple-element.29), channel_id=1, source_target_pairs={{0,1},{1,0},{2,3},{3,2},{4,5},{5,4},{6,7},{7,6},{8,9},{9,8},{10,11... | collective-permute-start | bytes 12296 | tf_op jit(solution)/shard_map/ppermute | solution.py:479
  17.2 5.7 %collective-permute-start.2 = (f32[8,128]{1,0:T(8,128)S(1)}, f32[8,128]{1,0:T(8,128)S(1)}, u32[]{:S(2)}, u32[]{:S(2)}) collective-permute-start(f32[8,128]{1,0:T(8,128)S(1)} %get-tuple-element.30), channel_id=1, source_target_pairs={{0,15},{1,2},{2,1},{3,4},{4,3},{5,6},{6,5},{7,8},{8,7},{9,10},{10,... | collective-permute-start | bytes 12296 | tf_op jit(solution)/shard_map/ppermute | solution.py:484
  20.1 7.8 %collective-permute-start.9 = (f32[16,128]{1,0:T(8,128)S(1)}, f32[16,128]{1,0:T(8,128)S(1)}, u32[]{:S(2)}, u32[]{:S(2)}) collective-permute-start(f32[16,128]{1,0:T(8,128)S(1)} %select_add_fusion.3), channel_id=1, source_target_pairs={{0,12},{1,13},{2,14},{3,15},{4,8},{5,9},{6,10},{7,11},{8,4},{9,5},... | collective-permute-start | bytes 24584 | tf_op jit(solution)/shard_map/ppermute | solution.py:479
  22.9 8.4 %copy-start.2 = (bf16[1,1,1,3,10,10,128]{6,3,5,4,2,1,0:T(4,128)(2,1)S(1)}, bf16[1,1,1,3,10,10,128]{6,3,5,4,2,1,0:T(4,128)(2,1)}, u32[]{:S(2)}) copy-start(bf16[1,1,1,3,10,10,128]{6,3,5,4,2,1,0:T(4,128)(2,1)} %param.7) | copy-start | bytes 230404
  23.1 9.3 %collective-permute-start.3 = (f32[56,128]{1,0:T(8,128)S(1)}, f32[56,128]{1,0:T(8,128)S(1)}, u32[]{:S(2)}, u32[]{:S(2)}) collective-permute-start(f32[56,128]{1,0:T(8,128)S(1)} %get-tuple-element.33), channel_id=1, source_target_pairs={{0,16},{16,0},{32,48},{48,32},{64,80},{80,64},{96,112},{112,96},{1... | collective-permute-start | bytes 86024 | tf_op jit(solution)/shard_map/ppermute | solution.py:479
  24.1 8.2 %collective-permute-start.4 = (f32[56,128]{1,0:T(8,128)S(1)}, f32[56,128]{1,0:T(8,128)S(1)}, u32[]{:S(2)}, u32[]{:S(2)}) collective-permute-start(f32[56,128]{1,0:T(8,128)S(1)} %get-tuple-element.34), channel_id=1, source_target_pairs={{0,112},{16,32},{32,16},{48,64},{64,48},{80,96},{96,80},{112,0},{1... | collective-permute-start | bytes 86024 | tf_op jit(solution)/shard_map/ppermute | solution.py:484
  27.9 7.8 %collective-permute-start.10 = (f32[16,128]{1,0:T(8,128)S(1)}, f32[16,128]{1,0:T(8,128)S(1)}, u32[]{:S(2)}, u32[]{:S(2)}) collective-permute-start(f32[16,128]{1,0:T(8,128)S(1)} %select_add_fusion.2), channel_id=1, source_target_pairs={{0,3},{1,2},{2,1},{3,0},{4,7},{5,6},{6,5},{7,4},{8,11},{9,10},{10,... | collective-permute-start | bytes 24584 | tf_op jit(solution)/shard_map/ppermute | solution.py:479
  32.3 0.7 %copy-start.3 = (f32[1,1,1,3,10,128]{5,2,4,3,1,0:T(1,128)S(1)}, f32[1,1,1,3,10,128]{5,2,4,3,1,0:T(1,128)}, u32[]{:S(2)}) copy-start(f32[1,1,1,3,10,128]{5,2,4,3,1,0:T(1,128)} %param.8) | copy-start | bytes 46084
  35.6 1.2 %collective-permute-start.5 = (f32[56,128]{1,0:T(8,128)S(1)}, f32[56,128]{1,0:T(8,128)S(1)}, u32[]{:S(2)}, u32[]{:S(2)}) collective-permute-start(f32[56,128]{1,0:T(8,128)S(1)} %get-tuple-element.38), channel_id=1, source_target_pairs={{0,128},{128,0},{1,129},{129,1},{2,130},{130,2},{3,131},{131,3},{4... | collective-permute-start | bytes 86024 | tf_op jit(solution)/shard_map/ppermute | solution.py:479
  37.0 4.1 %collective-permute-start.11 = (f32[80,128]{1,0:T(8,128)S(1)}, f32[80,128]{1,0:T(8,128)S(1)}, u32[]{:S(2)}, u32[]{:S(2)}) collective-permute-start(f32[80,128]{1,0:T(8,128)S(1)} %get-tuple-element.40), channel_id=1, source_target_pairs={{0,16},{16,0},{32,48},{48,32},{64,80},{80,64},{96,112},{112,96},{1... | collective-permute-start | bytes 122888 | tf_op jit(solution)/shard_map/ppermute | solution.py:479
  41.2 1.2 %collective-permute-start.13 = (f32[16,128]{1,0:T(8,128)S(1)}, f32[16,128]{1,0:T(8,128)S(1)}, u32[]{:S(2)}, u32[]{:S(2)}) collective-permute-start(f32[16,128]{1,0:T(8,128)S(1)} %fusion), channel_id=1, source_target_pairs={{0,128},{128,0},{1,129},{129,1},{2,130},{130,2},{3,131},{131,3},{4... | collective-permute-start | bytes 24584 | tf_op jit(solution)/shard_map/ppermute | solution.py:479
  41.2 5.2 %collective-permute-start.12 = (f32[64,128]{1,0:T(8,128)S(1)}, f32[64,128]{1,0:T(8,128)S(1)}, u32[]{:S(2)}, u32[]{:S(2)}) collective-permute-start(f32[64,128]{1,0:T(8,128)S(1)} %get-tuple-element.41), channel_id=1, source_target_pairs={{0,112},{16,32},{32,16},{48,64},{64,48},{80,96},{96,80},{112,0},{1... | collective-permute-start | bytes 98312 | tf_op jit(solution)/shard_map/ppermute | solution.py:484
  46.4 1.1 %copy-start.1 = (f32[8,8,8]{2,1,0:T(8,128)S(1)}, f32[8,8,8]{2,1,0:T(8,128)}, u32[]{:S(2)}) copy-start(f32[8,8,8]{2,1,0:T(8,128)} %basis_ref.3) | copy-start | bytes 6148
  46.7 5.9 %collective-permute-start.14 = (f32[24,128]{1,0:T(8,128)S(1)}, f32[24,128]{1,0:T(8,128)S(1)}, u32[]{:S(2)}, u32[]{:S(2)}) collective-permute-start(f32[24,128]{1,0:T(8,128)S(1)} %get-tuple-element.44), channel_id=1, source_target_pairs={{0,1},{1,0},{2,3},{3,2},{4,5},{5,4},{6,7},{7,6},{8,9},{9,8},{10,11... | collective-permute-start | bytes 36872 | tf_op jit(solution)/shard_map/ppermute | solution.py:479
  46.8 5.8 %copy-start = (f32[1,1,1,8,16,256]{5,4,3,2,1,0:T(8,128)S(1)}, f32[1,1,1,8,16,256]{5,4,3,2,1,0:T(8,128)}, u32[]{:S(2)}) copy-start(f32[1,1,1,8,16,256]{5,4,3,2,1,0:T(8,128)} %param.11) | copy-start | bytes 393220
  46.8 5.8 %collective-permute-start.15 = (f32[8,128]{1,0:T(8,128)S(1)}, f32[8,128]{1,0:T(8,128)S(1)}, u32[]{:S(2)}, u32[]{:S(2)}) collective-permute-start(f32[8,128]{1,0:T(8,128)S(1)} %get-tuple-element.45), channel_id=1, source_target_pairs={{0,15},{1,2},{2,1},{3,4},{4,3},{5,6},{6,5},{7,8},{8,7},{9,10},{10,... | collective-permute-start | bytes 12296 | tf_op jit(solution)/shard_map/ppermute | solution.py:484

commit v8 on v7

--- a/solution.py
+++ b/solution.py
@@ -513,11 +513,12 @@
     block = (core, core.reshape(512, 128), ends, ends.reshape(128, 128), za, zb)
     ya, yb = call(yface_kernel, [(56, 128), (56, 128)], [(256, 128)], 6)(*block)
     ya, yb = swap(ya, "gy", 1), swap_odd(yb, "gy")
-    running = climb(running, "gz", 4, 2)
+    four, twelve, eight = (swap(running, "gz", d) for d in (4, 12, 8))
     modes, edges = call(front_kernel, [(1696, 128), (320, 128)], [(848, 128)], 5)(core, ends, *block[4:], factors)
     (modes,) = call(modes_kernel, [(1696, 128)], [(640, 128)], 5)(modes, edges, ya, yb, factors)
-    running = climb(running, "gz", 12, 3)
     (modes,) = call(middle_kernel, [(1696, 128)], [(16, 128)], 3)(modes, factors, eigen)
+    both = jnp.where(level_of >= 3, four + (twelve + eight), four)
+    running = running + jnp.where(level_of >= 2, both, 0.0)
     running = climb(running, "gz", 3, 1)
     local, edge_l, edge_h, xs = call(
         points_kernel, [(10, 10, 8, 128), (10, 16, 128), (10, 16, 128), (56, 128)], [(1696, 128)], 2

time: 53.7 us -> 57.1 us (1.063)
  waiting for transfers between devices: 17.8 us -> 20.8 us
    ppermute x4, waiting for transfers between devices: 8.96 us -> 11.9 us  [swap_odd(): lax.ppermute(value, axis, [(i, (i + 1 if i % 2 else i - 1) % count) for i...]
    ppermute x12 -> x13, starting transfers between devices: 18.3 us -> 19.7 us  [swap(): lax.ppermute(value, axis, [(i, i ^ distance) for i in range(lax.axis_size...]
    ppermute x4, starting transfers between devices: 7.87 us -> 6.77 us  [swap_odd(): lax.ppermute(value, axis, [(i, (i + 1 if i % 2 else i - 1) % count) for i...]
    ppermute x12 -> x13, waiting for transfers between devices: 8.84 us -> 8.86 us  [swap(): lax.ppermute(value, axis, [(i, i ^ distance) for i in range(lax.axis_size...]
  transfers between devices with their start and end apart: 16 -> 17, of which waited for: 8 -> 8; matrix products, arithmetic and copies ran while one was open for 1% -> 1% of each run, Pallas kernels for 10% -> 9%
where the time goes in v8:
time: 57.1 us; the launch traced here: 56.9 us
  starting transfers between devices  26.5 us (46%)
  waiting for transfers between devices  20.8 us (36%)
  Pallas kernels  8.52 us (15%)
    ppermute x13, starting transfers between devices, swap(): lax.ppermute(value, axis, [(i, i ^ distance) for i in range(lax.axis_size...  19.7 us
    ppermute x4, waiting for transfers between devices, swap_odd(): lax.ppermute(value, axis, [(i, (i + 1 if i % 2 else i - 1) % count) for i...  11.9 us
    ppermute x13, waiting for transfers between devices, swap(): lax.ppermute(value, axis, [(i, i ^ distance) for i in range(lax.axis_size...  8.86 us
    ppermute x4, starting transfers between devices, swap_odd(): lax.ppermute(value, axis, [(i, (i + 1 if i % 2 else i - 1) % count) for i...  6.77 us
    pallas_call x1, Pallas kernels, work(): call(pre_kernel, [(8, 8, 8, 128), (32, 128), (16, 128), (16, 128)], [(2,...  1.84 us
    pallas_call x1, Pallas kernels, work(): call(points_kernel, [(10, 10, 8, 128), (10, 16, 128), (10, 16, 128), (56,...  1.38 us
    pallas_call x1, Pallas kernels, work(): call(middle_kernel, [(1696, 128)], [(16, 128)], 3)(modes, factors, eigen)  1.19 us
  transfers between devices with their start and end apart: 17, of which 8 were waited for; matrix products, arithmetic and copies ran while one was open for 1% of the time, Pallas kernels for 9%

profile of v8, /device:TPU:24, one launch (start us, length us, event | category | flops | bytes accessed | tf_op | source)
XLA Modules:
  0.0 56.9 jit_solution(16405589941032432984)
XLA Ops:
  0.0 1.8 %shard_map.64 = (f32[8,8,8,128]{3,2,1,0:T(8,128)S(1)}, f32[32,128]{1,0:T(8,128)S(1)}, f32[16,128]{1,0:T(8,128)S(1)}, f32[16,128]{1,0:T(8,128)S(1)}) custom-call(f32[256,256]{1,0:T(8,128)} %bitcast.16, f32[8,16,256]{2,1,0:T(8,128)} %bitcast.12, f32[8,8,8]{2,1,0:T(8,128)} %basis_ref.3, f32[16,16]{1,0:T(8,128)} %bitcast.17), custom_call_target="tpu_custom_call" | custom-call | tf_op jit(solution)/shard_map/pallas_call | solution.py:499
  1.8 3.4 %collective-permute-start.6 = (f32[16,128]{1,0:T(8,128)S(1)}, f32[16,128]{1,0:T(8,128)S(1)}, u32[]{:S(2)}, u32[]{:S(2)}) collective-permute-start(f32[16,128]{1,0:T(8,128)S(1)} %get-tuple-element.39), channel_id=1, source_target_pairs={{0,32},{16,48},{32,0},{48,16},{64,96},{80,112},{96,64},{112,80},{1... | collective-permute-start | bytes 24584 | tf_op jit(solution)/shard_map/ppermute | solution.py:479
  5.2 1.6 %collective-permute-done.6 = f32[16,128]{1,0:T(8,128)S(1)} collective-permute-done((f32[16,128]{1,0:T(8,128)S(1)}, f32[16,128]{1,0:T(8,128)S(1)}, u32[]{:S(2)}, u32[]{:S(2)}) %collective-permute-start.6) | collective-permute-done | bytes 8224 | tf_op jit(solution)/shard_map/ppermute | solution.py:479
  6.9 6.0 %collective-permute-start.7 = (f32[16,128]{1,0:T(8,128)S(1)}, f32[16,128]{1,0:T(8,128)S(1)}, u32[]{:S(2)}, u32[]{:S(2)}) collective-permute-start(f32[16,128]{1,0:T(8,128)S(1)} %select_add_fusion.3), channel_id=1, source_target_pairs={{0,96},{16,112},{32,64},{48,80},{64,32},{80,48},{96,0},{112,16},{1... | collective-permute-start | bytes 24584 | tf_op jit(solution)/shard_map/ppermute | solution.py:479
  12.9 1.6 %collective-permute-done.7 = f32[16,128]{1,0:T(8,128)S(1)} collective-permute-done((f32[16,128]{1,0:T(8,128)S(1)}, f32[16,128]{1,0:T(8,128)S(1)}, u32[]{:S(2)}, u32[]{:S(2)}) %collective-permute-start.7) | collective-permute-done | bytes 8224 | tf_op jit(solution)/shard_map/ppermute | solution.py:479
  14.6 1.3 %collective-permute-start.10 = (f32[16,128]{1,0:T(8,128)S(1)}, f32[16,128]{1,0:T(8,128)S(1)}, u32[]{:S(2)}, u32[]{:S(2)}) collective-permute-start(f32[16,128]{1,0:T(8,128)S(1)} %select_add_fusion.2), channel_id=1, source_target_pairs={{0,8},{1,9},{2,10},{3,11},{4,12},{5,13},{6,14},{7,15},{8,0},{9,1},... | collective-permute-start | bytes 24584 | tf_op jit(solution)/shard_map/ppermute | solution.py:479
  15.9 2.9 %collective-permute-start.9 = (f32[16,128]{1,0:T(8,128)S(1)}, f32[16,128]{1,0:T(8,128)S(1)}, u32[]{:S(2)}, u32[]{:S(2)}) collective-permute-start(f32[16,128]{1,0:T(8,128)S(1)} %select_add_fusion.2), channel_id=1, source_target_pairs={{0,12},{1,13},{2,14},{3,15},{4,8},{5,9},{6,10},{7,11},{8,4},{9,5},... | collective-permute-start | bytes 24584 | tf_op jit(solution)/shard_map/ppermute | solution.py:479
  18.7 0.2 shard_map.65
  18.9 1.6 %collective-permute-start.1 = (f32[8,128]{1,0:T(8,128)S(1)}, f32[8,128]{1,0:T(8,128)S(1)}, u32[]{:S(2)}, u32[]{:S(2)}) collective-permute-start(f32[8,128]{1,0:T(8,128)S(1)} %get-tuple-element.29), channel_id=1, source_target_pairs={{0,1},{1,0},{2,3},{3,2},{4,5},{5,4},{6,7},{7,6},{8,9},{9,8},{10,11... | collective-permute-start | bytes 12296 | tf_op jit(solution)/shard_map/ppermute | solution.py:479
  20.5 2.3 %collective-permute-start.2 = (f32[8,128]{1,0:T(8,128)S(1)}, f32[8,128]{1,0:T(8,128)S(1)}, u32[]{:S(2)}, u32[]{:S(2)}) collective-permute-start(f32[8,128]{1,0:T(8,128)S(1)} %get-tuple-element.30), channel_id=1, source_target_pairs={{0,15},{1,2},{2,1},{3,4},{4,3},{5,6},{6,5},{7,8},{8,7},{9,10},{10,... | collective-permute-start | bytes 12296 | tf_op jit(solution)/shard_map/ppermute | solution.py:484
  22.8 3.4 %collective-permute-done.2.zb_ref = f32[8,128]{1,0:T(8,128)S(1)} collective-permute-done((f32[8,128]{1,0:T(8,128)S(1)}, f32[8,128]{1,0:T(8,128)S(1)}, u32[]{:S(2)}, u32[]{:S(2)}) %collective-permute-start.2) | collective-permute-done | bytes 4128 | tf_op jit(solution)/shard_map/ppermute | solution.py:484
  26.2 0.2 shard_map.68
  26.4 1.1 %collective-permute-start.3 = (f32[56,128]{1,0:T(8,128)S(1)}, f32[56,128]{1,0:T(8,128)S(1)}, u32[]{:S(2)}, u32[]{:S(2)}) collective-permute-start(f32[56,128]{1,0:T(8,128)S(1)} %get-tuple-element.33), channel_id=1, source_target_pairs={{0,16},{16,0},{32,48},{48,32},{64,80},{80,64},{96,112},{112,96},{1... | collective-permute-start | bytes 86024 | tf_op jit(solution)/shard_map/ppermute | solution.py:479
  27.5 3.7 %collective-permute-start.4 = (f32[56,128]{1,0:T(8,128)S(1)}, f32[56,128]{1,0:T(8,128)S(1)}, u32[]{:S(2)}, u32[]{:S(2)}) collective-permute-start(f32[56,128]{1,0:T(8,128)S(1)} %get-tuple-element.34), channel_id=1, source_target_pairs={{0,112},{16,32},{32,16},{48,64},{64,48},{80,96},{96,80},{112,0},{1... | collective-permute-start | bytes 86024 | tf_op jit(solution)/shard_map/ppermute | solution.py:484
  31.3 3.3 %collective-permute-start.11 = (f32[16,128]{1,0:T(8,128)S(1)}, f32[16,128]{1,0:T(8,128)S(1)}, u32[]{:S(2)}, u32[]{:S(2)}) collective-permute-start(f32[16,128]{1,0:T(8,128)S(1)} %fusion.1), channel_id=1, source_target_pairs={{0,3},{1,2},{2,1},{3,0},{4,7},{5,6},{6,5},{7,4},{8,11},{9,10},{10,... | collective-permute-start | bytes 24584 | tf_op jit(solution)/shard_map/ppermute | solution.py:479
  34.6 1.1 %shard_map.67 = (f32[1696,128]{1,0:T(8,128)S(1)}, f32[320,128]{1,0:T(8,128)S(1)}) custom-call(f32[8,8,8,128]{3,2,1,0:T(8,128)S(1)} %get-tuple-element.26.core_ref, f32[2,8,8,128]{3,2,1,0:T(8,128)S(1)} %get-tuple-element.28.ends_ref, f32[8,128]{1,0:T(8,128)S(1)} %collective-permute-done.1.za_ref, f32[8,128]{1,0:T(8,128)S(1)} %collective-permute-done.2.zb_ref, ...), custom_call_target="tpu_custom_call" | custom-call | tf_op jit(solution)/shard_map/pallas_call | solution.py:517
  35.7 0.4 shard_map.69.u_ref
  36.1 0.3 copy-done.3
  36.4 1.2 %shard_map.70.u_ref = f32[1696,128]{1,0:T(8,128)S(1)} custom-call(f32[1696,128]{1,0:T(8,128)S(1)} %shard_map.69.u_ref, f32[848,128]{1,0:T(8,128)S(1)} %shard_map.66.s, f32[3,10,1,128]{3,2,1,0:T(1,128)S(1)} %bitcast.15), custom_call_target="tpu_custom_call" | custom-call | tf_op jit(solution)/shard_map/pallas_call | solution.py:519
  37.6 1.4 %shard_map.71 = (f32[10,10,8,128]{3,2,1,0:T(8,128)S(1)}, f32[10,16,128]{2,1,0:T(8,128)S(1)}, f32[10,16,128]{2,1,0:T(8,128)S(1)}, f32[56,128]{1,0:T(8,128)S(1)}) custom-call(f32[1696,128]{1,0:T(8,128)S(1)} %shard_map.70.u_ref, f32[848,128]{1,0:T(8,128)S(1)} %shard_map.66.s), custom_call_target="tpu_custom_call" | custom-call | tf_op jit(solution)/shard_map/pallas_call | solution.py:523
  39.1 1.1 %collective-permute-done.5.xr_ref = f32[56,128]{1,0:T(8,128)S(1)} collective-permute-done((f32[56,128]{1,0:T(8,128)S(1)}, f32[56,128]{1,0:T(8,128)S(1)}, u32[]{:S(2)}, u32[]{:S(2)}) %collective-permute-start.5) | collective-permute-done | bytes 28704 | tf_op jit(solution)/shard_map/ppermute | solution.py:479
  40.2 0.1 shard_map.72
  40.5 4.0 %collective-permute-done.12.ya_ref = f32[80,128]{1,0:T(8,128)S(1)} collective-permute-done((f32[80,128]{1,0:T(8,128)S(1)}, f32[80,128]{1,0:T(8,128)S(1)}, u32[]{:S(2)}, u32[]{:S(2)}) %collective-permute-start.12) | collective-permute-done | bytes 40992 | tf_op jit(solution)/shard_map/ppermute | solution.py:479
  44.6 0.6 %collective-permute-start.13 = (f32[64,128]{1,0:T(8,128)S(1)}, f32[64,128]{1,0:T(8,128)S(1)}, u32[]{:S(2)}, u32[]{:S(2)}) collective-permute-start(f32[64,128]{1,0:T(8,128)S(1)} %get-tuple-element.41), channel_id=1, source_target_pairs={{0,112},{16,32},{32,16},{48,64},{64,48},{80,96},{96,80},{112,0},{1... | collective-permute-start | bytes 98312 | tf_op jit(solution)/shard_map/ppermute | solution.py:484
  45.2 0.5 collective-permute-done.14
  45.8 4.0 %collective-permute-done.13.yb_ref = f32[64,128]{1,0:T(8,128)S(1)} collective-permute-done((f32[64,128]{1,0:T(8,128)S(1)}, f32[64,128]{1,0:T(8,128)S(1)}, u32[]{:S(2)}, u32[]{:S(2)}) %collective-permute-start.13) | collective-permute-done | bytes 32800 | tf_op jit(solution)/shard_map/ppermute | solution.py:484
  49.8 0.3 shard_map.74
  50.2 0.2 collective-permute-start.16
  50.4 0.2 copy-done.1
  50.5 0.9 %shard_map.73 = (f32[256,256]{1,0:T(8,128)S(1)}, f32[64,128]{1,0:T(8,128)S(1)}) custom-call(f32[10,10,8,128]{3,2,1,0:T(8,128)S(1)} %get-tuple-element.35.l_ref, f32[10,16,128]{2,1,0:T(8,128)S(1)} %get-tuple-element.36.hl_ref, f32[10,16,128]{2,1,0:T(8,128)S(1)} %get-tuple-element.37.hh_ref, f32[56,128]{1,0:T(8,128)S(1)} %collective-permute-done.5.xr_ref, ...), custom_call_target="tpu_custom_call" | custom-call | tf_op jit(solution)/shard_map/pallas_call | solution.py:534
  51.5 4.5 %collective-permute-done.16.zb_ref = f32[8,128]{1,0:T(8,128)S(1)} collective-permute-done((f32[8,128]{1,0:T(8,128)S(1)}, f32[8,128]{1,0:T(8,128)S(1)}, u32[]{:S(2)}, u32[]{:S(2)}) %collective-permute-start.16) | collective-permute-done | bytes 4128 | tf_op jit(solution)/shard_map/ppermute | solution.py:484
  56.0 0.9 %shard_map.75 = f32[256,256]{1,0:T(8,128)} custom-call(f32[256,256]{1,0:T(8,128)S(1)} %get-tuple-element.42.sum_ref, f32[64,128]{1,0:T(8,128)S(1)} %get-tuple-element.43.tile_ref, f32[24,128]{1,0:T(8,128)S(1)} %collective-permute-done.15.za_ref, f32[8,128]{1,0:T(8,128)S(1)} %collective-permute-done.16.zb_ref, f32[8,16,256]{2,1,0:T(8,128)S(1)} %bitcast.13, ...), custom_call_target="tpu_custom_call" | custom-call | tf_op jit(solution)/shard_map/pallas_call | solution.py:537
  (34 shorter events, 0.8 us)
Async XLA Ops:
  1.8 5.0 %collective-permute-start.6 = (f32[16,128]{1,0:T(8,128)S(1)}, f32[16,128]{1,0:T(8,128)S(1)}, u32[]{:S(2)}, u32[]{:S(2)}) collective-permute-start(f32[16,128]{1,0:T(8,128)S(1)} %get-tuple-element.39), channel_id=1, source_target_pairs={{0,32},{16,48},{32,0},{48,16},{64,96},{80,112},{96,64},{112,80},{1... | collective-permute-start | bytes 24584 | tf_op jit(solution)/shard_map/ppermute | solution.py:479
  5.2 13.5 %collective-permute-start = (f32[32,128]{1,0:T(8,128)S(1)}, f32[32,128]{1,0:T(8,128)S(1)}, u32[]{:S(2)}, u32[]{:S(2)}) collective-permute-start(f32[32,128]{1,0:T(8,128)S(1)} %get-tuple-element.27), channel_id=1, source_target_pairs={{0,128},{128,0},{1,129},{129,1},{2,130},{130,2},{3,131},{131,3},{4... | collective-permute-start | bytes 49160 | tf_op jit(solution)/shard_map/ppermute | solution.py:479
  6.9 7.6 %collective-permute-start.7 = (f32[16,128]{1,0:T(8,128)S(1)}, f32[16,128]{1,0:T(8,128)S(1)}, u32[]{:S(2)}, u32[]{:S(2)}) collective-permute-start(f32[16,128]{1,0:T(8,128)S(1)} %select_add_fusion.3), channel_id=1, source_target_pairs={{0,96},{16,112},{32,64},{48,80},{64,32},{80,48},{96,0},{112,16},{1... | collective-permute-start | bytes 24584 | tf_op jit(solution)/shard_map/ppermute | solution.py:479
  14.6 16.6 %collective-permute-start.10 = (f32[16,128]{1,0:T(8,128)S(1)}, f32[16,128]{1,0:T(8,128)S(1)}, u32[]{:S(2)}, u32[]{:S(2)}) collective-permute-start(f32[16,128]{1,0:T(8,128)S(1)} %select_add_fusion.2), channel_id=1, source_target_pairs={{0,8},{1,9},{2,10},{3,11},{4,12},{5,13},{6,14},{7,15},{8,0},{9,1},... | collective-permute-start | bytes 24584 | tf_op jit(solution)/shard_map/ppermute | solution.py:479
  15.8 15.3 %collective-permute-start.8 = (f32[16,128]{1,0:T(8,128)S(1)}, f32[16,128]{1,0:T(8,128)S(1)}, u32[]{:S(2)}, u32[]{:S(2)}) collective-permute-start(f32[16,128]{1,0:T(8,128)S(1)} %select_add_fusion.2), channel_id=1, source_target_pairs={{0,4},{1,5},{2,6},{3,7},{4,0},{5,1},{6,2},{7,3},{8,12},{9,13},{10,... | collective-permute-start | bytes 24584 | tf_op jit(solution)/shard_map/ppermute | solution.py:479
  15.9 15.3 %collective-permute-start.9 = (f32[16,128]{1,0:T(8,128)S(1)}, f32[16,128]{1,0:T(8,128)S(1)}, u32[]{:S(2)}, u32[]{:S(2)}) collective-permute-start(f32[16,128]{1,0:T(8,128)S(1)} %select_add_fusion.2), channel_id=1, source_target_pairs={{0,12},{1,13},{2,14},{3,15},{4,8},{5,9},{6,10},{7,11},{8,4},{9,5},... | collective-permute-start | bytes 24584 | tf_op jit(solution)/shard_map/ppermute | solution.py:479
  18.9 3.9 %collective-permute-start.1 = (f32[8,128]{1,0:T(8,128)S(1)}, f32[8,128]{1,0:T(8,128)S(1)}, u32[]{:S(2)}, u32[]{:S(2)}) collective-permute-start(f32[8,128]{1,0:T(8,128)S(1)} %get-tuple-element.29), channel_id=1, source_target_pairs={{0,1},{1,0},{2,3},{3,2},{4,5},{5,4},{6,7},{7,6},{8,9},{9,8},{10,11... | collective-permute-start | bytes 12296 | tf_op jit(solution)/shard_map/ppermute | solution.py:479
  20.5 5.7 %collective-permute-start.2 = (f32[8,128]{1,0:T(8,128)S(1)}, f32[8,128]{1,0:T(8,128)S(1)}, u32[]{:S(2)}, u32[]{:S(2)}) collective-permute-start(f32[8,128]{1,0:T(8,128)S(1)} %get-tuple-element.30), channel_id=1, source_target_pairs={{0,15},{1,2},{2,1},{3,4},{4,3},{5,6},{6,5},{7,8},{8,7},{9,10},{10,... | collective-permute-start | bytes 12296 | tf_op jit(solution)/shard_map/ppermute | solution.py:484
  26.2 8.4 %copy-start.2 = (bf16[1,1,1,3,10,10,128]{6,3,5,4,2,1,0:T(4,128)(2,1)S(1)}, bf16[1,1,1,3,10,10,128]{6,3,5,4,2,1,0:T(4,128)(2,1)}, u32[]{:S(2)}) copy-start(bf16[1,1,1,3,10,10,128]{6,3,5,4,2,1,0:T(4,128)(2,1)} %param.7) | copy-start | bytes 230404
  26.4 9.3 %collective-permute-start.3 = (f32[56,128]{1,0:T(8,128)S(1)}, f32[56,128]{1,0:T(8,128)S(1)}, u32[]{:S(2)}, u32[]{:S(2)}) collective-permute-start(f32[56,128]{1,0:T(8,128)S(1)} %get-tuple-element.33), channel_id=1, source_target_pairs={{0,16},{16,0},{32,48},{48,32},{64,80},{80,64},{96,112},{112,96},{1... | collective-permute-start | bytes 86024 | tf_op jit(solution)/shard_map/ppermute | solution.py:479
  27.5 8.2 %collective-permute-start.4 = (f32[56,128]{1,0:T(8,128)S(1)}, f32[56,128]{1,0:T(8,128)S(1)}, u32[]{:S(2)}, u32[]{:S(2)}) collective-permute-start(f32[56,128]{1,0:T(8,128)S(1)} %get-tuple-element.34), channel_id=1, source_target_pairs={{0,112},{16,32},{32,16},{48,64},{64,48},{80,96},{96,80},{112,0},{1... | collective-permute-start | bytes 86024 | tf_op jit(solution)/shard_map/ppermute | solution.py:484
  31.3 7.8 %collective-permute-start.11 = (f32[16,128]{1,0:T(8,128)S(1)}, f32[16,128]{1,0:T(8,128)S(1)}, u32[]{:S(2)}, u32[]{:S(2)}) collective-permute-start(f32[16,128]{1,0:T(8,128)S(1)} %fusion.1), channel_id=1, source_target_pairs={{0,3},{1,2},{2,1},{3,0},{4,7},{5,6},{6,5},{7,4},{8,11},{9,10},{10,... | collective-permute-start | bytes 24584 | tf_op jit(solution)/shard_map/ppermute | solution.py:479
  35.7 0.7 %copy-start.3 = (f32[1,1,1,3,10,128]{5,2,4,3,1,0:T(1,128)S(1)}, f32[1,1,1,3,10,128]{5,2,4,3,1,0:T(1,128)}, u32[]{:S(2)}) copy-start(f32[1,1,1,3,10,128]{5,2,4,3,1,0:T(1,128)} %param.8) | copy-start | bytes 46084
  39.0 1.2 %collective-permute-start.5 = (f32[56,128]{1,0:T(8,128)S(1)}, f32[56,128]{1,0:T(8,128)S(1)}, u32[]{:S(2)}, u32[]{:S(2)}) collective-permute-start(f32[56,128]{1,0:T(8,128)S(1)} %get-tuple-element.38), channel_id=1, source_target_pairs={{0,128},{128,0},{1,129},{129,1},{2,130},{130,2},{3,131},{131,3},{4... | collective-permute-start | bytes 86024 | tf_op jit(solution)/shard_map/ppermute | solution.py:479
  40.4 4.1 %collective-permute-start.12 = (f32[80,128]{1,0:T(8,128)S(1)}, f32[80,128]{1,0:T(8,128)S(1)}, u32[]{:S(2)}, u32[]{:S(2)}) collective-permute-start(f32[80,128]{1,0:T(8,128)S(1)} %get-tuple-element.40), channel_id=1, source_target_pairs={{0,16},{16,0},{32,48},{48,32},{64,80},{80,64},{96,112},{112,96},{1... | collective-permute-start | bytes 122888 | tf_op jit(solution)/shard_map/ppermute | solution.py:479
  44.5 1.2 %collective-permute-start.14 = (f32[16,128]{1,0:T(8,128)S(1)}, f32[16,128]{1,0:T(8,128)S(1)}, u32[]{:S(2)}, u32[]{:S(2)}) collective-permute-start(f32[16,128]{1,0:T(8,128)S(1)} %fusion.2), channel_id=1, source_target_pairs={{0,128},{128,0},{1,129},{129,1},{2,130},{130,2},{3,131},{131,3},{4... | collective-permute-start | bytes 24584 | tf_op jit(solution)/shard_map/ppermute | solution.py:479
  44.6 5.2 %collective-permute-start.13 = (f32[64,128]{1,0:T(8,128)S(1)}, f32[64,128]{1,0:T(8,128)S(1)}, u32[]{:S(2)}, u32[]{:S(2)}) collective-permute-start(f32[64,128]{1,0:T(8,128)S(1)} %get-tuple-element.41), channel_id=1, source_target_pairs={{0,112},{16,32},{32,16},{48,64},{64,48},{80,96},{96,80},{112,0},{1... | collective-permute-start | bytes 98312 | tf_op jit(solution)/shard_map/ppermute | solution.py:484
  49.8 0.8 %copy-start.1 = (f32[8,8,8]{2,1,0:T(8,128)S(1)}, f32[8,8,8]{2,1,0:T(8,128)}, u32[]{:S(2)}) copy-start(f32[8,8,8]{2,1,0:T(8,128)} %basis_ref.3) | copy-start | bytes 6148
  50.1 5.9 %collective-permute-start.15 = (f32[24,128]{1,0:T(8,128)S(1)}, f32[24,128]{1,0:T(8,128)S(1)}, u32[]{:S(2)}, u32[]{:S(2)}) collective-permute-start(f32[24,128]{1,0:T(8,128)S(1)} %get-tuple-element.44), channel_id=1, source_target_pairs={{0,1},{1,0},{2,3},{3,2},{4,5},{5,4},{6,7},{7,6},{8,9},{9,8},{10,11... | collective-permute-start | bytes 36872 | tf_op jit(solution)/shard_map/ppermute | solution.py:479
  50.2 5.8 %copy-start = (f32[1,1,1,8,16,256]{5,4,3,2,1,0:T(8,128)S(1)}, f32[1,1,1,8,16,256]{5,4,3,2,1,0:T(8,128)}, u32[]{:S(2)}) copy-start(f32[1,1,1,8,16,256]{5,4,3,2,1,0:T(8,128)} %param.11) | copy-start | bytes 393220
  50.2 5.8 %collective-permute-start.16 = (f32[8,128]{1,0:T(8,128)S(1)}, f32[8,128]{1,0:T(8,128)S(1)}, u32[]{:S(2)}, u32[]{:S(2)}) collective-permute-start(f32[8,128]{1,0:T(8,128)S(1)} %get-tuple-element.45), channel_id=1, source_target_pairs={{0,15},{1,2},{2,1},{3,4},{4,3},{5,6},{6,5},{7,8},{8,7},{9,10},{10,... | collective-permute-start | bytes 12296 | tf_op jit(solution)/shard_map/ppermute | solution.py:484

commit v9 on v8

--- a/solution.py
+++ b/solution.py
@@ -168,7 +168,8 @@
     yb_ref[40:56] = jnp.where(even_y, down, up)
 
 
-def factors_kernel(vec_ref, s_ref):
+def factors_kernel(vec_ref, eig_ref, s_ref, held_ref):
+    held_ref[...] = eig_ref[...]
     for a in range(10):
         for i in range(10):
             s_ref[(i * 10 + a) * 8 : (i * 10 + a) * 8 + 3] = vec_ref[i, a].astype(F32)
@@ -340,7 +341,7 @@
 
 
 def yfold_send_kernel(hl_ref, hh_ref, xr_ref, run_ref, ya_ref, yb_ref):
-    ya_ref[64:80] = run_ref[...]
+    ya_ref[40:56] = run_ref[...]
     gx = lax.axis_index("gx")
     even_y = lax.rem(lax.axis_index("gy"), 2) == 0
     low_q = (iotas(16)[0] & 32) == 0
@@ -348,16 +349,18 @@
     for i in range(4):
         down = jnp.where(low_q, low[i], roll(low[i + 4], 32))
         up = jnp.where(low_q, roll(high[i + 4], 96), high[i])
-        ya_ref[i * 16 : i * 16 + 16] = jnp.where(even_y, up, down)
-        yb_ref[i * 16 : i * 16 + 16] = jnp.where(even_y, down, up)
+        for ref, value in ((ya_ref, jnp.where(even_y, up, down)), (yb_ref, jnp.where(even_y, down, up))):
+            ref[i * 8 : i * 8 + 8] = value[:8]
+            ref[32 + 2 * i : 34 + 2 * i] = value[8:10]
 
 
 def fold_rows(hl_ref, hh_ref, xr_ref, ya_ref, yb_ref, rows_first, rows_last, gx):
     low_q = (iotas(16)[0] & 32) == 0
     low, high = edge_rows(hl_ref, hh_ref, xr_ref, gx)
     for i in range(8):
-        at = (i % 4) * 16
-        above, below = sides(ya_ref[at : at + 16], yb_ref[at : at + 16], "gy")
+        n = i % 4
+        rows = [jnp.concatenate([ref[n * 8 : n * 8 + 8], ref[32 + 2 * n : 40 + 2 * n]], 0) for ref in (ya_ref, yb_ref)]
+        above, below = sides(*rows, "gy")
         if i < 4:
             above, below = roll(above, 32), roll(below, 96)
         rows_last[pl.ds(i * 16, 16), :] = jnp.where(low_q, roll(low[i], 96), above)
@@ -509,7 +512,7 @@
     running = climb(running, "gy", 2, 5)
     za, zb = swap(za, "gz", 1), swap_odd(zb, "gz")
     running = climb(running, "gy", 6, 6)
-    (factors,) = call(factors_kernel, [(848, 128)], [], 1)(vectors)
+    factors, eigen = call(factors_kernel, [(848, 128), eigen.shape], [], 2)(vectors, eigen)
     block = (core, core.reshape(512, 128), ends, ends.reshape(128, 128), za, zb)
     ya, yb = call(yface_kernel, [(56, 128), (56, 128)], [(256, 128)], 6)(*block)
     ya, yb = swap(ya, "gy", 1), swap_odd(yb, "gy")
@@ -524,9 +527,9 @@
         points_kernel, [(10, 10, 8, 128), (10, 16, 128), (10, 16, 128), (56, 128)], [(1696, 128)], 2
     )(modes, factors)
     xr = swap(xs, "gx", 1)
-    ya, yb = call(yfold_send_kernel, [(80, 128), (64, 128)], [], 4)(edge_l, edge_h, xr, running)
+    ya, yb = call(yfold_send_kernel, [(56, 128), (48, 128)], [], 4)(edge_l, edge_h, xr, running)
     ya, yb = swap(ya, "gy", 1), swap_odd(yb, "gy")
-    running = running + jnp.where(level_of >= 4, ya[64:80], 0.0)
+    running = running + jnp.where(level_of >= 4, ya[40:56], 0.0)
     running = climb(running, "gx", 1, 7)
     parts = (local, edge_l, edge_h, xr, ya, yb)
     za, zb = call(zfold_send_kernel, [(24, 128), (8, 128)], [(128, 128)] * 2, 7)(*parts, running)

time: 57.1 us -> 56.5 us (0.989)
  no operation moved by 1% of the time
where the time goes in v9:
time: 56.5 us; the launch traced here: 56.4 us
  starting transfers between devices  26.4 us (47%)
  waiting for transfers between devices  20.6 us (36%)
  Pallas kernels  8.52 us (15%)
    ppermute x13, starting transfers between devices, swap(): lax.ppermute(value, axis, [(i, i ^ distance) for i in range(lax.axis_size...  19.7 us
    ppermute x4, waiting for transfers between devices, swap_odd(): lax.ppermute(value, axis, [(i, (i + 1 if i % 2 else i - 1) % count) for i...  11.8 us
    ppermute x13, waiting for transfers between devices, swap(): lax.ppermute(value, axis, [(i, i ^ distance) for i in range(lax.axis_size...  8.76 us
    ppermute x4, starting transfers between devices, swap_odd(): lax.ppermute(value, axis, [(i, (i + 1 if i % 2 else i - 1) % count) for i...  6.74 us
    pallas_call x1, Pallas kernels, work(): call(pre_kernel, [(8, 8, 8, 128), (32, 128), (16, 128), (16, 128)], [(2,...  1.84 us
    pallas_call x1, Pallas kernels, work(): call(points_kernel, [(10, 10, 8, 128), (10, 16, 128), (10, 16, 128), (56,...  1.38 us
    pallas_call x1, Pallas kernels, work(): call(middle_kernel, [(1696, 128)], [(16, 128)], 3)(modes, factors, eigen)  1.2 us
  transfers between devices with their start and end apart: 17, of which 8 were waited for; matrix products, arithmetic and copies ran while one was open for 1% of the time, Pallas kernels for 9%

profile of v9, /device:TPU:24, one launch (start us, length us, event | category | flops | bytes accessed | tf_op | source)
XLA Modules:
  0.0 56.4 jit_solution(15139939097658873101)
XLA Ops:
  0.0 1.8 %shard_map.64 = (f32[8,8,8,128]{3,2,1,0:T(8,128)S(1)}, f32[32,128]{1,0:T(8,128)S(1)}, f32[16,128]{1,0:T(8,128)S(1)}, f32[16,128]{1,0:T(8,128)S(1)}) custom-call(f32[256,256]{1,0:T(8,128)} %bitcast.16, f32[8,16,256]{2,1,0:T(8,128)} %bitcast.12, f32[8,8,8]{2,1,0:T(8,128)} %basis_ref.3, f32[16,16]{1,0:T(8,128)} %bitcast.17), custom_call_target="tpu_custom_call" | custom-call | tf_op jit(solution)/shard_map/pallas_call | solution.py:502
  1.8 3.4 %collective-permute-start.6 = (f32[16,128]{1,0:T(8,128)S(1)}, f32[16,128]{1,0:T(8,128)S(1)}, u32[]{:S(2)}, u32[]{:S(2)}) collective-permute-start(f32[16,128]{1,0:T(8,128)S(1)} %get-tuple-element.43), channel_id=1, source_target_pairs={{0,32},{16,48},{32,0},{48,16},{64,96},{80,112},{96,64},{112,80},{1... | collective-permute-start | bytes 24584 | tf_op jit(solution)/shard_map/ppermute | solution.py:482
  5.2 1.6 %collective-permute-done.6 = f32[16,128]{1,0:T(8,128)S(1)} collective-permute-done((f32[16,128]{1,0:T(8,128)S(1)}, f32[16,128]{1,0:T(8,128)S(1)}, u32[]{:S(2)}, u32[]{:S(2)}) %collective-permute-start.6) | collective-permute-done | bytes 8224 | tf_op jit(solution)/shard_map/ppermute | solution.py:482
  6.9 6.0 %collective-permute-start.7 = (f32[16,128]{1,0:T(8,128)S(1)}, f32[16,128]{1,0:T(8,128)S(1)}, u32[]{:S(2)}, u32[]{:S(2)}) collective-permute-start(f32[16,128]{1,0:T(8,128)S(1)} %select_add_fusion.3), channel_id=1, source_target_pairs={{0,96},{16,112},{32,64},{48,80},{64,32},{80,48},{96,0},{112,16},{1... | collective-permute-start | bytes 24584 | tf_op jit(solution)/shard_map/ppermute | solution.py:482
  12.9 1.6 %collective-permute-done.7 = f32[16,128]{1,0:T(8,128)S(1)} collective-permute-done((f32[16,128]{1,0:T(8,128)S(1)}, f32[16,128]{1,0:T(8,128)S(1)}, u32[]{:S(2)}, u32[]{:S(2)}) %collective-permute-start.7) | collective-permute-done | bytes 8224 | tf_op jit(solution)/shard_map/ppermute | solution.py:482
  14.6 1.3 %collective-permute-start.10 = (f32[16,128]{1,0:T(8,128)S(1)}, f32[16,128]{1,0:T(8,128)S(1)}, u32[]{:S(2)}, u32[]{:S(2)}) collective-permute-start(f32[16,128]{1,0:T(8,128)S(1)} %select_add_fusion.2), channel_id=1, source_target_pairs={{0,8},{1,9},{2,10},{3,11},{4,12},{5,13},{6,14},{7,15},{8,0},{9,1},... | collective-permute-start | bytes 24584 | tf_op jit(solution)/shard_map/ppermute | solution.py:482
  15.9 2.9 %collective-permute-start.9 = (f32[16,128]{1,0:T(8,128)S(1)}, f32[16,128]{1,0:T(8,128)S(1)}, u32[]{:S(2)}, u32[]{:S(2)}) collective-permute-start(f32[16,128]{1,0:T(8,128)S(1)} %select_add_fusion.2), channel_id=1, source_target_pairs={{0,12},{1,13},{2,14},{3,15},{4,8},{5,9},{6,10},{7,11},{8,4},{9,5},... | collective-permute-start | bytes 24584 | tf_op jit(solution)/shard_map/ppermute | solution.py:482
  18.7 0.2 shard_map.65
  18.9 1.6 %collective-permute-start.1 = (f32[8,128]{1,0:T(8,128)S(1)}, f32[8,128]{1,0:T(8,128)S(1)}, u32[]{:S(2)}, u32[]{:S(2)}) collective-permute-start(f32[8,128]{1,0:T(8,128)S(1)} %get-tuple-element.31), channel_id=1, source_target_pairs={{0,1},{1,0},{2,3},{3,2},{4,5},{5,4},{6,7},{7,6},{8,9},{9,8},{10,11... | collective-permute-start | bytes 12296 | tf_op jit(solution)/shard_map/ppermute | solution.py:482
  20.5 2.3 %collective-permute-start.2 = (f32[8,128]{1,0:T(8,128)S(1)}, f32[8,128]{1,0:T(8,128)S(1)}, u32[]{:S(2)}, u32[]{:S(2)}) collective-permute-start(f32[8,128]{1,0:T(8,128)S(1)} %get-tuple-element.32), channel_id=1, source_target_pairs={{0,15},{1,2},{2,1},{3,4},{4,3},{5,6},{6,5},{7,8},{8,7},{9,10},{10,... | collective-permute-start | bytes 12296 | tf_op jit(solution)/shard_map/ppermute | solution.py:487
  22.8 3.4 %collective-permute-done.2.zb_ref = f32[8,128]{1,0:T(8,128)S(1)} collective-permute-done((f32[8,128]{1,0:T(8,128)S(1)}, f32[8,128]{1,0:T(8,128)S(1)}, u32[]{:S(2)}, u32[]{:S(2)}) %collective-permute-start.2) | collective-permute-done | bytes 4128 | tf_op jit(solution)/shard_map/ppermute | solution.py:487
  26.2 0.2 shard_map.68
  26.4 1.1 %collective-permute-start.3 = (f32[56,128]{1,0:T(8,128)S(1)}, f32[56,128]{1,0:T(8,128)S(1)}, u32[]{:S(2)}, u32[]{:S(2)}) collective-permute-start(f32[56,128]{1,0:T(8,128)S(1)} %get-tuple-element.36), channel_id=1, source_target_pairs={{0,16},{16,0},{32,48},{48,32},{64,80},{80,64},{96,112},{112,96},{1... | collective-permute-start | bytes 86024 | tf_op jit(solution)/shard_map/ppermute | solution.py:482
  27.5 3.7 %collective-permute-start.4 = (f32[56,128]{1,0:T(8,128)S(1)}, f32[56,128]{1,0:T(8,128)S(1)}, u32[]{:S(2)}, u32[]{:S(2)}) collective-permute-start(f32[56,128]{1,0:T(8,128)S(1)} %get-tuple-element.37), channel_id=1, source_target_pairs={{0,112},{16,32},{32,16},{48,64},{64,48},{80,96},{96,80},{112,0},{1... | collective-permute-start | bytes 86024 | tf_op jit(solution)/shard_map/ppermute | solution.py:487
  31.3 3.3 %collective-permute-start.11 = (f32[16,128]{1,0:T(8,128)S(1)}, f32[16,128]{1,0:T(8,128)S(1)}, u32[]{:S(2)}, u32[]{:S(2)}) collective-permute-start(f32[16,128]{1,0:T(8,128)S(1)} %fusion.1), channel_id=1, source_target_pairs={{0,3},{1,2},{2,1},{3,0},{4,7},{5,6},{6,5},{7,4},{8,11},{9,10},{10,... | collective-permute-start | bytes 24584 | tf_op jit(solution)/shard_map/ppermute | solution.py:482
  34.6 1.1 %shard_map.67 = (f32[1696,128]{1,0:T(8,128)S(1)}, f32[320,128]{1,0:T(8,128)S(1)}) custom-call(f32[8,8,8,128]{3,2,1,0:T(8,128)S(1)} %get-tuple-element.28.core_ref, f32[2,8,8,128]{3,2,1,0:T(8,128)S(1)} %get-tuple-element.30.ends_ref, f32[8,128]{1,0:T(8,128)S(1)} %collective-permute-done.1.za_ref, f32[8,128]{1,0:T(8,128)S(1)} %collective-permute-done.2.zb_ref, ...), custom_call_target="tpu_custom_call" | custom-call | tf_op jit(solution)/shard_map/pallas_call | solution.py:520
  35.7 0.4 shard_map.69.u_ref
  36.1 1.2 %shard_map.70.u_ref = f32[1696,128]{1,0:T(8,128)S(1)} custom-call(f32[1696,128]{1,0:T(8,128)S(1)} %shard_map.69.u_ref, f32[848,128]{1,0:T(8,128)S(1)} %get-tuple-element.33.s, f32[3,10,1,128]{3,2,1,0:T(1,128)S(1)} %get-tuple-element.38.eig_ref), custom_call_target="tpu_custom_call" | custom-call | tf_op jit(solution)/shard_map/pallas_call | solution.py:522
  37.3 1.4 %shard_map.71 = (f32[10,10,8,128]{3,2,1,0:T(8,128)S(1)}, f32[10,16,128]{2,1,0:T(8,128)S(1)}, f32[10,16,128]{2,1,0:T(8,128)S(1)}, f32[56,128]{1,0:T(8,128)S(1)}) custom-call(f32[1696,128]{1,0:T(8,128)S(1)} %shard_map.70.u_ref, f32[848,128]{1,0:T(8,128)S(1)} %get-tuple-element.33.s), custom_call_target="tpu_custom_call" | custom-call | tf_op jit(solution)/shard_map/pallas_call | solution.py:526
  38.8 1.1 %collective-permute-done.5.xr_ref = f32[56,128]{1,0:T(8,128)S(1)} collective-permute-done((f32[56,128]{1,0:T(8,128)S(1)}, f32[56,128]{1,0:T(8,128)S(1)}, u32[]{:S(2)}, u32[]{:S(2)}) %collective-permute-start.5) | collective-permute-done | bytes 28704 | tf_op jit(solution)/shard_map/ppermute | solution.py:482
  39.9 0.1 shard_map.72
  40.1 3.8 %collective-permute-done.12.ya_ref = f32[56,128]{1,0:T(8,128)S(1)} collective-permute-done((f32[56,128]{1,0:T(8,128)S(1)}, f32[56,128]{1,0:T(8,128)S(1)}, u32[]{:S(2)}, u32[]{:S(2)}) %collective-permute-start.12) | collective-permute-done | bytes 28704 | tf_op jit(solution)/shard_map/ppermute | solution.py:482
  44.1 0.6 %collective-permute-start.13 = (f32[48,128]{1,0:T(8,128)S(1)}, f32[48,128]{1,0:T(8,128)S(1)}, u32[]{:S(2)}, u32[]{:S(2)}) collective-permute-start(f32[48,128]{1,0:T(8,128)S(1)} %get-tuple-element.45), channel_id=1, source_target_pairs={{0,112},{16,32},{32,16},{48,64},{64,48},{80,96},{96,80},{112,0},{1... | collective-permute-start | bytes 73736 | tf_op jit(solution)/shard_map/ppermute | solution.py:487
  44.7 0.5 collective-permute-done.14
  45.3 3.9 %collective-permute-done.13.yb_ref = f32[48,128]{1,0:T(8,128)S(1)} collective-permute-done((f32[48,128]{1,0:T(8,128)S(1)}, f32[48,128]{1,0:T(8,128)S(1)}, u32[]{:S(2)}, u32[]{:S(2)}) %collective-permute-start.13) | collective-permute-done | bytes 24608 | tf_op jit(solution)/shard_map/ppermute | solution.py:487
  49.2 0.3 shard_map.74
  49.5 0.1 collective-permute-start.15
  49.6 0.2 collective-permute-start.16
  49.8 0.2 copy-done.1
  50.0 0.9 %shard_map.73 = (f32[256,256]{1,0:T(8,128)S(1)}, f32[64,128]{1,0:T(8,128)S(1)}) custom-call(f32[10,10,8,128]{3,2,1,0:T(8,128)S(1)} %get-tuple-element.39.l_ref, f32[10,16,128]{2,1,0:T(8,128)S(1)} %get-tuple-element.40.hl_ref, f32[10,16,128]{2,1,0:T(8,128)S(1)} %get-tuple-element.41.hh_ref, f32[56,128]{1,0:T(8,128)S(1)} %collective-permute-done.5.xr_ref, ...), custom_call_target="tpu_custom_call" | custom-call | tf_op jit(solution)/shard_map/pallas_call | solution.py:537
  50.9 4.5 %collective-permute-done.16.zb_ref = f32[8,128]{1,0:T(8,128)S(1)} collective-permute-done((f32[8,128]{1,0:T(8,128)S(1)}, f32[8,128]{1,0:T(8,128)S(1)}, u32[]{:S(2)}, u32[]{:S(2)}) %collective-permute-start.16) | collective-permute-done | bytes 4128 | tf_op jit(solution)/shard_map/ppermute | solution.py:487
  55.5 0.9 %shard_map.75 = f32[256,256]{1,0:T(8,128)} custom-call(f32[256,256]{1,0:T(8,128)S(1)} %get-tuple-element.46.sum_ref, f32[64,128]{1,0:T(8,128)S(1)} %get-tuple-element.47.tile_ref, f32[24,128]{1,0:T(8,128)S(1)} %collective-permute-done.15.za_ref, f32[8,128]{1,0:T(8,128)S(1)} %collective-permute-done.16.zb_ref, f32[8,16,256]{2,1,0:T(8,128)S(1)} %bitcast.13, ...), custom_call_target="tpu_custom_call" | custom-call | tf_op jit(solution)/shard_map/pallas_call | solution.py:540
  (34 shorter events, 0.7 us)
Async XLA Ops:
  1.8 5.0 %collective-permute-start.6 = (f32[16,128]{1,0:T(8,128)S(1)}, f32[16,128]{1,0:T(8,128)S(1)}, u32[]{:S(2)}, u32[]{:S(2)}) collective-permute-start(f32[16,128]{1,0:T(8,128)S(1)} %get-tuple-element.43), channel_id=1, source_target_pairs={{0,32},{16,48},{32,0},{48,16},{64,96},{80,112},{96,64},{112,80},{1... | collective-permute-start | bytes 24584 | tf_op jit(solution)/shard_map/ppermute | solution.py:482
  5.2 13.5 %collective-permute-start = (f32[32,128]{1,0:T(8,128)S(1)}, f32[32,128]{1,0:T(8,128)S(1)}, u32[]{:S(2)}, u32[]{:S(2)}) collective-permute-start(f32[32,128]{1,0:T(8,128)S(1)} %get-tuple-element.29), channel_id=1, source_target_pairs={{0,128},{128,0},{1,129},{129,1},{2,130},{130,2},{3,131},{131,3},{4... | collective-permute-start | bytes 49160 | tf_op jit(solution)/shard_map/ppermute | solution.py:482
  6.9 7.6 %collective-permute-start.7 = (f32[16,128]{1,0:T(8,128)S(1)}, f32[16,128]{1,0:T(8,128)S(1)}, u32[]{:S(2)}, u32[]{:S(2)}) collective-permute-start(f32[16,128]{1,0:T(8,128)S(1)} %select_add_fusion.3), channel_id=1, source_target_pairs={{0,96},{16,112},{32,64},{48,80},{64,32},{80,48},{96,0},{112,16},{1... | collective-permute-start | bytes 24584 | tf_op jit(solution)/shard_map/ppermute | solution.py:482
  14.6 16.6 %collective-permute-start.10 = (f32[16,128]{1,0:T(8,128)S(1)}, f32[16,128]{1,0:T(8,128)S(1)}, u32[]{:S(2)}, u32[]{:S(2)}) collective-permute-start(f32[16,128]{1,0:T(8,128)S(1)} %select_add_fusion.2), channel_id=1, source_target_pairs={{0,8},{1,9},{2,10},{3,11},{4,12},{5,13},{6,14},{7,15},{8,0},{9,1},... | collective-permute-start | bytes 24584 | tf_op jit(solution)/shard_map/ppermute | solution.py:482
  15.8 15.3 %collective-permute-start.8 = (f32[16,128]{1,0:T(8,128)S(1)}, f32[16,128]{1,0:T(8,128)S(1)}, u32[]{:S(2)}, u32[]{:S(2)}) collective-permute-start(f32[16,128]{1,0:T(8,128)S(1)} %select_add_fusion.2), channel_id=1, source_target_pairs={{0,4},{1,5},{2,6},{3,7},{4,0},{5,1},{6,2},{7,3},{8,12},{9,13},{10,... | collective-permute-start | bytes 24584 | tf_op jit(solution)/shard_map/ppermute | solution.py:482
  15.9 15.3 %collective-permute-start.9 = (f32[16,128]{1,0:T(8,128)S(1)}, f32[16,128]{1,0:T(8,128)S(1)}, u32[]{:S(2)}, u32[]{:S(2)}) collective-permute-start(f32[16,128]{1,0:T(8,128)S(1)} %select_add_fusion.2), channel_id=1, source_target_pairs={{0,12},{1,13},{2,14},{3,15},{4,8},{5,9},{6,10},{7,11},{8,4},{9,5},... | collective-permute-start | bytes 24584 | tf_op jit(solution)/shard_map/ppermute | solution.py:482
  18.9 3.9 %collective-permute-start.1 = (f32[8,128]{1,0:T(8,128)S(1)}, f32[8,128]{1,0:T(8,128)S(1)}, u32[]{:S(2)}, u32[]{:S(2)}) collective-permute-start(f32[8,128]{1,0:T(8,128)S(1)} %get-tuple-element.31), channel_id=1, source_target_pairs={{0,1},{1,0},{2,3},{3,2},{4,5},{5,4},{6,7},{7,6},{8,9},{9,8},{10,11... | collective-permute-start | bytes 12296 | tf_op jit(solution)/shard_map/ppermute | solution.py:482
  20.5 5.7 %collective-permute-start.2 = (f32[8,128]{1,0:T(8,128)S(1)}, f32[8,128]{1,0:T(8,128)S(1)}, u32[]{:S(2)}, u32[]{:S(2)}) collective-permute-start(f32[8,128]{1,0:T(8,128)S(1)} %get-tuple-element.32), channel_id=1, source_target_pairs={{0,15},{1,2},{2,1},{3,4},{4,3},{5,6},{6,5},{7,8},{8,7},{9,10},{10,... | collective-permute-start | bytes 12296 | tf_op jit(solution)/shard_map/ppermute | solution.py:487
  26.2 8.4 %copy-start.2 = (bf16[1,1,1,3,10,10,128]{6,3,5,4,2,1,0:T(4,128)(2,1)S(1)}, bf16[1,1,1,3,10,10,128]{6,3,5,4,2,1,0:T(4,128)(2,1)}, u32[]{:S(2)}) copy-start(bf16[1,1,1,3,10,10,128]{6,3,5,4,2,1,0:T(4,128)(2,1)} %param.7) | copy-start | bytes 230404
  26.4 9.3 %collective-permute-start.3 = (f32[56,128]{1,0:T(8,128)S(1)}, f32[56,128]{1,0:T(8,128)S(1)}, u32[]{:S(2)}, u32[]{:S(2)}) collective-permute-start(f32[56,128]{1,0:T(8,128)S(1)} %get-tuple-element.36), channel_id=1, source_target_pairs={{0,16},{16,0},{32,48},{48,32},{64,80},{80,64},{96,112},{112,96},{1... | collective-permute-start | bytes 86024 | tf_op jit(solution)/shard_map/ppermute | solution.py:482
  27.5 8.2 %collective-permute-start.4 = (f32[56,128]{1,0:T(8,128)S(1)}, f32[56,128]{1,0:T(8,128)S(1)}, u32[]{:S(2)}, u32[]{:S(2)}) collective-permute-start(f32[56,128]{1,0:T(8,128)S(1)} %get-tuple-element.37), channel_id=1, source_target_pairs={{0,112},{16,32},{32,16},{48,64},{64,48},{80,96},{96,80},{112,0},{1... | collective-permute-start | bytes 86024 | tf_op jit(solution)/shard_map/ppermute | solution.py:487
  31.2 3.4 %copy-start.3 = (f32[1,1,1,3,10,128]{5,2,4,3,1,0:T(1,128)S(1)}, f32[1,1,1,3,10,128]{5,2,4,3,1,0:T(1,128)}, u32[]{:S(2)}) copy-start(f32[1,1,1,3,10,128]{5,2,4,3,1,0:T(1,128)} %param.8) | copy-start | bytes 46084
  31.3 7.5 %collective-permute-start.11 = (f32[16,128]{1,0:T(8,128)S(1)}, f32[16,128]{1,0:T(8,128)S(1)}, u32[]{:S(2)}, u32[]{:S(2)}) collective-permute-start(f32[16,128]{1,0:T(8,128)S(1)} %fusion.1), channel_id=1, source_target_pairs={{0,3},{1,2},{2,1},{3,0},{4,7},{5,6},{6,5},{7,4},{8,11},{9,10},{10,... | collective-permute-start | bytes 24584 | tf_op jit(solution)/shard_map/ppermute | solution.py:482
  38.7 1.2 %collective-permute-start.5 = (f32[56,128]{1,0:T(8,128)S(1)}, f32[56,128]{1,0:T(8,128)S(1)}, u32[]{:S(2)}, u32[]{:S(2)}) collective-permute-start(f32[56,128]{1,0:T(8,128)S(1)} %get-tuple-element.42), channel_id=1, source_target_pairs={{0,128},{128,0},{1,129},{129,1},{2,130},{130,2},{3,131},{131,3},{4... | collective-permute-start | bytes 86024 | tf_op jit(solution)/shard_map/ppermute | solution.py:482
  40.1 3.9 %collective-permute-start.12 = (f32[56,128]{1,0:T(8,128)S(1)}, f32[56,128]{1,0:T(8,128)S(1)}, u32[]{:S(2)}, u32[]{:S(2)}) collective-permute-start(f32[56,128]{1,0:T(8,128)S(1)} %get-tuple-element.44), channel_id=1, source_target_pairs={{0,16},{16,0},{32,48},{48,32},{64,80},{80,64},{96,112},{112,96},{1... | collective-permute-start | bytes 86024 | tf_op jit(solution)/shard_map/ppermute | solution.py:482
  44.1 1.2 %collective-permute-start.14 = (f32[16,128]{1,0:T(8,128)S(1)}, f32[16,128]{1,0:T(8,128)S(1)}, u32[]{:S(2)}, u32[]{:S(2)}) collective-permute-start(f32[16,128]{1,0:T(8,128)S(1)} %fusion.2), channel_id=1, source_target_pairs={{0,128},{128,0},{1,129},{129,1},{2,130},{130,2},{3,131},{131,3},{4... | collective-permute-start | bytes 24584 | tf_op jit(solution)/shard_map/ppermute | solution.py:482
  44.1 5.1 %collective-permute-start.13 = (f32[48,128]{1,0:T(8,128)S(1)}, f32[48,128]{1,0:T(8,128)S(1)}, u32[]{:S(2)}, u32[]{:S(2)}) collective-permute-start(f32[48,128]{1,0:T(8,128)S(1)} %get-tuple-element.45), channel_id=1, source_target_pairs={{0,112},{16,32},{32,16},{48,64},{64,48},{80,96},{96,80},{112,0},{1... | collective-permute-start | bytes 73736 | tf_op jit(solution)/shard_map/ppermute | solution.py:487
  49.2 0.8 %copy-start.1 = (f32[8,8,8]{2,1,0:T(8,128)S(1)}, f32[8,8,8]{2,1,0:T(8,128)}, u32[]{:S(2)}) copy-start(f32[8,8,8]{2,1,0:T(8,128)} %basis_ref.3) | copy-start | bytes 6148
  49.5 5.9 %collective-permute-start.15 = (f32[24,128]{1,0:T(8,128)S(1)}, f32[24,128]{1,0:T(8,128)S(1)}, u32[]{:S(2)}, u32[]{:S(2)}) collective-permute-start(f32[24,128]{1,0:T(8,128)S(1)} %get-tuple-element.48), channel_id=1, source_target_pairs={{0,1},{1,0},{2,3},{3,2},{4,5},{5,4},{6,7},{7,6},{8,9},{9,8},{10,11... | collective-permute-start | bytes 36872 | tf_op jit(solution)/shard_map/ppermute | solution.py:482
  49.6 5.8 %copy-start = (f32[1,1,1,8,16,256]{5,4,3,2,1,0:T(8,128)S(1)}, f32[1,1,1,8,16,256]{5,4,3,2,1,0:T(8,128)}, u32[]{:S(2)}) copy-start(f32[1,1,1,8,16,256]{5,4,3,2,1,0:T(8,128)} %param.11) | copy-start | bytes 393220
  49.6 5.8 %collective-permute-start.16 = (f32[8,128]{1,0:T(8,128)S(1)}, f32[8,128]{1,0:T(8,128)S(1)}, u32[]{:S(2)}, u32[]{:S(2)}) collective-permute-start(f32[8,128]{1,0:T(8,128)S(1)} %get-tuple-element.49), channel_id=1, source_target_pairs={{0,15},{1,2},{2,1},{3,4},{4,3},{5,6},{6,5},{7,8},{8,7},{9,10},{10,... | collective-permute-start | bytes 12296 | tf_op jit(solution)/shard_map/ppermute | solution.py:487

commit v10 on v9

--- a/solution.py
+++ b/solution.py
@@ -378,18 +378,39 @@
     return value + jnp.where(sub == 0, row(rows_first, at), jnp.where(sub == 7, row(rows_last, at), 0.0))
 
 
-def zfold_send_kernel(l_ref, hl_ref, hh_ref, xr_ref, ya_ref, yb_ref, run_ref, za_ref, zb_ref, rows_first, rows_last):
+def zplane_kernel(l_ref, hl_ref, hh_ref, xr_ref, plane_ref, rows_first, rows_last):
+    gx = lax.axis_index("gx")
+    lane, sub = iotas()
+    low_q = (iotas(16)[0] & 32) == 0
+    low, high = edge_rows(hl_ref, hh_ref, xr_ref, gx)
+    for i in range(8):
+        rows_last[pl.ds(i * 16, 16), :] = jnp.where(low_q, roll(low[i], 96), 0.0)
+        rows_first[pl.ds(i * 16, 16), :] = jnp.where(low_q, 0.0, roll(high[i], 32))
+    for n, k in enumerate((0, 9)):
+        for i in range(8):
+            plane_ref[n, i] = folded_xy(l_ref, xr_ref, rows_first, rows_last, i + 1, k, gx, lane, sub)
+
+
+def zfold_send_kernel(plane_ref, ya_ref, yb_ref, run_ref, za_ref, zb_ref):
     za_ref[8:24] = run_ref[...]
-    gx = lax.axis_index("gx")
     even_z = lax.rem(lax.axis_index("gz"), 2) == 0
     lane, sub = iotas()
     slot = lane & 31
-    fold_rows(hl_ref, hh_ref, xr_ref, ya_ref, yb_ref, rows_first, rows_last, gx)
+    low_q = (lane & 32) == 0
+
+    def folded(n, i):
+        at = (i % 4) * 8 if n == 0 else 33 + 2 * (i % 4)
+        above, below = sides(row(ya_ref, at), row(yb_ref, at), "gy")
+        if i < 4:
+            above, below = roll(above, 32), roll(below, 96)
+        received = jnp.where(sub == 0, jnp.where(low_q, below, 0.0), jnp.where(low_q, 0.0, above))
+        return plane_ref[n, i] + jnp.where((sub == 0) | (sub == 7), received, 0.0)
+
     down = jnp.zeros((8, 128), F32)
     up = jnp.zeros((8, 128), F32)
     for i in range(8):
-        down = jnp.where(slot == i, roll(folded_xy(l_ref, xr_ref, rows_first, rows_last, i + 1, 0, gx, lane, sub), i), down)
-        up = jnp.where(slot == i, roll(folded_xy(l_ref, xr_ref, rows_first, rows_last, i + 1, 9, gx, lane, sub), i - 31), up)
+        down = jnp.where(slot == i, roll(folded(0, i), i), down)
+        up = jnp.where(slot == i, roll(folded(1, i), i - 31), up)
     za_ref[:8] = jnp.where(even_z, up, down)
     zb_ref[...] = jnp.where(even_z, down, up)
 
@@ -456,9 +477,10 @@
                 last = sum_ref[at : at + 8, 128:] + high
                 total_ref[at : at + 8, :128] = first + jnp.where(lane == 0, roll(from_below, -source), 0.0)
                 total_ref[at : at + 8, 128:] = last + jnp.where(lane == 127, roll(from_above, 127 - source), 0.0)
-        rows = pl.ds(p * 128, 128)
-        copies.append(pltpu.make_async_copy(total_ref.at[rows, :], out_ref.at[rows, :], sems.at[p]))
-        copies[p].start()
+            if i % 4 == 3:
+                rows = pl.ds(p * 128 + (i // 4) * 64, 64)
+                copies.append(pltpu.make_async_copy(total_ref.at[rows, :], out_ref.at[rows, :], sems.at[p * 2 + i // 4]))
+                copies[-1].start()
     for copy in copies:
         copy.wait()
 
@@ -532,13 +554,14 @@
     running = running + jnp.where(level_of >= 4, ya[40:56], 0.0)
     running = climb(running, "gx", 1, 7)
     parts = (local, edge_l, edge_h, xr, ya, yb)
-    za, zb = call(zfold_send_kernel, [(24, 128), (8, 128)], [(128, 128)] * 2, 7)(*parts, running)
+    (planes,) = call(zplane_kernel, [(2, 8, 8, 128)], [(128, 128)] * 2, 4)(*parts[:4])
+    za, zb = call(zfold_send_kernel, [(24, 128), (8, 128)], [], 4)(planes, ya, yb, running)
     za, zb = swap(za, "gz", 1), swap_odd(zb, "gz")
     smooth, tile = call(
         gather_kernel, [(256, 256), (64, 128)], [(128, 128), (128, 128), (2, 256, 128), (8, 8, 8, 128)], 7
     )(*parts, coarse_basis)
     (out,) = call(
-        post_kernel, [(256, 256)], [(256, 256)], 7, semaphores=(pltpu.SemaphoreType.DMA((2,)),), out_space=pltpu.HBM
+        post_kernel, [(256, 256)], [(256, 256)], 7, semaphores=(pltpu.SemaphoreType.DMA((4,)),), out_space=pltpu.HBM
     )(smooth, tile, za, zb, sep, running, ownsol)
     return out.reshape(residual.shape)
 

time: 56.5 us -> 56.4 us (level)
  transfers between devices with their start and end apart: 17 -> 17, of which waited for: 8 -> 8; matrix products, arithmetic and copies ran while one was open for 1% -> 1% of each run, Pallas kernels for 9% -> 10%
where the time goes in v10:
time: 56.4 us; the launch traced here: 56.3 us
  starting transfers between devices  26.4 us (47%)
  waiting for transfers between devices  20.6 us (37%)
  Pallas kernels  8.62 us (15%)
    ppermute x13, starting transfers between devices, swap(): lax.ppermute(value, axis, [(i, i ^ distance) for i in range(lax.axis_size...  19.7 us
    ppermute x4, waiting for transfers between devices, swap_odd(): lax.ppermute(value, axis, [(i, (i + 1 if i % 2 else i - 1) % count) for i...  12 us
    ppermute x13, waiting for transfers between devices, swap(): lax.ppermute(value, axis, [(i, i ^ distance) for i in range(lax.axis_size...  8.55 us
    ppermute x4, starting transfers between devices, swap_odd(): lax.ppermute(value, axis, [(i, (i + 1 if i % 2 else i - 1) % count) for i...  6.74 us
    pallas_call x1, Pallas kernels, work(): call(pre_kernel, [(8, 8, 8, 128), (32, 128), (16, 128), (16, 128)], [(2,...  1.84 us
    pallas_call x1, Pallas kernels, work(): call(points_kernel, [(10, 10, 8, 128), (10, 16, 128), (10, 16, 128), (56,...  1.38 us
    pallas_call x1, Pallas kernels, work(): call(middle_kernel, [(1696, 128)], [(16, 128)], 3)(modes, factors, eigen)  1.2 us
  transfers between devices with their start and end apart: 17, of which 8 were waited for; matrix products, arithmetic and copies ran while one was open for 1% of the time, Pallas kernels for 10%

profile of v10, /device:TPU:24, one launch (start us, length us, event | category | flops | bytes accessed | tf_op | source)
XLA Modules:
  0.0 56.3 jit_solution(16442055239341841176)
XLA Ops:
  0.0 1.8 %shard_map.64 = (f32[8,8,8,128]{3,2,1,0:T(8,128)S(1)}, f32[32,128]{1,0:T(8,128)S(1)}, f32[16,128]{1,0:T(8,128)S(1)}, f32[16,128]{1,0:T(8,128)S(1)}) custom-call(f32[256,256]{1,0:T(8,128)} %bitcast.16, f32[8,16,256]{2,1,0:T(8,128)} %bitcast.12, f32[8,8,8]{2,1,0:T(8,128)} %basis_ref.3, f32[16,16]{1,0:T(8,128)} %bitcast.17), custom_call_target="tpu_custom_call" | custom-call | tf_op jit(solution)/shard_map/pallas_call | solution.py:524
  1.8 3.4 %collective-permute-start.6 = (f32[16,128]{1,0:T(8,128)S(1)}, f32[16,128]{1,0:T(8,128)S(1)}, u32[]{:S(2)}, u32[]{:S(2)}) collective-permute-start(f32[16,128]{1,0:T(8,128)S(1)} %get-tuple-element.43), channel_id=1, source_target_pairs={{0,32},{16,48},{32,0},{48,16},{64,96},{80,112},{96,64},{112,80},{1... | collective-permute-start | bytes 24584 | tf_op jit(solution)/shard_map/ppermute | solution.py:504
  5.2 1.6 %collective-permute-done.6 = f32[16,128]{1,0:T(8,128)S(1)} collective-permute-done((f32[16,128]{1,0:T(8,128)S(1)}, f32[16,128]{1,0:T(8,128)S(1)}, u32[]{:S(2)}, u32[]{:S(2)}) %collective-permute-start.6) | collective-permute-done | bytes 8224 | tf_op jit(solution)/shard_map/ppermute | solution.py:504
  6.9 6.0 %collective-permute-start.7 = (f32[16,128]{1,0:T(8,128)S(1)}, f32[16,128]{1,0:T(8,128)S(1)}, u32[]{:S(2)}, u32[]{:S(2)}) collective-permute-start(f32[16,128]{1,0:T(8,128)S(1)} %select_add_fusion.3), channel_id=1, source_target_pairs={{0,96},{16,112},{32,64},{48,80},{64,32},{80,48},{96,0},{112,16},{1... | collective-permute-start | bytes 24584 | tf_op jit(solution)/shard_map/ppermute | solution.py:504
  12.9 1.6 %collective-permute-done.7 = f32[16,128]{1,0:T(8,128)S(1)} collective-permute-done((f32[16,128]{1,0:T(8,128)S(1)}, f32[16,128]{1,0:T(8,128)S(1)}, u32[]{:S(2)}, u32[]{:S(2)}) %collective-permute-start.7) | collective-permute-done | bytes 8224 | tf_op jit(solution)/shard_map/ppermute | solution.py:504
  14.6 1.3 %collective-permute-start.10 = (f32[16,128]{1,0:T(8,128)S(1)}, f32[16,128]{1,0:T(8,128)S(1)}, u32[]{:S(2)}, u32[]{:S(2)}) collective-permute-start(f32[16,128]{1,0:T(8,128)S(1)} %select_add_fusion.2), channel_id=1, source_target_pairs={{0,8},{1,9},{2,10},{3,11},{4,12},{5,13},{6,14},{7,15},{8,0},{9,1},... | collective-permute-start | bytes 24584 | tf_op jit(solution)/shard_map/ppermute | solution.py:504
  15.9 2.9 %collective-permute-start.9 = (f32[16,128]{1,0:T(8,128)S(1)}, f32[16,128]{1,0:T(8,128)S(1)}, u32[]{:S(2)}, u32[]{:S(2)}) collective-permute-start(f32[16,128]{1,0:T(8,128)S(1)} %select_add_fusion.2), channel_id=1, source_target_pairs={{0,12},{1,13},{2,14},{3,15},{4,8},{5,9},{6,10},{7,11},{8,4},{9,5},... | collective-permute-start | bytes 24584 | tf_op jit(solution)/shard_map/ppermute | solution.py:504
  18.7 0.2 shard_map.65
  18.9 1.6 %collective-permute-start.1 = (f32[8,128]{1,0:T(8,128)S(1)}, f32[8,128]{1,0:T(8,128)S(1)}, u32[]{:S(2)}, u32[]{:S(2)}) collective-permute-start(f32[8,128]{1,0:T(8,128)S(1)} %get-tuple-element.31), channel_id=1, source_target_pairs={{0,1},{1,0},{2,3},{3,2},{4,5},{5,4},{6,7},{7,6},{8,9},{9,8},{10,11... | collective-permute-start | bytes 12296 | tf_op jit(solution)/shard_map/ppermute | solution.py:504
  20.5 2.3 %collective-permute-start.2 = (f32[8,128]{1,0:T(8,128)S(1)}, f32[8,128]{1,0:T(8,128)S(1)}, u32[]{:S(2)}, u32[]{:S(2)}) collective-permute-start(f32[8,128]{1,0:T(8,128)S(1)} %get-tuple-element.32), channel_id=1, source_target_pairs={{0,15},{1,2},{2,1},{3,4},{4,3},{5,6},{6,5},{7,8},{8,7},{9,10},{10,... | collective-permute-start | bytes 12296 | tf_op jit(solution)/shard_map/ppermute | solution.py:509
  22.8 3.4 %collective-permute-done.2.zb_ref = f32[8,128]{1,0:T(8,128)S(1)} collective-permute-done((f32[8,128]{1,0:T(8,128)S(1)}, f32[8,128]{1,0:T(8,128)S(1)}, u32[]{:S(2)}, u32[]{:S(2)}) %collective-permute-start.2) | collective-permute-done | bytes 4128 | tf_op jit(solution)/shard_map/ppermute | solution.py:509
  26.2 0.2 shard_map.68
  26.4 1.1 %collective-permute-start.3 = (f32[56,128]{1,0:T(8,128)S(1)}, f32[56,128]{1,0:T(8,128)S(1)}, u32[]{:S(2)}, u32[]{:S(2)}) collective-permute-start(f32[56,128]{1,0:T(8,128)S(1)} %get-tuple-element.36), channel_id=1, source_target_pairs={{0,16},{16,0},{32,48},{48,32},{64,80},{80,64},{96,112},{112,96},{1... | collective-permute-start | bytes 86024 | tf_op jit(solution)/shard_map/ppermute | solution.py:504
  27.5 3.7 %collective-permute-start.4 = (f32[56,128]{1,0:T(8,128)S(1)}, f32[56,128]{1,0:T(8,128)S(1)}, u32[]{:S(2)}, u32[]{:S(2)}) collective-permute-start(f32[56,128]{1,0:T(8,128)S(1)} %get-tuple-element.37), channel_id=1, source_target_pairs={{0,112},{16,32},{32,16},{48,64},{64,48},{80,96},{96,80},{112,0},{1... | collective-permute-start | bytes 86024 | tf_op jit(solution)/shard_map/ppermute | solution.py:509
  31.3 3.3 %collective-permute-start.11 = (f32[16,128]{1,0:T(8,128)S(1)}, f32[16,128]{1,0:T(8,128)S(1)}, u32[]{:S(2)}, u32[]{:S(2)}) collective-permute-start(f32[16,128]{1,0:T(8,128)S(1)} %fusion.1), channel_id=1, source_target_pairs={{0,3},{1,2},{2,1},{3,0},{4,7},{5,6},{6,5},{7,4},{8,11},{9,10},{10,... | collective-permute-start | bytes 24584 | tf_op jit(solution)/shard_map/ppermute | solution.py:504
  34.6 1.1 %shard_map.67 = (f32[1696,128]{1,0:T(8,128)S(1)}, f32[320,128]{1,0:T(8,128)S(1)}) custom-call(f32[8,8,8,128]{3,2,1,0:T(8,128)S(1)} %get-tuple-element.28.core_ref, f32[2,8,8,128]{3,2,1,0:T(8,128)S(1)} %get-tuple-element.30.ends_ref, f32[8,128]{1,0:T(8,128)S(1)} %collective-permute-done.1.za_ref, f32[8,128]{1,0:T(8,128)S(1)} %collective-permute-done.2.zb_ref, ...), custom_call_target="tpu_custom_call" | custom-call | tf_op jit(solution)/shard_map/pallas_call | solution.py:542
  35.7 0.4 shard_map.69.u_ref
  36.1 1.2 %shard_map.70.u_ref = f32[1696,128]{1,0:T(8,128)S(1)} custom-call(f32[1696,128]{1,0:T(8,128)S(1)} %shard_map.69.u_ref, f32[848,128]{1,0:T(8,128)S(1)} %get-tuple-element.33.s, f32[3,10,1,128]{3,2,1,0:T(1,128)S(1)} %get-tuple-element.38.eig_ref), custom_call_target="tpu_custom_call" | custom-call | tf_op jit(solution)/shard_map/pallas_call | solution.py:544
  37.3 1.4 %shard_map.71 = (f32[10,10,8,128]{3,2,1,0:T(8,128)S(1)}, f32[10,16,128]{2,1,0:T(8,128)S(1)}, f32[10,16,128]{2,1,0:T(8,128)S(1)}, f32[56,128]{1,0:T(8,128)S(1)}) custom-call(f32[1696,128]{1,0:T(8,128)S(1)} %shard_map.70.u_ref, f32[848,128]{1,0:T(8,128)S(1)} %get-tuple-element.33.s), custom_call_target="tpu_custom_call" | custom-call | tf_op jit(solution)/shard_map/pallas_call | solution.py:548
  38.8 1.1 %collective-permute-done.5.xr_ref = f32[56,128]{1,0:T(8,128)S(1)} collective-permute-done((f32[56,128]{1,0:T(8,128)S(1)}, f32[56,128]{1,0:T(8,128)S(1)}, u32[]{:S(2)}, u32[]{:S(2)}) %collective-permute-start.5) | collective-permute-done | bytes 28704 | tf_op jit(solution)/shard_map/ppermute | solution.py:504
  39.9 0.1 shard_map.72
  40.1 3.8 %collective-permute-done.12.ya_ref = f32[56,128]{1,0:T(8,128)S(1)} collective-permute-done((f32[56,128]{1,0:T(8,128)S(1)}, f32[56,128]{1,0:T(8,128)S(1)}, u32[]{:S(2)}, u32[]{:S(2)}) %collective-permute-start.12) | collective-permute-done | bytes 28704 | tf_op jit(solution)/shard_map/ppermute | solution.py:504
  44.1 0.6 %collective-permute-start.13 = (f32[48,128]{1,0:T(8,128)S(1)}, f32[48,128]{1,0:T(8,128)S(1)}, u32[]{:S(2)}, u32[]{:S(2)}) collective-permute-start(f32[48,128]{1,0:T(8,128)S(1)} %get-tuple-element.45), channel_id=1, source_target_pairs={{0,112},{16,32},{32,16},{48,64},{64,48},{80,96},{96,80},{112,0},{1... | collective-permute-start | bytes 73736 | tf_op jit(solution)/shard_map/ppermute | solution.py:509
  44.7 0.2 shard_map.74.plane_ref
  44.9 0.3 collective-permute-done.14
  45.3 3.9 %collective-permute-done.13.yb_ref = f32[48,128]{1,0:T(8,128)S(1)} collective-permute-done((f32[48,128]{1,0:T(8,128)S(1)}, f32[48,128]{1,0:T(8,128)S(1)}, u32[]{:S(2)}, u32[]{:S(2)}) %collective-permute-start.13) | collective-permute-done | bytes 24608 | tf_op jit(solution)/shard_map/ppermute | solution.py:509
  49.2 0.2 shard_map.75
  49.4 0.1 collective-permute-start.15
  49.5 0.2 collective-permute-start.16
  49.7 0.9 %shard_map.73 = (f32[256,256]{1,0:T(8,128)S(1)}, f32[64,128]{1,0:T(8,128)S(1)}) custom-call(f32[10,10,8,128]{3,2,1,0:T(8,128)S(1)} %get-tuple-element.39.l_ref, f32[10,16,128]{2,1,0:T(8,128)S(1)} %get-tuple-element.40.hl_ref, f32[10,16,128]{2,1,0:T(8,128)S(1)} %get-tuple-element.41.hh_ref, f32[56,128]{1,0:T(8,128)S(1)} %collective-permute-done.5.xr_ref, ...), custom_call_target="tpu_custom_call" | custom-call | tf_op jit(solution)/shard_map/pallas_call | solution.py:560
  50.7 4.7 %collective-permute-done.16.zb_ref = f32[8,128]{1,0:T(8,128)S(1)} collective-permute-done((f32[8,128]{1,0:T(8,128)S(1)}, f32[8,128]{1,0:T(8,128)S(1)}, u32[]{:S(2)}, u32[]{:S(2)}) %collective-permute-start.16) | collective-permute-done | bytes 4128 | tf_op jit(solution)/shard_map/ppermute | solution.py:509
  55.3 0.9 %shard_map.76 = f32[256,256]{1,0:T(8,128)} custom-call(f32[256,256]{1,0:T(8,128)S(1)} %get-tuple-element.46.sum_ref, f32[64,128]{1,0:T(8,128)S(1)} %get-tuple-element.47.tile_ref, f32[24,128]{1,0:T(8,128)S(1)} %collective-permute-done.15.za_ref, f32[8,128]{1,0:T(8,128)S(1)} %collective-permute-done.16.zb_ref, f32[8,16,256]{2,1,0:T(8,128)S(1)} %bitcast.13, ...), custom_call_target="tpu_custom_call" | custom-call | tf_op jit(solution)/shard_map/pallas_call | solution.py:563
  (35 shorter events, 0.7 us)
Async XLA Ops:
  1.8 5.0 %collective-permute-start.6 = (f32[16,128]{1,0:T(8,128)S(1)}, f32[16,128]{1,0:T(8,128)S(1)}, u32[]{:S(2)}, u32[]{:S(2)}) collective-permute-start(f32[16,128]{1,0:T(8,128)S(1)} %get-tuple-element.43), channel_id=1, source_target_pairs={{0,32},{16,48},{32,0},{48,16},{64,96},{80,112},{96,64},{112,80},{1... | collective-permute-start | bytes 24584 | tf_op jit(solution)/shard_map/ppermute | solution.py:504
  5.2 13.5 %collective-permute-start = (f32[32,128]{1,0:T(8,128)S(1)}, f32[32,128]{1,0:T(8,128)S(1)}, u32[]{:S(2)}, u32[]{:S(2)}) collective-permute-start(f32[32,128]{1,0:T(8,128)S(1)} %get-tuple-element.29), channel_id=1, source_target_pairs={{0,128},{128,0},{1,129},{129,1},{2,130},{130,2},{3,131},{131,3},{4... | collective-permute-start | bytes 49160 | tf_op jit(solution)/shard_map/ppermute | solution.py:504
  6.9 7.6 %collective-permute-start.7 = (f32[16,128]{1,0:T(8,128)S(1)}, f32[16,128]{1,0:T(8,128)S(1)}, u32[]{:S(2)}, u32[]{:S(2)}) collective-permute-start(f32[16,128]{1,0:T(8,128)S(1)} %select_add_fusion.3), channel_id=1, source_target_pairs={{0,96},{16,112},{32,64},{48,80},{64,32},{80,48},{96,0},{112,16},{1... | collective-permute-start | bytes 24584 | tf_op jit(solution)/shard_map/ppermute | solution.py:504
  14.6 16.6 %collective-permute-start.10 = (f32[16,128]{1,0:T(8,128)S(1)}, f32[16,128]{1,0:T(8,128)S(1)}, u32[]{:S(2)}, u32[]{:S(2)}) collective-permute-start(f32[16,128]{1,0:T(8,128)S(1)} %select_add_fusion.2), channel_id=1, source_target_pairs={{0,8},{1,9},{2,10},{3,11},{4,12},{5,13},{6,14},{7,15},{8,0},{9,1},... | collective-permute-start | bytes 24584 | tf_op jit(solution)/shard_map/ppermute | solution.py:504
  15.8 15.3 %collective-permute-start.8 = (f32[16,128]{1,0:T(8,128)S(1)}, f32[16,128]{1,0:T(8,128)S(1)}, u32[]{:S(2)}, u32[]{:S(2)}) collective-permute-start(f32[16,128]{1,0:T(8,128)S(1)} %select_add_fusion.2), channel_id=1, source_target_pairs={{0,4},{1,5},{2,6},{3,7},{4,0},{5,1},{6,2},{7,3},{8,12},{9,13},{10,... | collective-permute-start | bytes 24584 | tf_op jit(solution)/shard_map/ppermute | solution.py:504
  15.9 15.3 %collective-permute-start.9 = (f32[16,128]{1,0:T(8,128)S(1)}, f32[16,128]{1,0:T(8,128)S(1)}, u32[]{:S(2)}, u32[]{:S(2)}) collective-permute-start(f32[16,128]{1,0:T(8,128)S(1)} %select_add_fusion.2), channel_id=1, source_target_pairs={{0,12},{1,13},{2,14},{3,15},{4,8},{5,9},{6,10},{7,11},{8,4},{9,5},... | collective-permute-start | bytes 24584 | tf_op jit(solution)/shard_map/ppermute | solution.py:504
  18.9 3.9 %collective-permute-start.1 = (f32[8,128]{1,0:T(8,128)S(1)}, f32[8,128]{1,0:T(8,128)S(1)}, u32[]{:S(2)}, u32[]{:S(2)}) collective-permute-start(f32[8,128]{1,0:T(8,128)S(1)} %get-tuple-element.31), channel_id=1, source_target_pairs={{0,1},{1,0},{2,3},{3,2},{4,5},{5,4},{6,7},{7,6},{8,9},{9,8},{10,11... | collective-permute-start | bytes 12296 | tf_op jit(solution)/shard_map/ppermute | solution.py:504
  20.5 5.7 %collective-permute-start.2 = (f32[8,128]{1,0:T(8,128)S(1)}, f32[8,128]{1,0:T(8,128)S(1)}, u32[]{:S(2)}, u32[]{:S(2)}) collective-permute-start(f32[8,128]{1,0:T(8,128)S(1)} %get-tuple-element.32), channel_id=1, source_target_pairs={{0,15},{1,2},{2,1},{3,4},{4,3},{5,6},{6,5},{7,8},{8,7},{9,10},{10,... | collective-permute-start | bytes 12296 | tf_op jit(solution)/shard_map/ppermute | solution.py:509
  26.2 8.4 %copy-start.2 = (bf16[1,1,1,3,10,10,128]{6,3,5,4,2,1,0:T(4,128)(2,1)S(1)}, bf16[1,1,1,3,10,10,128]{6,3,5,4,2,1,0:T(4,128)(2,1)}, u32[]{:S(2)}) copy-start(bf16[1,1,1,3,10,10,128]{6,3,5,4,2,1,0:T(4,128)(2,1)} %param.7) | copy-start | bytes 230404
  26.4 9.3 %collective-permute-start.3 = (f32[56,128]{1,0:T(8,128)S(1)}, f32[56,128]{1,0:T(8,128)S(1)}, u32[]{:S(2)}, u32[]{:S(2)}) collective-permute-start(f32[56,128]{1,0:T(8,128)S(1)} %get-tuple-element.36), channel_id=1, source_target_pairs={{0,16},{16,0},{32,48},{48,32},{64,80},{80,64},{96,112},{112,96},{1... | collective-permute-start | bytes 86024 | tf_op jit(solution)/shard_map/ppermute | solution.py:504
  27.5 8.2 %collective-permute-start.4 = (f32[56,128]{1,0:T(8,128)S(1)}, f32[56,128]{1,0:T(8,128)S(1)}, u32[]{:S(2)}, u32[]{:S(2)}) collective-permute-start(f32[56,128]{1,0:T(8,128)S(1)} %get-tuple-element.37), channel_id=1, source_target_pairs={{0,112},{16,32},{32,16},{48,64},{64,48},{80,96},{96,80},{112,0},{1... | collective-permute-start | bytes 86024 | tf_op jit(solution)/shard_map/ppermute | solution.py:509
  31.2 3.4 %copy-start.3 = (f32[1,1,1,3,10,128]{5,2,4,3,1,0:T(1,128)S(1)}, f32[1,1,1,3,10,128]{5,2,4,3,1,0:T(1,128)}, u32[]{:S(2)}) copy-start(f32[1,1,1,3,10,128]{5,2,4,3,1,0:T(1,128)} %param.8) | copy-start | bytes 46084
  31.3 7.5 %collective-permute-start.11 = (f32[16,128]{1,0:T(8,128)S(1)}, f32[16,128]{1,0:T(8,128)S(1)}, u32[]{:S(2)}, u32[]{:S(2)}) collective-permute-start(f32[16,128]{1,0:T(8,128)S(1)} %fusion.1), channel_id=1, source_target_pairs={{0,3},{1,2},{2,1},{3,0},{4,7},{5,6},{6,5},{7,4},{8,11},{9,10},{10,... | collective-permute-start | bytes 24584 | tf_op jit(solution)/shard_map/ppermute | solution.py:504
  38.7 1.2 %collective-permute-start.5 = (f32[56,128]{1,0:T(8,128)S(1)}, f32[56,128]{1,0:T(8,128)S(1)}, u32[]{:S(2)}, u32[]{:S(2)}) collective-permute-start(f32[56,128]{1,0:T(8,128)S(1)} %get-tuple-element.42), channel_id=1, source_target_pairs={{0,128},{128,0},{1,129},{129,1},{2,130},{130,2},{3,131},{131,3},{4... | collective-permute-start | bytes 86024 | tf_op jit(solution)/shard_map/ppermute | solution.py:504
  40.0 3.9 %collective-permute-start.12 = (f32[56,128]{1,0:T(8,128)S(1)}, f32[56,128]{1,0:T(8,128)S(1)}, u32[]{:S(2)}, u32[]{:S(2)}) collective-permute-start(f32[56,128]{1,0:T(8,128)S(1)} %get-tuple-element.44), channel_id=1, source_target_pairs={{0,16},{16,0},{32,48},{48,32},{64,80},{80,64},{96,112},{112,96},{1... | collective-permute-start | bytes 86024 | tf_op jit(solution)/shard_map/ppermute | solution.py:504
  44.1 1.2 %collective-permute-start.14 = (f32[16,128]{1,0:T(8,128)S(1)}, f32[16,128]{1,0:T(8,128)S(1)}, u32[]{:S(2)}, u32[]{:S(2)}) collective-permute-start(f32[16,128]{1,0:T(8,128)S(1)} %fusion.2), channel_id=1, source_target_pairs={{0,128},{128,0},{1,129},{129,1},{2,130},{130,2},{3,131},{131,3},{4... | collective-permute-start | bytes 24584 | tf_op jit(solution)/shard_map/ppermute | solution.py:504
  44.1 5.1 %collective-permute-start.13 = (f32[48,128]{1,0:T(8,128)S(1)}, f32[48,128]{1,0:T(8,128)S(1)}, u32[]{:S(2)}, u32[]{:S(2)}) collective-permute-start(f32[48,128]{1,0:T(8,128)S(1)} %get-tuple-element.45), channel_id=1, source_target_pairs={{0,112},{16,32},{32,16},{48,64},{64,48},{80,96},{96,80},{112,0},{1... | collective-permute-start | bytes 73736 | tf_op jit(solution)/shard_map/ppermute | solution.py:509
  45.3 4.4 %copy-start.1 = (f32[8,8,8]{2,1,0:T(8,128)S(1)}, f32[8,8,8]{2,1,0:T(8,128)}, u32[]{:S(2)}) copy-start(f32[8,8,8]{2,1,0:T(8,128)} %basis_ref.3) | copy-start | bytes 6148
  49.4 5.9 %collective-permute-start.15 = (f32[24,128]{1,0:T(8,128)S(1)}, f32[24,128]{1,0:T(8,128)S(1)}, u32[]{:S(2)}, u32[]{:S(2)}) collective-permute-start(f32[24,128]{1,0:T(8,128)S(1)} %get-tuple-element.48), channel_id=1, source_target_pairs={{0,1},{1,0},{2,3},{3,2},{4,5},{5,4},{6,7},{7,6},{8,9},{9,8},{10,11... | collective-permute-start | bytes 36872 | tf_op jit(solution)/shard_map/ppermute | solution.py:504
  49.5 5.8 %copy-start = (f32[1,1,1,8,16,256]{5,4,3,2,1,0:T(8,128)S(1)}, f32[1,1,1,8,16,256]{5,4,3,2,1,0:T(8,128)}, u32[]{:S(2)}) copy-start(f32[1,1,1,8,16,256]{5,4,3,2,1,0:T(8,128)} %param.11) | copy-start | bytes 393220
  49.5 5.8 %collective-permute-start.16 = (f32[8,128]{1,0:T(8,128)S(1)}, f32[8,128]{1,0:T(8,128)S(1)}, u32[]{:S(2)}, u32[]{:S(2)}) collective-permute-start(f32[8,128]{1,0:T(8,128)S(1)} %get-tuple-element.49), channel_id=1, source_target_pairs={{0,15},{1,2},{2,1},{3,4},{4,3},{5,6},{6,5},{7,8},{8,7},{9,10},{10,... | collective-permute-start | bytes 12296 | tf_op jit(solution)/shard_map/ppermute | solution.py:509
